TPU v7x, 128 devices: a whole 4x4x4 slice. The times are simulated.
128 devices in a mesh: dp: 32 (over x, y, core), tensor: 4 (over z).
Axes of the slice: x: 4, y: 4, z: 4, core: 2. Of those that a mesh axis runs over, the one named last changes fastest.
Arguments:
- memory: bfloat16 [49152, 1280], P('dp'), may hold values from -6 to 6
- hidden: bfloat16 [49152, 2560], P('dp', 'tensor'), may hold values from -6 to 6
- grad_out: bfloat16 [49152, 2560], P('dp', 'tensor'), may hold values from -6 to 6
- key_weight: bfloat16 [1280, 2560], P('dp', 'tensor'), may hold values from -0.15625 to 0.15625
- value_weight: bfloat16 [1280, 2560], P('dp', 'tensor'), may hold values from -0.15625 to 0.15625
- row_ids: int32 [49152, 5], P('dp'), may hold values from 0 to 262143, as said below
- embed_table: float32 [262144, 256], P(('dp', 'tensor')), may hold values from -6 to 6
- first_moment: float32 [262144, 256], P(('dp', 'tensor')), may hold values from -0.6 to 0.6
- second_moment: float32 [262144, 256], P(('dp', 'tensor')), may hold values from 0.001 to 0.1
Outputs:
- key_weight_grad: float32 [1280, 2560], P('dp', 'tensor')
- value_weight_grad: float32 [1280, 2560], P('dp', 'tensor')
- new_table: float32 [262144, 256], P(('dp', 'tensor'))
- new_first: float32 [262144, 256], P(('dp', 'tensor'))
- new_second: float32 [262144, 256], P(('dp', 'tensor'))
Inputs may be any that keep to these rules, and one draw needn't show every extreme that they name: `row_ids`: the table's rows fall into 128 owners of 2048 consecutive rows each. Taking the tokens in aligned blocks of 384 consecutive tokens with all their 5 ids, at most 45 ids of one block fall in one owner's rows, and in every block some owner gets exactly 45 of them.
All inputs are finite; a program needn't handle non-finite values.
Results may differ from a plain program's by a relative error of at most 0.0043.
Values may be sent and summed in bfloat16 or wider, within the bound.
No kernel may reach another device: no remote copies, remote signals or barrier semaphores. Data moves between devices by JAX's collectives and lax.ppermute only.
A program may use at most 128 MiB of HBM per device.

v0:
```python
import math

import jax
import jax.numpy as jnp
from jax import lax
from jax.sharding import PartitionSpec as P

D = 2560


beta_one = 0.9
beta_two = 0.999
learn_rate = 0.01
adam_eps = 1e-08
norm_eps = 1e-06
correct_one = 0.9999734386011124
correct_two = 0.0952078528863


def in_one_piece(arrays, axis, dim, along):
    widths = [a.shape[along] for a in arrays]
    both = jnp.concatenate(arrays, axis=along)
    whole = lax.all_gather(both, axis, axis=dim, tiled=True)
    return tuple(jnp.split(whole, [sum(widths[:k]) for k in range(1, len(widths))], axis=along))


def sent_to_all(shard, axis):
    length = lax.axis_size(axis)
    return lax.all_to_all(
        jnp.broadcast_to(shard[None], (length, *shard.shape)), axis, 0, 0, tiled=True
    )


def over_copies(shard, axis):
    return sent_to_all(shard, axis).sum(axis=0)


def packed_total(arrays, axis):
    vector, at, done = (jnp.concatenate([a.reshape(-1) for a in arrays]), 0, [])
    subtotal = over_copies(vector, axis)
    for a in arrays:
        done.append(subtotal[at : at + a.size].reshape(a.shape))
        at += a.size
    return tuple(done)


def split_up(shard, dim, length):
    lengths = shard.shape
    tiles = shard.reshape(*lengths[:dim], length, lengths[dim] // length, *lengths[dim + 1 :])
    return jnp.moveaxis(tiles, dim, 0)


def sum_at_owner(shard, axis, dim):
    length = lax.axis_size(axis)
    tiles = lax.all_to_all(split_up(shard, dim, length), axis, 0, 0, tiled=True)
    return jnp.sum(tiles.astype(jnp.float32), axis=0)


def adam_update(table_grad, embed_table, first_moment, second_moment):
    new_first = beta_one * first_moment + (1.0 - beta_one) * table_grad
    new_second = beta_two * second_moment + (1.0 - beta_two) * table_grad * table_grad
    stepped = new_first / correct_one / (jnp.sqrt(new_second / correct_two) + adam_eps)
    return (embed_table - learn_rate * stepped, new_first, new_second)


def body(
    memory,
    hidden,
    grad_out,
    key_weight,
    value_weight,
    row_ids,
    embed_table,
    first_moment,
    second_moment,
):
    key_full, value_full = in_one_piece((key_weight, value_weight), "dp", 0, 1)
    key_proj = jnp.dot(memory, key_full, preferred_element_type=jnp.float32)
    value_proj = jnp.dot(memory, value_full, preferred_element_type=jnp.float32)
    hidden_float = hidden.astype(jnp.float32)
    grad_float = grad_out.astype(jnp.float32)
    root_width = math.sqrt(D)
    square_sum, cross_sum, output_sum = packed_total(
        (
            jnp.sum(key_proj * key_proj, axis=1, keepdims=True),
            jnp.sum(hidden_float * key_proj, axis=1, keepdims=True),
            jnp.sum(grad_float * value_proj, axis=1, keepdims=True),
        ),
        "tensor",
    )
    key_scale = jnp.sqrt(square_sum / D + norm_eps)
    gate_score = cross_sum / (key_scale * root_width)
    gate_value = jax.nn.sigmoid(gate_score)
    gate_grad = gate_value * (1.0 - gate_value) * output_sum
    key_grad = gate_grad * (
        hidden_float / (key_scale * root_width)
        - gate_score * key_proj / (D * key_scale * key_scale)
    )
    value_grad = gate_value * grad_float
    both_grads = jnp.concatenate(
        [key_grad.astype(jnp.bfloat16), value_grad.astype(jnp.bfloat16)], axis=1
    )
    width_local = key_full.shape[1]
    dp_count = lax.axis_size("dp")
    tensor_count = lax.axis_size("tensor")
    weight_grads = sum_at_owner(
        lax.dot_general(
            memory, both_grads, (((0,), (0,)), ((), ())), preferred_element_type=jnp.float32
        ).astype(jnp.bfloat16),
        "dp",
        0,
    )
    key_weight_grad = weight_grads[:, :width_local]
    value_weight_grad = weight_grads[:, width_local:]
    both_full = jnp.concatenate([key_full, value_full], axis=1)
    block_rows = memory.shape[0] // tensor_count
    memory_grad = sum_at_owner(
        lax.dot_general(
            both_grads, both_full, (((1,), (1,)), ((), ())), preferred_element_type=jnp.float32
        ).astype(jnp.bfloat16),
        "tensor",
        0,
    ).astype(jnp.bfloat16)
    row_width = embed_table.shape[1]
    rows_dev = embed_table.shape[0]
    pieces = memory_grad.reshape(-1, row_width)
    entries = pieces.shape[0]
    my_ids = lax.dynamic_slice_in_dim(
        row_ids, lax.axis_index("tensor") * block_rows, block_rows, 0
    ).reshape(-1)
    owners = dp_count * tensor_count
    capacity = max(2, 3 * entries // owners)
    owner_of = my_ids // rows_dev
    local_row = my_ids % rows_dev
    owner_hits = (owner_of[:, None] == jnp.arange(owners, dtype=jnp.int32)[None, :]).astype(
        jnp.bfloat16
    )
    earlier = (jnp.arange(entries)[None, :] < jnp.arange(entries)[:, None]).astype(jnp.bfloat16)
    before_counts = jnp.dot(earlier, owner_hits, preferred_element_type=jnp.float32)
    slot_rank = jnp.sum(before_counts * owner_hits.astype(jnp.float32), axis=1).astype(jnp.int32)
    slot_index = owner_of * capacity + slot_rank
    send_rows = jnp.zeros((owners * capacity, row_width), jnp.bfloat16).at[slot_index].set(pieces)
    send_ids = jnp.full((owners * capacity,), rows_dev, jnp.int32).at[slot_index].set(local_row)
    got_rows, got_ids = (
        lax.all_to_all(
            send_rows.reshape(owners, capacity, row_width),
            ("dp", "tensor"),
            split_axis=0,
            concat_axis=0,
            tiled=True,
        ),
        lax.all_to_all(
            send_ids.reshape(owners, capacity),
            ("dp", "tensor"),
            split_axis=0,
            concat_axis=0,
            tiled=True,
        ),
    )
    table_grad = (
        jnp.zeros((rows_dev, row_width), jnp.float32)
        .at[got_ids.reshape(-1)]
        .add(got_rows.reshape(-1, row_width).astype(jnp.float32), mode="drop")
    )
    new_table, new_first, new_second = adam_update(
        table_grad, embed_table, first_moment, second_moment
    )
    return (key_weight_grad, value_weight_grad, new_table, new_first, new_second)


def solution(mesh):
    return jax.shard_map(
        body,
        mesh=mesh,
        in_specs=(
            P("dp", None),
            P("dp", "tensor"),
            P("dp", "tensor"),
            P("dp", "tensor"),
            P("dp", "tensor"),
            P("dp", None),
            P(("dp", "tensor"), None),
            P(("dp", "tensor"), None),
            P(("dp", "tensor"), None),
        ),
        out_specs=(
            P("dp", "tensor"),
            P("dp", "tensor"),
            P(("dp", "tensor"), None),
            P(("dp", "tensor"), None),
            P(("dp", "tensor"), None),
        ),
        check_vma=False,
    )
```

profile of v0, /device:TPU:1, one launch (start us, length us, event | category | flops | bytes accessed | tf_op | source)
XLA Modules:
  0.0 305.5 jit_solution(6599306238760708099)
XLA Ops:
  7.2 0.0 copy-start
  7.2 0.0 all-gather.2.cloned.1.call-start
  7.2 1.5 pad_maximum_fusion.3
  8.7 0.0 all-gather.2.cloned.1.call-update
  8.8 0.1 copy.33
  8.9 0.2 reshape.197
  9.1 0.2 reshape.198
  9.4 1.8 fusion.16
  11.1 2.7 copy.30
  13.8 4.0 %copy.31 = bf16[1536,640]{0,1:T(8,128)(2,1)} copy(bf16[1536,640]{1,0:T(8,128)(2,1)} %param.11) | data formatting | bytes 3932160 | tf_op args[2]
  17.8 41.9 %all-gather.2.cloned.1.call-done = bf16[1280,1280]{1,0:T(8,128)(2,1)} async-done(((bf16[40,1280]{1,0:T(8,128)(2,1)}), bf16[1280,1280]{1,0:T(8,128)(2,1)}) %all-gather.2.cloned.1.call-update) | async-done | bytes 3276816 | tf_op jit(solution)/shard_map/all_gather | solution.py:23
  59.8 6.1 %fusion.5 = f32[1536]{0:T(1024)S(1)} fusion(bf16[1536,640]{0,1:T(8,128)(2,1)} %copy.31, bf16[1536,1280]{1,0:T(8,128)(2,1)} %param.9, bf16[1280,1280]{1,0:T(8,128)(2,1)} %all-gather.2.cloned.1.call-done), kind=kOutput, calls=%fused_computation.16 | convolution fusion | flops 2519529984 | bytes 7542784 | tf_op jit(solution)/shard_map/dot_general | solution.py:79
  65.9 4.7 %fusion.7 = (f32[1536]{0:T(1024)S(1)}, f32[1536]{0:T(1024)S(1)}, f32[640,1536]{1,0:T(8,128)}) fusion(bf16[1536,640]{0,1:T(8,128)(2,1)S(1)} %copy.30, bf16[1536,1280]{1,0:T(8,128)(2,1)S(1)} %copy-done.5, bf16[1280,1280]{1,0:T(8,128)(2,1)S(1)} %copy-done.6), kind=kOutput, calls=%fused_computation.21 | convolution fusion | flops 2521494528 | bytes 11481088 | tf_op jit(solution)/shard_map/dot_general | solution.py:78
  70.7 0.7 broadcast_in_dim.6
  71.3 4.1 %all-to-all-start = ((f32[4,1,4608]{2,1,0:T(1,128)}), f32[4,1,4608]{2,1,0:T(1,128)S(1)}, u32[]{:S(2)}, u32[]{:S(2)}) async-start(f32[4,1,4608]{2,1,0:T(1,128)} %broadcast_in_dim.6), calls=%async_computation | async-start | bytes 147456 | tf_op jit(solution)/shard_map/all_to_all | solution.py:29
  75.5 0.1 fusion.28
  75.5 10.0 %scatter_custom_fusion = s32[5760]{0:T(1024)S(1)} fusion(s32[1920]{0:T(1024)S(1)} %fusion.28, s32[1920]{0:T(1024)S(1)} %get-tuple-element.18, s32[]{:T(128)} %constant.23.clone.1), kind=kCustom, calls=%fused_computation.53 | custom fusion | bytes 23044 | tf_op jit(solution)/shard_map/scatter | solution.py:143
  85.5 0.8 all_to_all.21
  86.4 0.0 all-to-all-done
  86.4 8.0 %all-to-all-start.2 = ((s32[128,1,45]{2,1,0:T(1,128)}), s32[128,1,45]{2,1,0:T(1,128)S(1)}, u32[]{:S(2)}, u32[]{:S(2)}) async-start(s32[128,1,45]{2,1,0:T(1,128)} %bitcast.4), calls=%async_computation.2 | async-start | bytes 131072 | tf_op jit(solution)/shard_map/all_to_all | solution.py:152
  94.4 0.1 reduce_sum.69
  94.5 4.1 %fusion.4 = (bf16[1536,640]{0,1:T(8,128)(2,1)S(1)}, bf16[1536,640]{0,1:T(8,128)(2,1)S(1)}) fusion(bf16[1536,640]{0,1:T(8,128)(2,1)S(1)} %copy.30, f32[640,1536]{1,0:T(8,128)} %get-tuple-element.20, f32[1536]{0:T(1024)S(1)} %get-tuple-element.15, f32[1536]{0:T(1024)S(1)} %get-tuple-element.17, f32[1536]{0:T(1024)S(1)} %get-tuple-element.14, ...), kind=kLoop, calls=%fused_computation.15 | loop fusion | flops 9830400 | bytes 11827200 | tf_op jit(solution)/shard_map/convert_element_type | solution.py:101
  98.6 0.0 copy-start.2
  98.6 0.0 copy-start.4
  98.6 1.2 copy-done.2
  99.8 0.6 copy-done.4
  100.5 6.8 %convolution_convert_fusion = bf16[1536,1280]{1,0:T(8,128)(2,1)} fusion(bf16[1280,1280]{1,0:T(8,128)(2,1)S(1)} %copy-done.7, bf16[1536,640]{0,1:T(8,128)(2,1)S(1)} %get-tuple-element.22, bf16[1536,640]{0,1:T(8,128)(2,1)S(1)} %get-tuple-element.21), kind=kOutput, calls=%fused_computation.5 | convolution fusion | flops 5042995200 | bytes 11141120 | tf_op jit(solution)/shard_map/dot_general | solution.py:118
  107.3 4.9 %all-to-all-start.3 = ((bf16[4,384,1280]{2,1,0:T(8,128)(2,1)}), bf16[4,384,1280]{2,1,0:T(8,128)(2,1)}, u32[]{:S(2)}, u32[]{:S(2)}) async-start(bf16[4,384,1280]{2,1,0:T(8,128)(2,1)} %bitcast.23), calls=%async_computation.3 | async-start | bytes 7864320 | tf_op jit(solution)/shard_map/all_to_all | solution.py:55
  112.2 8.9 %convolution_convert_fusion.1 = bf16[1280,1280]{0,1:T(8,128)(2,1)} fusion(bf16[1536,1280]{1,0:T(8,128)(2,1)} %param.9, bf16[1536,640]{0,1:T(8,128)(2,1)} %copy-done.4, bf16[1536,640]{0,1:T(8,128)(2,1)S(1)} %copy-done.3), kind=kOutput, calls=%fused_computation.6 | convolution fusion | flops 5042667520 | bytes 11141120 | tf_op jit(solution)/shard_map/dot_general | solution.py:107
  121.1 36.6 %all-to-all-done.3 = bf16[4,384,1280]{2,1,0:T(8,128)(2,1)} async-done(((bf16[4,384,1280]{2,1,0:T(8,128)(2,1)}), bf16[4,384,1280]{2,1,0:T(8,128)(2,1)}, u32[]{:S(2)}, u32[]{:S(2)}) %all-to-all-start.3) | async-done | bytes 3932192 | tf_op jit(solution)/shard_map/all_to_all | solution.py:55
  157.8 8.8 %all-to-all-start.1 = ((bf16[32,40,1280]{2,1,0:T(8,128)(2,1)}), bf16[32,40,1280]{2,1,0:T(8,128)(2,1)S(1)}, u32[]{:S(2)}, u32[]{:S(2)}) async-start(bf16[32,40,1280]{2,1,0:T(8,128)(2,1)} %bitcast.24), calls=%async_computation.1 | async-start | bytes 6553600 | tf_op jit(solution)/shard_map/all_to_all | solution.py:55
  166.5 3.9 %reduce_sum.72 = bf16[384,1280]{1,0:T(8,128)(2,1)} reduce(bf16[4,384,1280]{2,1,0:T(8,128)(2,1)} %all-to-all-done.3, bf16[]{:T(256)} %constant.70.clone.1), dimensions={0}, to_apply=%region_7.8 | reduce | flops 1474560 | bytes 4915202 | tf_op jit(solution)/shard_map/reduce_sum | solution.py:56
  170.4 2.5 reshape.216
  173.0 12.9 %scatter_custom_fusion.1 = bf16[5760,256]{1,0:T(8,128)(2,1)} fusion(s32[1920]{0:T(1024)S(1)} %fusion.28, bf16[1920,256]{1,0:T(8,128)(2,1)} %reshape.216, bf16[]{:T(256)} %constant.70.clone.1), kind=kCustom, calls=%fused_computation.31 | custom fusion | bytes 2949632 | tf_op jit(solution)/shard_map/scatter | solution.py:142
  185.8 5.5 %reshape.202 = bf16[128,45,256]{2,1,0:T(8,128)(2,1)} reshape(bf16[5760,256]{1,0:T(8,128)(2,1)} %scatter_custom_fusion.1) | data formatting | bytes 5898240 | tf_op jit(solution)/shard_map/reshape | solution.py:146
  191.3 16.3 %all-to-all-done.1 = bf16[32,40,1280]{2,1,0:T(8,128)(2,1)S(1)} async-done(((bf16[32,40,1280]{2,1,0:T(8,128)(2,1)}), bf16[32,40,1280]{2,1,0:T(8,128)(2,1)S(1)}, u32[]{:S(2)}, u32[]{:S(2)}) %all-to-all-start.1) | async-done | bytes 3276832 | tf_op jit(solution)/shard_map/all_to_all | solution.py:55
  207.6 5.9 %all-to-all-start.4 = ((bf16[128,45,256]{2,1,0:T(8,128)(2,1)}), bf16[128,45,256]{2,1,0:T(8,128)(2,1)}, u32[]{:S(2)}, u32[]{:S(2)}) async-start(bf16[128,45,256]{2,1,0:T(8,128)(2,1)} %reshape.202), calls=%async_computation.4 | async-start | bytes 6291456 | tf_op jit(solution)/shard_map/all_to_all | solution.py:145
  213.5 0.5 broadcast.181
  214.0 0.8 reduce.9
  214.8 0.2 reshape.199
  215.1 0.1 fusion.21
  215.1 0.5 convert_reduce_fusion
  215.6 0.7 fusion.34
  216.3 39.0 %all-to-all-done.4 = bf16[128,45,256]{2,1,0:T(8,128)(2,1)} async-done(((bf16[128,45,256]{2,1,0:T(8,128)(2,1)}), bf16[128,45,256]{2,1,0:T(8,128)(2,1)}, u32[]{:S(2)}, u32[]{:S(2)}) %all-to-all-start.4) | async-done | bytes 2949152 | tf_op jit(solution)/shard_map/all_to_all | solution.py:145
  255.3 5.8 %reshape.224 = f32[5760,256]{1,0:T(8,128)} reshape(bf16[128,45,256]{2,1,0:T(8,128)(2,1)} %all-to-all-done.4) | data formatting | bytes 8847360 | tf_op jit(solution)/shard_map/convert_element_type | solution.py:163
  261.0 31.2 %scatter_custom_fusion.2 = f32[2048,256]{1,0:T(8,128)S(1)} fusion(s32[5760]{0:T(1024)S(1)} %fusion.21, f32[5760,256]{1,0:T(8,128)} %reshape.224, f32[]{:T(128)} %constant.27.clone.1), kind=kCustom, calls=%fused_computation.34 | custom fusion | flops 1474560 | bytes 2097664 | tf_op jit(solution)/shard_map/scatter-add | solution.py:163
  292.2 0.0 copy-start.1
  292.2 6.4 %multiply_subtract_fusion = (f32[2048,256]{1,0:T(8,128)}, f32[2048,256]{1,0:T(8,128)}, f32[2048,256]{1,0:T(8,128)}) fusion(f32[2048,256]{1,0:T(8,128)} %param.15, f32[2048,256]{1,0:T(8,128)S(1)} %scatter_custom_fusion.2, f32[2048,256]{1,0:T(8,128)} %param.16, f32[2048,256]{1,0:T(8,128)} %param.17), kind=kLoop, calls=%fused_computation.26 | loop fusion | flops 6815744 | bytes 14680064 | tf_op jit(solution)/shard_map/sub | solution.py:63
  (17 shorter events, 0.1 us)
Async XLA Ops:
  7.2 1.6 copy-start
  7.2 52.6 %all-gather.2.cloned.1.call-start = ((), (), s32[]{:S(2)}) async-start(), calls=%async_computation.5 | async-start | bytes 3379200 | tf_op jit(solution)/shard_map/all_gather | solution.py:23
  59.8 6.1 %copy-start.5 = (bf16[1536,1280]{1,0:T(8,128)(2,1)S(1)}, bf16[1536,1280]{1,0:T(8,128)(2,1)}, u32[]{:S(2)}) copy-start(bf16[1536,1280]{1,0:T(8,128)(2,1)} %param.9) | copy-start | bytes 11796484
  59.8 6.1 %copy-start.6 = (bf16[1280,1280]{1,0:T(8,128)(2,1)S(1)}, bf16[1280,1280]{1,0:T(8,128)(2,1)}, u32[]{:S(2)}) copy-start(bf16[1280,1280]{1,0:T(8,128)(2,1)} %all-gather.2.cloned.1.call-done) | copy-start | bytes 9830404
  71.3 15.1 %all-to-all-start = ((f32[4,1,4608]{2,1,0:T(1,128)}), f32[4,1,4608]{2,1,0:T(1,128)S(1)}, u32[]{:S(2)}, u32[]{:S(2)}) async-start(f32[4,1,4608]{2,1,0:T(1,128)} %broadcast_in_dim.6), calls=%async_computation | async-start | bytes 147456 | tf_op jit(solution)/shard_map/all_to_all | solution.py:29
  86.4 20.9 %all-to-all-start.2 = ((s32[128,1,45]{2,1,0:T(1,128)}), s32[128,1,45]{2,1,0:T(1,128)S(1)}, u32[]{:S(2)}, u32[]{:S(2)}) async-start(s32[128,1,45]{2,1,0:T(1,128)} %bitcast.4), calls=%async_computation.2 | async-start | bytes 131072 | tf_op jit(solution)/shard_map/all_to_all | solution.py:152
  94.5 6.0 %copy-start.7 = (bf16[1280,1280]{1,0:T(8,128)(2,1)S(1)}, bf16[1280,1280]{1,0:T(8,128)(2,1)}, u32[]{:S(2)}) copy-start(bf16[1280,1280]{1,0:T(8,128)(2,1)} %all-gather.2.cloned.1.call-done) | copy-start | bytes 9830404
  98.6 1.3 copy-start.2
  98.6 1.9 copy-start.4
  107.3 4.9 %copy-start.3 = (bf16[1536,640]{0,1:T(8,128)(2,1)S(1)}, bf16[1536,640]{0,1:T(8,128)(2,1)}, u32[]{:S(2)}) copy-start(bf16[1536,640]{0,1:T(8,128)(2,1)} %copy-done.2) | copy-start | bytes 5898244
  107.3 50.5 %all-to-all-start.3 = ((bf16[4,384,1280]{2,1,0:T(8,128)(2,1)}), bf16[4,384,1280]{2,1,0:T(8,128)(2,1)}, u32[]{:S(2)}, u32[]{:S(2)}) async-start(bf16[4,384,1280]{2,1,0:T(8,128)(2,1)} %bitcast.23), calls=%async_computation.3 | async-start | bytes 7864320 | tf_op jit(solution)/shard_map/all_to_all | solution.py:55
  157.8 49.9 %all-to-all-start.1 = ((bf16[32,40,1280]{2,1,0:T(8,128)(2,1)}), bf16[32,40,1280]{2,1,0:T(8,128)(2,1)S(1)}, u32[]{:S(2)}, u32[]{:S(2)}) async-start(bf16[32,40,1280]{2,1,0:T(8,128)(2,1)} %bitcast.24), calls=%async_computation.1 | async-start | bytes 6553600 | tf_op jit(solution)/shard_map/all_to_all | solution.py:55
  207.6 47.7 %all-to-all-start.4 = ((bf16[128,45,256]{2,1,0:T(8,128)(2,1)}), bf16[128,45,256]{2,1,0:T(8,128)(2,1)}, u32[]{:S(2)}, u32[]{:S(2)}) async-start(bf16[128,45,256]{2,1,0:T(8,128)(2,1)} %reshape.202), calls=%async_computation.4 | async-start | bytes 6291456 | tf_op jit(solution)/shard_map/all_to_all | solution.py:145
  292.2 6.4 %copy-start.1 = (s32[1536,5]{0,1:T(8,128)S(1)}, s32[1536,5]{0,1:T(8,128)}, u32[]{:S(2)}) copy-start(s32[1536,5]{0,1:T(8,128)} %param.14) | copy-start | bytes 92164
Sparse Core Ops, SparseCore 0:
  10.9 48.8 all-gather.1
where the time goes:
time: 306 us; the launch traced here: 305 us
  waiting for transfers between devices  134 us (44%)
  local copies, waits for them, and re-layouts  48.7 us (16%)
  other arithmetic  48.6 us (16%)
  starting transfers between devices  31.7 us (10%)
  matrix products  28.3 us (9%)
  between operations  14.3 us (5%)
    all_to_all x2, waiting for transfers between devices, sum_at_owner(): tiles = lax.all_to_all(split_up(shard, dim, length), axis, 0, 0, tiled=True)  52.9 us
    all_gather x1, waiting for transfers between devices, in_one_piece(): whole = lax.all_gather(both, axis, axis=dim, tiled=True)  41.9 us
    all_to_all x1, waiting for transfers between devices, body(): lax.all_to_all(send_rows.reshape(owners, capacity, row_width), ('dp', 'te...  39 us
    scatter-add x1, other arithmetic, body(): table_grad = jnp.zeros((rows_dev, row_width), jnp.float32).at[got_ids.res...  31.2 us
    all_to_all x2, starting transfers between devices, sum_at_owner(): tiles = lax.all_to_all(split_up(shard, dim, length), axis, 0, 0, tiled=True)  13.7 us
    scatter x1, local copies, waits for them, and re-layouts, body(): jnp.zeros((owners * capacity, row_width), jnp.bfloat16).at[slot_index]  12.9 us
    scatter x1, local copies, waits for them, and re-layouts, body(): jnp.full((owners * capacity,), rows_dev, jnp.int32).at[slot_index]  10 us
    dot_general x1, matrix products, body(): lax.dot_general(memory, both_grads, (((0,), (0,)), ((), ())), preferred_e...  8.89 us
  transfers between devices with their start and end apart: 6, of which 4 were waited for; matrix products, arithmetic and copies ran while one was open for 22% of the time, Pallas kernels for 0%

commit v1 on v0

--- a/solution.py
+++ b/solution.py
@@ -3,6 +3,8 @@
 import jax
 import jax.numpy as jnp
 from jax import lax
+from jax.experimental import pallas as pl
+from jax.experimental.pallas import tpu as pltpu
 from jax.sharding import PartitionSpec as P
 
 D = 2560
@@ -56,11 +58,140 @@
     return jnp.sum(tiles.astype(jnp.float32), axis=0)
 
 
-def adam_update(table_grad, embed_table, first_moment, second_moment):
-    new_first = beta_one * first_moment + (1.0 - beta_one) * table_grad
-    new_second = beta_two * second_moment + (1.0 - beta_two) * table_grad * table_grad
-    stepped = new_first / correct_one / (jnp.sqrt(new_second / correct_two) + adam_eps)
-    return (embed_table - learn_rate * stepped, new_first, new_second)
+SLOTS = 48
+TILE = 256
+
+
+def pack_kernel(tile_ref, spot_ref, parts_ref, out_ref, rows_ref):
+    lookups, width = tile_ref.shape[0], out_ref.shape[1]
+    tokens = parts_ref.shape[1]
+
+    @pl.when(pl.program_id(0) == 0)
+    def _():
+        for l in range(lookups):
+            total = parts_ref[0, :, l * width : (l + 1) * width].astype(jnp.float32)
+            for k in range(1, parts_ref.shape[0]):
+                total += parts_ref[k, :, l * width : (l + 1) * width].astype(jnp.float32)
+            rows_ref[l * tokens : (l + 1) * tokens, :] = total.astype(jnp.bfloat16)
+
+    steps = out_ref.shape[0] // TILE
+    place = lax.broadcasted_iota(jnp.int32, (TILE, tokens), 0).astype(jnp.bfloat16)
+    one, zero = jnp.ones((), jnp.bfloat16), jnp.zeros((), jnp.bfloat16)
+    for s in range(steps):
+        here = pl.program_id(0) * steps + s
+        total = jnp.zeros((TILE, width), jnp.float32)
+        for l in range(lookups):
+            spot = jnp.where(tile_ref[l : l + 1, :] == here, spot_ref[l : l + 1, :], -1)
+            spot = jnp.broadcast_to(spot.astype(jnp.bfloat16), (TILE, tokens))
+            hits = jnp.where(place == spot, one, zero)
+            total += jnp.dot(
+                hits,
+                rows_ref[l * tokens : (l + 1) * tokens, :],
+                preferred_element_type=jnp.float32,
+            )
+        out_ref[s * TILE : (s + 1) * TILE, :] = total.astype(jnp.bfloat16)
+
+
+def pack_rows(slot, parts, total_slots, width):
+    per_step = 3 * TILE
+    tokens = parts.shape[1]
+    lookups = slot.shape[0]
+    return pl.pallas_call(
+        pack_kernel,
+        out_shape=jax.ShapeDtypeStruct((total_slots, width), jnp.bfloat16),
+        grid=(total_slots // per_step,),
+        in_specs=[
+            pl.BlockSpec(slot.shape, lambda i: (0, 0)),
+            pl.BlockSpec(slot.shape, lambda i: (0, 0)),
+            pl.BlockSpec(parts.shape, lambda i: (0, 0, 0)),
+        ],
+        out_specs=pl.BlockSpec((per_step, width), lambda i: (i, 0)),
+        scratch_shapes=[pltpu.VMEM((lookups * tokens, width), jnp.bfloat16)],
+        compiler_params=pltpu.CompilerParams(vmem_limit_bytes=40 * 1024 * 1024),
+        name="pack_rows",
+    )(slot // TILE, slot % TILE, parts)
+
+
+def adam_kernel(
+    tile_ref, spot_ref, rows_ref, table_ref, first_ref, second_ref, new_table_ref, new_first_ref, new_second_ref
+):
+    steps = table_ref.shape[0] // TILE
+    width = table_ref.shape[1]
+    entries = rows_ref.shape[0]
+    chunk = 1024
+    place = lax.broadcasted_iota(jnp.int32, (TILE, chunk), 0).astype(jnp.bfloat16)
+    one, zero = jnp.ones((), jnp.bfloat16), jnp.zeros((), jnp.bfloat16)
+    for s in range(steps):
+        here = pl.program_id(0) * steps + s
+        grad = jnp.zeros((TILE, width), jnp.float32)
+        for k in range(0, entries, chunk):
+            spot = jnp.where(tile_ref[:, k : k + chunk] == here, spot_ref[:, k : k + chunk], -1)
+            spot = jnp.broadcast_to(spot.astype(jnp.bfloat16), (TILE, chunk))
+            hits = jnp.where(place == spot, one, zero)
+            grad += jnp.dot(hits, rows_ref[k : k + chunk, :], preferred_element_type=jnp.float32)
+        at = slice(s * TILE, (s + 1) * TILE)
+        new_first = beta_one * first_ref[at, :] + (1.0 - beta_one) * grad
+        new_second = beta_two * second_ref[at, :] + (1.0 - beta_two) * grad * grad
+        stepped = new_first / correct_one / (jnp.sqrt(new_second / correct_two) + adam_eps)
+        new_table_ref[at, :] = table_ref[at, :] - learn_rate * stepped
+        new_first_ref[at, :] = new_first
+        new_second_ref[at, :] = new_second
+
+
+def adam_rows(got_ids, got_rows, embed_table, first_moment, second_moment):
+    rows_dev, width = embed_table.shape
+    per_step = 2 * TILE
+    block = pl.BlockSpec((per_step, width), lambda i: (i, 0))
+    ids = got_ids.reshape(1, -1)
+    whole = pl.BlockSpec(ids.shape, lambda i: (0, 0))
+    return pl.pallas_call(
+        adam_kernel,
+        out_shape=(jax.ShapeDtypeStruct((rows_dev, width), jnp.float32),) * 3,
+        grid=(rows_dev // per_step,),
+        in_specs=[
+            whole,
+            whole,
+            pl.BlockSpec(got_rows.shape, lambda i: (0, 0)),
+            block,
+            block,
+            block,
+        ],
+        out_specs=(block,) * 3,
+        compiler_params=pltpu.CompilerParams(vmem_limit_bytes=40 * 1024 * 1024),
+        name="adam_rows",
+    )(ids // TILE, ids % TILE, got_rows, embed_table, first_moment, second_moment)
+
+
+def route(my_ids, owners, rows_dev):
+    ids = my_ids.T
+    lookups, tokens = ids.shape
+    flat = ids.reshape(-1)
+    entries = flat.shape[0]
+    owner_of = flat // rows_dev
+    local_row = flat % rows_dev
+    owner_hits = (owner_of[:, None] == jnp.arange(owners, dtype=jnp.int32)[None, :]).astype(
+        jnp.bfloat16
+    )
+    earlier = (jnp.arange(entries)[None, :] < jnp.arange(entries)[:, None]).astype(jnp.bfloat16)
+    before_counts = jnp.dot(earlier, owner_hits, preferred_element_type=jnp.float32)
+    slot_rank = jnp.sum(before_counts * owner_hits.astype(jnp.float32), axis=1).astype(jnp.int32)
+    slot = (owner_of * SLOTS + slot_rank).reshape(lookups, tokens)
+    rank_hits = slot_rank[:, None] == jnp.arange(SLOTS, dtype=jnp.int32)[None, :]
+    low = local_row % 64
+    high = local_row // 64
+    values = jnp.concatenate(
+        [
+            jnp.where(rank_hits, v[:, None], 0).astype(jnp.bfloat16)
+            for v in (high, low, jnp.ones_like(low))
+        ],
+        axis=1,
+    )
+    found = lax.dot_general(
+        owner_hits, values, (((0,), (0,)), ((), ())), preferred_element_type=jnp.float32
+    ).astype(jnp.int32)
+    got_high, got_low, filled = jnp.split(found, 3, axis=1)
+    send_ids = jnp.where(filled > 0, got_high * 64 + got_low, rows_dev)
+    return slot, send_ids
 
 
 def body(
@@ -74,6 +205,18 @@
     first_moment,
     second_moment,
 ):
+    dp_count = lax.axis_size("dp")
+    tensor_count = lax.axis_size("tensor")
+    owners = dp_count * tensor_count
+    rows_dev, row_width = embed_table.shape
+    block_rows = memory.shape[0] // tensor_count
+    my_ids = lax.dynamic_slice_in_dim(
+        row_ids, lax.axis_index("tensor") * block_rows, block_rows, 0
+    )
+    slot, send_ids = route(my_ids, owners, rows_dev)
+    got_ids = lax.all_to_all(
+        send_ids, ("dp", "tensor"), split_axis=0, concat_axis=0, tiled=True
+    )
     key_full, value_full = in_one_piece((key_weight, value_weight), "dp", 0, 1)
     key_proj = jnp.dot(memory, key_full, preferred_element_type=jnp.float32)
     value_proj = jnp.dot(memory, value_full, preferred_element_type=jnp.float32)
@@ -101,8 +244,6 @@
         [key_grad.astype(jnp.bfloat16), value_grad.astype(jnp.bfloat16)], axis=1
     )
     width_local = key_full.shape[1]
-    dp_count = lax.axis_size("dp")
-    tensor_count = lax.axis_size("tensor")
     weight_grads = sum_at_owner(
         lax.dot_general(
             memory, both_grads, (((0,), (0,)), ((), ())), preferred_element_type=jnp.float32
@@ -113,57 +254,27 @@
     key_weight_grad = weight_grads[:, :width_local]
     value_weight_grad = weight_grads[:, width_local:]
     both_full = jnp.concatenate([key_full, value_full], axis=1)
-    block_rows = memory.shape[0] // tensor_count
-    memory_grad = sum_at_owner(
+    memory_parts = lax.all_to_all(
         lax.dot_general(
             both_grads, both_full, (((1,), (1,)), ((), ())), preferred_element_type=jnp.float32
-        ).astype(jnp.bfloat16),
+        )
+        .astype(jnp.bfloat16)
+        .reshape(tensor_count, block_rows, -1),
         "tensor",
         0,
-    ).astype(jnp.bfloat16)
-    row_width = embed_table.shape[1]
-    rows_dev = embed_table.shape[0]
-    pieces = memory_grad.reshape(-1, row_width)
-    entries = pieces.shape[0]
-    my_ids = lax.dynamic_slice_in_dim(
-        row_ids, lax.axis_index("tensor") * block_rows, block_rows, 0
-    ).reshape(-1)
-    owners = dp_count * tensor_count
-    capacity = max(2, 3 * entries // owners)
-    owner_of = my_ids // rows_dev
-    local_row = my_ids % rows_dev
-    owner_hits = (owner_of[:, None] == jnp.arange(owners, dtype=jnp.int32)[None, :]).astype(
-        jnp.bfloat16
-    )
-    earlier = (jnp.arange(entries)[None, :] < jnp.arange(entries)[:, None]).astype(jnp.bfloat16)
-    before_counts = jnp.dot(earlier, owner_hits, preferred_element_type=jnp.float32)
-    slot_rank = jnp.sum(before_counts * owner_hits.astype(jnp.float32), axis=1).astype(jnp.int32)
-    slot_index = owner_of * capacity + slot_rank
-    send_rows = jnp.zeros((owners * capacity, row_width), jnp.bfloat16).at[slot_index].set(pieces)
-    send_ids = jnp.full((owners * capacity,), rows_dev, jnp.int32).at[slot_index].set(local_row)
-    got_rows, got_ids = (
-        lax.all_to_all(
-            send_rows.reshape(owners, capacity, row_width),
-            ("dp", "tensor"),
-            split_axis=0,
-            concat_axis=0,
-            tiled=True,
-        ),
-        lax.all_to_all(
-            send_ids.reshape(owners, capacity),
-            ("dp", "tensor"),
-            split_axis=0,
-            concat_axis=0,
-            tiled=True,
-        ),
-    )
-    table_grad = (
-        jnp.zeros((rows_dev, row_width), jnp.float32)
-        .at[got_ids.reshape(-1)]
-        .add(got_rows.reshape(-1, row_width).astype(jnp.float32), mode="drop")
-    )
-    new_table, new_first, new_second = adam_update(
-        table_grad, embed_table, first_moment, second_moment
+        0,
+        tiled=True,
+    )
+    send_rows = pack_rows(slot, memory_parts, owners * SLOTS, row_width)
+    got_rows = lax.all_to_all(
+        send_rows.reshape(owners, SLOTS, row_width),
+        ("dp", "tensor"),
+        split_axis=0,
+        concat_axis=0,
+        tiled=True,
+    )
+    new_table, new_first, new_second = adam_rows(
+        got_ids, got_rows.reshape(-1, row_width), embed_table, first_moment, second_moment
     )
     return (key_weight_grad, value_weight_grad, new_table, new_first, new_second)
 

time: 306 us -> 271 us (0.89)
  other arithmetic: 48.6 us -> 11.3 us
  local copies, waits for them, and re-layouts: 48.7 us -> 18.5 us
  Pallas kernels: 0 us -> 22.4 us
  waiting for transfers between devices: 134 us -> 144 us
    all_to_all x2 -> x3, waiting for transfers between devices: 39 us -> 75.4 us  [the longest x1 38.8 us: body(): lax.all_to_all(send_rows.reshape(owners, SLOTS, row_width), ('dp', 'tenso...]
    scatter-add x1 -> x0, other arithmetic: 31.2 us -> none  [body(): table_grad = jnp.zeros((rows_dev, row_width), jnp.float32).at[got_ids.res...]
    all_to_all x2 -> x1, waiting for transfers between devices: 52.9 us -> 26.1 us  [sum_at_owner(): tiles = lax.all_to_all(split_up(shard, dim, length), axis, 0, 0, tiled=True)]
    scatter x2 -> x0, local copies, waits for them, and re-layouts: 22.9 us -> none  [the longest x1 12.9 us: body(): jnp.zeros((owners * capacity, row_width), jnp.bfloat16).at[slot_index]]
    pallas_call x0 -> x2, Pallas kernels: none -> 22.4 us  [the longest x1 12.8 us: pack_rows(): pl.pallas_call(pack_kernel, out_shape=jax.ShapeDtypeStruct((total_slots,...]
    reshape x5 -> x2, local copies, waits for them, and re-layouts: 8.64 us -> 0.12 us  [the longest x1 0.11 us: adam_rows(): ids = got_ids.reshape(1, -1)]
    unnamed x18 -> x22, local copies, waits for them, and re-layouts: 8.61 us -> 15 us
    sub x1 -> x0, other arithmetic: 6.4 us -> none  [adam_update(): return (embed_table - learn_rate * stepped, new_first, new_second)]
  transfers between devices with their start and end apart: 6 -> 6, of which waited for: 4 -> 5; matrix products, arithmetic and copies ran while one was open for 22% -> 14% of each run, Pallas kernels for 0% -> 5%
where the time goes in v1:
time: 271 us; the launch traced here: 270 us
  waiting for transfers between devices  144 us (53%)
  starting transfers between devices  30.1 us (11%)
  matrix products  29.5 us (11%)
  Pallas kernels  22.4 us (8%)
  local copies, waits for them, and re-layouts  18.5 us (7%)
  between operations  14.2 us (5%)
  other arithmetic  11.3 us (4%)
    all_gather x1, waiting for transfers between devices, in_one_piece(): whole = lax.all_gather(both, axis, axis=dim, tiled=True)  39.1 us
    all_to_all x1, waiting for transfers between devices, body(): lax.all_to_all(send_rows.reshape(owners, SLOTS, row_width), ('dp', 'tenso...  38.8 us
    all_to_all x1, waiting for transfers between devices, body(): lax.all_to_all(lax.dot_general(both_grads, both_full, (((1,), (1,)), ((),...  36.7 us
    all_to_all x1, waiting for transfers between devices, sum_at_owner(): tiles = lax.all_to_all(split_up(shard, dim, length), axis, 0, 0, tiled=True)  26.1 us
    unnamed x22, local copies, waits for them, and re-layouts  15 us
    pallas_call x1, Pallas kernels, pack_rows(): pl.pallas_call(pack_kernel, out_shape=jax.ShapeDtypeStruct((total_slots,...  12.8 us
    pallas_call x1, Pallas kernels, adam_rows(): pl.pallas_call(adam_kernel, out_shape=(jax.ShapeDtypeStruct((rows_dev, wi...  9.56 us
    dot_general x1, matrix products, body(): lax.dot_general(memory, both_grads, (((0,), (0,)), ((), ())), preferred_e...  8.86 us
  transfers between devices with their start and end apart: 6, of which 5 were waited for; matrix products, arithmetic and copies ran while one was open for 14% of the time, Pallas kernels for 5%

profile of v1, /device:TPU:1, one launch (start us, length us, event | category | flops | bytes accessed | tf_op | source)
XLA Modules:
  0.0 270.4 jit_solution(5141082824534521866)
XLA Ops:
  7.2 0.0 all-gather.2.cloned.1.call-start
  7.2 1.5 pad_maximum_fusion.3
  8.7 0.0 all-gather.2.cloned.1.call-update
  8.7 0.7 dynamic-slice_bitcast_fusion
  9.5 1.8 fusion.13
  11.3 2.7 copy.26
  13.9 4.0 %copy.27 = bf16[1536,640]{0,1:T(8,128)(2,1)} copy(bf16[1536,640]{1,0:T(8,128)(2,1)} %param.11) | data formatting | bytes 3932160 | tf_op args[2]
  17.9 1.5 select_convert_fusion.2
  19.4 1.3 convolution_convert_fusion.2
  20.7 39.1 %all-gather.2.cloned.1.call-done = bf16[1280,1280]{1,0:T(8,128)(2,1)} async-done(((bf16[40,1280]{1,0:T(8,128)(2,1)}), bf16[1280,1280]{1,0:T(8,128)(2,1)}) %all-gather.2.cloned.1.call-update) | async-done | bytes 3276816 | tf_op jit(solution)/shard_map/all_gather | solution.py:25
  59.8 6.1 %fusion.5 = f32[1536]{0:T(1024)S(1)} fusion(bf16[1536,640]{0,1:T(8,128)(2,1)} %copy.27, bf16[1536,1280]{1,0:T(8,128)(2,1)} %param.9, bf16[1280,1280]{1,0:T(8,128)(2,1)} %all-gather.2.cloned.1.call-done), kind=kOutput, calls=%fused_computation.13 | convolution fusion | flops 2519529984 | bytes 7542784 | tf_op jit(solution)/shard_map/dot_general | solution.py:222
  65.9 0.0 copy-done.7
  65.9 0.0 copy-done.8
  65.9 4.7 %fusion.7 = (f32[1536]{0:T(1024)S(1)}, f32[1536]{0:T(1024)S(1)}, f32[640,1536]{1,0:T(8,128)}) fusion(bf16[1536,640]{0,1:T(8,128)(2,1)S(1)} %copy.26, bf16[1536,1280]{1,0:T(8,128)(2,1)S(1)} %copy-done.7, bf16[1280,1280]{1,0:T(8,128)(2,1)S(1)} %copy-done.8), kind=kOutput, calls=%fused_computation.18 | convolution fusion | flops 2521494528 | bytes 11481088 | tf_op jit(solution)/shard_map/dot_general | solution.py:221
  70.6 0.7 broadcast_in_dim.42
  71.3 4.1 %all-to-all-start = ((f32[4,1,4608]{2,1,0:T(1,128)}), f32[4,1,4608]{2,1,0:T(1,128)S(1)}, u32[]{:S(2)}, u32[]{:S(2)}) async-start(f32[4,1,4608]{2,1,0:T(1,128)} %broadcast_in_dim.42), calls=%async_computation | async-start | bytes 147456 | tf_op jit(solution)/shard_map/all_to_all | solution.py:31
  75.4 0.7 copy.29
  76.2 3.8 %all-to-all-done = f32[4,1,4608]{2,1,0:T(1,128)S(1)} async-done(((f32[4,1,4608]{2,1,0:T(1,128)}), f32[4,1,4608]{2,1,0:T(1,128)S(1)}, u32[]{:S(2)}, u32[]{:S(2)}) %all-to-all-start) | async-done | bytes 73760 | tf_op jit(solution)/shard_map/all_to_all | solution.py:31
  80.0 6.8 %all-to-all-start.2 = ((s32[128,1,48]{2,1,0:T(1,128)}), s32[128,1,48]{2,1,0:T(1,128)S(1)}, u32[]{:S(2)}, u32[]{:S(2)}) async-start(s32[128,1,48]{2,1,0:T(1,128)} %copy.29), calls=%async_computation.2 | async-start | bytes 131072 | tf_op jit(solution)/shard_map/all_to_all | solution.py:217
  86.7 0.1 reduce_sum.57
  86.9 4.0 %fusion.4 = (bf16[1536,640]{0,1:T(8,128)(2,1)S(1)}, bf16[1536,640]{0,1:T(8,128)(2,1)S(1)}) fusion(bf16[1536,640]{0,1:T(8,128)(2,1)S(1)} %copy.26, f32[640,1536]{1,0:T(8,128)} %get-tuple-element.31, f32[1536]{0:T(1024)S(1)} %get-tuple-element.22, f32[1536]{0:T(1024)S(1)} %get-tuple-element.24, f32[1536]{0:T(1024)S(1)} %get-tuple-element.21, ...), kind=kLoop, calls=%fused_computation.12 | loop fusion | flops 9830400 | bytes 11827200 | tf_op jit(solution)/shard_map/convert_element_type | solution.py:244
  90.9 0.0 copy-start.4
  90.9 0.0 copy-start.6
  91.0 1.2 copy-done.4
  92.2 0.6 copy-done.6
  92.9 6.8 %convolution_convert_fusion = bf16[1536,1280]{1,0:T(8,128)(2,1)} fusion(bf16[1280,1280]{1,0:T(8,128)(2,1)S(1)} %copy-done.9, bf16[1536,640]{0,1:T(8,128)(2,1)S(1)} %get-tuple-element.33, bf16[1536,640]{0,1:T(8,128)(2,1)S(1)} %get-tuple-element.32), kind=kOutput, calls=%fused_computation.2 | convolution fusion | flops 5042995200 | bytes 11141120 | tf_op jit(solution)/shard_map/dot_general | solution.py:258
  99.6 0.0 all-to-all-done.2
  99.6 4.9 %all-to-all-start.3 = ((bf16[4,384,1280]{2,1,0:T(8,128)(2,1)}), bf16[4,384,1280]{2,1,0:T(8,128)(2,1)}, u32[]{:S(2)}, u32[]{:S(2)}) async-start(bf16[4,384,1280]{2,1,0:T(8,128)(2,1)} %bitcast.29), calls=%async_computation.3 | async-start | bytes 7864320 | tf_op jit(solution)/shard_map/all_to_all | solution.py:257
  104.6 8.9 %convolution_convert_fusion.1 = bf16[1280,1280]{0,1:T(8,128)(2,1)} fusion(bf16[1536,1280]{1,0:T(8,128)(2,1)} %param.9, bf16[1536,640]{0,1:T(8,128)(2,1)} %copy-done.6, bf16[1536,640]{0,1:T(8,128)(2,1)S(1)} %copy-done.5), kind=kOutput, calls=%fused_computation.3 | convolution fusion | flops 5042667520 | bytes 11141120 | tf_op jit(solution)/shard_map/dot_general | solution.py:248
  113.4 36.7 %all-to-all-done.3.parts_ref = bf16[4,384,1280]{2,1,0:T(8,128)(2,1)} async-done(((bf16[4,384,1280]{2,1,0:T(8,128)(2,1)}), bf16[4,384,1280]{2,1,0:T(8,128)(2,1)}, u32[]{:S(2)}, u32[]{:S(2)}) %all-to-all-start.3) | async-done | bytes 3932192 | tf_op jit(solution)/shard_map/all_to_all | solution.py:257
  150.1 8.8 %all-to-all-start.1 = ((bf16[32,40,1280]{2,1,0:T(8,128)(2,1)}), bf16[32,40,1280]{2,1,0:T(8,128)(2,1)S(1)}, u32[]{:S(2)}, u32[]{:S(2)}) async-start(bf16[32,40,1280]{2,1,0:T(8,128)(2,1)} %bitcast.30), calls=%async_computation.1 | async-start | bytes 6553600 | tf_op jit(solution)/shard_map/all_to_all | solution.py:57
  158.9 0.7 add_select_fusion
  159.6 0.5 broadcast.327
  160.2 0.8 reduce.4
  161.0 0.1 reshape.296
  161.1 12.8 %pack_rows.1 = bf16[6144,256]{1,0:T(8,128)(2,1)} custom-call(s32[5,384]{1,0:T(8,128)S(1)} %get-tuple-element.20.tile_ref, s32[5,384]{1,0:T(8,128)S(1)} %get-tuple-element.19.spot_ref, bf16[4,384,1280]{2,1,0:T(8,128)(2,1)} %all-to-all-done.3.parts_ref), custom_call_target="tpu_custom_call" | custom-call | tf_op jit(solution)/shard_map/pack_rows/pallas_call | solution.py:99
  173.9 26.1 %all-to-all-done.1 = bf16[32,40,1280]{2,1,0:T(8,128)(2,1)S(1)} async-done(((bf16[32,40,1280]{2,1,0:T(8,128)(2,1)}), bf16[32,40,1280]{2,1,0:T(8,128)(2,1)S(1)}, u32[]{:S(2)}, u32[]{:S(2)}) %all-to-all-start.1) | async-done | bytes 3276832 | tf_op jit(solution)/shard_map/all_to_all | solution.py:57
  200.0 1.7 copy-done.3
  201.7 5.5 %all-to-all-start.4 = ((bf16[128,48,256]{2,1,0:T(8,128)(2,1)}), bf16[128,48,256]{2,1,0:T(8,128)(2,1)S(1)}, u32[]{:S(2)}, u32[]{:S(2)}) async-start(bf16[128,48,256]{2,1,0:T(8,128)(2,1)} %bitcast.7), calls=%async_computation.4 | async-start | bytes 6291456 | tf_op jit(solution)/shard_map/all_to_all | solution.py:269
  207.2 0.1 and_select_fusion
  207.2 0.1 and_select_fusion.1.tile_ref
  207.3 2.4 convert_reduce_fusion
  209.8 0.7 fusion.41
  210.4 38.8 %all-to-all-done.4 = bf16[128,48,256]{2,1,0:T(8,128)(2,1)S(1)} async-done(((bf16[128,48,256]{2,1,0:T(8,128)(2,1)}), bf16[128,48,256]{2,1,0:T(8,128)(2,1)S(1)}, u32[]{:S(2)}, u32[]{:S(2)}) %all-to-all-start.4) | async-done | bytes 3145760 | tf_op jit(solution)/shard_map/all_to_all | solution.py:269
  249.2 1.6 copy-done
  250.8 1.6 copy-done.1
  252.4 1.6 copy-done.2
  254.0 9.6 %adam_rows.1 = (f32[2048,256]{1,0:T(8,128)}, f32[2048,256]{1,0:T(8,128)}, f32[2048,256]{1,0:T(8,128)}) custom-call(s32[1,6144]{1,0:T(1,128)S(1)} %and_select_fusion.1.tile_ref, s32[1,6144]{1,0:T(1,128)S(1)} %get-tuple-element.13.spot_ref, bf16[6144,256]{1,0:T(8,128)(2,1)S(1)} %bitcast.28, f32[2048,256]{1,0:T(8,128)S(1)} %copy-done, ...), custom_call_target="tpu_custom_call" | custom-call | tf_op jit(solution)/shard_map/adam_rows/pallas_call | solution.py:147
  (18 shorter events, 0.1 us)
Async XLA Ops:
  7.2 52.6 %all-gather.2.cloned.1.call-start = ((), (), s32[]{:S(2)}) async-start(), calls=%async_computation.5 | async-start | bytes 3379200 | tf_op jit(solution)/shard_map/all_gather | solution.py:25
  59.8 6.1 %copy-start.7 = (bf16[1536,1280]{1,0:T(8,128)(2,1)S(1)}, bf16[1536,1280]{1,0:T(8,128)(2,1)}, u32[]{:S(2)}) copy-start(bf16[1536,1280]{1,0:T(8,128)(2,1)} %param.9) | copy-start | bytes 11796484
  59.8 6.1 %copy-start.8 = (bf16[1280,1280]{1,0:T(8,128)(2,1)S(1)}, bf16[1280,1280]{1,0:T(8,128)(2,1)}, u32[]{:S(2)}) copy-start(bf16[1280,1280]{1,0:T(8,128)(2,1)} %all-gather.2.cloned.1.call-done) | copy-start | bytes 9830404
  71.3 8.7 %all-to-all-start = ((f32[4,1,4608]{2,1,0:T(1,128)}), f32[4,1,4608]{2,1,0:T(1,128)S(1)}, u32[]{:S(2)}, u32[]{:S(2)}) async-start(f32[4,1,4608]{2,1,0:T(1,128)} %broadcast_in_dim.42), calls=%async_computation | async-start | bytes 147456 | tf_op jit(solution)/shard_map/all_to_all | solution.py:31
  80.0 19.7 %all-to-all-start.2 = ((s32[128,1,48]{2,1,0:T(1,128)}), s32[128,1,48]{2,1,0:T(1,128)S(1)}, u32[]{:S(2)}, u32[]{:S(2)}) async-start(s32[128,1,48]{2,1,0:T(1,128)} %copy.29), calls=%async_computation.2 | async-start | bytes 131072 | tf_op jit(solution)/shard_map/all_to_all | solution.py:217
  86.9 6.0 %copy-start.9 = (bf16[1280,1280]{1,0:T(8,128)(2,1)S(1)}, bf16[1280,1280]{1,0:T(8,128)(2,1)}, u32[]{:S(2)}) copy-start(bf16[1280,1280]{1,0:T(8,128)(2,1)} %all-gather.2.cloned.1.call-done) | copy-start | bytes 9830404
  90.9 1.3 copy-start.4
  90.9 1.9 copy-start.6
  99.6 4.9 %copy-start.5 = (bf16[1536,640]{0,1:T(8,128)(2,1)S(1)}, bf16[1536,640]{0,1:T(8,128)(2,1)}, u32[]{:S(2)}) copy-start(bf16[1536,640]{0,1:T(8,128)(2,1)} %copy-done.4) | copy-start | bytes 5898244
  99.6 50.5 %all-to-all-start.3 = ((bf16[4,384,1280]{2,1,0:T(8,128)(2,1)}), bf16[4,384,1280]{2,1,0:T(8,128)(2,1)}, u32[]{:S(2)}, u32[]{:S(2)}) async-start(bf16[4,384,1280]{2,1,0:T(8,128)(2,1)} %bitcast.29), calls=%async_computation.3 | async-start | bytes 7864320 | tf_op jit(solution)/shard_map/all_to_all | solution.py:257
  150.1 49.9 %all-to-all-start.1 = ((bf16[32,40,1280]{2,1,0:T(8,128)(2,1)}), bf16[32,40,1280]{2,1,0:T(8,128)(2,1)S(1)}, u32[]{:S(2)}, u32[]{:S(2)}) async-start(bf16[32,40,1280]{2,1,0:T(8,128)(2,1)} %bitcast.30), calls=%async_computation.1 | async-start | bytes 6553600 | tf_op jit(solution)/shard_map/all_to_all | solution.py:57
  200.0 1.7 copy-start.3
  201.7 47.6 %all-to-all-start.4 = ((bf16[128,48,256]{2,1,0:T(8,128)(2,1)}), bf16[128,48,256]{2,1,0:T(8,128)(2,1)S(1)}, u32[]{:S(2)}, u32[]{:S(2)}) async-start(bf16[128,48,256]{2,1,0:T(8,128)(2,1)} %bitcast.7), calls=%async_computation.4 | async-start | bytes 6291456 | tf_op jit(solution)/shard_map/all_to_all | solution.py:269
  249.2 1.6 copy-start
  250.8 1.6 copy-start.1
  252.4 1.6 copy-start.2
Sparse Core Ops, SparseCore 0:
  10.9 48.8 all-gather.1

commit v2 on v1

v2 whole, which is shorter than its diff:
```python
import math

import jax
import jax.numpy as jnp
from jax import lax
from jax.experimental import pallas as pl
from jax.experimental.pallas import tpu as pltpu
from jax.sharding import PartitionSpec as P

D = 2560


beta_one = 0.9
beta_two = 0.999
learn_rate = 0.01
adam_eps = 1e-08
norm_eps = 1e-06
correct_one = 0.9999734386011124
correct_two = 0.0952078528863


def dp_index(x, y, c):
    return (x % 4) * 8 + (y % 4) * 2 + c


def along_x(d):
    return [
        (dp_index(x, y, c), dp_index(x + d, y, c))
        for x in range(4)
        for y in range(4)
        for c in range(2)
    ]


def along_y(d):
    return [
        (dp_index(x, y, c), dp_index(x, y + d, c))
        for x in range(4)
        for y in range(4)
        for c in range(2)
    ]


def other_core():
    return [
        (dp_index(x, y, c), dp_index(x, y, 1 - c))
        for x in range(4)
        for y in range(4)
        for c in range(2)
    ]


def along_z(d):
    return [(z, (z + d) % 4) for z in range(4)]


STEPS = (1, 2, 3)


def ring_gather(shard, perm_of):
    return [shard] + [lax.ppermute(shard, "dp", perm_of(d)) for d in STEPS]


def ring_sum(tiles, here, perm_of):
    own = lax.dynamic_index_in_dim(tiles, here, 0, keepdims=False).astype(jnp.float32)
    got = [
        lax.ppermute(
            lax.dynamic_index_in_dim(tiles, (here + d) % 4, 0, keepdims=False), "dp", perm_of(d)
        )
        for d in STEPS
    ]
    for g in got:
        own += g.astype(jnp.float32)
    return own


def gather_weights(key_weight, value_weight):
    key_x = ring_gather(key_weight, along_x)
    value_y = ring_gather(value_weight, along_y)
    key_x = jnp.stack(key_x)
    value_y = jnp.stack(value_y)
    key_x, value_y = lax.optimization_barrier((key_x, value_y))
    key_all = jnp.stack(ring_gather(key_x, along_y))
    value_all = jnp.stack(ring_gather(value_y, along_x))
    return jnp.stack([key_all, value_all])


def sum_weight_grads(weight_grads, x, y, c):
    width = weight_grads.shape[1]
    tiles = weight_grads.reshape(16, 2, -1, width)
    sent = lax.dynamic_index_in_dim(tiles, 1 - c, 1, keepdims=False)
    kept = lax.dynamic_index_in_dim(tiles, c, 1, keepdims=False)
    got = lax.ppermute(sent, "dp", other_core())
    both = (kept.astype(jnp.float32) + got.astype(jnp.float32)).astype(jnp.bfloat16)
    both = both.reshape(4, 4, -1, width)
    half = width // 2
    key_part = ring_sum(both[:, :, :, :half], x, along_x).astype(jnp.bfloat16)
    value_part = ring_sum(jnp.swapaxes(both[:, :, :, half:], 0, 1), y, along_y).astype(jnp.bfloat16)
    return (ring_sum(key_part, y, along_y), ring_sum(value_part, x, along_x))


def project_kernel(
    spot_ref, mine_ref, got_ref, memory_ref, hidden_ref, grad_ref, weight_ref, key_proj_ref, sums_ref
):
    half = hidden_ref.shape[1]

    @pl.when(pl.program_id(0) == 0)
    def _():
        x, y, c = spot_ref[0], spot_ref[1], spot_ref[2]
        rows = mine_ref.shape[2]
        for one in range(4):
            for two in range(4):
                for half_index in range(2):
                    a = mine_ref[half_index, one * 4 + two].astype(jnp.float32)
                    b = got_ref[half_index, one * 4 + two].astype(jnp.float32)
                    low = jnp.where(c == 0, a, b)
                    high = jnp.where(c == 0, b, a)
                    dx, dy = (two, one) if half_index == 0 else (one, two)
                    at = ((x + 4 - dx) % 4) * 4 + (y + 4 - dy) % 4
                    both = jnp.concatenate([low, high], axis=0).astype(jnp.bfloat16)
                    weight_ref[
                        pl.ds(pl.multiple_of(at * (2 * rows), 16), 2 * rows),
                        half_index * half : (half_index + 1) * half,
                    ] = both

    memory = memory_ref[...]
    key_proj = jnp.dot(memory, weight_ref[:, :half], preferred_element_type=jnp.float32)
    value_proj = jnp.dot(memory, weight_ref[:, half:], preferred_element_type=jnp.float32)
    key_proj_ref[...] = key_proj
    hidden = hidden_ref[...].astype(jnp.float32)
    grad = grad_ref[...].astype(jnp.float32)
    square_sum = jnp.sum(key_proj * key_proj, axis=1, keepdims=True)
    cross_sum = jnp.sum(hidden * key_proj, axis=1, keepdims=True)
    output_sum = jnp.sum(grad * value_proj, axis=1, keepdims=True)
    lane = lax.broadcasted_iota(jnp.int32, (memory.shape[0], 128), 1)
    sums = jnp.where(lane == 0, square_sum, jnp.where(lane == 1, cross_sum, output_sum))
    sums_ref[...] = sums.T[:8, :]


def project(spot, mine, got, memory, hidden, grad_out):
    tokens, mem = memory.shape
    half = hidden.shape[1]
    tile = tokens // 4
    fixed = lambda i, s: (0, 0)
    return pl.pallas_call(
        project_kernel,
        out_shape=(
            jax.ShapeDtypeStruct((mem, 2 * half), jnp.bfloat16),
            jax.ShapeDtypeStruct((tokens, half), jnp.float32),
            jax.ShapeDtypeStruct((8, tokens), jnp.float32),
        ),
        grid_spec=pltpu.PrefetchScalarGridSpec(
            num_scalar_prefetch=1,
            grid=(4,),
            in_specs=[
                pl.BlockSpec(mine.shape, lambda i, s: (0, 0, 0, 0)),
                pl.BlockSpec(got.shape, lambda i, s: (0, 0, 0, 0)),
                pl.BlockSpec((tile, mem), lambda i, s: (i, 0)),
                pl.BlockSpec((tile, half), lambda i, s: (i, 0)),
                pl.BlockSpec((tile, half), lambda i, s: (i, 0)),
            ],
            out_specs=(
                pl.BlockSpec((mem, 2 * half), fixed),
                pl.BlockSpec((tile, half), lambda i, s: (i, 0)),
                pl.BlockSpec((8, tile), lambda i, s: (0, i)),
            ),
        ),
        compiler_params=pltpu.CompilerParams(vmem_limit_bytes=44 * 1024 * 1024),
        name="project",
    )(spot, mine, got, memory, hidden, grad_out)


def grads_of(sums_refs, hidden_ref, grad_ref, key_proj_ref, weight_ref, both_ref):
    half = hidden_ref.shape[1]
    sums = sums_refs[0][...] + sums_refs[1][...] + sums_refs[2][...] + sums_refs[3][...]
    root_width = math.sqrt(D)
    key_scale = jnp.sqrt(sums[0:1, :] / D + norm_eps)
    gate_score = sums[1:2, :] / (key_scale * root_width)
    gate_value = 1.0 / (1.0 + jnp.exp(-gate_score))
    gate_grad = gate_value * (1.0 - gate_value) * sums[2:3, :]
    by_hidden = 1.0 / (key_scale * root_width)
    by_key = gate_score / (D * key_scale * key_scale)
    row = lax.broadcasted_iota(jnp.int32, (128, sums.shape[1]), 0)
    coded = jnp.where(
        row == 0,
        gate_value,
        jnp.where(row == 1, gate_grad, jnp.where(row == 2, by_hidden, by_key)),
    ).T
    hidden = hidden_ref[...].astype(jnp.float32)
    key_grad = coded[:, 1:2] * (hidden * coded[:, 2:3] - key_proj_ref[...] * coded[:, 3:4])
    value_grad = coded[:, 0:1] * grad_ref[...].astype(jnp.float32)
    both_ref[:, :half] = key_grad.astype(jnp.bfloat16)
    both_ref[:, half:] = value_grad.astype(jnp.bfloat16)
    return lax.dot_general(
        both_ref[...],
        weight_ref[...],
        (((1,), (1,)), ((), ())),
        preferred_element_type=jnp.float32,
    ).astype(jnp.bfloat16)


def grads_kernel(order_ref, *refs):
    sums_refs, (hidden_ref, grad_ref, key_proj_ref, weight_ref), rest = refs[:4], refs[4:8], refs[8:]
    if len(rest) % 2 == 0:
        rest = rest[1:]
    both_ref, outs = rest[0], rest[1:]
    memory_grad = grads_of(sums_refs, hidden_ref, grad_ref, key_proj_ref, weight_ref, both_ref)
    half = outs[0].shape[1]
    for k in range(len(outs) // 2):

        @pl.when(pl.program_id(0) == k)
        def _():
            outs[2 * k][...] = memory_grad[:, :half]
            outs[2 * k + 1][...] = memory_grad[:, half:]


def grads(order, sums, hidden, grad_out, key_proj, weights, both):
    steps = order.shape[0]
    tokens, half = hidden.shape
    tile = tokens // 4
    mem = weights.shape[0]
    at = lambda i, o: (o[i], 0)
    out_half = pl.BlockSpec((tile, mem // 2), lambda i, o: (0, 0))
    whole = pl.BlockSpec((tile, 2 * half), at)
    given = () if both is None else (both,)
    return pl.pallas_call(
        grads_kernel,
        out_shape=(
            jax.ShapeDtypeStruct((tokens, 2 * half), jnp.bfloat16),
            *([jax.ShapeDtypeStruct((tile, mem // 2), jnp.bfloat16)] * (2 * steps)),
        ),
        grid_spec=pltpu.PrefetchScalarGridSpec(
            num_scalar_prefetch=1,
            grid=(steps,),
            in_specs=[pl.BlockSpec((8, tile), lambda i, o: (0, o[i]))] * 4
            + [pl.BlockSpec((tile, half), at)] * 3
            + [pl.BlockSpec(weights.shape, lambda i, o: (0, 0))]
            + [pl.BlockSpec(memory_space=pl.ANY)] * len(given),
            out_specs=(whole, *([out_half] * (2 * steps))),
        ),
        input_output_aliases={9: 0} if given else {},
        compiler_params=pltpu.CompilerParams(vmem_limit_bytes=44 * 1024 * 1024),
        name="grads_far" if both is None else "grads_near",
    )(order, *sums, hidden, grad_out, key_proj, weights, *given)


SLOTS = 48
TILE = 256


def pack_kernel(tile_ref, spot_ref, l1, l2, l3, r1, r2, r3, out_ref, sum_ref, rows_ref):
    lookups, width = tile_ref.shape[0], out_ref.shape[1]
    tokens, half = l1.shape

    @pl.when(pl.program_id(0) == 0)
    def _():
        f32 = jnp.float32
        left = l1[...].astype(f32) + l2[...].astype(f32) + l3[...].astype(f32)
        right = r1[...].astype(f32) + r2[...].astype(f32) + r3[...].astype(f32)
        sum_ref[:, :half] = left.astype(jnp.bfloat16)
        sum_ref[:, half:] = right.astype(jnp.bfloat16)
        for l in range(lookups):
            rows_ref[l * tokens : (l + 1) * tokens, :] = sum_ref[:, l * width : (l + 1) * width]

    steps = out_ref.shape[0] // TILE
    place = lax.broadcasted_iota(jnp.int32, (TILE, lookups * tokens), 0).astype(jnp.bfloat16)
    one, zero = jnp.ones((), jnp.bfloat16), jnp.zeros((), jnp.bfloat16)
    hits = []
    for s in range(steps):
        here = pl.program_id(0) * steps + s
        spot = jnp.concatenate(
            [
                jnp.where(tile_ref[l : l + 1, :] == here, spot_ref[l : l + 1, :], -1)
                for l in range(lookups)
            ],
            axis=1,
        )
        spot = jnp.broadcast_to(spot.astype(jnp.bfloat16), place.shape)
        hits.append(jnp.where(place == spot, one, zero))
    out_ref[...] = jnp.dot(
        jnp.concatenate(hits, axis=0), rows_ref[...], preferred_element_type=jnp.float32
    ).astype(jnp.bfloat16)


def pack_rows(slot, parts, total_slots, width):
    per_step = 3 * TILE
    tokens, half = parts[0].shape
    lookups = slot.shape[0]
    return pl.pallas_call(
        pack_kernel,
        out_shape=jax.ShapeDtypeStruct((total_slots, width), jnp.bfloat16),
        grid=(total_slots // per_step,),
        in_specs=[pl.BlockSpec(slot.shape, lambda i: (0, 0))] * 2
        + [pl.BlockSpec((tokens, half), lambda i: (0, 0))] * 6,
        out_specs=pl.BlockSpec((per_step, width), lambda i: (i, 0)),
        scratch_shapes=[
            pltpu.VMEM((tokens, 2 * half), jnp.bfloat16),
            pltpu.VMEM((lookups * tokens, width), jnp.bfloat16),
        ],
        compiler_params=pltpu.CompilerParams(vmem_limit_bytes=40 * 1024 * 1024),
        name="pack_rows",
    )(slot // TILE, slot % TILE, *parts)


def adam_kernel(
    tile_ref, spot_ref, rows_ref, table_ref, first_ref, second_ref, new_table_ref, new_first_ref, new_second_ref
):
    steps = table_ref.shape[0] // TILE
    width = table_ref.shape[1]
    entries = rows_ref.shape[0]
    chunk = 1024
    place = lax.broadcasted_iota(jnp.int32, (TILE, chunk), 0).astype(jnp.bfloat16)
    one, zero = jnp.ones((), jnp.bfloat16), jnp.zeros((), jnp.bfloat16)
    for s in range(steps):
        here = pl.program_id(0) * steps + s
        grad = jnp.zeros((TILE, width), jnp.float32)
        for k in range(0, entries, chunk):
            spot = jnp.where(tile_ref[:, k : k + chunk] == here, spot_ref[:, k : k + chunk], -1)
            spot = jnp.broadcast_to(spot.astype(jnp.bfloat16), (TILE, chunk))
            hits = jnp.where(place == spot, one, zero)
            grad += jnp.dot(hits, rows_ref[k : k + chunk, :], preferred_element_type=jnp.float32)
        at = slice(s * TILE, (s + 1) * TILE)
        new_first = beta_one * first_ref[at, :] + (1.0 - beta_one) * grad
        new_second = beta_two * second_ref[at, :] + (1.0 - beta_two) * grad * grad
        stepped = new_first / correct_one / (jnp.sqrt(new_second / correct_two) + adam_eps)
        new_table_ref[at, :] = table_ref[at, :] - learn_rate * stepped
        new_first_ref[at, :] = new_first
        new_second_ref[at, :] = new_second


def adam_rows(got_ids, got_rows, embed_table, first_moment, second_moment):
    rows_dev, width = embed_table.shape
    per_step = 2 * TILE
    block = pl.BlockSpec((per_step, width), lambda i: (i, 0))
    ids = got_ids.reshape(1, -1)
    whole = pl.BlockSpec(ids.shape, lambda i: (0, 0))
    return pl.pallas_call(
        adam_kernel,
        out_shape=(jax.ShapeDtypeStruct((rows_dev, width), jnp.float32),) * 3,
        grid=(rows_dev // per_step,),
        in_specs=[
            whole,
            whole,
            pl.BlockSpec(got_rows.shape, lambda i: (0, 0)),
            block,
            block,
            block,
        ],
        out_specs=(block,) * 3,
        compiler_params=pltpu.CompilerParams(vmem_limit_bytes=40 * 1024 * 1024),
        name="adam_rows",
    )(ids // TILE, ids % TILE, got_rows, embed_table, first_moment, second_moment)


def route(my_ids, owners, rows_dev):
    ids = my_ids.T
    lookups, tokens = ids.shape
    flat = ids.reshape(-1)
    entries = flat.shape[0]
    owner_of = flat // rows_dev
    local_row = flat % rows_dev
    owner_hits = (owner_of[:, None] == jnp.arange(owners, dtype=jnp.int32)[None, :]).astype(
        jnp.bfloat16
    )
    earlier = (jnp.arange(entries)[None, :] < jnp.arange(entries)[:, None]).astype(jnp.bfloat16)
    before_counts = jnp.dot(earlier, owner_hits, preferred_element_type=jnp.float32)
    slot_rank = jnp.sum(before_counts * owner_hits.astype(jnp.float32), axis=1).astype(jnp.int32)
    slot = (owner_of * SLOTS + slot_rank).reshape(lookups, tokens)
    rank_hits = slot_rank[:, None] == jnp.arange(SLOTS, dtype=jnp.int32)[None, :]
    low = local_row % 64
    high = local_row // 64
    values = jnp.concatenate(
        [
            jnp.where(rank_hits, v[:, None], 0).astype(jnp.bfloat16)
            for v in (high, low, jnp.ones_like(low))
        ],
        axis=1,
    )
    found = lax.dot_general(
        owner_hits, values, (((0,), (0,)), ((), ())), preferred_element_type=jnp.float32
    ).astype(jnp.int32)
    got_high, got_low, filled = jnp.split(found, 3, axis=1)
    send_ids = jnp.where(filled > 0, got_high * 64 + got_low, rows_dev)
    return slot, send_ids


def body(
    memory,
    hidden,
    grad_out,
    key_weight,
    value_weight,
    row_ids,
    embed_table,
    first_moment,
    second_moment,
):
    dp_count = lax.axis_size("dp")
    tensor_count = lax.axis_size("tensor")
    owners = dp_count * tensor_count
    rows_dev, row_width = embed_table.shape
    block_rows = memory.shape[0] // tensor_count
    my_ids = lax.dynamic_slice_in_dim(
        row_ids, lax.axis_index("tensor") * block_rows, block_rows, 0
    )
    at = lax.axis_index("dp")
    z = lax.axis_index("tensor")
    x, y, c = at // 8, (at // 2) % 4, at % 2
    slot, send_ids = route(my_ids, owners, rows_dev)
    got_ids = lax.all_to_all(
        send_ids, ("dp", "tensor"), split_axis=0, concat_axis=0, tiled=True
    )
    mine = gather_weights(key_weight, value_weight)
    mine, got_ids, slot = lax.optimization_barrier((mine, got_ids, slot))
    mine = mine.reshape(2, 16, *key_weight.shape)
    got = lax.ppermute(mine, "dp", other_core())
    spot = jnp.stack([x, y, c]).astype(jnp.int32)
    weights, key_proj, sums = project(spot, mine, got, memory, hidden, grad_out)
    sums = [sums] + [lax.ppermute(sums, "tensor", along_z(d)) for d in STEPS]
    far = ((z + 2) % 4)[None].astype(jnp.int32)
    near = jnp.stack([(z + 1) % 4, (z + 3) % 4, z]).astype(jnp.int32)
    both, far_left, far_right = grads(
        far, sums, hidden, grad_out, key_proj, weights, None
    )
    up = lax.ppermute(far_left, "tensor", along_z(1))
    down = lax.ppermute(far_right, "tensor", along_z(3))
    both, next_left, next_right, last_left, last_right, own_left, own_right = grads(
        near, sums, hidden, grad_out, key_proj, weights, both
    )
    from_last_right = lax.ppermute(next_right, "tensor", along_z(1))
    from_next_left = lax.ppermute(last_left, "tensor", along_z(3))
    from_last_left = lax.ppermute(
        (up.astype(jnp.float32) + next_left.astype(jnp.float32)).astype(jnp.bfloat16),
        "tensor",
        along_z(1),
    )
    from_next_right = lax.ppermute(
        (down.astype(jnp.float32) + last_right.astype(jnp.float32)).astype(jnp.bfloat16),
        "tensor",
        along_z(3),
    )
    key_weight_grad, value_weight_grad = sum_weight_grads(
        lax.dot_general(
            memory, both, (((0,), (0,)), ((), ())), preferred_element_type=jnp.float32
        ).astype(jnp.bfloat16),
        x,
        y,
        c,
    )
    send_rows = pack_rows(
        slot,
        (own_left, from_last_left, from_next_left, own_right, from_last_right, from_next_right),
        owners * SLOTS,
        row_width,
    )
    got_rows = lax.all_to_all(
        send_rows.reshape(owners, SLOTS, row_width),
        ("dp", "tensor"),
        split_axis=0,
        concat_axis=0,
        tiled=True,
    )
    new_table, new_first, new_second = adam_rows(
        got_ids, got_rows.reshape(-1, row_width), embed_table, first_moment, second_moment
    )
    return (key_weight_grad, value_weight_grad, new_table, new_first, new_second)


def solution(mesh):
    return jax.shard_map(
        body,
        mesh=mesh,
        in_specs=(
            P("dp", None),
            P("dp", "tensor"),
            P("dp", "tensor"),
            P("dp", "tensor"),
            P("dp", "tensor"),
            P("dp", None),
            P(("dp", "tensor"), None),
            P(("dp", "tensor"), None),
            P(("dp", "tensor"), None),
        ),
        out_specs=(
            P("dp", "tensor"),
            P("dp", "tensor"),
            P(("dp", "tensor"), None),
            P(("dp", "tensor"), None),
            P(("dp", "tensor"), None),
        ),
        check_vma=False,
    )
```

time: 271 us -> 229 us (0.85)
  waiting for transfers between devices: 144 us -> 75.7 us
  starting transfers between devices: 30.1 us -> 72.6 us
  Pallas kernels: 22.4 us -> 43.3 us
  matrix products: 29.5 us -> 10.8 us
  between operations: 14.2 us -> 1.08 us
  local copies, waits for them, and re-layouts: 18.5 us -> 14.4 us
  other arithmetic: 11.3 us -> 8.43 us
    ppermute x0 -> x35, waiting for transfers between devices: none -> 75.7 us  [the longest x12 36.7 us: ring_sum(): lax.ppermute(lax.dynamic_index_in_dim(tiles, (here + d) % 4, 0, keepdims=...]
    all_to_all x3 -> x0, waiting for transfers between devices: 66.5 us -> none  [the longest x1 36.7 us: body(): lax.all_to_all(lax.dot_general(both_grads, both_full, (((1,), (1,)), ((),...]
    ppermute x0 -> x35, starting transfers between devices: none -> 51.8 us  [the longest x12 18 us: ring_gather(): return [shard] + [lax.ppermute(shard, 'dp', perm_of(d)) for d in STEPS]]
    all_gather x1 -> x0, waiting for transfers between devices: 39.1 us -> none  [in_one_piece(): whole = lax.all_gather(both, axis, axis=dim, tiled=True)]
    all_to_all x1, waiting for transfers between devices: 38.8 us -> 0.01 us  [body(): lax.all_to_all(send_rows.reshape(owners, SLOTS, row_width), ('dp', 'tenso...]
    pallas_call x0 -> x3, Pallas kernels: none -> 24.3 us  [the longest x1 12.2 us: project(): pl.pallas_call(project_kernel, out_shape=(jax.ShapeDtypeStruct((mem, 2 *...]
    dot_general x4 -> x1, matrix products: 26.5 us -> 7.76 us  [body(): lax.dot_general(memory, both, (((0,), (0,)), ((), ())), preferred_element...]
    all_to_all x3 -> x0, starting transfers between devices: 17.8 us -> none  [the longest x1 8.78 us: sum_at_owner(): tiles = lax.all_to_all(split_up(shard, dim, length), axis, 0, 0, tiled=True)]
  transfers between devices with their start and end apart: 6 -> 37, of which waited for: 5 -> 13; matrix products, arithmetic and copies ran while one was open for 14% -> 10% of each run, Pallas kernels for 5% -> 8%
where the time goes in v2:
time: 229 us; the launch traced here: 226 us
  waiting for transfers between devices  75.7 us (33%)
  starting transfers between devices  72.6 us (32%)
  Pallas kernels  43.3 us (19%)
  local copies, waits for them, and re-layouts  14.4 us (6%)
  matrix products  10.8 us (5%)
  other arithmetic  8.43 us (4%)
    ppermute x12, waiting for transfers between devices, ring_sum(): lax.ppermute(lax.dynamic_index_in_dim(tiles, (here + d) % 4, 0, keepdims=...  36.7 us
    ppermute x12, starting transfers between devices, ring_gather(): return [shard] + [lax.ppermute(shard, 'dp', perm_of(d)) for d in STEPS]  18 us
    ppermute x12, starting transfers between devices, ring_sum(): lax.ppermute(lax.dynamic_index_in_dim(tiles, (here + d) % 4, 0, keepdims=...  17 us
    ppermute x12, waiting for transfers between devices, ring_gather(): return [shard] + [lax.ppermute(shard, 'dp', perm_of(d)) for d in STEPS]  13.6 us
    pallas_call x1, Pallas kernels, project(): pl.pallas_call(project_kernel, out_shape=(jax.ShapeDtypeStruct((mem, 2 *...  12.2 us
    pallas_call x2, Pallas kernels, grads(): pl.pallas_call(grads_kernel, out_shape=(jax.ShapeDtypeStruct((tokens, 2 *...  12.1 us
    ppermute x1, waiting for transfers between devices, body(): down = lax.ppermute(far_right, 'tensor', along_z(3))  11.4 us
    unnamed x24, local copies, waits for them, and re-layouts  11.2 us
  transfers between devices with their start and end apart: 37, of which 13 were waited for; matrix products, arithmetic and copies ran while one was open for 10% of the time, Pallas kernels for 8%

profile of v2, /device:TPU:1, one launch (start us, length us, event | category | flops | bytes accessed | tf_op | source)
XLA Modules:
  0.0 226.4 jit_solution(6327825455950335455)
XLA Ops:
  0.6 2.1 collective-permute-start
  4.1 1.6 collective-permute-start.1
  7.0 1.4 collective-permute-start.5
  9.2 1.8 fusion.3
  11.0 1.5 select_convert_fusion.2
  13.8 1.7 collective-permute-start.4
  15.6 2.7 %collective-permute-done.4 = bf16[40,640]{1,0:T(8,128)(2,1)S(1)} collective-permute-done((bf16[40,640]{1,0:T(8,128)(2,1)S(1)}, bf16[40,640]{1,0:T(8,128)(2,1)S(1)}, u32[]{:S(2)}, u32[]{:S(2)}) %collective-permute-start.4) | collective-permute-done | bytes 51232 | tf_op jit(solution)/shard_map/ppermute | solution.py:61
  18.4 1.5 collective-permute-start.8
  20.7 9.7 %all-to-all-start = ((s32[128,1,48]{2,1,0:T(1,128)}), s32[128,1,48]{2,1,0:T(1,128)S(1)}, u32[]{:S(2)}, u32[]{:S(2)}) async-start(s32[128,1,48]{2,1,0:T(1,128)} %copy.18), calls=%async_computation | async-start | bytes 131072 | tf_op jit(solution)/shard_map/all_to_all | solution.py:410
  30.5 3.0 %collective-permute-start.7 = (bf16[4,40,640]{2,1,0:T(8,128)(2,1)S(1)}, bf16[4,40,640]{2,1,0:T(8,128)(2,1)S(1)}, u32[]{:S(2)}, u32[]{:S(2)}) collective-permute-start(bf16[4,40,640]{2,1,0:T(8,128)(2,1)S(1)} %pad_maximum_fusion.1), channel_id=1, source_target_pairs={{0,16},{4,20},{8,24},{12,28},{16,0},{20,4},{24,8},{28,12},{32,48},... | collective-permute-start | bytes 614408 | tf_op jit(solution)/shard_map/ppermute | solution.py:61
  33.8 2.4 %collective-permute-start.11 = (bf16[4,40,640]{2,1,0:T(8,128)(2,1)S(1)}, bf16[4,40,640]{2,1,0:T(8,128)(2,1)S(1)}, u32[]{:S(2)}, u32[]{:S(2)}) collective-permute-start(bf16[4,40,640]{2,1,0:T(8,128)(2,1)S(1)} %pad_maximum_fusion.2), channel_id=1, source_target_pairs={{0,96},{4,100},{8,104},{12,108},{16,112},{20,116},{24,120},{28,124... | collective-permute-start | bytes 614408 | tf_op jit(solution)/shard_map/ppermute | solution.py:61
  38.4 5.6 %collective-permute-done.6 = bf16[4,40,640]{2,1,0:T(8,128)(2,1)S(1)} collective-permute-done((bf16[4,40,640]{2,1,0:T(8,128)(2,1)S(1)}, bf16[4,40,640]{2,1,0:T(8,128)(2,1)S(1)}, u32[]{:S(2)}, u32[]{:S(2)}) %collective-permute-start.6) | collective-permute-done | bytes 204832 | tf_op jit(solution)/shard_map/ppermute | solution.py:61
  44.2 4.9 %collective-permute-done.9 = bf16[4,40,640]{2,1,0:T(8,128)(2,1)S(1)} collective-permute-done((bf16[4,40,640]{2,1,0:T(8,128)(2,1)S(1)}, bf16[4,40,640]{2,1,0:T(8,128)(2,1)S(1)}, u32[]{:S(2)}, u32[]{:S(2)}) %collective-permute-start.9) | collective-permute-done | bytes 204832 | tf_op jit(solution)/shard_map/ppermute | solution.py:61
  51.1 3.4 %collective-permute-done.12.got_ref = bf16[2,16,40,640]{3,2,1,0:T(8,128)(2,1)} collective-permute-done((bf16[2,16,40,640]{3,2,1,0:T(8,128)(2,1)}, bf16[2,16,40,640]{3,2,1,0:T(8,128)(2,1)}, u32[]{:S(2)}, u32[]{:S(2)}) %collective-permute-start.12) | collective-permute-done | bytes 1638432 | tf_op jit(solution)/shard_map/ppermute | solution.py:416
  54.5 1.5 copy-done.1
  56.1 1.4 copy-done.4
  57.5 12.2 %project.1 = (bf16[1280,1280]{1,0:T(8,128)(2,1)}, f32[1536,640]{1,0:T(8,128)}, f32[8,1536]{1,0:T(8,128)S(1)}) custom-call(s32[3]{0:T(128)S(1)} %pad_add_fusion.1.spot_ref, bf16[2,16,40,640]{3,2,1,0:T(8,128)(2,1)S(1)} %bitcast.88, bf16[2,16,40,640]{3,2,1,0:T(8,128)(2,1)} %collective-permute-done.12.got_ref, bf16[1536,1280]{1,0:T(8,128)(2,1)} %memory_ref.1, ...), custom_call_target="tpu_custom_call" | custom-call | tf_op jit(solution)/shard_map/project/pallas_call | solution.py:145
  69.8 3.2 %collective-permute-start.15 = (f32[8,1536]{1,0:T(8,128)S(1)}, f32[8,1536]{1,0:T(8,128)S(1)}, u32[]{:S(2)}, u32[]{:S(2)}) collective-permute-start(f32[8,1536]{1,0:T(8,128)S(1)} %get-tuple-element.29.refs_0_), channel_id=1, source_target_pairs={{0,3},{1,0},{2,1},{3,2},{4,7},{5,4},{6,5},{7,6},{8,11},{9,8},{10,9... | collective-permute-start | bytes 147464 | tf_op jit(solution)/shard_map/ppermute | solution.py:419
  74.2 3.4 %collective-permute-done.14.refs_2_ = f32[8,1536]{1,0:T(8,128)S(1)} collective-permute-done((f32[8,1536]{1,0:T(8,128)S(1)}, f32[8,1536]{1,0:T(8,128)S(1)}, u32[]{:S(2)}, u32[]{:S(2)}) %collective-permute-start.14) | collective-permute-done | bytes 49184 | tf_op jit(solution)/shard_map/ppermute | solution.py:419
  77.7 1.5 copy-done.2
  79.2 1.9 copy-done.3
  81.2 3.1 %grads_far.1 = (bf16[1536,1280]{1,0:T(8,128)(2,1)}, bf16[384,640]{1,0:T(8,128)(2,1)S(1)}, bf16[384,640]{1,0:T(8,128)(2,1)S(1)}) custom-call(s32[1]{0:T(128)} %bitcast.28.order_ref, f32[8,1536]{1,0:T(8,128)S(1)} %get-tuple-element.29.refs_0_, f32[8,1536]{1,0:T(8,128)S(1)} %collective-permute-done.13.refs_1_, f32[8,1536]{1,0:T(8,128)S(1)} %collective-permute-done.14.refs_2_, ...), custom_call_target="tpu_custom_call" | custom-call | tf_op jit(solution)/shard_map/grads_far/pallas_call | solution.py:226
  84.3 9.0 %grads_near.1 = (bf16[1536,1280]{1,0:T(8,128)(2,1)}, bf16[384,640]{1,0:T(8,128)(2,1)S(1)}, bf16[384,640]{1,0:T(8,128)(2,1)S(1)}, bf16[384,640]{1,0:T(8,128)(2,1)...) custom-call(s32[3]{0:T(128)S(1)} %pad_add_fusion.order_ref, ...), custom_call_target="tpu_custom_call", output_to_operand_aliasing={{0}: (9, {})} | custom-call | tf_op jit(solution)/shard_map/grads_near/pallas_call | solution.py:226
  93.4 7.8 %convolution_convert_fusion = bf16[1280,1280]{0,1:T(8,128)(2,1)S(1)} fusion(bf16[1536,1280]{1,0:T(8,128)(2,1)} %get-tuple-element.33, bf16[1536,1280]{1,0:T(8,128)(2,1)S(1)} %copy-done.8), kind=kOutput, calls=%fused_computation.2 | convolution fusion | flops 5034803200 | bytes 11141120 | tf_op jit(solution)/shard_map/dot_general | solution.py:443
  101.1 2.8 %collective-permute-start.31 = (bf16[384,640]{1,0:T(8,128)(2,1)S(1)}, bf16[384,640]{1,0:T(8,128)(2,1)S(1)}, u32[]{:S(2)}, u32[]{:S(2)}) collective-permute-start(bf16[384,640]{1,0:T(8,128)(2,1)S(1)} %get-tuple-element.39), channel_id=1, source_target_pairs={{0,3},{1,0},{2,1},{3,2},{4,7},{5,4},{6,5},{7,6},{8,11},{9,8},{10,9... | collective-permute-start | bytes 1474568 | tf_op jit(solution)/shard_map/ppermute | solution.py:431
  103.9 2.7 %collective-permute-start.33 = (bf16[384,640]{1,0:T(8,128)(2,1)S(1)}, bf16[384,640]{1,0:T(8,128)(2,1)S(1)}, u32[]{:S(2)}, u32[]{:S(2)}) collective-permute-start(bf16[384,640]{1,0:T(8,128)(2,1)S(1)} %get-tuple-element.42), channel_id=1, source_target_pairs={{0,3},{1,0},{2,1},{3,2},{4,7},{5,4},{6,5},{7,6},{8,11},{9,8},{10,9... | collective-permute-start | bytes 1474568 | tf_op jit(solution)/shard_map/ppermute | solution.py:426
  107.9 3.2 %collective-permute-start.16 = (bf16[16,40,1280]{2,1,0:T(8,128)(2,1)}, bf16[16,40,1280]{2,1,0:T(8,128)(2,1)}, u32[]{:S(2)}, u32[]{:S(2)}) collective-permute-start(bf16[16,40,1280]{2,1,0:T(8,128)(2,1)} %dynamic-slice_bitcast_fusion), channel_id=1, source_target_pairs={{0,4},{4,0},{8,12},{12,8},{16,20},{20,16},{24,28},{28,24},{32,36},... | collective-permute-start | bytes 4915208 | tf_op jit(solution)/shard_map/ppermute | solution.py:93
  111.3 11.4 %collective-permute-done.33 = bf16[384,640]{1,0:T(8,128)(2,1)S(1)} collective-permute-done((bf16[384,640]{1,0:T(8,128)(2,1)S(1)}, bf16[384,640]{1,0:T(8,128)(2,1)S(1)}, u32[]{:S(2)}, u32[]{:S(2)}) %collective-permute-start.33) | collective-permute-done | bytes 491552 | tf_op jit(solution)/shard_map/ppermute | solution.py:426
  122.8 3.5 %collective-permute-start.34 = (bf16[384,640]{1,0:T(8,128)(2,1)S(1)}, bf16[384,640]{1,0:T(8,128)(2,1)S(1)}, u32[]{:S(2)}, u32[]{:S(2)}) collective-permute-start(bf16[384,640]{1,0:T(8,128)(2,1)S(1)} %add_convert_fusion), channel_id=1, source_target_pairs={{0,3},{1,0},{2,1},{3,2},{4,7},{5,4},{6,5},{7,6},{8,11},{9,8},{10,9... | collective-permute-start | bytes 1474568 | tf_op jit(solution)/shard_map/ppermute | solution.py:437
  126.4 7.1 %collective-permute-done.34.r3 = bf16[384,640]{1,0:T(8,128)(2,1)S(1)} collective-permute-done((bf16[384,640]{1,0:T(8,128)(2,1)S(1)}, bf16[384,640]{1,0:T(8,128)(2,1)S(1)}, u32[]{:S(2)}, u32[]{:S(2)}) %collective-permute-start.34) | collective-permute-done | bytes 491552 | tf_op jit(solution)/shard_map/ppermute | solution.py:437
  133.5 9.4 %pack_rows.1 = bf16[6144,256]{1,0:T(8,128)(2,1)} custom-call(s32[5,384]{1,0:T(8,128)S(1)} %get-tuple-element.64.tile_ref, s32[5,384]{1,0:T(8,128)S(1)} %get-tuple-element.63.spot_ref, bf16[384,640]{1,0:T(8,128)(2,1)S(1)} %get-tuple-element.36.l1, bf16[384,640]{1,0:T(8,128)(2,1)S(1)} %collective-permute-done.30.l2, ...), custom_call_target="tpu_custom_call" | custom-call | tf_op jit(solution)/shard_map/pack_rows/pallas_call | solution.py:289
  142.9 11.1 %all-to-all-start.1 = ((bf16[128,48,256]{2,1,0:T(8,128)(2,1)}), bf16[128,48,256]{2,1,0:T(8,128)(2,1)S(1)}, u32[]{:S(2)}, u32[]{:S(2)}) async-start(bf16[128,48,256]{2,1,0:T(8,128)(2,1)} %bitcast.51), calls=%async_computation.1 | async-start | bytes 6291456 | tf_op jit(solution)/shard_map/all_to_all | solution.py:456
  154.0 2.3 %fusion.1 = bf16[16,40,1280]{2,1,0:T(8,128)(2,1)S(1)} fusion(bf16[16,40,1280]{2,1,0:T(8,128)(2,1)} %collective-permute-done.16, bf16[16,2,40,1280]{3,2,1,0:T(8,128)(2,1)} %bitcast.91, s32[]{:T(128)S(6)} %select_n.203), kind=kLoop, calls=%fused_computation.4 | loop fusion | flops 3276800 | bytes 4915204 | tf_op jit(solution)/shard_map/convert_element_type | solution.py:94
  156.6 1.5 collective-permute-start.23
  159.4 1.6 collective-permute-start.24
  162.4 1.5 collective-permute-start.19
  163.9 30.9 %collective-permute-done.23 = bf16[4,40,640]{2,1,0:T(8,128)(2,1)S(1)} collective-permute-done((bf16[4,40,640]{2,1,0:T(8,128)(2,1)S(1)}, bf16[4,40,640]{2,1,0:T(8,128)(2,1)S(1)}, u32[]{:S(2)}, u32[]{:S(2)}) %collective-permute-start.23) | collective-permute-done | bytes 204832 | tf_op jit(solution)/shard_map/ppermute | solution.py:67
  194.8 2.8 %collective-permute-start.18 = (bf16[4,40,640]{2,1,0:T(8,128)(2,1)S(1)}, bf16[4,40,640]{2,1,0:T(8,128)(2,1)S(1)}, u32[]{:S(2)}, u32[]{:S(2)}) collective-permute-start(bf16[4,40,640]{2,1,0:T(8,128)(2,1)S(1)} %get-tuple-element.56), channel_id=1, source_target_pairs={{0,64},{4,68},{8,72},{12,76},{16,80},{20,84},{24,88},{28,92},{32,9... | collective-permute-start | bytes 614408 | tf_op jit(solution)/shard_map/ppermute | solution.py:67
  197.6 1.9 collective-permute-done.24
  199.7 1.4 collective-permute-start.26
  201.1 1.4 collective-permute-start.28
  202.4 1.6 collective-permute-start.27
  204.8 2.1 collective-permute-start.22
  208.7 2.7 %collective-permute-done.21 = bf16[40,640]{1,0:T(8,128)(2,1)S(1)} collective-permute-done((bf16[40,640]{1,0:T(8,128)(2,1)S(1)}, bf16[40,640]{1,0:T(8,128)(2,1)S(1)}, u32[]{:S(2)}, u32[]{:S(2)}) %collective-permute-start.21) | collective-permute-done | bytes 51232 | tf_op jit(solution)/shard_map/ppermute | solution.py:67
  212.1 1.6 copy-done.5
  213.7 1.6 copy-done.6
  215.2 1.6 copy-done.7
  216.8 9.6 %adam_rows.1 = (f32[2048,256]{1,0:T(8,128)}, f32[2048,256]{1,0:T(8,128)}, f32[2048,256]{1,0:T(8,128)}) custom-call(s32[1,6144]{1,0:T(1,128)S(1)} %and_select_fusion.1.tile_ref, s32[1,6144]{1,0:T(1,128)S(1)} %get-tuple-element.47.spot_ref, bf16[6144,256]{1,0:T(8,128)(2,1)S(1)} %bitcast.86, f32[2048,256]{1,0:T(8,128)S(1)} %copy-done.5, ...), custom_call_target="tpu_custom_call" | custom-call | tf_op jit(solution)/shard_map/adam_rows/pallas_call | solution.py:337
  (91 shorter events, 19.6 us)
Async XLA Ops:
  0.6 13.2 %collective-permute-start = (bf16[40,640]{1,0:T(8,128)(2,1)}, bf16[40,640]{1,0:T(8,128)(2,1)S(1)}, u32[]{:S(2)}, u32[]{:S(2)}) collective-permute-start(bf16[40,640]{1,0:T(8,128)(2,1)} %param.12), channel_id=1, source_target_pairs={{0,32},{4,36},{8,40},{12,44},{16,48},{20,52},{24,56},{28,60},{32,6... | collective-permute-start | bytes 153608 | tf_op jit(solution)/shard_map/ppermute | solution.py:61
  2.7 12.8 %collective-permute-start.2 = (bf16[40,640]{1,0:T(8,128)(2,1)}, bf16[40,640]{1,0:T(8,128)(2,1)S(1)}, u32[]{:S(2)}, u32[]{:S(2)}) collective-permute-start(bf16[40,640]{1,0:T(8,128)(2,1)} %param.12), channel_id=1, source_target_pairs={{0,96},{4,100},{8,104},{12,108},{16,112},{20,116},{24,120},{28,124... | collective-permute-start | bytes 153608 | tf_op jit(solution)/shard_map/ppermute | solution.py:61
  4.1 11.5 %collective-permute-start.1 = (bf16[40,640]{1,0:T(8,128)(2,1)}, bf16[40,640]{1,0:T(8,128)(2,1)S(1)}, u32[]{:S(2)}, u32[]{:S(2)}) collective-permute-start(bf16[40,640]{1,0:T(8,128)(2,1)} %param.12), channel_id=1, source_target_pairs={{0,64},{4,68},{8,72},{12,76},{16,80},{20,84},{24,88},{28,92},{32,9... | collective-permute-start | bytes 153608 | tf_op jit(solution)/shard_map/ppermute | solution.py:61
  5.7 9.9 %collective-permute-start.3 = (bf16[40,640]{1,0:T(8,128)(2,1)}, bf16[40,640]{1,0:T(8,128)(2,1)S(1)}, u32[]{:S(2)}, u32[]{:S(2)}) collective-permute-start(bf16[40,640]{1,0:T(8,128)(2,1)} %param.13), channel_id=1, source_target_pairs={{0,8},{4,12},{8,16},{12,20},{16,24},{20,28},{24,0},{28,4},{32,40},... | collective-permute-start | bytes 153608 | tf_op jit(solution)/shard_map/ppermute | solution.py:61
  7.0 8.6 %collective-permute-start.5 = (bf16[40,640]{1,0:T(8,128)(2,1)}, bf16[40,640]{1,0:T(8,128)(2,1)S(1)}, u32[]{:S(2)}, u32[]{:S(2)}) collective-permute-start(bf16[40,640]{1,0:T(8,128)(2,1)} %param.13), channel_id=1, source_target_pairs={{0,24},{4,28},{8,0},{12,4},{16,8},{20,12},{24,16},{28,20},{32,56},... | collective-permute-start | bytes 153608 | tf_op jit(solution)/shard_map/ppermute | solution.py:61
  11.0 2.8 %copy-start.11 = (bf16[40,640]{1,0:T(8,128)(2,1)S(1)}, bf16[40,640]{1,0:T(8,128)(2,1)}, u32[]{:S(2)}) copy-start(bf16[40,640]{1,0:T(8,128)(2,1)} %param.13) | copy-start | bytes 153604
  11.0 4.5 %copy-start.10 = (bf16[40,640]{1,0:T(8,128)(2,1)S(1)}, bf16[40,640]{1,0:T(8,128)(2,1)}, u32[]{:S(2)}) copy-start(bf16[40,640]{1,0:T(8,128)(2,1)} %param.12) | copy-start | bytes 153604
  13.8 4.5 %collective-permute-start.4 = (bf16[40,640]{1,0:T(8,128)(2,1)S(1)}, bf16[40,640]{1,0:T(8,128)(2,1)S(1)}, u32[]{:S(2)}, u32[]{:S(2)}) collective-permute-start(bf16[40,640]{1,0:T(8,128)(2,1)S(1)} %copy-done.11), channel_id=1, source_target_pairs={{0,16},{4,20},{8,24},{12,28},{16,0},{20,4},{24,8},{28,12},{32,48},... | collective-permute-start | bytes 153608 | tf_op jit(solution)/shard_map/ppermute | solution.py:61
  18.4 18.3 %collective-permute-start.8 = (bf16[4,40,640]{2,1,0:T(8,128)(2,1)S(1)}, bf16[4,40,640]{2,1,0:T(8,128)(2,1)S(1)}, u32[]{:S(2)}, u32[]{:S(2)}) collective-permute-start(bf16[4,40,640]{2,1,0:T(8,128)(2,1)S(1)} %pad_maximum_fusion.1), channel_id=1, source_target_pairs={{0,24},{4,28},{8,0},{12,4},{16,8},{20,12},{24,16},{28,20},{32,56},... | collective-permute-start | bytes 614408 | tf_op jit(solution)/shard_map/ppermute | solution.py:61
  20.7 29.9 %all-to-all-start = ((s32[128,1,48]{2,1,0:T(1,128)}), s32[128,1,48]{2,1,0:T(1,128)S(1)}, u32[]{:S(2)}, u32[]{:S(2)}) async-start(s32[128,1,48]{2,1,0:T(1,128)} %copy.18), calls=%async_computation | async-start | bytes 131072 | tf_op jit(solution)/shard_map/all_to_all | solution.py:410
  30.5 7.9 %collective-permute-start.7 = (bf16[4,40,640]{2,1,0:T(8,128)(2,1)S(1)}, bf16[4,40,640]{2,1,0:T(8,128)(2,1)S(1)}, u32[]{:S(2)}, u32[]{:S(2)}) collective-permute-start(bf16[4,40,640]{2,1,0:T(8,128)(2,1)S(1)} %pad_maximum_fusion.1), channel_id=1, source_target_pairs={{0,16},{4,20},{8,24},{12,28},{16,0},{20,4},{24,8},{28,12},{32,48},... | collective-permute-start | bytes 614408 | tf_op jit(solution)/shard_map/ppermute | solution.py:61
  33.4 10.6 %collective-permute-start.6 = (bf16[4,40,640]{2,1,0:T(8,128)(2,1)S(1)}, bf16[4,40,640]{2,1,0:T(8,128)(2,1)S(1)}, u32[]{:S(2)}, u32[]{:S(2)}) collective-permute-start(bf16[4,40,640]{2,1,0:T(8,128)(2,1)S(1)} %pad_maximum_fusion.1), channel_id=1, source_target_pairs={{0,8},{4,12},{8,16},{12,20},{16,24},{20,28},{24,0},{28,4},{32,40},... | collective-permute-start | bytes 614408 | tf_op jit(solution)/shard_map/ppermute | solution.py:61
  33.8 10.4 %collective-permute-start.11 = (bf16[4,40,640]{2,1,0:T(8,128)(2,1)S(1)}, bf16[4,40,640]{2,1,0:T(8,128)(2,1)S(1)}, u32[]{:S(2)}, u32[]{:S(2)}) collective-permute-start(bf16[4,40,640]{2,1,0:T(8,128)(2,1)S(1)} %pad_maximum_fusion.2), channel_id=1, source_target_pairs={{0,96},{4,100},{8,104},{12,108},{16,112},{20,116},{24,120},{28,124... | collective-permute-start | bytes 614408 | tf_op jit(solution)/shard_map/ppermute | solution.py:61
  36.2 8.0 %collective-permute-start.10 = (bf16[4,40,640]{2,1,0:T(8,128)(2,1)S(1)}, bf16[4,40,640]{2,1,0:T(8,128)(2,1)S(1)}, u32[]{:S(2)}, u32[]{:S(2)}) collective-permute-start(bf16[4,40,640]{2,1,0:T(8,128)(2,1)S(1)} %pad_maximum_fusion.2), channel_id=1, source_target_pairs={{0,64},{4,68},{8,72},{12,76},{16,80},{20,84},{24,88},{28,92},{32,9... | collective-permute-start | bytes 614408 | tf_op jit(solution)/shard_map/ppermute | solution.py:61
  36.8 12.3 %collective-permute-start.9 = (bf16[4,40,640]{2,1,0:T(8,128)(2,1)S(1)}, bf16[4,40,640]{2,1,0:T(8,128)(2,1)S(1)}, u32[]{:S(2)}, u32[]{:S(2)}) collective-permute-start(bf16[4,40,640]{2,1,0:T(8,128)(2,1)S(1)} %pad_maximum_fusion.2), channel_id=1, source_target_pairs={{0,32},{4,36},{8,40},{12,44},{16,48},{20,52},{24,56},{28,60},{32,6... | collective-permute-start | bytes 614408 | tf_op jit(solution)/shard_map/ppermute | solution.py:61
  49.2 5.3 %copy-start = (bf16[1536,640]{1,0:T(8,128)(2,1)S(1)}, bf16[1536,640]{1,0:T(8,128)(2,1)}, u32[]{:S(2)}) copy-start(bf16[1536,640]{1,0:T(8,128)(2,1)} %refs_4_.3) | copy-start | bytes 5898244
  50.6 4.0 %collective-permute-start.12 = (bf16[2,16,40,640]{3,2,1,0:T(8,128)(2,1)}, bf16[2,16,40,640]{3,2,1,0:T(8,128)(2,1)}, u32[]{:S(2)}, u32[]{:S(2)}) collective-permute-start(bf16[2,16,40,640]{3,2,1,0:T(8,128)(2,1)} %bitcast.87), channel_id=1, source_target_pairs={{0,4},{4,0},{8,12},{12,8},{16,20},{20,16},{24,28},{28,24},{32,36},... | collective-permute-start | bytes 4915208 | tf_op jit(solution)/shard_map/ppermute | solution.py:416
  54.5 1.5 copy-start.1
  69.8 4.4 %collective-permute-start.15 = (f32[8,1536]{1,0:T(8,128)S(1)}, f32[8,1536]{1,0:T(8,128)S(1)}, u32[]{:S(2)}, u32[]{:S(2)}) collective-permute-start(f32[8,1536]{1,0:T(8,128)S(1)} %get-tuple-element.29.refs_0_), channel_id=1, source_target_pairs={{0,3},{1,0},{2,1},{3,2},{4,7},{5,4},{6,5},{7,6},{8,11},{9,8},{10,9... | collective-permute-start | bytes 147464 | tf_op jit(solution)/shard_map/ppermute | solution.py:419
  73.0 4.6 %collective-permute-start.14 = (f32[8,1536]{1,0:T(8,128)S(1)}, f32[8,1536]{1,0:T(8,128)S(1)}, u32[]{:S(2)}, u32[]{:S(2)}) collective-permute-start(f32[8,1536]{1,0:T(8,128)S(1)} %get-tuple-element.29.refs_0_), channel_id=1, source_target_pairs={{0,2},{1,3},{2,0},{3,1},{4,6},{5,7},{6,4},{7,5},{8,10},{9,11},{10,... | collective-permute-start | bytes 147464 | tf_op jit(solution)/shard_map/ppermute | solution.py:419
  73.0 4.7 %collective-permute-start.13 = (f32[8,1536]{1,0:T(8,128)S(1)}, f32[8,1536]{1,0:T(8,128)S(1)}, u32[]{:S(2)}, u32[]{:S(2)}) collective-permute-start(f32[8,1536]{1,0:T(8,128)S(1)} %get-tuple-element.29.refs_0_), channel_id=1, source_target_pairs={{0,1},{1,2},{2,3},{3,0},{4,5},{5,6},{6,7},{7,4},{8,9},{9,10},{10,1... | collective-permute-start | bytes 147464 | tf_op jit(solution)/shard_map/ppermute | solution.py:419
  77.7 1.5 copy-start.2
  79.2 1.9 copy-start.3
  84.2 26.8 %collective-permute-start.29 = (bf16[384,640]{1,0:T(8,128)(2,1)S(1)}, bf16[384,640]{1,0:T(8,128)(2,1)S(1)}, u32[]{:S(2)}, u32[]{:S(2)}) collective-permute-start(bf16[384,640]{1,0:T(8,128)(2,1)S(1)} %get-tuple-element.37), channel_id=1, source_target_pairs={{0,1},{1,2},{2,3},{3,0},{4,5},{5,6},{6,7},{7,4},{8,9},{9,10},{10,1... | collective-permute-start | bytes 1474568 | tf_op jit(solution)/shard_map/ppermute | solution.py:425
  84.3 9.0 %copy-start.8 = (bf16[1536,1280]{1,0:T(8,128)(2,1)S(1)}, bf16[1536,1280]{1,0:T(8,128)(2,1)}, u32[]{:S(2)}) copy-start(bf16[1536,1280]{1,0:T(8,128)(2,1)} %memory_ref.1) | copy-start | bytes 11796484
  101.1 9.9 %copy-start.9 = (bf16[1280,1280]{0,1:T(8,128)(2,1)}, bf16[1280,1280]{0,1:T(8,128)(2,1)S(1)}, u32[]{:S(2)}) copy-start(bf16[1280,1280]{0,1:T(8,128)(2,1)S(1)} %convolution_convert_fusion) | copy-start | bytes 9830404
  101.1 25.2 %collective-permute-start.31 = (bf16[384,640]{1,0:T(8,128)(2,1)S(1)}, bf16[384,640]{1,0:T(8,128)(2,1)S(1)}, u32[]{:S(2)}, u32[]{:S(2)}) collective-permute-start(bf16[384,640]{1,0:T(8,128)(2,1)S(1)} %get-tuple-element.39), channel_id=1, source_target_pairs={{0,3},{1,0},{2,1},{3,2},{4,7},{5,4},{6,5},{7,6},{8,11},{9,8},{10,9... | collective-permute-start | bytes 1474568 | tf_op jit(solution)/shard_map/ppermute | solution.py:431
  103.9 22.4 %collective-permute-start.32 = (bf16[384,640]{1,0:T(8,128)(2,1)S(1)}, bf16[384,640]{1,0:T(8,128)(2,1)S(1)}, u32[]{:S(2)}, u32[]{:S(2)}) collective-permute-start(bf16[384,640]{1,0:T(8,128)(2,1)S(1)} %get-tuple-element.41), channel_id=1, source_target_pairs={{0,1},{1,2},{2,3},{3,0},{4,5},{5,6},{6,7},{7,4},{8,9},{9,10},{10,1... | collective-permute-start | bytes 1474568 | tf_op jit(solution)/shard_map/ppermute | solution.py:430
  103.9 18.7 %collective-permute-start.33 = (bf16[384,640]{1,0:T(8,128)(2,1)S(1)}, bf16[384,640]{1,0:T(8,128)(2,1)S(1)}, u32[]{:S(2)}, u32[]{:S(2)}) collective-permute-start(bf16[384,640]{1,0:T(8,128)(2,1)S(1)} %get-tuple-element.42), channel_id=1, source_target_pairs={{0,3},{1,0},{2,1},{3,2},{4,7},{5,4},{6,5},{7,6},{8,11},{9,8},{10,9... | collective-permute-start | bytes 1474568 | tf_op jit(solution)/shard_map/ppermute | solution.py:426
  107.9 46.1 %collective-permute-start.16 = (bf16[16,40,1280]{2,1,0:T(8,128)(2,1)}, bf16[16,40,1280]{2,1,0:T(8,128)(2,1)}, u32[]{:S(2)}, u32[]{:S(2)}) collective-permute-start(bf16[16,40,1280]{2,1,0:T(8,128)(2,1)} %dynamic-slice_bitcast_fusion), channel_id=1, source_target_pairs={{0,4},{4,0},{8,12},{12,8},{16,20},{20,16},{24,28},{28,24},{32,36},... | collective-permute-start | bytes 4915208 | tf_op jit(solution)/shard_map/ppermute | solution.py:93
  111.2 15.2 %collective-permute-start.30 = (bf16[384,640]{1,0:T(8,128)(2,1)S(1)}, bf16[384,640]{1,0:T(8,128)(2,1)S(1)}, u32[]{:S(2)}, u32[]{:S(2)}) collective-permute-start(bf16[384,640]{1,0:T(8,128)(2,1)S(1)} %add_convert_fusion.1), channel_id=1, source_target_pairs={{0,1},{1,2},{2,3},{3,0},{4,5},{5,6},{6,7},{7,4},{8,9},{9,10},{10,1... | collective-permute-start | bytes 1474568 | tf_op jit(solution)/shard_map/ppermute | solution.py:432
  122.8 10.7 %collective-permute-start.34 = (bf16[384,640]{1,0:T(8,128)(2,1)S(1)}, bf16[384,640]{1,0:T(8,128)(2,1)S(1)}, u32[]{:S(2)}, u32[]{:S(2)}) collective-permute-start(bf16[384,640]{1,0:T(8,128)(2,1)S(1)} %add_convert_fusion), channel_id=1, source_target_pairs={{0,3},{1,0},{2,1},{3,2},{4,7},{5,4},{6,5},{7,6},{8,11},{9,8},{10,9... | collective-permute-start | bytes 1474568 | tf_op jit(solution)/shard_map/ppermute | solution.py:437
  142.9 69.1 %all-to-all-start.1 = ((bf16[128,48,256]{2,1,0:T(8,128)(2,1)}), bf16[128,48,256]{2,1,0:T(8,128)(2,1)S(1)}, u32[]{:S(2)}, u32[]{:S(2)}) async-start(bf16[128,48,256]{2,1,0:T(8,128)(2,1)} %bitcast.51), calls=%async_computation.1 | async-start | bytes 6291456 | tf_op jit(solution)/shard_map/all_to_all | solution.py:456
  156.6 38.3 %collective-permute-start.23 = (bf16[4,40,640]{2,1,0:T(8,128)(2,1)S(1)}, bf16[4,40,640]{2,1,0:T(8,128)(2,1)S(1)}, u32[]{:S(2)}, u32[]{:S(2)}) collective-permute-start(bf16[4,40,640]{2,1,0:T(8,128)(2,1)S(1)} %get-tuple-element.51), channel_id=1, source_target_pairs={{0,8},{4,12},{8,16},{12,20},{16,24},{20,28},{24,0},{28,4},{32,40},... | collective-permute-start | bytes 614408 | tf_op jit(solution)/shard_map/ppermute | solution.py:67
  158.0 39.6 %collective-permute-start.25 = (bf16[4,40,640]{2,1,0:T(8,128)(2,1)S(1)}, bf16[4,40,640]{2,1,0:T(8,128)(2,1)S(1)}, u32[]{:S(2)}, u32[]{:S(2)}) collective-permute-start(bf16[4,40,640]{2,1,0:T(8,128)(2,1)S(1)} %get-tuple-element.52), channel_id=1, source_target_pairs={{0,24},{4,28},{8,0},{12,4},{16,8},{20,12},{24,16},{28,20},{32,56},... | collective-permute-start | bytes 614408 | tf_op jit(solution)/shard_map/ppermute | solution.py:67
  159.4 40.2 %collective-permute-start.24 = (bf16[4,40,640]{2,1,0:T(8,128)(2,1)S(1)}, bf16[4,40,640]{2,1,0:T(8,128)(2,1)S(1)}, u32[]{:S(2)}, u32[]{:S(2)}) collective-permute-start(bf16[4,40,640]{2,1,0:T(8,128)(2,1)S(1)} %get-tuple-element.53), channel_id=1, source_target_pairs={{0,16},{4,20},{8,24},{12,28},{16,0},{20,4},{24,8},{28,12},{32,48},... | collective-permute-start | bytes 614408 | tf_op jit(solution)/shard_map/ppermute | solution.py:67
  161.2 41.3 %collective-permute-start.17 = (bf16[4,40,640]{2,1,0:T(8,128)(2,1)S(1)}, bf16[4,40,640]{2,1,0:T(8,128)(2,1)S(1)}, u32[]{:S(2)}, u32[]{:S(2)}) collective-permute-start(bf16[4,40,640]{2,1,0:T(8,128)(2,1)S(1)} %get-tuple-element.54), channel_id=1, source_target_pairs={{0,32},{4,36},{8,40},{12,44},{16,48},{20,52},{24,56},{28,60},{32,6... | collective-permute-start | bytes 614408 | tf_op jit(solution)/shard_map/ppermute | solution.py:67
  162.4 41.6 %collective-permute-start.19 = (bf16[4,40,640]{2,1,0:T(8,128)(2,1)S(1)}, bf16[4,40,640]{2,1,0:T(8,128)(2,1)S(1)}, u32[]{:S(2)}, u32[]{:S(2)}) collective-permute-start(bf16[4,40,640]{2,1,0:T(8,128)(2,1)S(1)} %get-tuple-element.55), channel_id=1, source_target_pairs={{0,96},{4,100},{8,104},{12,108},{16,112},{20,116},{24,120},{28,124... | collective-permute-start | bytes 614408 | tf_op jit(solution)/shard_map/ppermute | solution.py:67
  194.8 9.2 %collective-permute-start.18 = (bf16[4,40,640]{2,1,0:T(8,128)(2,1)S(1)}, bf16[4,40,640]{2,1,0:T(8,128)(2,1)S(1)}, u32[]{:S(2)}, u32[]{:S(2)}) collective-permute-start(bf16[4,40,640]{2,1,0:T(8,128)(2,1)S(1)} %get-tuple-element.56), channel_id=1, source_target_pairs={{0,64},{4,68},{8,72},{12,76},{16,80},{20,84},{24,88},{28,92},{32,9... | collective-permute-start | bytes 614408 | tf_op jit(solution)/shard_map/ppermute | solution.py:67
  199.7 7.2 %collective-permute-start.26 = (bf16[40,640]{1,0:T(8,128)(2,1)S(1)}, bf16[40,640]{1,0:T(8,128)(2,1)S(1)}, u32[]{:S(2)}, u32[]{:S(2)}) collective-permute-start(bf16[40,640]{1,0:T(8,128)(2,1)S(1)} %get-tuple-element.57), channel_id=1, source_target_pairs={{0,32},{4,36},{8,40},{12,44},{16,48},{20,52},{24,56},{28,60},{32,6... | collective-permute-start | bytes 153608 | tf_op jit(solution)/shard_map/ppermute | solution.py:67
  201.1 5.9 %collective-permute-start.28 = (bf16[40,640]{1,0:T(8,128)(2,1)S(1)}, bf16[40,640]{1,0:T(8,128)(2,1)S(1)}, u32[]{:S(2)}, u32[]{:S(2)}) collective-permute-start(bf16[40,640]{1,0:T(8,128)(2,1)S(1)} %get-tuple-element.58), channel_id=1, source_target_pairs={{0,96},{4,100},{8,104},{12,108},{16,112},{20,116},{24,120},{28,124... | collective-permute-start | bytes 153608 | tf_op jit(solution)/shard_map/ppermute | solution.py:67
  202.4 4.5 %collective-permute-start.27 = (bf16[40,640]{1,0:T(8,128)(2,1)S(1)}, bf16[40,640]{1,0:T(8,128)(2,1)S(1)}, u32[]{:S(2)}, u32[]{:S(2)}) collective-permute-start(bf16[40,640]{1,0:T(8,128)(2,1)S(1)} %get-tuple-element.59), channel_id=1, source_target_pairs={{0,64},{4,68},{8,72},{12,76},{16,80},{20,84},{24,88},{28,92},{32,9... | collective-permute-start | bytes 153608 | tf_op jit(solution)/shard_map/ppermute | solution.py:67
  204.2 4.5 %collective-permute-start.20 = (bf16[40,640]{1,0:T(8,128)(2,1)S(1)}, bf16[40,640]{1,0:T(8,128)(2,1)S(1)}, u32[]{:S(2)}, u32[]{:S(2)}) collective-permute-start(bf16[40,640]{1,0:T(8,128)(2,1)S(1)} %get-tuple-element.60), channel_id=1, source_target_pairs={{0,8},{4,12},{8,16},{12,20},{16,24},{20,28},{24,0},{28,4},{32,40},... | collective-permute-start | bytes 153608 | tf_op jit(solution)/shard_map/ppermute | solution.py:67
  204.8 3.9 %collective-permute-start.22 = (bf16[40,640]{1,0:T(8,128)(2,1)S(1)}, bf16[40,640]{1,0:T(8,128)(2,1)S(1)}, u32[]{:S(2)}, u32[]{:S(2)}) collective-permute-start(bf16[40,640]{1,0:T(8,128)(2,1)S(1)} %get-tuple-element.61), channel_id=1, source_target_pairs={{0,24},{4,28},{8,0},{12,4},{16,8},{20,12},{24,16},{28,20},{32,56},... | collective-permute-start | bytes 153608 | tf_op jit(solution)/shard_map/ppermute | solution.py:67
  206.9 4.5 %collective-permute-start.21 = (bf16[40,640]{1,0:T(8,128)(2,1)S(1)}, bf16[40,640]{1,0:T(8,128)(2,1)S(1)}, u32[]{:S(2)}, u32[]{:S(2)}) collective-permute-start(bf16[40,640]{1,0:T(8,128)(2,1)S(1)} %get-tuple-element.62), channel_id=1, source_target_pairs={{0,16},{4,20},{8,24},{12,28},{16,0},{20,4},{24,8},{28,12},{32,48},... | collective-permute-start | bytes 153608 | tf_op jit(solution)/shard_map/ppermute | solution.py:67
  212.1 1.6 copy-start.5
  213.7 1.6 copy-start.6
  215.2 1.6 copy-start.7
  (1 other events, 1.4 us)

commit v3 on v2

--- a/solution.py
+++ b/solution.py
@@ -55,6 +55,10 @@
 
 
 STEPS = (1, 2, 3)
+
+
+def in_hbm(*arrays):
+    return tuple(pltpu.with_memory_space_constraint(a, pltpu.HBM) for a in arrays)
 
 
 def ring_gather(shard, perm_of):
@@ -74,29 +78,39 @@
     return own
 
 
-def gather_weights(key_weight, value_weight):
+def gather_weights(key_weight, value_weight, send_ids):
     key_x = ring_gather(key_weight, along_x)
     value_y = ring_gather(value_weight, along_y)
     key_x = jnp.stack(key_x)
     value_y = jnp.stack(value_y)
     key_x, value_y = lax.optimization_barrier((key_x, value_y))
-    key_all = jnp.stack(ring_gather(key_x, along_y))
-    value_all = jnp.stack(ring_gather(value_y, along_x))
-    return jnp.stack([key_all, value_all])
-
-
-def sum_weight_grads(weight_grads, x, y, c):
-    width = weight_grads.shape[1]
-    tiles = weight_grads.reshape(16, 2, -1, width)
+    key_all = ring_gather(key_x, along_y)
+    value_all = ring_gather(value_y, along_x)
+    key_all[1], send_ids = lax.optimization_barrier((key_all[1], send_ids))
+    got_ids = lax.all_to_all(
+        send_ids, ("dp", "tensor"), split_axis=0, concat_axis=0, tiled=True
+    )
+    return (jnp.stack([jnp.stack(key_all), jnp.stack(value_all)]), got_ids)
+
+
+def core_halves(weight_grads, c):
+    tiles = weight_grads.reshape(16, 2, -1, weight_grads.shape[1])
     sent = lax.dynamic_index_in_dim(tiles, 1 - c, 1, keepdims=False)
     kept = lax.dynamic_index_in_dim(tiles, c, 1, keepdims=False)
+    return (sent, kept)
+
+
+def sum_on_chip(sent, kept):
     got = lax.ppermute(sent, "dp", other_core())
     both = (kept.astype(jnp.float32) + got.astype(jnp.float32)).astype(jnp.bfloat16)
-    both = both.reshape(4, 4, -1, width)
-    half = width // 2
+    return both.reshape(4, 4, *both.shape[1:])
+
+
+def sum_one_axis(both, x, y):
+    half = both.shape[3] // 2
     key_part = ring_sum(both[:, :, :, :half], x, along_x).astype(jnp.bfloat16)
     value_part = ring_sum(jnp.swapaxes(both[:, :, :, half:], 0, 1), y, along_y).astype(jnp.bfloat16)
-    return (ring_sum(key_part, y, along_y), ring_sum(value_part, x, along_x))
+    return (key_part, value_part)
 
 
 def project_kernel(
@@ -146,31 +160,31 @@
         project_kernel,
         out_shape=(
             jax.ShapeDtypeStruct((mem, 2 * half), jnp.bfloat16),
-            jax.ShapeDtypeStruct((tokens, half), jnp.float32),
+            pltpu.HBM((tokens, half), jnp.float32),
             jax.ShapeDtypeStruct((8, tokens), jnp.float32),
         ),
         grid_spec=pltpu.PrefetchScalarGridSpec(
             num_scalar_prefetch=1,
             grid=(4,),
             in_specs=[
-                pl.BlockSpec(mine.shape, lambda i, s: (0, 0, 0, 0)),
-                pl.BlockSpec(got.shape, lambda i, s: (0, 0, 0, 0)),
+                pl.BlockSpec(mine.shape, lambda i, s: (0, 0, 0, 0), pipeline_mode=pl.Buffered(1)),
+                pl.BlockSpec(got.shape, lambda i, s: (0, 0, 0, 0), pipeline_mode=pl.Buffered(1)),
                 pl.BlockSpec((tile, mem), lambda i, s: (i, 0)),
                 pl.BlockSpec((tile, half), lambda i, s: (i, 0)),
                 pl.BlockSpec((tile, half), lambda i, s: (i, 0)),
             ],
             out_specs=(
-                pl.BlockSpec((mem, 2 * half), fixed),
+                pl.BlockSpec((mem, 2 * half), fixed, pipeline_mode=pl.Buffered(1)),
                 pl.BlockSpec((tile, half), lambda i, s: (i, 0)),
                 pl.BlockSpec((8, tile), lambda i, s: (0, i)),
             ),
         ),
-        compiler_params=pltpu.CompilerParams(vmem_limit_bytes=44 * 1024 * 1024),
+        compiler_params=pltpu.CompilerParams(vmem_limit_bytes=30 * 1024 * 1024),
         name="project",
-    )(spot, mine, got, memory, hidden, grad_out)
-
-
-def grads_of(sums_refs, hidden_ref, grad_ref, key_proj_ref, weight_ref, both_ref):
+    )(spot, *in_hbm(mine, got, memory, hidden, grad_out))
+
+
+def gates_of(sums_refs, hidden_ref, grad_ref, key_proj_ref, both_ref):
     half = hidden_ref.shape[1]
     sums = sums_refs[0][...] + sums_refs[1][...] + sums_refs[2][...] + sums_refs[3][...]
     root_width = math.sqrt(D)
@@ -191,57 +205,61 @@
     value_grad = coded[:, 0:1] * grad_ref[...].astype(jnp.float32)
     both_ref[:, :half] = key_grad.astype(jnp.bfloat16)
     both_ref[:, half:] = value_grad.astype(jnp.bfloat16)
-    return lax.dot_general(
-        both_ref[...],
-        weight_ref[...],
-        (((1,), (1,)), ((), ())),
-        preferred_element_type=jnp.float32,
-    ).astype(jnp.bfloat16)
 
 
 def grads_kernel(order_ref, *refs):
-    sums_refs, (hidden_ref, grad_ref, key_proj_ref, weight_ref), rest = refs[:4], refs[4:8], refs[8:]
-    if len(rest) % 2 == 0:
-        rest = rest[1:]
-    both_ref, outs = rest[0], rest[1:]
-    memory_grad = grads_of(sums_refs, hidden_ref, grad_ref, key_proj_ref, weight_ref, both_ref)
+    both_ref, outs = refs[8], refs[9:]
     half = outs[0].shape[1]
-    for k in range(len(outs) // 2):
-
-        @pl.when(pl.program_id(0) == k)
-        def _():
-            outs[2 * k][...] = memory_grad[:, :half]
-            outs[2 * k + 1][...] = memory_grad[:, half:]
-
-
-def grads(order, sums, hidden, grad_out, key_proj, weights, both):
+    gates_of(refs[:4], *refs[4:7], both_ref)
+
+    @pl.when(pl.program_id(0) < len(outs) // 2)
+    def _():
+        memory_grad = lax.dot_general(
+            both_ref[...],
+            refs[7][...],
+            (((1,), (1,)), ((), ())),
+            preferred_element_type=jnp.float32,
+        ).astype(jnp.bfloat16)
+        for k in range(len(outs) // 2):
+
+            @pl.when(pl.program_id(0) == k)
+            def _():
+                outs[2 * k][...] = memory_grad[:, :half]
+                outs[2 * k + 1][...] = memory_grad[:, half:]
+
+
+def grads(order, products, sums, hidden, grad_out, key_proj, weights):
     steps = order.shape[0]
     tokens, half = hidden.shape
     tile = tokens // 4
     mem = weights.shape[0]
     at = lambda i, o: (o[i], 0)
-    out_half = pl.BlockSpec((tile, mem // 2), lambda i, o: (0, 0))
-    whole = pl.BlockSpec((tile, 2 * half), at)
-    given = () if both is None else (both,)
+    fixed = lambda i, o: (0, 0)
+    one = pl.Buffered(1)
+    if steps == 1:
+        both_shape, both_spec = (tile, 2 * half), pl.BlockSpec((tile, 2 * half), fixed)
+    else:
+        both_shape, both_spec = (tokens, 2 * half), pl.BlockSpec((tile, 2 * half), at)
     return pl.pallas_call(
         grads_kernel,
         out_shape=(
-            jax.ShapeDtypeStruct((tokens, 2 * half), jnp.bfloat16),
-            *([jax.ShapeDtypeStruct((tile, mem // 2), jnp.bfloat16)] * (2 * steps)),
+            pltpu.HBM(both_shape, jnp.bfloat16),
+            *([jax.ShapeDtypeStruct((tile, mem // 2), jnp.bfloat16)] * (2 * products)),
         ),
         grid_spec=pltpu.PrefetchScalarGridSpec(
             num_scalar_prefetch=1,
             grid=(steps,),
             in_specs=[pl.BlockSpec((8, tile), lambda i, o: (0, o[i]))] * 4
             + [pl.BlockSpec((tile, half), at)] * 3
-            + [pl.BlockSpec(weights.shape, lambda i, o: (0, 0))]
-            + [pl.BlockSpec(memory_space=pl.ANY)] * len(given),
-            out_specs=(whole, *([out_half] * (2 * steps))),
+            + [pl.BlockSpec(weights.shape, fixed, pipeline_mode=one)],
+            out_specs=(
+                both_spec,
+                *([pl.BlockSpec((tile, mem // 2), fixed, pipeline_mode=one)] * (2 * products)),
+            ),
         ),
-        input_output_aliases={9: 0} if given else {},
-        compiler_params=pltpu.CompilerParams(vmem_limit_bytes=44 * 1024 * 1024),
-        name="grads_far" if both is None else "grads_near",
-    )(order, *sums, hidden, grad_out, key_proj, weights, *given)
+        compiler_params=pltpu.CompilerParams(vmem_limit_bytes=26 * 1024 * 1024),
+        name="grads_far" if steps == 1 else "grads_near",
+    )(order, *sums, *in_hbm(hidden, grad_out, key_proj), weights)
 
 
 SLOTS = 48
@@ -297,7 +315,7 @@
             pltpu.VMEM((tokens, 2 * half), jnp.bfloat16),
             pltpu.VMEM((lookups * tokens, width), jnp.bfloat16),
         ],
-        compiler_params=pltpu.CompilerParams(vmem_limit_bytes=40 * 1024 * 1024),
+        compiler_params=pltpu.CompilerParams(vmem_limit_bytes=26 * 1024 * 1024),
         name="pack_rows",
     )(slot // TILE, slot % TILE, *parts)
 
@@ -347,9 +365,9 @@
             block,
         ],
         out_specs=(block,) * 3,
-        compiler_params=pltpu.CompilerParams(vmem_limit_bytes=40 * 1024 * 1024),
+        compiler_params=pltpu.CompilerParams(vmem_limit_bytes=26 * 1024 * 1024),
         name="adam_rows",
-    )(ids // TILE, ids % TILE, got_rows, embed_table, first_moment, second_moment)
+    )(ids // TILE, ids % TILE, got_rows, *in_hbm(embed_table, first_moment, second_moment))
 
 
 def route(my_ids, owners, rows_dev):
@@ -407,10 +425,7 @@
     z = lax.axis_index("tensor")
     x, y, c = at // 8, (at // 2) % 4, at % 2
     slot, send_ids = route(my_ids, owners, rows_dev)
-    got_ids = lax.all_to_all(
-        send_ids, ("dp", "tensor"), split_axis=0, concat_axis=0, tiled=True
-    )
-    mine = gather_weights(key_weight, value_weight)
+    mine, got_ids = gather_weights(key_weight, value_weight, send_ids)
     mine, got_ids, slot = lax.optimization_barrier((mine, got_ids, slot))
     mine = mine.reshape(2, 16, *key_weight.shape)
     got = lax.ppermute(mine, "dp", other_core())
@@ -418,41 +433,40 @@
     weights, key_proj, sums = project(spot, mine, got, memory, hidden, grad_out)
     sums = [sums] + [lax.ppermute(sums, "tensor", along_z(d)) for d in STEPS]
     far = ((z + 2) % 4)[None].astype(jnp.int32)
-    near = jnp.stack([(z + 1) % 4, (z + 3) % 4, z]).astype(jnp.int32)
-    both, far_left, far_right = grads(
-        far, sums, hidden, grad_out, key_proj, weights, None
-    )
+    near = jnp.stack([(z + 1) % 4, (z + 3) % 4, z, (z + 2) % 4]).astype(jnp.int32)
+    _, far_left, far_right = grads(far, 1, sums, hidden, grad_out, key_proj, weights)
     up = lax.ppermute(far_left, "tensor", along_z(1))
     down = lax.ppermute(far_right, "tensor", along_z(3))
     both, next_left, next_right, last_left, last_right, own_left, own_right = grads(
-        near, sums, hidden, grad_out, key_proj, weights, both
+        near, 3, sums, hidden, grad_out, key_proj, weights
     )
     from_last_right = lax.ppermute(next_right, "tensor", along_z(1))
     from_next_left = lax.ppermute(last_left, "tensor", along_z(3))
-    from_last_left = lax.ppermute(
-        (up.astype(jnp.float32) + next_left.astype(jnp.float32)).astype(jnp.bfloat16),
-        "tensor",
-        along_z(1),
-    )
-    from_next_right = lax.ppermute(
-        (down.astype(jnp.float32) + last_right.astype(jnp.float32)).astype(jnp.bfloat16),
-        "tensor",
-        along_z(3),
-    )
-    key_weight_grad, value_weight_grad = sum_weight_grads(
-        lax.dot_general(
-            memory, both, (((0,), (0,)), ((), ())), preferred_element_type=jnp.float32
-        ).astype(jnp.bfloat16),
-        x,
-        y,
-        c,
-    )
+    next_left = (up.astype(jnp.float32) + next_left.astype(jnp.float32)).astype(jnp.bfloat16)
+    last_right = (down.astype(jnp.float32) + last_right.astype(jnp.float32)).astype(jnp.bfloat16)
+    both, next_left, last_right = lax.optimization_barrier((both, next_left, last_right))
+    from_last_left = lax.ppermute(next_left, "tensor", along_z(1))
+    from_next_right = lax.ppermute(last_right, "tensor", along_z(3))
+    weight_grads = lax.dot_general(
+        memory, both, (((0,), (0,)), ((), ())), preferred_element_type=jnp.float32
+    ).astype(jnp.bfloat16)
+    sent, kept = core_halves(weight_grads, c)
+    sent, kept, from_last_right, from_next_left = lax.optimization_barrier(
+        (sent, kept, from_last_right, from_next_left)
+    )
+    chip_grads = sum_on_chip(sent, kept)
+    chip_grads, slot, from_last_left, from_next_right = lax.optimization_barrier(
+        (chip_grads, slot, from_last_left, from_next_right)
+    )
+    key_part, value_part = sum_one_axis(chip_grads, x, y)
     send_rows = pack_rows(
         slot,
         (own_left, from_last_left, from_next_left, own_right, from_last_right, from_next_right),
         owners * SLOTS,
         row_width,
     )
+    key_weight_grad = ring_sum(key_part, y, along_y)
+    value_weight_grad = ring_sum(value_part, x, along_x)
     got_rows = lax.all_to_all(
         send_rows.reshape(owners, SLOTS, row_width),
         ("dp", "tensor"),

time: 229 us -> 212 us (0.926)
  waiting for transfers between devices: 75.7 us -> 66.2 us
  local copies, waits for them, and re-layouts: 14.4 us -> 5.51 us
  starting transfers between devices: 72.6 us -> 68 us
  Pallas kernels: 43.3 us -> 47.3 us
    ppermute x1, waiting for transfers between devices: 11.4 us -> 0.01 us  [body(): down = lax.ppermute(far_right, 'tensor', along_z(3))]
    unnamed x24 -> x16, local copies, waits for them, and re-layouts: 11.2 us -> 0.83 us
    ppermute x12, waiting for transfers between devices: 13.6 us -> 3.31 us  [ring_gather(): return [shard] + [lax.ppermute(shard, 'dp', perm_of(d)) for d in STEPS]]
    all_to_all x1, waiting for transfers between devices: 0.01 us -> 9.1 us  [gather_weights(): lax.all_to_all(send_ids, ('dp', 'tensor'), split_axis=0, concat_axis=0, t...]
    all_to_all x1, starting transfers between devices: 9.74 us -> 15.7 us  [gather_weights(): lax.all_to_all(send_ids, ('dp', 'tensor'), split_axis=0, concat_axis=0, t...]
    all_to_all x1, starting transfers between devices: 11.1 us -> 6.68 us  [body(): lax.all_to_all(send_rows.reshape(owners, SLOTS, row_width), ('dp', 'tenso...]
    ppermute x12, starting transfers between devices: 18 us -> 15.2 us  [ring_gather(): return [shard] + [lax.ppermute(shard, 'dp', perm_of(d)) for d in STEPS]]
    pallas_call x2, Pallas kernels: 12.1 us -> 14.5 us  [grads(): pl.pallas_call(grads_kernel, out_shape=(pltpu.HBM(both_shape, jnp.bfloat1...]
  transfers between devices with their start and end apart: 37 -> 37, of which waited for: 13 -> 13; matrix products, arithmetic and copies ran while one was open for 10% -> 12% of each run, Pallas kernels for 8% -> 5%
where the time goes in v3:
time: 212 us; the launch traced here: 210 us
  starting transfers between devices  68 us (32%)
  waiting for transfers between devices  66.2 us (31%)
  Pallas kernels  47.3 us (22%)
  matrix products  10.8 us (5%)
  other arithmetic  10.7 us (5%)
  local copies, waits for them, and re-layouts  5.51 us (3%)
    ppermute x12, waiting for transfers between devices, ring_sum(): lax.ppermute(lax.dynamic_index_in_dim(tiles, (here + d) % 4, 0, keepdims=...  37.5 us
    ppermute x12, starting transfers between devices, ring_sum(): lax.ppermute(lax.dynamic_index_in_dim(tiles, (here + d) % 4, 0, keepdims=...  17 us
    all_to_all x1, starting transfers between devices, gather_weights(): lax.all_to_all(send_ids, ('dp', 'tensor'), split_axis=0, concat_axis=0, t...  15.7 us
    ppermute x12, starting transfers between devices, ring_gather(): return [shard] + [lax.ppermute(shard, 'dp', perm_of(d)) for d in STEPS]  15.2 us
    pallas_call x2, Pallas kernels, grads(): pl.pallas_call(grads_kernel, out_shape=(pltpu.HBM(both_shape, jnp.bfloat1...  14.5 us
    pallas_call x1, Pallas kernels, project(): pl.pallas_call(project_kernel, out_shape=(jax.ShapeDtypeStruct((mem, 2 *...  12.4 us
    pallas_call x1, Pallas kernels, adam_rows(): pl.pallas_call(adam_kernel, out_shape=(jax.ShapeDtypeStruct((rows_dev, wi...  11 us
    pallas_call x1, Pallas kernels, pack_rows(): pl.pallas_call(pack_kernel, out_shape=jax.ShapeDtypeStruct((total_slots,...  9.44 us
  transfers between devices with their start and end apart: 37, of which 13 were waited for; matrix products, arithmetic and copies ran while one was open for 12% of the time, Pallas kernels for 5%

profile of v3, /device:TPU:1, one launch (start us, length us, event | category | flops | bytes accessed | tf_op | source)
XLA Modules:
  0.0 209.6 jit_solution(14587065535516800366)
XLA Ops:
  0.6 2.1 %collective-permute-start = (bf16[40,640]{1,0:T(8,128)(2,1)}, bf16[40,640]{1,0:T(8,128)(2,1)S(1)}, u32[]{:S(2)}, u32[]{:S(2)}) collective-permute-start(bf16[40,640]{1,0:T(8,128)(2,1)} %param.12), channel_id=1, source_target_pairs={{0,32},{4,36},{8,40},{12,44},{16,48},{20,52},{24,56},{28,60},{32,6... | collective-permute-start | bytes 153608 | tf_op jit(solution)/shard_map/ppermute | solution.py:65
  2.7 1.4 collective-permute-start.2
  4.1 1.6 collective-permute-start.1
  5.7 1.3 collective-permute-start.3
  7.0 1.4 collective-permute-start.5
  9.2 1.8 fusion.2
  11.0 1.5 select_convert_fusion.2
  12.6 1.3 convolution_convert_fusion.1
  13.9 1.7 collective-permute-start.4
  15.7 2.7 %collective-permute-done.4 = bf16[40,640]{1,0:T(8,128)(2,1)S(1)} collective-permute-done((bf16[40,640]{1,0:T(8,128)(2,1)S(1)}, bf16[40,640]{1,0:T(8,128)(2,1)S(1)}, u32[]{:S(2)}, u32[]{:S(2)}) %collective-permute-start.4) | collective-permute-done | bytes 51232 | tf_op jit(solution)/shard_map/ppermute | solution.py:65
  18.5 2.7 %collective-permute-start.8 = (bf16[4,40,640]{2,1,0:T(8,128)(2,1)S(1)}, bf16[4,40,640]{2,1,0:T(8,128)(2,1)S(1)}, u32[]{:S(2)}, u32[]{:S(2)}) collective-permute-start(bf16[4,40,640]{2,1,0:T(8,128)(2,1)S(1)} %pad_maximum_fusion.1), channel_id=1, source_target_pairs={{0,24},{4,28},{8,0},{12,4},{16,8},{20,12},{24,16},{28,20},{32,56},... | collective-permute-start | bytes 614408 | tf_op jit(solution)/shard_map/ppermute | solution.py:65
  22.5 1.2 collective-permute-start.10
  26.1 15.7 %all-to-all-start = ((s32[128,1,48]{2,1,0:T(1,128)}), s32[128,1,48]{2,1,0:T(1,128)S(1)}, u32[]{:S(2)}, u32[]{:S(2)}) async-start(s32[128,1,48]{2,1,0:T(1,128)} %copy.16), calls=%async_computation | async-start | bytes 131072 | tf_op jit(solution)/shard_map/all_to_all | solution.py:90
  42.3 9.1 %all-to-all-done = s32[128,1,48]{2,1,0:T(1,128)S(1)} async-done(((s32[128,1,48]{2,1,0:T(1,128)}), s32[128,1,48]{2,1,0:T(1,128)S(1)}, u32[]{:S(2)}, u32[]{:S(2)}) %all-to-all-start) | async-done | bytes 24608 | tf_op jit(solution)/shard_map/all_to_all | solution.py:90
  51.9 3.2 %collective-permute-done.12.got_ref = bf16[2,16,40,640]{3,2,1,0:T(8,128)(2,1)} collective-permute-done((bf16[2,16,40,640]{3,2,1,0:T(8,128)(2,1)S(1)}, bf16[2,16,40,640]{3,2,1,0:T(8,128)(2,1)}, u32[]{:S(2)}, u32[]{:S(2)}) %collective-permute-start.12) | collective-permute-done | bytes 1638432 | tf_op jit(solution)/shard_map/ppermute | solution.py:431
  55.1 12.4 %project.1 = (bf16[1280,1280]{1,0:T(8,128)(2,1)S(1)}, f32[1536,640]{1,0:T(8,128)}, f32[8,1536]{1,0:T(8,128)S(1)}) custom-call(s32[3]{0:T(128)S(1)} %pad_add_fusion.1.spot_ref, bf16[2,16,40,640]{3,2,1,0:T(8,128)(2,1)} %bitcast.85, bf16[2,16,40,640]{3,2,1,0:T(8,128)(2,1)} %collective-permute-done.12.got_ref, bf16[1536,1280]{1,0:T(8,128)(2,1)} %memory_ref.1, ...), custom_call_target="tpu_custom_call" | custom-call | tf_op jit(solution)/shard_map/project/pallas_call | solution.py:159
  68.4 1.5 collective-permute-start.14
  70.5 2.4 %collective-permute-done.14.refs_2_ = f32[8,1536]{1,0:T(8,128)S(1)} collective-permute-done((f32[8,1536]{1,0:T(8,128)S(1)}, f32[8,1536]{1,0:T(8,128)S(1)}, u32[]{:S(2)}, u32[]{:S(2)}) %collective-permute-start.14) | collective-permute-done | bytes 49184 | tf_op jit(solution)/shard_map/ppermute | solution.py:434
  72.8 1.8 collective-permute-done.13.refs_1_
  74.7 4.2 %grads_far.1 = (bf16[384,1280]{1,0:T(8,128)(2,1)}, bf16[384,640]{1,0:T(8,128)(2,1)}, bf16[384,640]{1,0:T(8,128)(2,1)}) custom-call(s32[1]{0:T(128)} %bitcast.3.order_ref, f32[8,1536]{1,0:T(8,128)S(1)} %get-tuple-element.43.refs_0_, f32[8,1536]{1,0:T(8,128)S(1)} %collective-permute-done.13.refs_1_, f32[8,1536]{1,0:T(8,128)S(1)} %collective-permute-done.14.refs_2_, ...), custom_call_target="tpu_custom_call" | custom-call | tf_op jit(solution)/shard_map/grads_far/pallas_call | solution.py:243
  78.9 2.7 %collective-permute-start.17 = (bf16[384,640]{1,0:T(8,128)(2,1)}, bf16[384,640]{1,0:T(8,128)(2,1)}, u32[]{:S(2)}, u32[]{:S(2)}) collective-permute-start(bf16[384,640]{1,0:T(8,128)(2,1)} %get-tuple-element.49), channel_id=1, source_target_pairs={{0,3},{1,0},{2,1},{3,2},{4,7},{5,4},{6,5},{7,6},{8,11},{9,8},{10,9... | collective-permute-start | bytes 1474568 | tf_op jit(solution)/shard_map/ppermute | solution.py:439
  81.7 10.3 %grads_near.1 = (bf16[1536,1280]{1,0:T(8,128)(2,1)}, bf16[384,640]{1,0:T(8,128)(2,1)S(1)}, bf16[384,640]{1,0:T(8,128)(2,1)S(1)}, bf16[384,640]{1,0:T(8,128)(2,1)...) custom-call(s32[4]{0:T(128)S(1)} %pad_add_fusion.order_ref, ...), custom_call_target="tpu_custom_call" | custom-call | tf_op jit(solution)/shard_map/grads_near/pallas_call | solution.py:243
  92.8 2.7 %collective-permute-start.19 = (bf16[384,640]{1,0:T(8,128)(2,1)S(1)}, bf16[384,640]{1,0:T(8,128)(2,1)S(1)}, u32[]{:S(2)}, u32[]{:S(2)}) collective-permute-start(bf16[384,640]{1,0:T(8,128)(2,1)S(1)} %get-tuple-element.53), channel_id=1, source_target_pairs={{0,3},{1,0},{2,1},{3,2},{4,7},{5,4},{6,5},{7,6},{8,11},{9,8},{10,9... | collective-permute-start | bytes 1474568 | tf_op jit(solution)/shard_map/ppermute | solution.py:444
  95.5 1.1 add_convert_fusion.2
  96.6 1.9 add_convert_fusion.1
  98.5 7.8 %convolution_convert_fusion = bf16[1280,1280]{0,1:T(8,128)(2,1)S(1)} fusion(bf16[1536,1280]{1,0:T(8,128)(2,1)} %get-tuple-element.51, bf16[1536,1280]{1,0:T(8,128)(2,1)S(1)} %copy-done.5), kind=kOutput, calls=%fused_computation.2 | convolution fusion | flops 5034803200 | bytes 11141120 | tf_op jit(solution)/shard_map/dot_general | solution.py:450
  106.3 1.4 dynamic-slice_bitcast_fusion
  107.8 2.5 %collective-permute-start.20 = (bf16[16,40,1280]{2,1,0:T(8,128)(2,1)}, bf16[16,40,1280]{2,1,0:T(8,128)(2,1)}, u32[]{:S(2)}, u32[]{:S(2)}) collective-permute-start(bf16[16,40,1280]{2,1,0:T(8,128)(2,1)} %get-tuple-element.55), channel_id=1, source_target_pairs={{0,4},{4,0},{8,12},{12,8},{16,20},{20,16},{24,28},{28,24},{32,36},... | collective-permute-start | bytes 4915208 | tf_op jit(solution)/shard_map/ppermute | solution.py:104
  110.5 2.7 %collective-permute-start.22 = (bf16[384,640]{1,0:T(8,128)(2,1)}, bf16[384,640]{1,0:T(8,128)(2,1)S(1)}, u32[]{:S(2)}, u32[]{:S(2)}) collective-permute-start(bf16[384,640]{1,0:T(8,128)(2,1)} %add_convert_fusion.1), channel_id=1, source_target_pairs={{0,3},{1,0},{2,1},{3,2},{4,7},{5,4},{6,5},{7,6},{8,11},{9,8},{10,9... | collective-permute-start | bytes 1474568 | tf_op jit(solution)/shard_map/ppermute | solution.py:449
  113.8 3.0 %add_convert_fusion = bf16[16,40,1280]{2,1,0:T(8,128)(2,1)} fusion(bf16[16,40,1280]{2,1,0:T(8,128)(2,1)} %collective-permute-done.20, bf16[16,40,1280]{2,1,0:T(8,128)(2,1)S(1)} %get-tuple-element.54), kind=kLoop, calls=%fused_computation.3 | loop fusion | flops 3276800 | bytes 4915200 | tf_op jit(solution)/shard_map/convert_element_type | solution.py:105
  116.7 7.6 %collective-permute-done.21.l2 = bf16[384,640]{1,0:T(8,128)(2,1)S(1)} collective-permute-done((bf16[384,640]{1,0:T(8,128)(2,1)S(1)}, bf16[384,640]{1,0:T(8,128)(2,1)S(1)}, u32[]{:S(2)}, u32[]{:S(2)}) %collective-permute-start.21) | collective-permute-done | bytes 491552 | tf_op jit(solution)/shard_map/ppermute | solution.py:448
  124.4 9.4 %pack_rows.1 = bf16[6144,256]{1,0:T(8,128)(2,1)} custom-call(s32[5,384]{1,0:T(8,128)S(1)} %get-tuple-element.90.tile_ref, s32[5,384]{1,0:T(8,128)S(1)} %get-tuple-element.89.spot_ref, bf16[384,640]{1,0:T(8,128)(2,1)S(1)} %copy-done.1, bf16[384,640]{1,0:T(8,128)(2,1)S(1)} %collective-permute-done.21.l2, bf16[384,640]{1,0:T(8,128)(2,1)S(1)} %collective-permute-done.19.l3, ...), custom_call_target="tpu_custom_call" | custom-call | tf_op jit(solution)/shard_map/pack_rows/pallas_call | solution.py:307
  133.9 6.7 %all-to-all-start.1 = ((bf16[128,48,256]{2,1,0:T(8,128)(2,1)}), bf16[128,48,256]{2,1,0:T(8,128)(2,1)S(1)}, u32[]{:S(2)}, u32[]{:S(2)}) async-start(bf16[128,48,256]{2,1,0:T(8,128)(2,1)} %bitcast.51), calls=%async_computation.1 | async-start | bytes 6291456 | tf_op jit(solution)/shard_map/all_to_all | solution.py:470
  140.6 1.5 fusion.33
  142.2 1.5 collective-permute-start.29
  143.7 1.3 collective-permute-start.31
  145.1 1.6 collective-permute-start.30
  146.9 1.3 collective-permute-start.23
  148.1 1.5 collective-permute-start.25
  149.6 31.8 %collective-permute-done.29 = bf16[4,40,640]{2,1,0:T(8,128)(2,1)S(1)} collective-permute-done((bf16[4,40,640]{2,1,0:T(8,128)(2,1)S(1)}, bf16[4,40,640]{2,1,0:T(8,128)(2,1)S(1)}, u32[]{:S(2)}, u32[]{:S(2)}) %collective-permute-start.29) | collective-permute-done | bytes 204832 | tf_op jit(solution)/shard_map/ppermute | solution.py:71
  181.4 2.8 %collective-permute-start.24 = (bf16[4,40,640]{2,1,0:T(8,128)(2,1)S(1)}, bf16[4,40,640]{2,1,0:T(8,128)(2,1)S(1)}, u32[]{:S(2)}, u32[]{:S(2)}) collective-permute-start(bf16[4,40,640]{2,1,0:T(8,128)(2,1)S(1)} %get-tuple-element.82), channel_id=1, source_target_pairs={{0,64},{4,68},{8,72},{12,76},{16,80},{20,84},{24,88},{28,92},{32,9... | collective-permute-start | bytes 614408 | tf_op jit(solution)/shard_map/ppermute | solution.py:71
  184.2 1.9 collective-permute-done.30
  186.2 1.4 collective-permute-start.32
  187.6 1.4 collective-permute-start.34
  189.0 1.6 collective-permute-start.33
  191.4 2.1 collective-permute-start.28
  195.3 2.7 %collective-permute-done.27 = bf16[40,640]{1,0:T(8,128)(2,1)S(1)} collective-permute-done((bf16[40,640]{1,0:T(8,128)(2,1)S(1)}, bf16[40,640]{1,0:T(8,128)(2,1)S(1)}, u32[]{:S(2)}, u32[]{:S(2)}) %collective-permute-start.27) | collective-permute-done | bytes 51232 | tf_op jit(solution)/shard_map/ppermute | solution.py:71
  198.6 11.0 %adam_rows.1 = (f32[2048,256]{1,0:T(8,128)}, f32[2048,256]{1,0:T(8,128)}, f32[2048,256]{1,0:T(8,128)}) custom-call(s32[1,6144]{1,0:T(1,128)S(1)} %and_select_fusion.1.tile_ref, s32[1,6144]{1,0:T(1,128)S(1)} %get-tuple-element.71.spot_ref, bf16[6144,256]{1,0:T(8,128)(2,1)S(1)} %bitcast.82, f32[2048,256]{1,0:T(8,128)} %table_ref.1, f32[2048,256]{1,0:T(8,128)} %first_ref.1, ...), custom_call_target="tpu_custom_call" | custom-call | tf_op jit(solution)/shard_map/adam_rows/pallas_call | solution.py:355
  (83 shorter events, 12.4 us)
Async XLA Ops:
  0.6 13.2 %collective-permute-start = (bf16[40,640]{1,0:T(8,128)(2,1)}, bf16[40,640]{1,0:T(8,128)(2,1)S(1)}, u32[]{:S(2)}, u32[]{:S(2)}) collective-permute-start(bf16[40,640]{1,0:T(8,128)(2,1)} %param.12), channel_id=1, source_target_pairs={{0,32},{4,36},{8,40},{12,44},{16,48},{20,52},{24,56},{28,60},{32,6... | collective-permute-start | bytes 153608 | tf_op jit(solution)/shard_map/ppermute | solution.py:65
  2.7 12.8 %collective-permute-start.2 = (bf16[40,640]{1,0:T(8,128)(2,1)}, bf16[40,640]{1,0:T(8,128)(2,1)S(1)}, u32[]{:S(2)}, u32[]{:S(2)}) collective-permute-start(bf16[40,640]{1,0:T(8,128)(2,1)} %param.12), channel_id=1, source_target_pairs={{0,96},{4,100},{8,104},{12,108},{16,112},{20,116},{24,120},{28,124... | collective-permute-start | bytes 153608 | tf_op jit(solution)/shard_map/ppermute | solution.py:65
  4.1 11.5 %collective-permute-start.1 = (bf16[40,640]{1,0:T(8,128)(2,1)}, bf16[40,640]{1,0:T(8,128)(2,1)S(1)}, u32[]{:S(2)}, u32[]{:S(2)}) collective-permute-start(bf16[40,640]{1,0:T(8,128)(2,1)} %param.12), channel_id=1, source_target_pairs={{0,64},{4,68},{8,72},{12,76},{16,80},{20,84},{24,88},{28,92},{32,9... | collective-permute-start | bytes 153608 | tf_op jit(solution)/shard_map/ppermute | solution.py:65
  5.7 9.9 %collective-permute-start.3 = (bf16[40,640]{1,0:T(8,128)(2,1)}, bf16[40,640]{1,0:T(8,128)(2,1)S(1)}, u32[]{:S(2)}, u32[]{:S(2)}) collective-permute-start(bf16[40,640]{1,0:T(8,128)(2,1)} %param.13), channel_id=1, source_target_pairs={{0,8},{4,12},{8,16},{12,20},{16,24},{20,28},{24,0},{28,4},{32,40},... | collective-permute-start | bytes 153608 | tf_op jit(solution)/shard_map/ppermute | solution.py:65
  7.0 8.6 %collective-permute-start.5 = (bf16[40,640]{1,0:T(8,128)(2,1)}, bf16[40,640]{1,0:T(8,128)(2,1)S(1)}, u32[]{:S(2)}, u32[]{:S(2)}) collective-permute-start(bf16[40,640]{1,0:T(8,128)(2,1)} %param.13), channel_id=1, source_target_pairs={{0,24},{4,28},{8,0},{12,4},{16,8},{20,12},{24,16},{28,20},{32,56},... | collective-permute-start | bytes 153608 | tf_op jit(solution)/shard_map/ppermute | solution.py:65
  11.0 2.8 %copy-start.7 = (bf16[40,640]{1,0:T(8,128)(2,1)S(1)}, bf16[40,640]{1,0:T(8,128)(2,1)}, u32[]{:S(2)}) copy-start(bf16[40,640]{1,0:T(8,128)(2,1)} %param.13) | copy-start | bytes 153604
  11.0 4.6 %copy-start.6 = (bf16[40,640]{1,0:T(8,128)(2,1)S(1)}, bf16[40,640]{1,0:T(8,128)(2,1)}, u32[]{:S(2)}) copy-start(bf16[40,640]{1,0:T(8,128)(2,1)} %param.12) | copy-start | bytes 153604
  13.9 4.5 %collective-permute-start.4 = (bf16[40,640]{1,0:T(8,128)(2,1)S(1)}, bf16[40,640]{1,0:T(8,128)(2,1)S(1)}, u32[]{:S(2)}, u32[]{:S(2)}) collective-permute-start(bf16[40,640]{1,0:T(8,128)(2,1)S(1)} %copy-done.7), channel_id=1, source_target_pairs={{0,16},{4,20},{8,24},{12,28},{16,0},{20,4},{24,8},{28,12},{32,48},... | collective-permute-start | bytes 153608 | tf_op jit(solution)/shard_map/ppermute | solution.py:65
  18.4 5.9 %collective-permute-start.6 = (bf16[4,40,640]{2,1,0:T(8,128)(2,1)S(1)}, bf16[4,40,640]{2,1,0:T(8,128)(2,1)S(1)}, u32[]{:S(2)}, u32[]{:S(2)}) collective-permute-start(bf16[4,40,640]{2,1,0:T(8,128)(2,1)S(1)} %pad_maximum_fusion.1), channel_id=1, source_target_pairs={{0,8},{4,12},{8,16},{12,20},{16,24},{20,28},{24,0},{28,4},{32,40},... | collective-permute-start | bytes 614408 | tf_op jit(solution)/shard_map/ppermute | solution.py:65
  18.5 23.4 %collective-permute-start.8 = (bf16[4,40,640]{2,1,0:T(8,128)(2,1)S(1)}, bf16[4,40,640]{2,1,0:T(8,128)(2,1)S(1)}, u32[]{:S(2)}, u32[]{:S(2)}) collective-permute-start(bf16[4,40,640]{2,1,0:T(8,128)(2,1)S(1)} %pad_maximum_fusion.1), channel_id=1, source_target_pairs={{0,24},{4,28},{8,0},{12,4},{16,8},{20,12},{24,16},{28,20},{32,56},... | collective-permute-start | bytes 614408 | tf_op jit(solution)/shard_map/ppermute | solution.py:65
  21.3 20.7 %collective-permute-start.7 = (bf16[4,40,640]{2,1,0:T(8,128)(2,1)S(1)}, bf16[4,40,640]{2,1,0:T(8,128)(2,1)S(1)}, u32[]{:S(2)}, u32[]{:S(2)}) collective-permute-start(bf16[4,40,640]{2,1,0:T(8,128)(2,1)S(1)} %pad_maximum_fusion.1), channel_id=1, source_target_pairs={{0,16},{4,20},{8,24},{12,28},{16,0},{20,4},{24,8},{28,12},{32,48},... | collective-permute-start | bytes 614408 | tf_op jit(solution)/shard_map/ppermute | solution.py:65
  21.7 20.1 %collective-permute-start.11 = (bf16[4,40,640]{2,1,0:T(8,128)(2,1)S(1)}, bf16[4,40,640]{2,1,0:T(8,128)(2,1)S(1)}, u32[]{:S(2)}, u32[]{:S(2)}) collective-permute-start(bf16[4,40,640]{2,1,0:T(8,128)(2,1)S(1)} %pad_maximum_fusion.2), channel_id=1, source_target_pairs={{0,96},{4,100},{8,104},{12,108},{16,112},{20,116},{24,120},{28,124... | collective-permute-start | bytes 614408 | tf_op jit(solution)/shard_map/ppermute | solution.py:65
  22.5 19.3 %collective-permute-start.10 = (bf16[4,40,640]{2,1,0:T(8,128)(2,1)S(1)}, bf16[4,40,640]{2,1,0:T(8,128)(2,1)S(1)}, u32[]{:S(2)}, u32[]{:S(2)}) collective-permute-start(bf16[4,40,640]{2,1,0:T(8,128)(2,1)S(1)} %pad_maximum_fusion.2), channel_id=1, source_target_pairs={{0,64},{4,68},{8,72},{12,76},{16,80},{20,84},{24,88},{28,92},{32,9... | collective-permute-start | bytes 614408 | tf_op jit(solution)/shard_map/ppermute | solution.py:65
  24.3 17.5 %collective-permute-start.9 = (bf16[4,40,640]{2,1,0:T(8,128)(2,1)S(1)}, bf16[4,40,640]{2,1,0:T(8,128)(2,1)S(1)}, u32[]{:S(2)}, u32[]{:S(2)}) collective-permute-start(bf16[4,40,640]{2,1,0:T(8,128)(2,1)S(1)} %pad_maximum_fusion.2), channel_id=1, source_target_pairs={{0,32},{4,36},{8,40},{12,44},{16,48},{20,52},{24,56},{28,60},{32,6... | collective-permute-start | bytes 614408 | tf_op jit(solution)/shard_map/ppermute | solution.py:65
  26.1 25.3 %all-to-all-start = ((s32[128,1,48]{2,1,0:T(1,128)}), s32[128,1,48]{2,1,0:T(1,128)S(1)}, u32[]{:S(2)}, u32[]{:S(2)}) async-start(s32[128,1,48]{2,1,0:T(1,128)} %copy.16), calls=%async_computation | async-start | bytes 131072 | tf_op jit(solution)/shard_map/all_to_all | solution.py:90
  42.3 9.6 %copy-start.4 = (bf16[2,4,4,40,640]{4,3,2,1,0:T(8,128)(2,1)}, bf16[2,4,4,40,640]{4,3,2,1,0:T(8,128)(2,1)S(1)}, u32[]{:S(2)}) copy-start(bf16[2,4,4,40,640]{4,3,2,1,0:T(8,128)(2,1)S(1)} %pad_maximum_fusion) | copy-start | bytes 4915204
  51.4 3.7 %collective-permute-start.12 = (bf16[2,16,40,640]{3,2,1,0:T(8,128)(2,1)S(1)}, bf16[2,16,40,640]{3,2,1,0:T(8,128)(2,1)}, u32[]{:S(2)}, u32[]{:S(2)}) collective-permute-start(bf16[2,16,40,640]{3,2,1,0:T(8,128)(2,1)S(1)} %bitcast.84), channel_id=1, source_target_pairs={{0,4},{4,0},{8,12},{12,8},{16,20},{20,16},{24,28},{28,24},{32,36},... | collective-permute-start | bytes 4915208 | tf_op jit(solution)/shard_map/ppermute | solution.py:431
  67.5 2.9 %collective-permute-start.15 = (f32[8,1536]{1,0:T(8,128)S(1)}, f32[8,1536]{1,0:T(8,128)S(1)}, u32[]{:S(2)}, u32[]{:S(2)}) collective-permute-start(f32[8,1536]{1,0:T(8,128)S(1)} %get-tuple-element.43.refs_0_), channel_id=1, source_target_pairs={{0,3},{1,0},{2,1},{3,2},{4,7},{5,4},{6,5},{7,6},{8,11},{9,8},{10,9... | collective-permute-start | bytes 147464 | tf_op jit(solution)/shard_map/ppermute | solution.py:434
  68.4 4.4 %collective-permute-start.14 = (f32[8,1536]{1,0:T(8,128)S(1)}, f32[8,1536]{1,0:T(8,128)S(1)}, u32[]{:S(2)}, u32[]{:S(2)}) collective-permute-start(f32[8,1536]{1,0:T(8,128)S(1)} %get-tuple-element.43.refs_0_), channel_id=1, source_target_pairs={{0,2},{1,3},{2,0},{3,1},{4,6},{5,7},{6,4},{7,5},{8,10},{9,11},{10,... | collective-permute-start | bytes 147464 | tf_op jit(solution)/shard_map/ppermute | solution.py:434
  69.9 4.8 %collective-permute-start.13 = (f32[8,1536]{1,0:T(8,128)S(1)}, f32[8,1536]{1,0:T(8,128)S(1)}, u32[]{:S(2)}, u32[]{:S(2)}) collective-permute-start(f32[8,1536]{1,0:T(8,128)S(1)} %get-tuple-element.43.refs_0_), channel_id=1, source_target_pairs={{0,1},{1,2},{2,3},{3,0},{4,5},{5,6},{6,7},{7,4},{8,9},{9,10},{10,1... | collective-permute-start | bytes 147464 | tf_op jit(solution)/shard_map/ppermute | solution.py:434
  78.9 16.5 %collective-permute-start.16 = (bf16[384,640]{1,0:T(8,128)(2,1)}, bf16[384,640]{1,0:T(8,128)(2,1)}, u32[]{:S(2)}, u32[]{:S(2)}) collective-permute-start(bf16[384,640]{1,0:T(8,128)(2,1)} %get-tuple-element.47), channel_id=1, source_target_pairs={{0,1},{1,2},{2,3},{3,0},{4,5},{5,6},{6,7},{7,4},{8,9},{9,10},{10,1... | collective-permute-start | bytes 1474568 | tf_op jit(solution)/shard_map/ppermute | solution.py:438
  78.9 17.7 %collective-permute-start.17 = (bf16[384,640]{1,0:T(8,128)(2,1)}, bf16[384,640]{1,0:T(8,128)(2,1)}, u32[]{:S(2)}, u32[]{:S(2)}) collective-permute-start(bf16[384,640]{1,0:T(8,128)(2,1)} %get-tuple-element.49), channel_id=1, source_target_pairs={{0,3},{1,0},{2,1},{3,2},{4,7},{5,4},{6,5},{7,6},{8,11},{9,8},{10,9... | collective-permute-start | bytes 1474568 | tf_op jit(solution)/shard_map/ppermute | solution.py:439
  81.7 16.9 %copy-start.5 = (bf16[1536,1280]{1,0:T(8,128)(2,1)S(1)}, bf16[1536,1280]{1,0:T(8,128)(2,1)}, u32[]{:S(2)}) copy-start(bf16[1536,1280]{1,0:T(8,128)(2,1)} %memory_ref.1) | copy-start | bytes 11796484
  92.0 0.8 copy-start.2
  92.8 13.6 %copy-start = (bf16[384,640]{1,0:T(8,128)(2,1)}, bf16[384,640]{1,0:T(8,128)(2,1)S(1)}, u32[]{:S(2)}) copy-start(bf16[384,640]{1,0:T(8,128)(2,1)S(1)} %get-tuple-element.62.l1) | copy-start | bytes 1474564
  92.8 15.0 %collective-permute-start.18 = (bf16[384,640]{1,0:T(8,128)(2,1)S(1)}, bf16[384,640]{1,0:T(8,128)(2,1)S(1)}, u32[]{:S(2)}, u32[]{:S(2)}) collective-permute-start(bf16[384,640]{1,0:T(8,128)(2,1)S(1)} %get-tuple-element.52), channel_id=1, source_target_pairs={{0,1},{1,2},{2,3},{3,0},{4,5},{5,6},{6,7},{7,4},{8,9},{9,10},{10,1... | collective-permute-start | bytes 1474568 | tf_op jit(solution)/shard_map/ppermute | solution.py:443
  92.8 15.0 %collective-permute-start.19 = (bf16[384,640]{1,0:T(8,128)(2,1)S(1)}, bf16[384,640]{1,0:T(8,128)(2,1)S(1)}, u32[]{:S(2)}, u32[]{:S(2)}) collective-permute-start(bf16[384,640]{1,0:T(8,128)(2,1)S(1)} %get-tuple-element.53), channel_id=1, source_target_pairs={{0,3},{1,0},{2,1},{3,2},{4,7},{5,4},{6,5},{7,6},{8,11},{9,8},{10,9... | collective-permute-start | bytes 1474568 | tf_op jit(solution)/shard_map/ppermute | solution.py:444
  107.8 6.0 %collective-permute-start.20 = (bf16[16,40,1280]{2,1,0:T(8,128)(2,1)}, bf16[16,40,1280]{2,1,0:T(8,128)(2,1)}, u32[]{:S(2)}, u32[]{:S(2)}) collective-permute-start(bf16[16,40,1280]{2,1,0:T(8,128)(2,1)} %get-tuple-element.55), channel_id=1, source_target_pairs={{0,4},{4,0},{8,12},{12,8},{16,20},{20,16},{24,28},{28,24},{32,36},... | collective-permute-start | bytes 4915208 | tf_op jit(solution)/shard_map/ppermute | solution.py:104
  110.4 14.0 %copy-start.1 = (bf16[384,640]{1,0:T(8,128)(2,1)S(1)}, bf16[384,640]{1,0:T(8,128)(2,1)}, u32[]{:S(2)}) copy-start(bf16[384,640]{1,0:T(8,128)(2,1)} %copy-done) | copy-start | bytes 1474564
  110.4 14.0 %copy-start.3 = (bf16[384,640]{1,0:T(8,128)(2,1)S(1)}, bf16[384,640]{1,0:T(8,128)(2,1)}, u32[]{:S(2)}) copy-start(bf16[384,640]{1,0:T(8,128)(2,1)} %copy-done.2) | copy-start | bytes 1474564
  110.4 14.0 %collective-permute-start.21 = (bf16[384,640]{1,0:T(8,128)(2,1)S(1)}, bf16[384,640]{1,0:T(8,128)(2,1)S(1)}, u32[]{:S(2)}, u32[]{:S(2)}) collective-permute-start(bf16[384,640]{1,0:T(8,128)(2,1)S(1)} %add_convert_fusion.2), channel_id=1, source_target_pairs={{0,1},{1,2},{2,3},{3,0},{4,5},{5,6},{6,7},{7,4},{8,9},{9,10},{10,1... | collective-permute-start | bytes 1474568 | tf_op jit(solution)/shard_map/ppermute | solution.py:448
  110.5 13.9 %collective-permute-start.22 = (bf16[384,640]{1,0:T(8,128)(2,1)}, bf16[384,640]{1,0:T(8,128)(2,1)S(1)}, u32[]{:S(2)}, u32[]{:S(2)}) collective-permute-start(bf16[384,640]{1,0:T(8,128)(2,1)} %add_convert_fusion.1), channel_id=1, source_target_pairs={{0,3},{1,0},{2,1},{3,2},{4,7},{5,4},{6,5},{7,6},{8,11},{9,8},{10,9... | collective-permute-start | bytes 1474568 | tf_op jit(solution)/shard_map/ppermute | solution.py:449
  133.9 64.8 %all-to-all-start.1 = ((bf16[128,48,256]{2,1,0:T(8,128)(2,1)}), bf16[128,48,256]{2,1,0:T(8,128)(2,1)S(1)}, u32[]{:S(2)}, u32[]{:S(2)}) async-start(bf16[128,48,256]{2,1,0:T(8,128)(2,1)} %bitcast.51), calls=%async_computation.1 | async-start | bytes 6291456 | tf_op jit(solution)/shard_map/all_to_all | solution.py:470
  142.2 39.1 %collective-permute-start.29 = (bf16[4,40,640]{2,1,0:T(8,128)(2,1)S(1)}, bf16[4,40,640]{2,1,0:T(8,128)(2,1)S(1)}, u32[]{:S(2)}, u32[]{:S(2)}) collective-permute-start(bf16[4,40,640]{2,1,0:T(8,128)(2,1)S(1)} %get-tuple-element.77), channel_id=1, source_target_pairs={{0,8},{4,12},{8,16},{12,20},{16,24},{20,28},{24,0},{28,4},{32,40},... | collective-permute-start | bytes 614408 | tf_op jit(solution)/shard_map/ppermute | solution.py:71
  143.7 40.4 %collective-permute-start.31 = (bf16[4,40,640]{2,1,0:T(8,128)(2,1)S(1)}, bf16[4,40,640]{2,1,0:T(8,128)(2,1)S(1)}, u32[]{:S(2)}, u32[]{:S(2)}) collective-permute-start(bf16[4,40,640]{2,1,0:T(8,128)(2,1)S(1)} %get-tuple-element.78), channel_id=1, source_target_pairs={{0,24},{4,28},{8,0},{12,4},{16,8},{20,12},{24,16},{28,20},{32,56},... | collective-permute-start | bytes 614408 | tf_op jit(solution)/shard_map/ppermute | solution.py:71
  145.1 41.0 %collective-permute-start.30 = (bf16[4,40,640]{2,1,0:T(8,128)(2,1)S(1)}, bf16[4,40,640]{2,1,0:T(8,128)(2,1)S(1)}, u32[]{:S(2)}, u32[]{:S(2)}) collective-permute-start(bf16[4,40,640]{2,1,0:T(8,128)(2,1)S(1)} %get-tuple-element.79), channel_id=1, source_target_pairs={{0,16},{4,20},{8,24},{12,28},{16,0},{20,4},{24,8},{28,12},{32,48},... | collective-permute-start | bytes 614408 | tf_op jit(solution)/shard_map/ppermute | solution.py:71
  146.9 42.1 %collective-permute-start.23 = (bf16[4,40,640]{2,1,0:T(8,128)(2,1)S(1)}, bf16[4,40,640]{2,1,0:T(8,128)(2,1)S(1)}, u32[]{:S(2)}, u32[]{:S(2)}) collective-permute-start(bf16[4,40,640]{2,1,0:T(8,128)(2,1)S(1)} %get-tuple-element.80), channel_id=1, source_target_pairs={{0,32},{4,36},{8,40},{12,44},{16,48},{20,52},{24,56},{28,60},{32,6... | collective-permute-start | bytes 614408 | tf_op jit(solution)/shard_map/ppermute | solution.py:71
  148.1 42.5 %collective-permute-start.25 = (bf16[4,40,640]{2,1,0:T(8,128)(2,1)S(1)}, bf16[4,40,640]{2,1,0:T(8,128)(2,1)S(1)}, u32[]{:S(2)}, u32[]{:S(2)}) collective-permute-start(bf16[4,40,640]{2,1,0:T(8,128)(2,1)S(1)} %get-tuple-element.81), channel_id=1, source_target_pairs={{0,96},{4,100},{8,104},{12,108},{16,112},{20,116},{24,120},{28,124... | collective-permute-start | bytes 614408 | tf_op jit(solution)/shard_map/ppermute | solution.py:71
  181.4 9.2 %collective-permute-start.24 = (bf16[4,40,640]{2,1,0:T(8,128)(2,1)S(1)}, bf16[4,40,640]{2,1,0:T(8,128)(2,1)S(1)}, u32[]{:S(2)}, u32[]{:S(2)}) collective-permute-start(bf16[4,40,640]{2,1,0:T(8,128)(2,1)S(1)} %get-tuple-element.82), channel_id=1, source_target_pairs={{0,64},{4,68},{8,72},{12,76},{16,80},{20,84},{24,88},{28,92},{32,9... | collective-permute-start | bytes 614408 | tf_op jit(solution)/shard_map/ppermute | solution.py:71
  186.2 7.2 %collective-permute-start.32 = (bf16[40,640]{1,0:T(8,128)(2,1)S(1)}, bf16[40,640]{1,0:T(8,128)(2,1)S(1)}, u32[]{:S(2)}, u32[]{:S(2)}) collective-permute-start(bf16[40,640]{1,0:T(8,128)(2,1)S(1)} %get-tuple-element.83), channel_id=1, source_target_pairs={{0,32},{4,36},{8,40},{12,44},{16,48},{20,52},{24,56},{28,60},{32,6... | collective-permute-start | bytes 153608 | tf_op jit(solution)/shard_map/ppermute | solution.py:71
  187.6 5.9 %collective-permute-start.34 = (bf16[40,640]{1,0:T(8,128)(2,1)S(1)}, bf16[40,640]{1,0:T(8,128)(2,1)S(1)}, u32[]{:S(2)}, u32[]{:S(2)}) collective-permute-start(bf16[40,640]{1,0:T(8,128)(2,1)S(1)} %get-tuple-element.84), channel_id=1, source_target_pairs={{0,96},{4,100},{8,104},{12,108},{16,112},{20,116},{24,120},{28,124... | collective-permute-start | bytes 153608 | tf_op jit(solution)/shard_map/ppermute | solution.py:71
  189.0 4.5 %collective-permute-start.33 = (bf16[40,640]{1,0:T(8,128)(2,1)S(1)}, bf16[40,640]{1,0:T(8,128)(2,1)S(1)}, u32[]{:S(2)}, u32[]{:S(2)}) collective-permute-start(bf16[40,640]{1,0:T(8,128)(2,1)S(1)} %get-tuple-element.85), channel_id=1, source_target_pairs={{0,64},{4,68},{8,72},{12,76},{16,80},{20,84},{24,88},{28,92},{32,9... | collective-permute-start | bytes 153608 | tf_op jit(solution)/shard_map/ppermute | solution.py:71
  190.7 4.5 %collective-permute-start.26 = (bf16[40,640]{1,0:T(8,128)(2,1)S(1)}, bf16[40,640]{1,0:T(8,128)(2,1)S(1)}, u32[]{:S(2)}, u32[]{:S(2)}) collective-permute-start(bf16[40,640]{1,0:T(8,128)(2,1)S(1)} %get-tuple-element.86), channel_id=1, source_target_pairs={{0,8},{4,12},{8,16},{12,20},{16,24},{20,28},{24,0},{28,4},{32,40},... | collective-permute-start | bytes 153608 | tf_op jit(solution)/shard_map/ppermute | solution.py:71
  191.4 3.9 %collective-permute-start.28 = (bf16[40,640]{1,0:T(8,128)(2,1)S(1)}, bf16[40,640]{1,0:T(8,128)(2,1)S(1)}, u32[]{:S(2)}, u32[]{:S(2)}) collective-permute-start(bf16[40,640]{1,0:T(8,128)(2,1)S(1)} %get-tuple-element.87), channel_id=1, source_target_pairs={{0,24},{4,28},{8,0},{12,4},{16,8},{20,12},{24,16},{28,20},{32,56},... | collective-permute-start | bytes 153608 | tf_op jit(solution)/shard_map/ppermute | solution.py:71
  193.5 4.5 %collective-permute-start.27 = (bf16[40,640]{1,0:T(8,128)(2,1)S(1)}, bf16[40,640]{1,0:T(8,128)(2,1)S(1)}, u32[]{:S(2)}, u32[]{:S(2)}) collective-permute-start(bf16[40,640]{1,0:T(8,128)(2,1)S(1)} %get-tuple-element.88), channel_id=1, source_target_pairs={{0,16},{4,20},{8,24},{12,28},{16,0},{20,4},{24,8},{28,12},{32,48},... | collective-permute-start | bytes 153608 | tf_op jit(solution)/shard_map/ppermute | solution.py:71

commit v4 on v3

--- a/solution.py
+++ b/solution.py
@@ -65,32 +65,29 @@
     return [shard] + [lax.ppermute(shard, "dp", perm_of(d)) for d in STEPS]
 
 
-def ring_sum(tiles, here, perm_of):
-    own = lax.dynamic_index_in_dim(tiles, here, 0, keepdims=False).astype(jnp.float32)
-    got = [
+def ring_pieces(tiles, here, perm_of):
+    own = lax.dynamic_index_in_dim(tiles, here, 0, keepdims=False)
+    return [own] + [
         lax.ppermute(
             lax.dynamic_index_in_dim(tiles, (here + d) % 4, 0, keepdims=False), "dp", perm_of(d)
         )
         for d in STEPS
     ]
-    for g in got:
-        own += g.astype(jnp.float32)
-    return own
-
-
-def gather_weights(key_weight, value_weight, send_ids):
+
+
+def ring_sum(tiles, here, perm_of):
+    return sum(p.astype(jnp.float32) for p in ring_pieces(tiles, here, perm_of))
+
+
+def gather_weights(key_weight, value_weight, row_ids):
     key_x = ring_gather(key_weight, along_x)
     value_y = ring_gather(value_weight, along_y)
     key_x = jnp.stack(key_x)
     value_y = jnp.stack(value_y)
-    key_x, value_y = lax.optimization_barrier((key_x, value_y))
+    key_x, value_y, row_ids = lax.optimization_barrier((key_x, value_y, row_ids))
     key_all = ring_gather(key_x, along_y)
     value_all = ring_gather(value_y, along_x)
-    key_all[1], send_ids = lax.optimization_barrier((key_all[1], send_ids))
-    got_ids = lax.all_to_all(
-        send_ids, ("dp", "tensor"), split_axis=0, concat_axis=0, tiled=True
-    )
-    return (jnp.stack([jnp.stack(key_all), jnp.stack(value_all)]), got_ids)
+    return (jnp.stack([jnp.stack(key_all), jnp.stack(value_all)]), row_ids)
 
 
 def core_halves(weight_grads, c):
@@ -263,12 +260,15 @@
 
 
 SLOTS = 48
+SLOT_CAP = 45
 TILE = 256
 
 
-def pack_kernel(tile_ref, spot_ref, l1, l2, l3, r1, r2, r3, out_ref, sum_ref, rows_ref):
-    lookups, width = tile_ref.shape[0], out_ref.shape[1]
+def pack_kernel(tile_ref, spot_ref, numbers_ref, l1, l2, l3, r1, r2, r3, out_ref, sum_ref, rows_ref):
+    width = out_ref.shape[1]
     tokens, half = l1.shape
+    entries = tile_ref.shape[1]
+    lookups = 2 * half // width
 
     @pl.when(pl.program_id(0) == 0)
     def _():
@@ -279,20 +279,15 @@
         sum_ref[:, half:] = right.astype(jnp.bfloat16)
         for l in range(lookups):
             rows_ref[l * tokens : (l + 1) * tokens, :] = sum_ref[:, l * width : (l + 1) * width]
+        rows_ref[lookups * tokens :, :] = numbers_ref[...]
 
     steps = out_ref.shape[0] // TILE
-    place = lax.broadcasted_iota(jnp.int32, (TILE, lookups * tokens), 0).astype(jnp.bfloat16)
+    place = lax.broadcasted_iota(jnp.int32, (TILE, entries), 0).astype(jnp.bfloat16)
     one, zero = jnp.ones((), jnp.bfloat16), jnp.zeros((), jnp.bfloat16)
     hits = []
     for s in range(steps):
         here = pl.program_id(0) * steps + s
-        spot = jnp.concatenate(
-            [
-                jnp.where(tile_ref[l : l + 1, :] == here, spot_ref[l : l + 1, :], -1)
-                for l in range(lookups)
-            ],
-            axis=1,
-        )
+        spot = jnp.where(tile_ref[...] == here, spot_ref[...], -1)
         spot = jnp.broadcast_to(spot.astype(jnp.bfloat16), place.shape)
         hits.append(jnp.where(place == spot, one, zero))
     out_ref[...] = jnp.dot(
@@ -300,24 +295,26 @@
     ).astype(jnp.bfloat16)
 
 
-def pack_rows(slot, parts, total_slots, width):
+def pack_rows(slot, numbers, parts, total_slots, width):
     per_step = 3 * TILE
     tokens, half = parts[0].shape
-    lookups = slot.shape[0]
+    fixed = lambda i: (0, 0)
+    one = pl.Buffered(1)
     return pl.pallas_call(
         pack_kernel,
         out_shape=jax.ShapeDtypeStruct((total_slots, width), jnp.bfloat16),
         grid=(total_slots // per_step,),
-        in_specs=[pl.BlockSpec(slot.shape, lambda i: (0, 0))] * 2
-        + [pl.BlockSpec((tokens, half), lambda i: (0, 0))] * 6,
+        in_specs=[pl.BlockSpec(slot.shape, fixed)] * 2
+        + [pl.BlockSpec(numbers.shape, fixed)]
+        + [pl.BlockSpec((tokens, half), fixed, pipeline_mode=one)] * 6,
         out_specs=pl.BlockSpec((per_step, width), lambda i: (i, 0)),
         scratch_shapes=[
             pltpu.VMEM((tokens, 2 * half), jnp.bfloat16),
-            pltpu.VMEM((lookups * tokens, width), jnp.bfloat16),
+            pltpu.VMEM((slot.shape[1], width), jnp.bfloat16),
         ],
         compiler_params=pltpu.CompilerParams(vmem_limit_bytes=26 * 1024 * 1024),
         name="pack_rows",
-    )(slot // TILE, slot % TILE, *parts)
+    )(slot // TILE, slot % TILE, numbers, *parts)
 
 
 def adam_kernel(
@@ -346,12 +343,14 @@
         new_second_ref[at, :] = new_second
 
 
-def adam_rows(got_ids, got_rows, embed_table, first_moment, second_moment):
+def adam_rows(got, embed_table, first_moment, second_moment):
     rows_dev, width = embed_table.shape
     per_step = 2 * TILE
     block = pl.BlockSpec((per_step, width), lambda i: (i, 0))
-    ids = got_ids.reshape(1, -1)
-    whole = pl.BlockSpec(ids.shape, lambda i: (0, 0))
+    tile = got[:, SLOT_CAP, :SLOTS].astype(jnp.int32).reshape(1, -1)
+    spot = got[:, SLOT_CAP + 1, :SLOTS].astype(jnp.int32).reshape(1, -1)
+    got_rows = got.reshape(-1, width)
+    whole = pl.BlockSpec(tile.shape, lambda i: (0, 0))
     return pl.pallas_call(
         adam_kernel,
         out_shape=(jax.ShapeDtypeStruct((rows_dev, width), jnp.float32),) * 3,
@@ -367,10 +366,10 @@
         out_specs=(block,) * 3,
         compiler_params=pltpu.CompilerParams(vmem_limit_bytes=26 * 1024 * 1024),
         name="adam_rows",
-    )(ids // TILE, ids % TILE, got_rows, *in_hbm(embed_table, first_moment, second_moment))
-
-
-def route(my_ids, owners, rows_dev):
+    )(tile, spot, got_rows, *in_hbm(embed_table, first_moment, second_moment))
+
+
+def route(my_ids, owners, rows_dev, row_width):
     ids = my_ids.T
     lookups, tokens = ids.shape
     flat = ids.reshape(-1)
@@ -383,10 +382,10 @@
     earlier = (jnp.arange(entries)[None, :] < jnp.arange(entries)[:, None]).astype(jnp.bfloat16)
     before_counts = jnp.dot(earlier, owner_hits, preferred_element_type=jnp.float32)
     slot_rank = jnp.sum(before_counts * owner_hits.astype(jnp.float32), axis=1).astype(jnp.int32)
-    slot = (owner_of * SLOTS + slot_rank).reshape(lookups, tokens)
+    slot = owner_of * SLOTS + slot_rank
     rank_hits = slot_rank[:, None] == jnp.arange(SLOTS, dtype=jnp.int32)[None, :]
-    low = local_row % 64
-    high = local_row // 64
+    low = local_row % TILE
+    high = local_row // TILE
     values = jnp.concatenate(
         [
             jnp.where(rank_hits, v[:, None], 0).astype(jnp.bfloat16)
@@ -396,10 +395,14 @@
     )
     found = lax.dot_general(
         owner_hits, values, (((0,), (0,)), ((), ())), preferred_element_type=jnp.float32
-    ).astype(jnp.int32)
+    )
     got_high, got_low, filled = jnp.split(found, 3, axis=1)
-    send_ids = jnp.where(filled > 0, got_high * 64 + got_low, rows_dev)
-    return slot, send_ids
+    got_high = jnp.where(filled > 0, got_high, rows_dev // TILE)
+    numbers = jnp.concatenate([got_high, got_low], axis=0).astype(jnp.bfloat16)
+    numbers = jnp.pad(numbers, ((0, 0), (0, row_width - SLOTS)))
+    owner = jnp.arange(owners, dtype=jnp.int32) * SLOTS
+    number_slot = jnp.concatenate([owner + SLOT_CAP, owner + SLOT_CAP + 1])
+    return (jnp.concatenate([slot.reshape(1, -1), number_slot[None, :]], axis=1), numbers)
 
 
 def body(
@@ -418,15 +421,15 @@
     owners = dp_count * tensor_count
     rows_dev, row_width = embed_table.shape
     block_rows = memory.shape[0] // tensor_count
+    mine, row_ids = gather_weights(key_weight, value_weight, row_ids)
     my_ids = lax.dynamic_slice_in_dim(
         row_ids, lax.axis_index("tensor") * block_rows, block_rows, 0
     )
     at = lax.axis_index("dp")
     z = lax.axis_index("tensor")
     x, y, c = at // 8, (at // 2) % 4, at % 2
-    slot, send_ids = route(my_ids, owners, rows_dev)
-    mine, got_ids = gather_weights(key_weight, value_weight, send_ids)
-    mine, got_ids, slot = lax.optimization_barrier((mine, got_ids, slot))
+    slot, numbers = route(my_ids, owners, rows_dev, row_width)
+    mine, numbers, slot = lax.optimization_barrier((mine, numbers, slot))
     mine = mine.reshape(2, 16, *key_weight.shape)
     got = lax.ppermute(mine, "dp", other_core())
     spot = jnp.stack([x, y, c]).astype(jnp.int32)
@@ -461,12 +464,14 @@
     key_part, value_part = sum_one_axis(chip_grads, x, y)
     send_rows = pack_rows(
         slot,
+        numbers,
         (own_left, from_last_left, from_next_left, own_right, from_last_right, from_next_right),
         owners * SLOTS,
         row_width,
     )
-    key_weight_grad = ring_sum(key_part, y, along_y)
-    value_weight_grad = ring_sum(value_part, x, along_x)
+    send_rows, key_part, value_part = lax.optimization_barrier((send_rows, key_part, value_part))
+    key_pieces = ring_pieces(key_part, y, along_y)
+    value_pieces = ring_pieces(value_part, x, along_x)
     got_rows = lax.all_to_all(
         send_rows.reshape(owners, SLOTS, row_width),
         ("dp", "tensor"),
@@ -475,8 +480,13 @@
         tiled=True,
     )
     new_table, new_first, new_second = adam_rows(
-        got_ids, got_rows.reshape(-1, row_width), embed_table, first_moment, second_moment
-    )
+        got_rows, embed_table, first_moment, second_moment
+    )
+    key_pieces, value_pieces, new_second = lax.optimization_barrier(
+        (key_pieces, value_pieces, new_second)
+    )
+    key_weight_grad = sum(p.astype(jnp.float32) for p in key_pieces)
+    value_weight_grad = sum(p.astype(jnp.float32) for p in value_pieces)
     return (key_weight_grad, value_weight_grad, new_table, new_first, new_second)
 
 

time: 212 us -> 201 us (0.948)
  waiting for transfers between devices: 66.2 us -> 52.3 us
  other arithmetic: 10.7 us -> 15.1 us
    all_to_all x1 -> x0, starting transfers between devices: 15.7 us -> none  [gather_weights(): lax.all_to_all(send_ids, ('dp', 'tensor'), split_axis=0, concat_axis=0, t...]
    all_to_all x1 -> x0, waiting for transfers between devices: 9.1 us -> none  [gather_weights(): lax.all_to_all(send_ids, ('dp', 'tensor'), split_axis=0, concat_axis=0, t...]
    ppermute x12, waiting for transfers between devices: 37.5 us -> 31.6 us  [ring_pieces(): lax.ppermute(lax.dynamic_index_in_dim(tiles, (here + d) % 4, 0, keepdims=...]
    ppermute x1, starting transfers between devices: 0.43 us -> 4.66 us  [body(): got = lax.ppermute(mine, 'dp', other_core())]
    ppermute x3, starting transfers between devices: 2.34 us -> 5.68 us  [body(): sums = [sums] + [lax.ppermute(sums, 'tensor', along_z(d)) for d in STEPS]]
    ppermute x12, starting transfers between devices: 17 us -> 20 us  [ring_pieces(): lax.ppermute(lax.dynamic_index_in_dim(tiles, (here + d) % 4, 0, keepdims=...]
    all_to_all x1, starting transfers between devices: 6.68 us -> 9.16 us  [body(): lax.all_to_all(send_rows.reshape(owners, SLOTS, row_width), ('dp', 'tenso...]
    ppermute x12, starting transfers between devices: 15.2 us -> 17.6 us  [ring_gather(): return [shard] + [lax.ppermute(shard, 'dp', perm_of(d)) for d in STEPS]]
  transfers between devices with their start and end apart: 37 -> 36, of which waited for: 13 -> 11; matrix products, arithmetic and copies ran while one was open for 12% -> 12% of each run, Pallas kernels for 5% -> 15%
where the time goes in v4:
time: 201 us; the launch traced here: 200 us
  starting transfers between devices  67.3 us (33%)
  waiting for transfers between devices  52.3 us (26%)
  Pallas kernels  47.4 us (24%)
  other arithmetic  15.1 us (8%)
  matrix products  10.8 us (5%)
  local copies, waits for them, and re-layouts  6.45 us (3%)
    ppermute x12, waiting for transfers between devices, ring_pieces(): lax.ppermute(lax.dynamic_index_in_dim(tiles, (here + d) % 4, 0, keepdims=...  31.6 us
    ppermute x12, starting transfers between devices, ring_pieces(): lax.ppermute(lax.dynamic_index_in_dim(tiles, (here + d) % 4, 0, keepdims=...  20 us
    ppermute x12, starting transfers between devices, ring_gather(): return [shard] + [lax.ppermute(shard, 'dp', perm_of(d)) for d in STEPS]  17.6 us
    pallas_call x2, Pallas kernels, grads(): pl.pallas_call(grads_kernel, out_shape=(pltpu.HBM(both_shape, jnp.bfloat1...  14.6 us
    pallas_call x1, Pallas kernels, project(): pl.pallas_call(project_kernel, out_shape=(jax.ShapeDtypeStruct((mem, 2 *...  12.4 us
    pallas_call x1, Pallas kernels, adam_rows(): pl.pallas_call(adam_kernel, out_shape=(jax.ShapeDtypeStruct((rows_dev, wi...  11 us
    pallas_call x1, Pallas kernels, pack_rows(): pl.pallas_call(pack_kernel, out_shape=jax.ShapeDtypeStruct((total_slots,...  9.43 us
    all_to_all x1, starting transfers between devices, body(): lax.all_to_all(send_rows.reshape(owners, SLOTS, row_width), ('dp', 'tenso...  9.16 us
  transfers between devices with their start and end apart: 36, of which 11 were waited for; matrix products, arithmetic and copies ran while one was open for 12% of the time, Pallas kernels for 15%

profile of v4, /device:TPU:1, one launch (start us, length us, event | category | flops | bytes accessed | tf_op | source)
XLA Modules:
  0.0 200.3 jit_solution(11527948513718426472)
XLA Ops:
  0.6 3.4 %collective-permute-start.2 = (bf16[40,640]{1,0:T(8,128)(2,1)}, bf16[40,640]{1,0:T(8,128)(2,1)S(1)}, u32[]{:S(2)}, u32[]{:S(2)}) collective-permute-start(bf16[40,640]{1,0:T(8,128)(2,1)} %param.12), channel_id=1, source_target_pairs={{0,96},{4,100},{8,104},{12,108},{16,112},{20,116},{24,120},{28,124... | collective-permute-start | bytes 153608 | tf_op jit(solution)/shard_map/ppermute | solution.py:65
  4.0 1.7 collective-permute-start.1
  5.7 1.3 collective-permute-start.3
  7.0 2.6 %collective-permute-start.4 = (bf16[40,640]{1,0:T(8,128)(2,1)}, bf16[40,640]{1,0:T(8,128)(2,1)S(1)}, u32[]{:S(2)}, u32[]{:S(2)}) collective-permute-start(bf16[40,640]{1,0:T(8,128)(2,1)} %param.13), channel_id=1, source_target_pairs={{0,16},{4,20},{8,24},{12,28},{16,0},{20,4},{24,8},{28,12},{32,48},... | collective-permute-start | bytes 153608 | tf_op jit(solution)/shard_map/ppermute | solution.py:65
  12.0 1.8 collective-permute-done.5
  14.7 3.3 %collective-permute-start.7 = (bf16[4,40,640]{2,1,0:T(8,128)(2,1)S(1)}, bf16[4,40,640]{2,1,0:T(8,128)(2,1)S(1)}, u32[]{:S(2)}, u32[]{:S(2)}) collective-permute-start(bf16[4,40,640]{2,1,0:T(8,128)(2,1)S(1)} %pad_maximum_fusion.1), channel_id=1, source_target_pairs={{0,16},{4,20},{8,24},{12,28},{16,0},{20,4},{24,8},{28,12},{32,48},... | collective-permute-start | bytes 614408 | tf_op jit(solution)/shard_map/ppermute | solution.py:65
  18.0 1.5 collective-permute-start.9
  21.0 1.8 fusion.2
  22.9 1.5 select_convert_fusion.2
  25.0 1.3 fusion.3
  26.3 1.7 collective-permute-start.11
  31.0 1.2 maximum_bitcast_fusion.1
  32.3 4.7 %collective-permute-start.12 = (bf16[2,16,40,640]{3,2,1,0:T(8,128)(2,1)S(1)}, bf16[2,16,40,640]{3,2,1,0:T(8,128)(2,1)}, u32[]{:S(2)}, u32[]{:S(2)}) collective-permute-start(bf16[2,16,40,640]{3,2,1,0:T(8,128)(2,1)S(1)} %bitcast.84), channel_id=1, source_target_pairs={{0,4},{4,0},{8,12},{12,8},{16,20},{20,16},{24,28},{28,24},{32,36},... | collective-permute-start | bytes 4915208 | tf_op jit(solution)/shard_map/ppermute | solution.py:434
  37.1 3.2 %collective-permute-done.12.got_ref = bf16[2,16,40,640]{3,2,1,0:T(8,128)(2,1)} collective-permute-done((bf16[2,16,40,640]{3,2,1,0:T(8,128)(2,1)S(1)}, bf16[2,16,40,640]{3,2,1,0:T(8,128)(2,1)}, u32[]{:S(2)}, u32[]{:S(2)}) %collective-permute-start.12) | collective-permute-done | bytes 1638432 | tf_op jit(solution)/shard_map/ppermute | solution.py:434
  40.3 12.4 %project.1 = (bf16[1280,1280]{1,0:T(8,128)(2,1)S(1)}, f32[1536,640]{1,0:T(8,128)}, f32[8,1536]{1,0:T(8,128)S(1)}) custom-call(s32[3]{0:T(128)S(1)} %pad_add_fusion.3.spot_ref, bf16[2,16,40,640]{3,2,1,0:T(8,128)(2,1)} %bitcast.85, bf16[2,16,40,640]{3,2,1,0:T(8,128)(2,1)} %collective-permute-done.12.got_ref, bf16[1536,1280]{1,0:T(8,128)(2,1)} %memory_ref.1, ...), custom_call_target="tpu_custom_call" | custom-call | tf_op jit(solution)/shard_map/project/pallas_call | solution.py:156
  52.6 1.6 collective-permute-start.13
  54.3 3.3 %collective-permute-start.14 = (f32[8,1536]{1,0:T(8,128)S(1)}, f32[8,1536]{1,0:T(8,128)S(1)}, u32[]{:S(2)}, u32[]{:S(2)}) collective-permute-start(f32[8,1536]{1,0:T(8,128)S(1)} %get-tuple-element.53.refs_0_), channel_id=1, source_target_pairs={{0,2},{1,3},{2,0},{3,1},{4,6},{5,7},{6,4},{7,5},{8,10},{9,11},{10,... | collective-permute-start | bytes 147464 | tf_op jit(solution)/shard_map/ppermute | solution.py:437
  58.3 1.5 collective-permute-done.14.refs_2_
  60.8 4.2 %grads_far.1 = (bf16[384,1280]{1,0:T(8,128)(2,1)}, bf16[384,640]{1,0:T(8,128)(2,1)}, bf16[384,640]{1,0:T(8,128)(2,1)}) custom-call(s32[1]{0:T(128)} %bitcast.3.order_ref, f32[8,1536]{1,0:T(8,128)S(1)} %get-tuple-element.53.refs_0_, f32[8,1536]{1,0:T(8,128)S(1)} %collective-permute-done.13.refs_1_, f32[8,1536]{1,0:T(8,128)S(1)} %collective-permute-done.14.refs_2_, ...), custom_call_target="tpu_custom_call" | custom-call | tf_op jit(solution)/shard_map/grads_far/pallas_call | solution.py:240
  65.1 1.8 collective-permute-start.17
  66.9 10.3 %grads_near.1 = (bf16[1536,1280]{1,0:T(8,128)(2,1)}, bf16[384,640]{1,0:T(8,128)(2,1)S(1)}, bf16[384,640]{1,0:T(8,128)(2,1)S(1)}, bf16[384,640]{1,0:T(8,128)(2,1)...) custom-call(s32[4]{0:T(128)S(1)} %pad_add_fusion.2.order_ref, ...), custom_call_target="tpu_custom_call" | custom-call | tf_op jit(solution)/shard_map/grads_near/pallas_call | solution.py:240
  77.3 2.8 %collective-permute-start.19 = (bf16[384,640]{1,0:T(8,128)(2,1)S(1)}, bf16[384,640]{1,0:T(8,128)(2,1)S(1)}, u32[]{:S(2)}, u32[]{:S(2)}) collective-permute-start(bf16[384,640]{1,0:T(8,128)(2,1)S(1)} %get-tuple-element.63), channel_id=1, source_target_pairs={{0,3},{1,0},{2,1},{3,2},{4,7},{5,4},{6,5},{7,6},{8,11},{9,8},{10,9... | collective-permute-start | bytes 1474568 | tf_op jit(solution)/shard_map/ppermute | solution.py:447
  81.2 1.9 add_convert_fusion.2
  83.2 7.8 %convolution_convert_fusion = bf16[1280,1280]{0,1:T(8,128)(2,1)S(1)} fusion(bf16[1536,1280]{1,0:T(8,128)(2,1)} %get-tuple-element.61, bf16[1536,1280]{1,0:T(8,128)(2,1)S(1)} %copy-done.6), kind=kOutput, calls=%fused_computation.2 | convolution fusion | flops 5034803200 | bytes 11141120 | tf_op jit(solution)/shard_map/dot_general | solution.py:453
  91.0 1.4 dynamic-slice_bitcast_fusion
  92.4 2.9 %collective-permute-start.20 = (bf16[16,40,1280]{2,1,0:T(8,128)(2,1)}, bf16[16,40,1280]{2,1,0:T(8,128)(2,1)}, u32[]{:S(2)}, u32[]{:S(2)}) collective-permute-start(bf16[16,40,1280]{2,1,0:T(8,128)(2,1)} %get-tuple-element.65), channel_id=1, source_target_pairs={{0,4},{4,0},{8,12},{12,8},{16,20},{20,16},{24,28},{28,24},{32,36},... | collective-permute-start | bytes 4915208 | tf_op jit(solution)/shard_map/ppermute | solution.py:101
  95.3 2.7 %collective-permute-start.22 = (bf16[384,640]{1,0:T(8,128)(2,1)S(1)}, bf16[384,640]{1,0:T(8,128)(2,1)S(1)}, u32[]{:S(2)}, u32[]{:S(2)}) collective-permute-start(bf16[384,640]{1,0:T(8,128)(2,1)S(1)} %add_convert_fusion.1), channel_id=1, source_target_pairs={{0,3},{1,0},{2,1},{3,2},{4,7},{5,4},{6,5},{7,6},{8,11},{9,8},{10,9... | collective-permute-start | bytes 1474568 | tf_op jit(solution)/shard_map/ppermute | solution.py:452
  98.7 1.8 add_convert_fusion
  100.6 8.8 %collective-permute-done.21.l2 = bf16[384,640]{1,0:T(8,128)(2,1)S(1)} collective-permute-done((bf16[384,640]{1,0:T(8,128)(2,1)}, bf16[384,640]{1,0:T(8,128)(2,1)S(1)}, u32[]{:S(2)}, u32[]{:S(2)}) %collective-permute-start.21) | collective-permute-done | bytes 491552 | tf_op jit(solution)/shard_map/ppermute | solution.py:451
  109.6 1.8 collective-permute-start.26
  111.6 2.3 %collective-permute-start.28 = (bf16[4,40,640]{2,1,0:T(8,128)(2,1)S(1)}, bf16[4,40,640]{2,1,0:T(8,128)(2,1)S(1)}, u32[]{:S(2)}, u32[]{:S(2)}) collective-permute-start(bf16[4,40,640]{2,1,0:T(8,128)(2,1)S(1)} %get-tuple-element.102), channel_id=1, source_target_pairs={{0,24},{4,28},{8,0},{12,4},{16,8},{20,12},{24,16},{28,20},{32,56},... | collective-permute-start | bytes 614408 | tf_op jit(solution)/shard_map/ppermute | solution.py:71
  113.9 1.3 collective-permute-start.23
  115.2 2.8 %collective-permute-start.24 = (bf16[4,40,640]{2,1,0:T(8,128)(2,1)S(1)}, bf16[4,40,640]{2,1,0:T(8,128)(2,1)S(1)}, u32[]{:S(2)}, u32[]{:S(2)}) collective-permute-start(bf16[4,40,640]{2,1,0:T(8,128)(2,1)S(1)} %get-tuple-element.106), channel_id=1, source_target_pairs={{0,64},{4,68},{8,72},{12,76},{16,80},{20,84},{24,88},{28,92},{32,9... | collective-permute-start | bytes 614408 | tf_op jit(solution)/shard_map/ppermute | solution.py:71
  118.1 9.4 %pack_rows.1 = bf16[6144,256]{1,0:T(8,128)(2,1)S(1)} custom-call(s32[1,2176]{1,0:T(1,128)S(1)} %and_select_fusion.1.tile_ref, s32[1,2176]{1,0:T(1,128)S(1)} %get-tuple-element.95.spot_ref, bf16[256,256]{1,0:T(8,128)(2,1)S(1)} %pad.4.numbers_ref, bf16[384,640]{1,0:T(8,128)(2,1)S(1)} %copy-done.2, bf16[384,640]{1,0:T(8,128)(2,1)S(1)} %collective-permute-done.21.l2, ...), custom_call_target="tpu_custom_call" | custom-call | tf_op jit(solution)/shard_map/pack_rows/pallas_call | solution.py:303
  127.5 1.6 copy-done
  129.8 3.9 %collective-permute-done.25 = bf16[4,40,640]{2,1,0:T(8,128)(2,1)S(1)} collective-permute-done((bf16[4,40,640]{2,1,0:T(8,128)(2,1)S(1)}, bf16[4,40,640]{2,1,0:T(8,128)(2,1)S(1)}, u32[]{:S(2)}, u32[]{:S(2)}) %collective-permute-start.25) | collective-permute-done | bytes 204832 | tf_op jit(solution)/shard_map/ppermute | solution.py:71
  133.9 9.2 %all-to-all-start = ((bf16[128,48,256]{2,1,0:T(8,128)(2,1)}), bf16[128,48,256]{2,1,0:T(8,128)(2,1)S(1)}, u32[]{:S(2)}, u32[]{:S(2)}) async-start(bf16[128,48,256]{2,1,0:T(8,128)(2,1)} %bitcast.82), calls=%async_computation | async-start | bytes 6291456 | tf_op jit(solution)/shard_map/all_to_all | solution.py:475
  143.7 1.4 collective-permute-start.32
  145.1 2.4 %collective-permute-start.33 = (bf16[40,640]{1,0:T(8,128)(2,1)}, bf16[40,640]{1,0:T(8,128)(2,1)S(1)}, u32[]{:S(2)}, u32[]{:S(2)}) collective-permute-start(bf16[40,640]{1,0:T(8,128)(2,1)} %get-tuple-element.108), channel_id=1, source_target_pairs={{0,64},{4,68},{8,72},{12,76},{16,80},{20,84},{24,88},{28,92},{32,9... | collective-permute-start | bytes 153608 | tf_op jit(solution)/shard_map/ppermute | solution.py:71
  147.5 1.2 collective-permute-start.34
  149.4 1.2 collective-permute-start.29
  150.5 2.5 %collective-permute-start.30 = (bf16[40,640]{1,0:T(8,128)(2,1)}, bf16[40,640]{1,0:T(8,128)(2,1)}, u32[]{:S(2)}, u32[]{:S(2)}) collective-permute-start(bf16[40,640]{1,0:T(8,128)(2,1)} %get-tuple-element.112), channel_id=1, source_target_pairs={{0,16},{4,20},{8,24},{12,28},{16,0},{20,4},{24,8},{28,12},{32,48},... | collective-permute-start | bytes 153608 | tf_op jit(solution)/shard_map/ppermute | solution.py:71
  153.0 27.6 %collective-permute-done.32 = bf16[40,640]{1,0:T(8,128)(2,1)S(1)} collective-permute-done((bf16[40,640]{1,0:T(8,128)(2,1)S(1)}, bf16[40,640]{1,0:T(8,128)(2,1)S(1)}, u32[]{:S(2)}, u32[]{:S(2)}) %collective-permute-start.32) | collective-permute-done | bytes 51232 | tf_op jit(solution)/shard_map/ppermute | solution.py:71
  180.6 2.6 %collective-permute-start.31 = (bf16[40,640]{1,0:T(8,128)(2,1)}, bf16[40,640]{1,0:T(8,128)(2,1)}, u32[]{:S(2)}, u32[]{:S(2)}) collective-permute-start(bf16[40,640]{1,0:T(8,128)(2,1)} %get-tuple-element.111), channel_id=1, source_target_pairs={{0,24},{4,28},{8,0},{12,4},{16,8},{20,12},{24,16},{28,20},{32,56},... | collective-permute-start | bytes 153608 | tf_op jit(solution)/shard_map/ppermute | solution.py:71
  183.2 2.3 %all-to-all-done = bf16[128,48,256]{2,1,0:T(8,128)(2,1)S(1)} async-done(((bf16[128,48,256]{2,1,0:T(8,128)(2,1)}), bf16[128,48,256]{2,1,0:T(8,128)(2,1)S(1)}, u32[]{:S(2)}, u32[]{:S(2)}) %all-to-all-start) | async-done | bytes 3145760 | tf_op jit(solution)/shard_map/all_to_all | solution.py:475
  186.3 11.0 %adam_rows.1 = (f32[2048,256]{1,0:T(8,128)}, f32[2048,256]{1,0:T(8,128)}, f32[2048,256]{1,0:T(8,128)}) custom-call(s32[1,6144]{1,0:T(1,128)S(1)} %reshape.247.tile_ref, s32[1,6144]{1,0:T(1,128)S(1)} %reshape.248.spot_ref, bf16[6144,256]{1,0:T(8,128)(2,1)S(1)} %bitcast.81, f32[2048,256]{1,0:T(8,128)} %table_ref.1, f32[2048,256]{1,0:T(8,128)} %first_ref.1, ...), custom_call_target="tpu_custom_call" | custom-call | tf_op jit(solution)/shard_map/adam_rows/pallas_call | solution.py:354
  197.3 1.5 convert_add_fusion.2
  198.8 1.5 convert_add_fusion.3
  (92 shorter events, 15.8 us)
Async XLA Ops:
  0.6 9.0 %collective-permute-start.2 = (bf16[40,640]{1,0:T(8,128)(2,1)}, bf16[40,640]{1,0:T(8,128)(2,1)S(1)}, u32[]{:S(2)}, u32[]{:S(2)}) collective-permute-start(bf16[40,640]{1,0:T(8,128)(2,1)} %param.12), channel_id=1, source_target_pairs={{0,96},{4,100},{8,104},{12,108},{16,112},{20,116},{24,120},{28,124... | collective-permute-start | bytes 153608 | tf_op jit(solution)/shard_map/ppermute | solution.py:65
  4.0 6.8 %collective-permute-start = (bf16[40,640]{1,0:T(8,128)(2,1)}, bf16[40,640]{1,0:T(8,128)(2,1)S(1)}, u32[]{:S(2)}, u32[]{:S(2)}) collective-permute-start(bf16[40,640]{1,0:T(8,128)(2,1)} %param.12), channel_id=1, source_target_pairs={{0,32},{4,36},{8,40},{12,44},{16,48},{20,52},{24,56},{28,60},{32,6... | collective-permute-start | bytes 153608 | tf_op jit(solution)/shard_map/ppermute | solution.py:65
  4.0 6.8 %collective-permute-start.1 = (bf16[40,640]{1,0:T(8,128)(2,1)}, bf16[40,640]{1,0:T(8,128)(2,1)S(1)}, u32[]{:S(2)}, u32[]{:S(2)}) collective-permute-start(bf16[40,640]{1,0:T(8,128)(2,1)} %param.12), channel_id=1, source_target_pairs={{0,64},{4,68},{8,72},{12,76},{16,80},{20,84},{24,88},{28,92},{32,9... | collective-permute-start | bytes 153608 | tf_op jit(solution)/shard_map/ppermute | solution.py:65
  5.7 5.9 %collective-permute-start.3 = (bf16[40,640]{1,0:T(8,128)(2,1)}, bf16[40,640]{1,0:T(8,128)(2,1)S(1)}, u32[]{:S(2)}, u32[]{:S(2)}) collective-permute-start(bf16[40,640]{1,0:T(8,128)(2,1)} %param.13), channel_id=1, source_target_pairs={{0,8},{4,12},{8,16},{12,20},{16,24},{20,28},{24,0},{28,4},{32,40},... | collective-permute-start | bytes 153608 | tf_op jit(solution)/shard_map/ppermute | solution.py:65
  7.0 4.9 %collective-permute-start.4 = (bf16[40,640]{1,0:T(8,128)(2,1)}, bf16[40,640]{1,0:T(8,128)(2,1)S(1)}, u32[]{:S(2)}, u32[]{:S(2)}) collective-permute-start(bf16[40,640]{1,0:T(8,128)(2,1)} %param.13), channel_id=1, source_target_pairs={{0,16},{4,20},{8,24},{12,28},{16,0},{20,4},{24,8},{28,12},{32,48},... | collective-permute-start | bytes 153608 | tf_op jit(solution)/shard_map/ppermute | solution.py:65
  9.7 4.1 %collective-permute-start.5 = (bf16[40,640]{1,0:T(8,128)(2,1)}, bf16[40,640]{1,0:T(8,128)(2,1)S(1)}, u32[]{:S(2)}, u32[]{:S(2)}) collective-permute-start(bf16[40,640]{1,0:T(8,128)(2,1)} %param.13), channel_id=1, source_target_pairs={{0,24},{4,28},{8,0},{12,4},{16,8},{20,12},{24,16},{28,20},{32,56},... | collective-permute-start | bytes 153608 | tf_op jit(solution)/shard_map/ppermute | solution.py:65
  14.6 11.7 %collective-permute-start.6 = (bf16[4,40,640]{2,1,0:T(8,128)(2,1)S(1)}, bf16[4,40,640]{2,1,0:T(8,128)(2,1)S(1)}, u32[]{:S(2)}, u32[]{:S(2)}) collective-permute-start(bf16[4,40,640]{2,1,0:T(8,128)(2,1)S(1)} %pad_maximum_fusion.1), channel_id=1, source_target_pairs={{0,8},{4,12},{8,16},{12,20},{16,24},{20,28},{24,0},{28,4},{32,40},... | collective-permute-start | bytes 614408 | tf_op jit(solution)/shard_map/ppermute | solution.py:65
  14.7 13.5 %collective-permute-start.7 = (bf16[4,40,640]{2,1,0:T(8,128)(2,1)S(1)}, bf16[4,40,640]{2,1,0:T(8,128)(2,1)S(1)}, u32[]{:S(2)}, u32[]{:S(2)}) collective-permute-start(bf16[4,40,640]{2,1,0:T(8,128)(2,1)S(1)} %pad_maximum_fusion.1), channel_id=1, source_target_pairs={{0,16},{4,20},{8,24},{12,28},{16,0},{20,4},{24,8},{28,12},{32,48},... | collective-permute-start | bytes 614408 | tf_op jit(solution)/shard_map/ppermute | solution.py:65
  18.0 10.2 %collective-permute-start.8 = (bf16[4,40,640]{2,1,0:T(8,128)(2,1)S(1)}, bf16[4,40,640]{2,1,0:T(8,128)(2,1)S(1)}, u32[]{:S(2)}, u32[]{:S(2)}) collective-permute-start(bf16[4,40,640]{2,1,0:T(8,128)(2,1)S(1)} %pad_maximum_fusion.1), channel_id=1, source_target_pairs={{0,24},{4,28},{8,0},{12,4},{16,8},{20,12},{24,16},{28,20},{32,56},... | collective-permute-start | bytes 614408 | tf_op jit(solution)/shard_map/ppermute | solution.py:65
  18.0 11.9 %collective-permute-start.9 = (bf16[4,40,640]{2,1,0:T(8,128)(2,1)S(1)}, bf16[4,40,640]{2,1,0:T(8,128)(2,1)}, u32[]{:S(2)}, u32[]{:S(2)}) collective-permute-start(bf16[4,40,640]{2,1,0:T(8,128)(2,1)S(1)} %pad_maximum_fusion.2), channel_id=1, source_target_pairs={{0,32},{4,36},{8,40},{12,44},{16,48},{20,52},{24,56},{28,60},{32,6... | collective-permute-start | bytes 614408 | tf_op jit(solution)/shard_map/ppermute | solution.py:65
  19.5 10.4 %collective-permute-start.10 = (bf16[4,40,640]{2,1,0:T(8,128)(2,1)S(1)}, bf16[4,40,640]{2,1,0:T(8,128)(2,1)}, u32[]{:S(2)}, u32[]{:S(2)}) collective-permute-start(bf16[4,40,640]{2,1,0:T(8,128)(2,1)S(1)} %pad_maximum_fusion.2), channel_id=1, source_target_pairs={{0,64},{4,68},{8,72},{12,76},{16,80},{20,84},{24,88},{28,92},{32,9... | collective-permute-start | bytes 614408 | tf_op jit(solution)/shard_map/ppermute | solution.py:65
  26.3 4.7 %collective-permute-start.11 = (bf16[4,40,640]{2,1,0:T(8,128)(2,1)S(1)}, bf16[4,40,640]{2,1,0:T(8,128)(2,1)S(1)}, u32[]{:S(2)}, u32[]{:S(2)}) collective-permute-start(bf16[4,40,640]{2,1,0:T(8,128)(2,1)S(1)} %pad_maximum_fusion.2), channel_id=1, source_target_pairs={{0,96},{4,100},{8,104},{12,108},{16,112},{20,116},{24,120},{28,124... | collective-permute-start | bytes 614408 | tf_op jit(solution)/shard_map/ppermute | solution.py:65
  28.2 0.7 copy-start.7
  32.3 4.8 %copy-start.5 = (bf16[2,4,4,40,640]{4,3,2,1,0:T(8,128)(2,1)}, bf16[2,4,4,40,640]{4,3,2,1,0:T(8,128)(2,1)S(1)}, u32[]{:S(2)}) copy-start(bf16[2,4,4,40,640]{4,3,2,1,0:T(8,128)(2,1)S(1)} %pad_maximum_fusion) | copy-start | bytes 4915204
  32.3 7.9 %collective-permute-start.12 = (bf16[2,16,40,640]{3,2,1,0:T(8,128)(2,1)S(1)}, bf16[2,16,40,640]{3,2,1,0:T(8,128)(2,1)}, u32[]{:S(2)}, u32[]{:S(2)}) collective-permute-start(bf16[2,16,40,640]{3,2,1,0:T(8,128)(2,1)S(1)} %bitcast.84), channel_id=1, source_target_pairs={{0,4},{4,0},{8,12},{12,8},{16,20},{20,16},{24,28},{28,24},{32,36},... | collective-permute-start | bytes 4915208 | tf_op jit(solution)/shard_map/ppermute | solution.py:434
  52.6 5.7 %collective-permute-start.13 = (f32[8,1536]{1,0:T(8,128)S(1)}, f32[8,1536]{1,0:T(8,128)S(1)}, u32[]{:S(2)}, u32[]{:S(2)}) collective-permute-start(f32[8,1536]{1,0:T(8,128)S(1)} %get-tuple-element.53.refs_0_), channel_id=1, source_target_pairs={{0,1},{1,2},{2,3},{3,0},{4,5},{5,6},{6,7},{7,4},{8,9},{9,10},{10,1... | collective-permute-start | bytes 147464 | tf_op jit(solution)/shard_map/ppermute | solution.py:437
  54.3 5.5 %collective-permute-start.14 = (f32[8,1536]{1,0:T(8,128)S(1)}, f32[8,1536]{1,0:T(8,128)S(1)}, u32[]{:S(2)}, u32[]{:S(2)}) collective-permute-start(f32[8,1536]{1,0:T(8,128)S(1)} %get-tuple-element.53.refs_0_), channel_id=1, source_target_pairs={{0,2},{1,3},{2,0},{3,1},{4,6},{5,7},{6,4},{7,5},{8,10},{9,11},{10,... | collective-permute-start | bytes 147464 | tf_op jit(solution)/shard_map/ppermute | solution.py:437
  57.6 3.2 %collective-permute-start.15 = (f32[8,1536]{1,0:T(8,128)S(1)}, f32[8,1536]{1,0:T(8,128)}, u32[]{:S(2)}, u32[]{:S(2)}) collective-permute-start(f32[8,1536]{1,0:T(8,128)S(1)} %get-tuple-element.53.refs_0_), channel_id=1, source_target_pairs={{0,3},{1,0},{2,1},{3,2},{4,7},{5,4},{6,5},{7,6},{8,11},{9,8},{10,9... | collective-permute-start | bytes 147464 | tf_op jit(solution)/shard_map/ppermute | solution.py:437
  65.1 15.0 %collective-permute-start.17 = (bf16[384,640]{1,0:T(8,128)(2,1)}, bf16[384,640]{1,0:T(8,128)(2,1)}, u32[]{:S(2)}, u32[]{:S(2)}) collective-permute-start(bf16[384,640]{1,0:T(8,128)(2,1)} %get-tuple-element.59), channel_id=1, source_target_pairs={{0,3},{1,0},{2,1},{3,2},{4,7},{5,4},{6,5},{7,6},{8,11},{9,8},{10,9... | collective-permute-start | bytes 1474568 | tf_op jit(solution)/shard_map/ppermute | solution.py:442
  66.8 14.4 %collective-permute-start.16 = (bf16[384,640]{1,0:T(8,128)(2,1)}, bf16[384,640]{1,0:T(8,128)(2,1)}, u32[]{:S(2)}, u32[]{:S(2)}) collective-permute-start(bf16[384,640]{1,0:T(8,128)(2,1)} %get-tuple-element.57), channel_id=1, source_target_pairs={{0,1},{1,2},{2,3},{3,0},{4,5},{5,6},{6,7},{7,4},{8,9},{9,10},{10,1... | collective-permute-start | bytes 1474568 | tf_op jit(solution)/shard_map/ppermute | solution.py:441
  66.9 16.3 %copy-start.6 = (bf16[1536,1280]{1,0:T(8,128)(2,1)S(1)}, bf16[1536,1280]{1,0:T(8,128)(2,1)}, u32[]{:S(2)}) copy-start(bf16[1536,1280]{1,0:T(8,128)(2,1)} %memory_ref.1) | copy-start | bytes 11796484
  77.2 5.9 %copy-start.1 = (bf16[384,640]{1,0:T(8,128)(2,1)}, bf16[384,640]{1,0:T(8,128)(2,1)S(1)}, u32[]{:S(2)}) copy-start(bf16[384,640]{1,0:T(8,128)(2,1)S(1)} %get-tuple-element.71.l1) | copy-start | bytes 1474564
  77.2 5.9 %copy-start.3 = (bf16[384,640]{1,0:T(8,128)(2,1)}, bf16[384,640]{1,0:T(8,128)(2,1)S(1)}, u32[]{:S(2)}) copy-start(bf16[384,640]{1,0:T(8,128)(2,1)S(1)} %get-tuple-element.74.r1) | copy-start | bytes 1474564
  77.2 15.1 %collective-permute-start.18 = (bf16[384,640]{1,0:T(8,128)(2,1)S(1)}, bf16[384,640]{1,0:T(8,128)(2,1)S(1)}, u32[]{:S(2)}, u32[]{:S(2)}) collective-permute-start(bf16[384,640]{1,0:T(8,128)(2,1)S(1)} %get-tuple-element.62), channel_id=1, source_target_pairs={{0,1},{1,2},{2,3},{3,0},{4,5},{5,6},{6,7},{7,4},{8,9},{9,10},{10,1... | collective-permute-start | bytes 1474568 | tf_op jit(solution)/shard_map/ppermute | solution.py:446
  77.3 15.0 %collective-permute-start.19 = (bf16[384,640]{1,0:T(8,128)(2,1)S(1)}, bf16[384,640]{1,0:T(8,128)(2,1)S(1)}, u32[]{:S(2)}, u32[]{:S(2)}) collective-permute-start(bf16[384,640]{1,0:T(8,128)(2,1)S(1)} %get-tuple-element.63), channel_id=1, source_target_pairs={{0,3},{1,0},{2,1},{3,2},{4,7},{5,4},{6,5},{7,6},{8,11},{9,8},{10,9... | collective-permute-start | bytes 1474568 | tf_op jit(solution)/shard_map/ppermute | solution.py:447
  92.4 6.4 %collective-permute-start.20 = (bf16[16,40,1280]{2,1,0:T(8,128)(2,1)}, bf16[16,40,1280]{2,1,0:T(8,128)(2,1)}, u32[]{:S(2)}, u32[]{:S(2)}) collective-permute-start(bf16[16,40,1280]{2,1,0:T(8,128)(2,1)} %get-tuple-element.65), channel_id=1, source_target_pairs={{0,4},{4,0},{8,12},{12,8},{16,20},{20,16},{24,28},{28,24},{32,36},... | collective-permute-start | bytes 4915208 | tf_op jit(solution)/shard_map/ppermute | solution.py:101
  95.3 14.0 %collective-permute-start.21 = (bf16[384,640]{1,0:T(8,128)(2,1)}, bf16[384,640]{1,0:T(8,128)(2,1)S(1)}, u32[]{:S(2)}, u32[]{:S(2)}) collective-permute-start(bf16[384,640]{1,0:T(8,128)(2,1)} %add_convert_fusion.2), channel_id=1, source_target_pairs={{0,1},{1,2},{2,3},{3,0},{4,5},{5,6},{6,7},{7,4},{8,9},{9,10},{10,1... | collective-permute-start | bytes 1474568 | tf_op jit(solution)/shard_map/ppermute | solution.py:451
  95.3 14.0 %collective-permute-start.22 = (bf16[384,640]{1,0:T(8,128)(2,1)S(1)}, bf16[384,640]{1,0:T(8,128)(2,1)S(1)}, u32[]{:S(2)}, u32[]{:S(2)}) collective-permute-start(bf16[384,640]{1,0:T(8,128)(2,1)S(1)} %add_convert_fusion.1), channel_id=1, source_target_pairs={{0,3},{1,0},{2,1},{3,2},{4,7},{5,4},{6,5},{7,6},{8,11},{9,8},{10,9... | collective-permute-start | bytes 1474568 | tf_op jit(solution)/shard_map/ppermute | solution.py:452
  109.3 8.6 %copy-start.9 = (s32[1,2176]{1,0:T(1,128)S(1)}, s32[1,2176]{1,0:T(1,128)}, u32[]{:S(2)}) copy-start(s32[1,2176]{1,0:T(1,128)} %pad_add_fusion) | copy-start | bytes 26116
  109.3 8.7 %copy-start.2 = (bf16[384,640]{1,0:T(8,128)(2,1)S(1)}, bf16[384,640]{1,0:T(8,128)(2,1)}, u32[]{:S(2)}) copy-start(bf16[384,640]{1,0:T(8,128)(2,1)} %copy-done.1) | copy-start | bytes 1474564
  109.3 8.7 %copy-start.4 = (bf16[384,640]{1,0:T(8,128)(2,1)S(1)}, bf16[384,640]{1,0:T(8,128)(2,1)}, u32[]{:S(2)}) copy-start(bf16[384,640]{1,0:T(8,128)(2,1)} %copy-done.3) | copy-start | bytes 1474564
  109.6 19.6 %collective-permute-start.26 = (bf16[4,40,640]{2,1,0:T(8,128)(2,1)S(1)}, bf16[4,40,640]{2,1,0:T(8,128)(2,1)S(1)}, u32[]{:S(2)}, u32[]{:S(2)}) collective-permute-start(bf16[4,40,640]{2,1,0:T(8,128)(2,1)S(1)} %get-tuple-element.101), channel_id=1, source_target_pairs={{0,8},{4,12},{8,16},{12,20},{16,24},{20,28},{24,0},{28,4},{32,40},... | collective-permute-start | bytes 614408 | tf_op jit(solution)/shard_map/ppermute | solution.py:71
  111.4 18.3 %collective-permute-start.27 = (bf16[4,40,640]{2,1,0:T(8,128)(2,1)S(1)}, bf16[4,40,640]{2,1,0:T(8,128)(2,1)S(1)}, u32[]{:S(2)}, u32[]{:S(2)}) collective-permute-start(bf16[4,40,640]{2,1,0:T(8,128)(2,1)S(1)} %get-tuple-element.103), channel_id=1, source_target_pairs={{0,16},{4,20},{8,24},{12,28},{16,0},{20,4},{24,8},{28,12},{32,48},... | collective-permute-start | bytes 614408 | tf_op jit(solution)/shard_map/ppermute | solution.py:71
  111.6 18.1 %collective-permute-start.28 = (bf16[4,40,640]{2,1,0:T(8,128)(2,1)S(1)}, bf16[4,40,640]{2,1,0:T(8,128)(2,1)S(1)}, u32[]{:S(2)}, u32[]{:S(2)}) collective-permute-start(bf16[4,40,640]{2,1,0:T(8,128)(2,1)S(1)} %get-tuple-element.102), channel_id=1, source_target_pairs={{0,24},{4,28},{8,0},{12,4},{16,8},{20,12},{24,16},{28,20},{32,56},... | collective-permute-start | bytes 614408 | tf_op jit(solution)/shard_map/ppermute | solution.py:71
  113.9 15.9 %collective-permute-start.23 = (bf16[4,40,640]{2,1,0:T(8,128)(2,1)S(1)}, bf16[4,40,640]{2,1,0:T(8,128)(2,1)S(1)}, u32[]{:S(2)}, u32[]{:S(2)}) collective-permute-start(bf16[4,40,640]{2,1,0:T(8,128)(2,1)S(1)} %get-tuple-element.104), channel_id=1, source_target_pairs={{0,32},{4,36},{8,40},{12,44},{16,48},{20,52},{24,56},{28,60},{32,6... | collective-permute-start | bytes 614408 | tf_op jit(solution)/shard_map/ppermute | solution.py:71
  115.2 14.6 %collective-permute-start.24 = (bf16[4,40,640]{2,1,0:T(8,128)(2,1)S(1)}, bf16[4,40,640]{2,1,0:T(8,128)(2,1)S(1)}, u32[]{:S(2)}, u32[]{:S(2)}) collective-permute-start(bf16[4,40,640]{2,1,0:T(8,128)(2,1)S(1)} %get-tuple-element.106), channel_id=1, source_target_pairs={{0,64},{4,68},{8,72},{12,76},{16,80},{20,84},{24,88},{28,92},{32,9... | collective-permute-start | bytes 614408 | tf_op jit(solution)/shard_map/ppermute | solution.py:71
  127.5 1.6 copy-start
  129.1 4.6 %collective-permute-start.25 = (bf16[4,40,640]{2,1,0:T(8,128)(2,1)S(1)}, bf16[4,40,640]{2,1,0:T(8,128)(2,1)S(1)}, u32[]{:S(2)}, u32[]{:S(2)}) collective-permute-start(bf16[4,40,640]{2,1,0:T(8,128)(2,1)S(1)} %get-tuple-element.105), channel_id=1, source_target_pairs={{0,96},{4,100},{8,104},{12,108},{16,112},{20,116},{24,120},{28,124... | collective-permute-start | bytes 614408 | tf_op jit(solution)/shard_map/ppermute | solution.py:71
  133.9 51.7 %all-to-all-start = ((bf16[128,48,256]{2,1,0:T(8,128)(2,1)}), bf16[128,48,256]{2,1,0:T(8,128)(2,1)S(1)}, u32[]{:S(2)}, u32[]{:S(2)}) async-start(bf16[128,48,256]{2,1,0:T(8,128)(2,1)} %bitcast.82), calls=%async_computation | async-start | bytes 6291456 | tf_op jit(solution)/shard_map/all_to_all | solution.py:475
  143.7 36.9 %collective-permute-start.32 = (bf16[40,640]{1,0:T(8,128)(2,1)S(1)}, bf16[40,640]{1,0:T(8,128)(2,1)S(1)}, u32[]{:S(2)}, u32[]{:S(2)}) collective-permute-start(bf16[40,640]{1,0:T(8,128)(2,1)S(1)} %get-tuple-element.109), channel_id=1, source_target_pairs={{0,32},{4,36},{8,40},{12,44},{16,48},{20,52},{24,56},{28,60},{32,6... | collective-permute-start | bytes 153608 | tf_op jit(solution)/shard_map/ppermute | solution.py:71
  145.1 52.1 %collective-permute-start.33 = (bf16[40,640]{1,0:T(8,128)(2,1)}, bf16[40,640]{1,0:T(8,128)(2,1)S(1)}, u32[]{:S(2)}, u32[]{:S(2)}) collective-permute-start(bf16[40,640]{1,0:T(8,128)(2,1)} %get-tuple-element.108), channel_id=1, source_target_pairs={{0,64},{4,68},{8,72},{12,76},{16,80},{20,84},{24,88},{28,92},{32,9... | collective-permute-start | bytes 153608 | tf_op jit(solution)/shard_map/ppermute | solution.py:71
  147.5 49.8 %collective-permute-start.34 = (bf16[40,640]{1,0:T(8,128)(2,1)}, bf16[40,640]{1,0:T(8,128)(2,1)}, u32[]{:S(2)}, u32[]{:S(2)}) collective-permute-start(bf16[40,640]{1,0:T(8,128)(2,1)} %get-tuple-element.107), channel_id=1, source_target_pairs={{0,96},{4,100},{8,104},{12,108},{16,112},{20,116},{24,120},{28,124... | collective-permute-start | bytes 153608 | tf_op jit(solution)/shard_map/ppermute | solution.py:71
  149.4 47.9 %collective-permute-start.29 = (bf16[40,640]{1,0:T(8,128)(2,1)}, bf16[40,640]{1,0:T(8,128)(2,1)}, u32[]{:S(2)}, u32[]{:S(2)}) collective-permute-start(bf16[40,640]{1,0:T(8,128)(2,1)} %get-tuple-element.113), channel_id=1, source_target_pairs={{0,8},{4,12},{8,16},{12,20},{16,24},{20,28},{24,0},{28,4},{32,40},... | collective-permute-start | bytes 153608 | tf_op jit(solution)/shard_map/ppermute | solution.py:71
  150.5 46.7 %collective-permute-start.30 = (bf16[40,640]{1,0:T(8,128)(2,1)}, bf16[40,640]{1,0:T(8,128)(2,1)}, u32[]{:S(2)}, u32[]{:S(2)}) collective-permute-start(bf16[40,640]{1,0:T(8,128)(2,1)} %get-tuple-element.112), channel_id=1, source_target_pairs={{0,16},{4,20},{8,24},{12,28},{16,0},{20,4},{24,8},{28,12},{32,48},... | collective-permute-start | bytes 153608 | tf_op jit(solution)/shard_map/ppermute | solution.py:71
  180.6 16.6 %collective-permute-start.31 = (bf16[40,640]{1,0:T(8,128)(2,1)}, bf16[40,640]{1,0:T(8,128)(2,1)}, u32[]{:S(2)}, u32[]{:S(2)}) collective-permute-start(bf16[40,640]{1,0:T(8,128)(2,1)} %get-tuple-element.111), channel_id=1, source_target_pairs={{0,24},{4,28},{8,0},{12,4},{16,8},{20,12},{24,16},{28,20},{32,56},... | collective-permute-start | bytes 153608 | tf_op jit(solution)/shard_map/ppermute | solution.py:71
  186.2 11.1 %copy-start.8 = (bf16[40,640]{1,0:T(8,128)(2,1)S(1)}, bf16[40,640]{1,0:T(8,128)(2,1)}, u32[]{:S(2)}) copy-start(bf16[40,640]{1,0:T(8,128)(2,1)} %get-tuple-element.86) | copy-start | bytes 153604

commit v5 on v4

--- a/solution.py
+++ b/solution.py
@@ -90,24 +90,10 @@
     return (jnp.stack([jnp.stack(key_all), jnp.stack(value_all)]), row_ids)
 
 
-def core_halves(weight_grads, c):
-    tiles = weight_grads.reshape(16, 2, -1, weight_grads.shape[1])
-    sent = lax.dynamic_index_in_dim(tiles, 1 - c, 1, keepdims=False)
-    kept = lax.dynamic_index_in_dim(tiles, c, 1, keepdims=False)
-    return (sent, kept)
-
-
 def sum_on_chip(sent, kept):
     got = lax.ppermute(sent, "dp", other_core())
     both = (kept.astype(jnp.float32) + got.astype(jnp.float32)).astype(jnp.bfloat16)
     return both.reshape(4, 4, *both.shape[1:])
-
-
-def sum_one_axis(both, x, y):
-    half = both.shape[3] // 2
-    key_part = ring_sum(both[:, :, :, :half], x, along_x).astype(jnp.bfloat16)
-    value_part = ring_sum(jnp.swapaxes(both[:, :, :, half:], 0, 1), y, along_y).astype(jnp.bfloat16)
-    return (key_part, value_part)
 
 
 def project_kernel(
@@ -151,7 +137,7 @@
 def project(spot, mine, got, memory, hidden, grad_out):
     tokens, mem = memory.shape
     half = hidden.shape[1]
-    tile = tokens // 4
+    tile = tokens // 2
     fixed = lambda i, s: (0, 0)
     return pl.pallas_call(
         project_kernel,
@@ -162,7 +148,7 @@
         ),
         grid_spec=pltpu.PrefetchScalarGridSpec(
             num_scalar_prefetch=1,
-            grid=(4,),
+            grid=(2,),
             in_specs=[
                 pl.BlockSpec(mine.shape, lambda i, s: (0, 0, 0, 0), pipeline_mode=pl.Buffered(1)),
                 pl.BlockSpec(got.shape, lambda i, s: (0, 0, 0, 0), pipeline_mode=pl.Buffered(1)),
@@ -176,7 +162,7 @@
                 pl.BlockSpec((8, tile), lambda i, s: (0, i)),
             ),
         ),
-        compiler_params=pltpu.CompilerParams(vmem_limit_bytes=30 * 1024 * 1024),
+        compiler_params=pltpu.CompilerParams(vmem_limit_bytes=36 * 1024 * 1024),
         name="project",
     )(spot, *in_hbm(mine, got, memory, hidden, grad_out))
 
@@ -205,11 +191,62 @@
 
 
 def grads_kernel(order_ref, *refs):
-    both_ref, outs = refs[8], refs[9:]
+    outs, both_ref = refs[8:-1], refs[-1]
     half = outs[0].shape[1]
     gates_of(refs[:4], *refs[4:7], both_ref)
-
-    @pl.when(pl.program_id(0) < len(outs) // 2)
+    memory_grad = lax.dot_general(
+        both_ref[...],
+        refs[7][...],
+        (((1,), (1,)), ((), ())),
+        preferred_element_type=jnp.float32,
+    ).astype(jnp.bfloat16)
+    for k in range(len(outs) // 2):
+
+        @pl.when(pl.program_id(0) == k)
+        def _():
+            outs[2 * k][...] = memory_grad[:, :half]
+            outs[2 * k + 1][...] = memory_grad[:, half:]
+
+
+def grads(order, sums, hidden, grad_out, key_proj, weights):
+    steps = order.shape[0]
+    tokens, half = hidden.shape
+    tile = tokens // 4
+    mem = weights.shape[0]
+    at = lambda i, o: (o[i], 0)
+    fixed = lambda i, o: (0, 0)
+    one = pl.Buffered(1)
+    return pl.pallas_call(
+        grads_kernel,
+        out_shape=(pltpu.HBM((tile, mem // 2), jnp.bfloat16),) * (2 * steps),
+        grid_spec=pltpu.PrefetchScalarGridSpec(
+            num_scalar_prefetch=1,
+            grid=(steps,),
+            in_specs=[pl.BlockSpec((8, tile), lambda i, o: (0, o[i]))] * 4
+            + [pl.BlockSpec((tile, half), at)] * 3
+            + [pl.BlockSpec(weights.shape, fixed, pipeline_mode=one)],
+            out_specs=(pl.BlockSpec((tile, mem // 2), fixed, pipeline_mode=one),) * (2 * steps),
+            scratch_shapes=[pltpu.VMEM((tile, 2 * half), jnp.bfloat16)],
+        ),
+        compiler_params=pltpu.CompilerParams(vmem_limit_bytes=26 * 1024 * 1024),
+        name="grads_far" if steps == 1 else "grads_near",
+    )(order, *sums, *in_hbm(hidden, grad_out, key_proj), weights)
+
+
+def own_kernel(order_ref, *refs):
+    memory_ref = refs[8]
+    left_ref, right_ref, sent_ref, kept_ref, both_ref, total_ref = refs[9:]
+    half = left_ref.shape[1]
+    step = pl.program_id(0)
+    gates_of(refs[:4], *refs[4:7], both_ref)
+    product = lax.dot_general(
+        memory_ref[...],
+        both_ref[...],
+        (((0,), (0,)), ((), ())),
+        preferred_element_type=jnp.float32,
+    )
+
+    @pl.when(step == 0)
     def _():
         memory_grad = lax.dot_general(
             both_ref[...],
@@ -217,46 +254,55 @@
             (((1,), (1,)), ((), ())),
             preferred_element_type=jnp.float32,
         ).astype(jnp.bfloat16)
-        for k in range(len(outs) // 2):
-
-            @pl.when(pl.program_id(0) == k)
-            def _():
-                outs[2 * k][...] = memory_grad[:, :half]
-                outs[2 * k + 1][...] = memory_grad[:, half:]
-
-
-def grads(order, products, sums, hidden, grad_out, key_proj, weights):
-    steps = order.shape[0]
+        left_ref[...] = memory_grad[:, :half]
+        right_ref[...] = memory_grad[:, half:]
+        total_ref[...] = product
+
+    @pl.when(step > 0)
+    def _():
+        total_ref[...] += product
+
+    @pl.when(step == pl.num_programs(0) - 1)
+    def _():
+        first = order_ref[4] == 0
+        rows = sent_ref.shape[1]
+        for k in range(sent_ref.shape[0]):
+            low = total_ref[2 * k * rows : (2 * k + 1) * rows, :]
+            high = total_ref[(2 * k + 1) * rows : (2 * k + 2) * rows, :]
+            sent_ref[k] = jnp.where(first, high, low).astype(jnp.bfloat16)
+            kept_ref[k] = jnp.where(first, low, high).astype(jnp.bfloat16)
+
+
+def own_grads(order, rows, sums, hidden, grad_out, key_proj, weights, memory):
     tokens, half = hidden.shape
     tile = tokens // 4
     mem = weights.shape[0]
     at = lambda i, o: (o[i], 0)
     fixed = lambda i, o: (0, 0)
+    fixed_three = lambda i, o: (0, 0, 0)
     one = pl.Buffered(1)
-    if steps == 1:
-        both_shape, both_spec = (tile, 2 * half), pl.BlockSpec((tile, 2 * half), fixed)
-    else:
-        both_shape, both_spec = (tokens, 2 * half), pl.BlockSpec((tile, 2 * half), at)
+    halves = (mem // (2 * rows), rows, 2 * half)
     return pl.pallas_call(
-        grads_kernel,
-        out_shape=(
-            pltpu.HBM(both_shape, jnp.bfloat16),
-            *([jax.ShapeDtypeStruct((tile, mem // 2), jnp.bfloat16)] * (2 * products)),
-        ),
+        own_kernel,
+        out_shape=(pltpu.HBM((tile, mem // 2), jnp.bfloat16),) * 2
+        + (pltpu.HBM(halves, jnp.bfloat16),) * 2,
         grid_spec=pltpu.PrefetchScalarGridSpec(
             num_scalar_prefetch=1,
-            grid=(steps,),
+            grid=(4,),
             in_specs=[pl.BlockSpec((8, tile), lambda i, o: (0, o[i]))] * 4
             + [pl.BlockSpec((tile, half), at)] * 3
-            + [pl.BlockSpec(weights.shape, fixed, pipeline_mode=one)],
-            out_specs=(
-                both_spec,
-                *([pl.BlockSpec((tile, mem // 2), fixed, pipeline_mode=one)] * (2 * products)),
-            ),
+            + [pl.BlockSpec(weights.shape, fixed, pipeline_mode=one)]
+            + [pl.BlockSpec((tile, mem), at)],
+            out_specs=(pl.BlockSpec((tile, mem // 2), fixed, pipeline_mode=one),) * 2
+            + (pl.BlockSpec(halves, fixed_three, pipeline_mode=one),) * 2,
+            scratch_shapes=[
+                pltpu.VMEM((tile, 2 * half), jnp.bfloat16),
+                pltpu.VMEM((mem, 2 * half), jnp.float32),
+            ],
         ),
-        compiler_params=pltpu.CompilerParams(vmem_limit_bytes=26 * 1024 * 1024),
-        name="grads_far" if steps == 1 else "grads_near",
-    )(order, *sums, *in_hbm(hidden, grad_out, key_proj), weights)
+        compiler_params=pltpu.CompilerParams(vmem_limit_bytes=36 * 1024 * 1024),
+        name="grads_own",
+    )(order, *sums, *in_hbm(hidden, grad_out, key_proj), weights, *in_hbm(memory))
 
 
 SLOTS = 48
@@ -302,7 +348,7 @@
     one = pl.Buffered(1)
     return pl.pallas_call(
         pack_kernel,
-        out_shape=jax.ShapeDtypeStruct((total_slots, width), jnp.bfloat16),
+        out_shape=pltpu.HBM((total_slots, width), jnp.bfloat16),
         grid=(total_slots // per_step,),
         in_specs=[pl.BlockSpec(slot.shape, fixed)] * 2
         + [pl.BlockSpec(numbers.shape, fixed)]
@@ -321,26 +367,29 @@
     tile_ref, spot_ref, rows_ref, table_ref, first_ref, second_ref, new_table_ref, new_first_ref, new_second_ref
 ):
     steps = table_ref.shape[0] // TILE
-    width = table_ref.shape[1]
     entries = rows_ref.shape[0]
-    chunk = 1024
+    chunk = 2048
     place = lax.broadcasted_iota(jnp.int32, (TILE, chunk), 0).astype(jnp.bfloat16)
     one, zero = jnp.ones((), jnp.bfloat16), jnp.zeros((), jnp.bfloat16)
-    for s in range(steps):
-        here = pl.program_id(0) * steps + s
-        grad = jnp.zeros((TILE, width), jnp.float32)
-        for k in range(0, entries, chunk):
+    grad = jnp.zeros(table_ref.shape, jnp.float32)
+    for k in range(0, entries, chunk):
+        hits = []
+        for s in range(steps):
+            here = pl.program_id(0) * steps + s
             spot = jnp.where(tile_ref[:, k : k + chunk] == here, spot_ref[:, k : k + chunk], -1)
             spot = jnp.broadcast_to(spot.astype(jnp.bfloat16), (TILE, chunk))
-            hits = jnp.where(place == spot, one, zero)
-            grad += jnp.dot(hits, rows_ref[k : k + chunk, :], preferred_element_type=jnp.float32)
-        at = slice(s * TILE, (s + 1) * TILE)
-        new_first = beta_one * first_ref[at, :] + (1.0 - beta_one) * grad
-        new_second = beta_two * second_ref[at, :] + (1.0 - beta_two) * grad * grad
-        stepped = new_first / correct_one / (jnp.sqrt(new_second / correct_two) + adam_eps)
-        new_table_ref[at, :] = table_ref[at, :] - learn_rate * stepped
-        new_first_ref[at, :] = new_first
-        new_second_ref[at, :] = new_second
+            hits.append(jnp.where(place == spot, one, zero))
+        grad += jnp.dot(
+            jnp.concatenate(hits, axis=0),
+            rows_ref[k : k + chunk, :],
+            preferred_element_type=jnp.float32,
+        )
+    new_first = beta_one * first_ref[...] + (1.0 - beta_one) * grad
+    new_second = beta_two * second_ref[...] + (1.0 - beta_two) * grad * grad
+    stepped = new_first / correct_one / (jnp.sqrt(new_second / correct_two) + adam_eps)
+    new_table_ref[...] = table_ref[...] - learn_rate * stepped
+    new_first_ref[...] = new_first
+    new_second_ref[...] = new_second
 
 
 def adam_rows(got, embed_table, first_moment, second_moment):
@@ -436,32 +485,34 @@
     weights, key_proj, sums = project(spot, mine, got, memory, hidden, grad_out)
     sums = [sums] + [lax.ppermute(sums, "tensor", along_z(d)) for d in STEPS]
     far = ((z + 2) % 4)[None].astype(jnp.int32)
-    near = jnp.stack([(z + 1) % 4, (z + 3) % 4, z, (z + 2) % 4]).astype(jnp.int32)
-    _, far_left, far_right = grads(far, 1, sums, hidden, grad_out, key_proj, weights)
+    near = jnp.stack([(z + 1) % 4, (z + 3) % 4]).astype(jnp.int32)
+    own = jnp.stack([z, (z + 2) % 4, (z + 1) % 4, (z + 3) % 4, c]).astype(jnp.int32)
+    known = (sums, hidden, grad_out, key_proj, weights)
+    far_left, far_right = grads(far, *known)
+    far_left, far_right, near = lax.optimization_barrier((far_left, far_right, near))
     up = lax.ppermute(far_left, "tensor", along_z(1))
     down = lax.ppermute(far_right, "tensor", along_z(3))
-    both, next_left, next_right, last_left, last_right, own_left, own_right = grads(
-        near, 3, sums, hidden, grad_out, key_proj, weights
-    )
+    next_left, next_right, last_left, last_right = grads(near, *known)
     from_last_right = lax.ppermute(next_right, "tensor", along_z(1))
     from_next_left = lax.ppermute(last_left, "tensor", along_z(3))
     next_left = (up.astype(jnp.float32) + next_left.astype(jnp.float32)).astype(jnp.bfloat16)
     last_right = (down.astype(jnp.float32) + last_right.astype(jnp.float32)).astype(jnp.bfloat16)
-    both, next_left, last_right = lax.optimization_barrier((both, next_left, last_right))
+    next_left, last_right, own = lax.optimization_barrier((next_left, last_right, own))
+    own_left, own_right, sent, kept = own_grads(own, key_weight.shape[0], *known, memory)
+    sent, kept, from_last_right, from_next_left = lax.optimization_barrier(
+        (sent, kept, from_last_right, from_next_left)
+    )
     from_last_left = lax.ppermute(next_left, "tensor", along_z(1))
     from_next_right = lax.ppermute(last_right, "tensor", along_z(3))
-    weight_grads = lax.dot_general(
-        memory, both, (((0,), (0,)), ((), ())), preferred_element_type=jnp.float32
-    ).astype(jnp.bfloat16)
-    sent, kept = core_halves(weight_grads, c)
-    sent, kept, from_last_right, from_next_left = lax.optimization_barrier(
-        (sent, kept, from_last_right, from_next_left)
-    )
     chip_grads = sum_on_chip(sent, kept)
-    chip_grads, slot, from_last_left, from_next_right = lax.optimization_barrier(
-        (chip_grads, slot, from_last_left, from_next_right)
-    )
-    key_part, value_part = sum_one_axis(chip_grads, x, y)
+    half = chip_grads.shape[3] // 2
+    key_chip = chip_grads[:, :, :, :half]
+    value_chip = jnp.swapaxes(chip_grads[:, :, :, half:], 0, 1)
+    key_part = ring_sum(key_chip, x, along_x).astype(jnp.bfloat16)
+    slot, key_part, value_chip, from_last_left, from_next_right = lax.optimization_barrier(
+        (slot, key_part, value_chip, from_last_left, from_next_right)
+    )
+    value_part = ring_sum(value_chip, y, along_y).astype(jnp.bfloat16)
     send_rows = pack_rows(
         slot,
         numbers,

time: 201 us -> 210 us (1.045)
  Pallas kernels: 47.4 us -> 63.5 us
  matrix products: 10.8 us -> 3.02 us
  starting transfers between devices: 67.3 us -> 60.8 us
  local copies, waits for them, and re-layouts: 6.45 us -> 11.4 us
  other arithmetic: 15.1 us -> 17.6 us
    pallas_call x3 -> x4, Pallas kernels: 24 us -> 40 us  [the longest x1 18.2 us: own_grads(): pl.pallas_call(own_kernel, out_shape=(pltpu.HBM((tile, mem // 2), jnp.bfl...]
    ppermute x1, waiting for transfers between devices: 8.75 us -> 0.01 us  [body(): from_last_left = lax.ppermute(next_left, 'tensor', along_z(1))]
    dot_general x1 -> x0, matrix products: 7.77 us -> none  [body(): lax.dot_general(memory, both, (((0,), (0,)), ((), ())), preferred_element...]
    ppermute x12, waiting for transfers between devices: 3.11 us -> 8.05 us  [ring_gather(): return [shard] + [lax.ppermute(shard, 'dp', perm_of(d)) for d in STEPS]]
    all_to_all x1, starting transfers between devices: 9.16 us -> 4.57 us  [body(): lax.all_to_all(send_rows.reshape(owners, SLOTS, row_width), ('dp', 'tenso...]
    ppermute x12, waiting for transfers between devices: 31.6 us -> 35.8 us  [ring_pieces(): lax.ppermute(lax.dynamic_index_in_dim(tiles, (here + d) % 4, 0, keepdims=...]
    ppermute x12, starting transfers between devices: 17.6 us -> 13.7 us  [ring_gather(): return [shard] + [lax.ppermute(shard, 'dp', perm_of(d)) for d in STEPS]]
    convert_element_type x2, other arithmetic: 0.24 us -> 3.07 us  [the longest x1 1.73 us: body(): value_part = ring_sum(value_chip, y, along_y).astype(jnp.bfloat16)]
  transfers between devices with their start and end apart: 36 -> 36, of which waited for: 11 -> 13; matrix products, arithmetic and copies ran while one was open for 12% -> 10% of each run, Pallas kernels for 15% -> 22%
where the time goes in v5:
time: 210 us; the launch traced here: 209 us
  Pallas kernels  63.5 us (30%)
  starting transfers between devices  60.8 us (29%)
  waiting for transfers between devices  52 us (25%)
  other arithmetic  17.6 us (8%)
  local copies, waits for them, and re-layouts  11.4 us (5%)
  matrix products  3.02 us (1%)
    ppermute x12, waiting for transfers between devices, ring_pieces(): lax.ppermute(lax.dynamic_index_in_dim(tiles, (here + d) % 4, 0, keepdims=...  35.8 us
    ppermute x12, starting transfers between devices, ring_pieces(): lax.ppermute(lax.dynamic_index_in_dim(tiles, (here + d) % 4, 0, keepdims=...  20.6 us
    pallas_call x1, Pallas kernels, own_grads(): pl.pallas_call(own_kernel, out_shape=(pltpu.HBM((tile, mem // 2), jnp.bfl...  18.2 us
    ppermute x12, starting transfers between devices, ring_gather(): return [shard] + [lax.ppermute(shard, 'dp', perm_of(d)) for d in STEPS]  13.7 us
    pallas_call x1, Pallas kernels, project(): pl.pallas_call(project_kernel, out_shape=(jax.ShapeDtypeStruct((mem, 2 *...  12.6 us
    pallas_call x2, Pallas kernels, grads(): pl.pallas_call(grads_kernel, out_shape=(pltpu.HBM((tile, mem // 2), jnp.b...  11.5 us
    pallas_call x1, Pallas kernels, adam_rows(): pl.pallas_call(adam_kernel, out_shape=(jax.ShapeDtypeStruct((rows_dev, wi...  10.9 us
    pallas_call x1, Pallas kernels, pack_rows(): pl.pallas_call(pack_kernel, out_shape=pltpu.HBM((total_slots, width), jnp...  10.3 us
  transfers between devices with their start and end apart: 36, of which 13 were waited for; matrix products, arithmetic and copies ran while one was open for 10% of the time, Pallas kernels for 22%

profile of v5, /device:TPU:1, one launch (start us, length us, event | category | flops | bytes accessed | tf_op | source)
XLA Modules:
  0.0 209.4 jit_solution(9629372207360147028)
XLA Ops:
  0.6 3.4 %collective-permute-start.2 = (bf16[40,640]{1,0:T(8,128)(2,1)}, bf16[40,640]{1,0:T(8,128)(2,1)S(1)}, u32[]{:S(2)}, u32[]{:S(2)}) collective-permute-start(bf16[40,640]{1,0:T(8,128)(2,1)} %param.12), channel_id=1, source_target_pairs={{0,96},{4,100},{8,104},{12,108},{16,112},{20,116},{24,120},{28,124... | collective-permute-start | bytes 153608 | tf_op jit(solution)/shard_map/ppermute | solution.py:65
  5.1 2.7 %collective-permute-start.5 = (bf16[40,640]{1,0:T(8,128)(2,1)}, bf16[40,640]{1,0:T(8,128)(2,1)S(1)}, u32[]{:S(2)}, u32[]{:S(2)}) collective-permute-start(bf16[40,640]{1,0:T(8,128)(2,1)} %param.13), channel_id=1, source_target_pairs={{0,24},{4,28},{8,0},{12,4},{16,8},{20,12},{24,16},{28,20},{32,56},... | collective-permute-start | bytes 153608 | tf_op jit(solution)/shard_map/ppermute | solution.py:65
  10.1 2.5 %collective-permute-done.4 = bf16[40,640]{1,0:T(8,128)(2,1)S(1)} collective-permute-done((bf16[40,640]{1,0:T(8,128)(2,1)}, bf16[40,640]{1,0:T(8,128)(2,1)S(1)}, u32[]{:S(2)}, u32[]{:S(2)}) %collective-permute-start.4) | collective-permute-done | bytes 51232 | tf_op jit(solution)/shard_map/ppermute | solution.py:65
  13.9 2.1 %collective-permute-start.11 = (bf16[4,40,640]{2,1,0:T(8,128)(2,1)S(1)}, bf16[4,40,640]{2,1,0:T(8,128)(2,1)S(1)}, u32[]{:S(2)}, u32[]{:S(2)}) collective-permute-start(bf16[4,40,640]{2,1,0:T(8,128)(2,1)S(1)} %pad_maximum_fusion.2), channel_id=1, source_target_pairs={{0,96},{4,100},{8,104},{12,108},{16,112},{20,116},{24,120},{28,124... | collective-permute-start | bytes 614408 | tf_op jit(solution)/shard_map/ppermute | solution.py:65
  16.1 1.2 collective-permute-start.10
  19.1 1.8 fusion.2
  20.9 1.5 select_convert_fusion.2
  23.1 1.2 fusion.3
  25.6 4.8 %collective-permute-done.6 = bf16[4,40,640]{2,1,0:T(8,128)(2,1)S(1)} collective-permute-done((bf16[4,40,640]{2,1,0:T(8,128)(2,1)S(1)}, bf16[4,40,640]{2,1,0:T(8,128)(2,1)S(1)}, u32[]{:S(2)}, u32[]{:S(2)}) %collective-permute-start.6) | collective-permute-done | bytes 204832 | tf_op jit(solution)/shard_map/ppermute | solution.py:65
  30.7 5.3 %collective-permute-start.12 = (bf16[2,16,40,640]{3,2,1,0:T(8,128)(2,1)S(1)}, bf16[2,16,40,640]{3,2,1,0:T(8,128)(2,1)}, u32[]{:S(2)}, u32[]{:S(2)}) collective-permute-start(bf16[2,16,40,640]{3,2,1,0:T(8,128)(2,1)S(1)} %bitcast.77), channel_id=1, source_target_pairs={{0,4},{4,0},{8,12},{12,8},{16,20},{20,16},{24,28},{28,24},{32,36},... | collective-permute-start | bytes 4915208 | tf_op jit(solution)/shard_map/ppermute | solution.py:483
  36.1 3.2 %collective-permute-done.12.got_ref = bf16[2,16,40,640]{3,2,1,0:T(8,128)(2,1)} collective-permute-done((bf16[2,16,40,640]{3,2,1,0:T(8,128)(2,1)S(1)}, bf16[2,16,40,640]{3,2,1,0:T(8,128)(2,1)}, u32[]{:S(2)}, u32[]{:S(2)}) %collective-permute-start.12) | collective-permute-done | bytes 1638432 | tf_op jit(solution)/shard_map/ppermute | solution.py:483
  39.3 12.6 %project.1 = (bf16[1280,1280]{1,0:T(8,128)(2,1)S(1)}, f32[1536,640]{1,0:T(8,128)}, f32[8,1536]{1,0:T(8,128)S(1)}) custom-call(s32[3]{0:T(128)S(1)} %pad_add_fusion.2.spot_ref, bf16[2,16,40,640]{3,2,1,0:T(8,128)(2,1)} %bitcast.78, bf16[2,16,40,640]{3,2,1,0:T(8,128)(2,1)} %collective-permute-done.12.got_ref, bf16[1536,1280]{1,0:T(8,128)(2,1)} %refs_8_.1, ...), custom_call_target="tpu_custom_call" | custom-call | tf_op jit(solution)/shard_map/project/pallas_call | solution.py:142
  51.8 1.6 collective-permute-start.13
  53.5 3.3 %collective-permute-start.14 = (f32[8,1536]{1,0:T(8,128)S(1)}, f32[8,1536]{1,0:T(8,128)S(1)}, u32[]{:S(2)}, u32[]{:S(2)}) collective-permute-start(f32[8,1536]{1,0:T(8,128)S(1)} %get-tuple-element.59.refs_0_), channel_id=1, source_target_pairs={{0,2},{1,3},{2,0},{3,1},{4,6},{5,7},{6,4},{7,5},{8,10},{9,11},{10,... | collective-permute-start | bytes 147464 | tf_op jit(solution)/shard_map/ppermute | solution.py:486
  59.0 1.0 collective-permute-done.15.refs_3_
  60.0 4.2 %grads_far.1 = (bf16[384,640]{1,0:T(8,128)(2,1)}, bf16[384,640]{1,0:T(8,128)(2,1)}) custom-call(s32[1]{0:T(128)} %bitcast.20.order_ref, f32[8,1536]{1,0:T(8,128)S(1)} %get-tuple-element.59.refs_0_, f32[8,1536]{1,0:T(8,128)S(1)} %collective-permute-done.13.refs_1_, f32[8,1536]{1,0:T(8,128)S(1)} %collective-permute-done.14.refs_2_, ...), custom_call_target="tpu_custom_call" | custom-call | tf_op jit(solution)/shard_map/grads_far/pallas_call | solution.py:219
  64.2 2.7 %collective-permute-start.17 = (bf16[384,640]{1,0:T(8,128)(2,1)}, bf16[384,640]{1,0:T(8,128)(2,1)}, u32[]{:S(2)}, u32[]{:S(2)}) collective-permute-start(bf16[384,640]{1,0:T(8,128)(2,1)} %get-tuple-element.67), channel_id=1, source_target_pairs={{0,3},{1,0},{2,1},{3,2},{4,7},{5,4},{6,5},{7,6},{8,11},{9,8},{10,9... | collective-permute-start | bytes 1474568 | tf_op jit(solution)/shard_map/ppermute | solution.py:494
  68.2 7.4 %grads_near.1 = (bf16[384,640]{1,0:T(8,128)(2,1)}, bf16[384,640]{1,0:T(8,128)(2,1)}, bf16[384,640]{1,0:T(8,128)(2,1)}, bf16[384,640]{1,0:T(8,128)(2,1)}) custom-call(s32[2]{0:T(128)S(1)} %copy-done.7, f32[8,1536]{1,0:T(8,128)S(1)} %get-tuple-element.59.refs_0_, f32[8,1536]{1,0:T(8,128)S(1)} %collective-permute-done.13.refs_1_, ...), custom_call_target="tpu_custom_call" | custom-call | tf_op jit(solution)/shard_map/grads_near/pallas_call | solution.py:219
  75.5 2.7 %collective-permute-start.19 = (bf16[384,640]{1,0:T(8,128)(2,1)}, bf16[384,640]{1,0:T(8,128)(2,1)S(1)}, u32[]{:S(2)}, u32[]{:S(2)}) collective-permute-start(bf16[384,640]{1,0:T(8,128)(2,1)} %get-tuple-element.73), channel_id=1, source_target_pairs={{0,3},{1,0},{2,1},{3,2},{4,7},{5,4},{6,5},{7,6},{8,11},{9,8},{10,9... | collective-permute-start | bytes 1474568 | tf_op jit(solution)/shard_map/ppermute | solution.py:497
  78.2 2.1 add_convert_fusion.2
  80.3 2.1 add_convert_fusion.1
  82.3 18.2 %grads_own.1 = (bf16[384,640]{1,0:T(8,128)(2,1)}, bf16[384,640]{1,0:T(8,128)(2,1)}, bf16[16,40,1280]{2,1,0:T(8,128)(2,1)}, bf16[16,40,1280]{2,1,0:T(8,128)(2,1)}) custom-call(s32[5]{0:T(128)S(1)} %copy-done.6, f32[8,1536]{1,0:T(8,128)S(1)} %get-tuple-element.59.refs_0_, f32[8,1536]{1,0:T(8,128)S(1)} %collective-permute-done.13.refs_1_, ...), custom_call_target="tpu_custom_call" | custom-call | tf_op jit(solution)/shard_map/grads_own/pallas_call | solution.py:285
  102.1 3.0 %collective-permute-start.20 = (bf16[16,40,1280]{2,1,0:T(8,128)(2,1)}, bf16[16,40,1280]{2,1,0:T(8,128)(2,1)S(1)}, u32[]{:S(2)}, u32[]{:S(2)}) collective-permute-start(bf16[16,40,1280]{2,1,0:T(8,128)(2,1)} %get-tuple-element.75), channel_id=1, source_target_pairs={{0,4},{4,0},{8,12},{12,8},{16,20},{20,16},{24,28},{28,24},{32,36},... | collective-permute-start | bytes 4915208 | tf_op jit(solution)/shard_map/ppermute | solution.py:94
  105.1 2.7 %collective-permute-start.25 = (bf16[384,640]{1,0:T(8,128)(2,1)}, bf16[384,640]{1,0:T(8,128)(2,1)S(1)}, u32[]{:S(2)}, u32[]{:S(2)}) collective-permute-start(bf16[384,640]{1,0:T(8,128)(2,1)} %add_convert_fusion.1), channel_id=1, source_target_pairs={{0,3},{1,0},{2,1},{3,2},{4,7},{5,4},{6,5},{7,6},{8,11},{9,8},{10,9... | collective-permute-start | bytes 1474568 | tf_op jit(solution)/shard_map/ppermute | solution.py:506
  108.5 1.8 add_convert_fusion
  110.3 1.0 slice_bitcast_fusion
  113.1 2.9 %collective-permute-start.23 = (bf16[4,40,640]{2,1,0:T(8,128)(2,1)}, bf16[4,40,640]{2,1,0:T(8,128)(2,1)S(1)}, u32[]{:S(2)}, u32[]{:S(2)}) collective-permute-start(bf16[4,40,640]{2,1,0:T(8,128)(2,1)} %get-tuple-element.113), channel_id=1, source_target_pairs={{0,96},{4,100},{8,104},{12,108},{16,112},{20,116},{24,120},{28,124... | collective-permute-start | bytes 614408 | tf_op jit(solution)/shard_map/ppermute | solution.py:71
  116.6 8.1 %collective-permute-done.23 = bf16[4,40,640]{2,1,0:T(8,128)(2,1)S(1)} collective-permute-done((bf16[4,40,640]{2,1,0:T(8,128)(2,1)}, bf16[4,40,640]{2,1,0:T(8,128)(2,1)S(1)}, u32[]{:S(2)}, u32[]{:S(2)}) %collective-permute-start.23) | collective-permute-done | bytes 204832 | tf_op jit(solution)/shard_map/ppermute | solution.py:71
  126.0 3.2 %collective-permute-done.21 = bf16[4,40,640]{2,1,0:T(8,128)(2,1)} collective-permute-done((bf16[4,40,640]{2,1,0:T(8,128)(2,1)}, bf16[4,40,640]{2,1,0:T(8,128)(2,1)}, u32[]{:S(2)}, u32[]{:S(2)}) %collective-permute-start.21) | collective-permute-done | bytes 204832 | tf_op jit(solution)/shard_map/ppermute | solution.py:71
  129.2 1.3 fusion.17
  130.6 1.2 dynamic-slice_bitcast_fusion.2
  131.8 1.6 collective-permute-start.28
  134.1 10.3 %pack_rows.1 = bf16[6144,256]{1,0:T(8,128)(2,1)} custom-call(s32[1,2176]{1,0:T(1,128)S(1)} %and_select_fusion.1.tile_ref, s32[1,2176]{1,0:T(1,128)S(1)} %get-tuple-element.105.spot_ref, bf16[256,256]{1,0:T(8,128)(2,1)S(1)} %pad.4.numbers_ref, bf16[384,640]{1,0:T(8,128)(2,1)S(1)} %copy-done.4, bf16[384,640]{1,0:T(8,128)(2,1)S(1)} %collective-permute-done.24.l2, ...), custom_call_target="tpu_custom_call" | custom-call | tf_op jit(solution)/shard_map/pack_rows/pallas_call | solution.py:349
  144.4 1.4 collective-permute-done.26
  145.8 1.7 fusion.14
  147.6 4.6 %all-to-all-start = ((bf16[128,48,256]{2,1,0:T(8,128)(2,1)}), bf16[128,48,256]{2,1,0:T(8,128)(2,1)S(1)}, u32[]{:S(2)}, u32[]{:S(2)}) async-start(bf16[128,48,256]{2,1,0:T(8,128)(2,1)} %bitcast.75), calls=%async_computation | async-start | bytes 6291456 | tf_op jit(solution)/shard_map/all_to_all | solution.py:526
  152.8 1.4 collective-permute-start.29
  154.2 2.4 %collective-permute-start.30 = (bf16[40,640]{1,0:T(8,128)(2,1)}, bf16[40,640]{1,0:T(8,128)(2,1)}, u32[]{:S(2)}, u32[]{:S(2)}) collective-permute-start(bf16[40,640]{1,0:T(8,128)(2,1)} %get-tuple-element.120), channel_id=1, source_target_pairs={{0,16},{4,20},{8,24},{12,28},{16,0},{20,4},{24,8},{28,12},{32,48},... | collective-permute-start | bytes 153608 | tf_op jit(solution)/shard_map/ppermute | solution.py:71
  156.7 1.1 collective-permute-start.31
  157.8 1.5 dynamic-slice_bitcast_fusion.6
  159.3 1.2 collective-permute-start.32
  160.5 2.4 %collective-permute-start.33 = (bf16[40,640]{1,0:T(8,128)(2,1)}, bf16[40,640]{1,0:T(8,128)(2,1)}, u32[]{:S(2)}, u32[]{:S(2)}) collective-permute-start(bf16[40,640]{1,0:T(8,128)(2,1)} %get-tuple-element.116), channel_id=1, source_target_pairs={{0,64},{4,68},{8,72},{12,76},{16,80},{20,84},{24,88},{28,92},{32,9... | collective-permute-start | bytes 153608 | tf_op jit(solution)/shard_map/ppermute | solution.py:71
  162.9 23.0 %collective-permute-done.29 = bf16[40,640]{1,0:T(8,128)(2,1)S(1)} collective-permute-done((bf16[40,640]{1,0:T(8,128)(2,1)S(1)}, bf16[40,640]{1,0:T(8,128)(2,1)S(1)}, u32[]{:S(2)}, u32[]{:S(2)}) %collective-permute-start.29) | collective-permute-done | bytes 51232 | tf_op jit(solution)/shard_map/ppermute | solution.py:71
  186.0 6.3 %collective-permute-start.34 = (bf16[40,640]{1,0:T(8,128)(2,1)}, bf16[40,640]{1,0:T(8,128)(2,1)}, u32[]{:S(2)}, u32[]{:S(2)}) collective-permute-start(bf16[40,640]{1,0:T(8,128)(2,1)} %get-tuple-element.115), channel_id=1, source_target_pairs={{0,96},{4,100},{8,104},{12,108},{16,112},{20,116},{24,120},{28,124... | collective-permute-start | bytes 153608 | tf_op jit(solution)/shard_map/ppermute | solution.py:71
  192.3 2.4 %all-to-all-done = bf16[128,48,256]{2,1,0:T(8,128)(2,1)S(1)} async-done(((bf16[128,48,256]{2,1,0:T(8,128)(2,1)}), bf16[128,48,256]{2,1,0:T(8,128)(2,1)S(1)}, u32[]{:S(2)}, u32[]{:S(2)}) %all-to-all-start) | async-done | bytes 3145760 | tf_op jit(solution)/shard_map/all_to_all | solution.py:526
  195.4 10.9 %adam_rows.1 = (f32[2048,256]{1,0:T(8,128)}, f32[2048,256]{1,0:T(8,128)}, f32[2048,256]{1,0:T(8,128)}) custom-call(s32[1,6144]{1,0:T(1,128)S(1)} %reshape.235.tile_ref, s32[1,6144]{1,0:T(1,128)S(1)} %reshape.236.spot_ref, bf16[6144,256]{1,0:T(8,128)(2,1)S(1)} %bitcast.74, f32[2048,256]{1,0:T(8,128)} %table_ref.1, f32[2048,256]{1,0:T(8,128)} %first_ref.1, ...), custom_call_target="tpu_custom_call" | custom-call | tf_op jit(solution)/shard_map/adam_rows/pallas_call | solution.py:403
  206.4 1.5 convert_add_fusion.3
  207.9 1.5 convert_add_fusion.2
  (98 shorter events, 20.2 us)
Async XLA Ops:
  0.6 7.6 %collective-permute-start.2 = (bf16[40,640]{1,0:T(8,128)(2,1)}, bf16[40,640]{1,0:T(8,128)(2,1)S(1)}, u32[]{:S(2)}, u32[]{:S(2)}) collective-permute-start(bf16[40,640]{1,0:T(8,128)(2,1)} %param.12), channel_id=1, source_target_pairs={{0,96},{4,100},{8,104},{12,108},{16,112},{20,116},{24,120},{28,124... | collective-permute-start | bytes 153608 | tf_op jit(solution)/shard_map/ppermute | solution.py:65
  4.0 5.0 %collective-permute-start.1 = (bf16[40,640]{1,0:T(8,128)(2,1)}, bf16[40,640]{1,0:T(8,128)(2,1)S(1)}, u32[]{:S(2)}, u32[]{:S(2)}) collective-permute-start(bf16[40,640]{1,0:T(8,128)(2,1)} %param.12), channel_id=1, source_target_pairs={{0,64},{4,68},{8,72},{12,76},{16,80},{20,84},{24,88},{28,92},{32,9... | collective-permute-start | bytes 153608 | tf_op jit(solution)/shard_map/ppermute | solution.py:65
  4.5 4.7 %collective-permute-start = (bf16[40,640]{1,0:T(8,128)(2,1)}, bf16[40,640]{1,0:T(8,128)(2,1)S(1)}, u32[]{:S(2)}, u32[]{:S(2)}) collective-permute-start(bf16[40,640]{1,0:T(8,128)(2,1)} %param.12), channel_id=1, source_target_pairs={{0,32},{4,36},{8,40},{12,44},{16,48},{20,52},{24,56},{28,60},{32,6... | collective-permute-start | bytes 153608 | tf_op jit(solution)/shard_map/ppermute | solution.py:65
  5.1 4.9 %collective-permute-start.5 = (bf16[40,640]{1,0:T(8,128)(2,1)}, bf16[40,640]{1,0:T(8,128)(2,1)S(1)}, u32[]{:S(2)}, u32[]{:S(2)}) collective-permute-start(bf16[40,640]{1,0:T(8,128)(2,1)} %param.13), channel_id=1, source_target_pairs={{0,24},{4,28},{8,0},{12,4},{16,8},{20,12},{24,16},{28,20},{32,56},... | collective-permute-start | bytes 153608 | tf_op jit(solution)/shard_map/ppermute | solution.py:65
  7.9 4.7 %collective-permute-start.4 = (bf16[40,640]{1,0:T(8,128)(2,1)}, bf16[40,640]{1,0:T(8,128)(2,1)S(1)}, u32[]{:S(2)}, u32[]{:S(2)}) collective-permute-start(bf16[40,640]{1,0:T(8,128)(2,1)} %param.13), channel_id=1, source_target_pairs={{0,16},{4,20},{8,24},{12,28},{16,0},{20,4},{24,8},{28,12},{32,48},... | collective-permute-start | bytes 153608 | tf_op jit(solution)/shard_map/ppermute | solution.py:65
  8.2 4.8 %collective-permute-start.3 = (bf16[40,640]{1,0:T(8,128)(2,1)}, bf16[40,640]{1,0:T(8,128)(2,1)S(1)}, u32[]{:S(2)}, u32[]{:S(2)}) collective-permute-start(bf16[40,640]{1,0:T(8,128)(2,1)} %param.13), channel_id=1, source_target_pairs={{0,8},{4,12},{8,16},{12,20},{16,24},{20,28},{24,0},{28,4},{32,40},... | collective-permute-start | bytes 153608 | tf_op jit(solution)/shard_map/ppermute | solution.py:65
  13.9 10.4 %collective-permute-start.11 = (bf16[4,40,640]{2,1,0:T(8,128)(2,1)S(1)}, bf16[4,40,640]{2,1,0:T(8,128)(2,1)S(1)}, u32[]{:S(2)}, u32[]{:S(2)}) collective-permute-start(bf16[4,40,640]{2,1,0:T(8,128)(2,1)S(1)} %pad_maximum_fusion.2), channel_id=1, source_target_pairs={{0,96},{4,100},{8,104},{12,108},{16,112},{20,116},{24,120},{28,124... | collective-permute-start | bytes 614408 | tf_op jit(solution)/shard_map/ppermute | solution.py:65
  16.1 9.4 %collective-permute-start.10 = (bf16[4,40,640]{2,1,0:T(8,128)(2,1)S(1)}, bf16[4,40,640]{2,1,0:T(8,128)(2,1)S(1)}, u32[]{:S(2)}, u32[]{:S(2)}) collective-permute-start(bf16[4,40,640]{2,1,0:T(8,128)(2,1)S(1)} %pad_maximum_fusion.2), channel_id=1, source_target_pairs={{0,64},{4,68},{8,72},{12,76},{16,80},{20,84},{24,88},{28,92},{32,9... | collective-permute-start | bytes 614408 | tf_op jit(solution)/shard_map/ppermute | solution.py:65
  17.3 8.1 %collective-permute-start.9 = (bf16[4,40,640]{2,1,0:T(8,128)(2,1)S(1)}, bf16[4,40,640]{2,1,0:T(8,128)(2,1)S(1)}, u32[]{:S(2)}, u32[]{:S(2)}) collective-permute-start(bf16[4,40,640]{2,1,0:T(8,128)(2,1)S(1)} %pad_maximum_fusion.2), channel_id=1, source_target_pairs={{0,32},{4,36},{8,40},{12,44},{16,48},{20,52},{24,56},{28,60},{32,6... | collective-permute-start | bytes 614408 | tf_op jit(solution)/shard_map/ppermute | solution.py:65
  17.3 8.3 %collective-permute-start.8 = (bf16[4,40,640]{2,1,0:T(8,128)(2,1)S(1)}, bf16[4,40,640]{2,1,0:T(8,128)(2,1)S(1)}, u32[]{:S(2)}, u32[]{:S(2)}) collective-permute-start(bf16[4,40,640]{2,1,0:T(8,128)(2,1)S(1)} %pad_maximum_fusion.1), channel_id=1, source_target_pairs={{0,24},{4,28},{8,0},{12,4},{16,8},{20,12},{24,16},{28,20},{32,56},... | collective-permute-start | bytes 614408 | tf_op jit(solution)/shard_map/ppermute | solution.py:65
  17.6 8.0 %collective-permute-start.7 = (bf16[4,40,640]{2,1,0:T(8,128)(2,1)S(1)}, bf16[4,40,640]{2,1,0:T(8,128)(2,1)S(1)}, u32[]{:S(2)}, u32[]{:S(2)}) collective-permute-start(bf16[4,40,640]{2,1,0:T(8,128)(2,1)S(1)} %pad_maximum_fusion.1), channel_id=1, source_target_pairs={{0,16},{4,20},{8,24},{12,28},{16,0},{20,4},{24,8},{28,12},{32,48},... | collective-permute-start | bytes 614408 | tf_op jit(solution)/shard_map/ppermute | solution.py:65
  24.4 6.1 %collective-permute-start.6 = (bf16[4,40,640]{2,1,0:T(8,128)(2,1)S(1)}, bf16[4,40,640]{2,1,0:T(8,128)(2,1)S(1)}, u32[]{:S(2)}, u32[]{:S(2)}) collective-permute-start(bf16[4,40,640]{2,1,0:T(8,128)(2,1)S(1)} %pad_maximum_fusion.1), channel_id=1, source_target_pairs={{0,8},{4,12},{8,16},{12,20},{16,24},{20,28},{24,0},{28,4},{32,40},... | collective-permute-start | bytes 614408 | tf_op jit(solution)/shard_map/ppermute | solution.py:65
  30.7 5.4 %copy-start.8 = (bf16[2,4,4,40,640]{4,3,2,1,0:T(8,128)(2,1)}, bf16[2,4,4,40,640]{4,3,2,1,0:T(8,128)(2,1)S(1)}, u32[]{:S(2)}) copy-start(bf16[2,4,4,40,640]{4,3,2,1,0:T(8,128)(2,1)S(1)} %pad_maximum_fusion) | copy-start | bytes 4915204
  30.7 8.5 %collective-permute-start.12 = (bf16[2,16,40,640]{3,2,1,0:T(8,128)(2,1)S(1)}, bf16[2,16,40,640]{3,2,1,0:T(8,128)(2,1)}, u32[]{:S(2)}, u32[]{:S(2)}) collective-permute-start(bf16[2,16,40,640]{3,2,1,0:T(8,128)(2,1)S(1)} %bitcast.77), channel_id=1, source_target_pairs={{0,4},{4,0},{8,12},{12,8},{16,20},{20,16},{24,28},{28,24},{32,36},... | collective-permute-start | bytes 4915208 | tf_op jit(solution)/shard_map/ppermute | solution.py:483
  51.8 6.3 %collective-permute-start.13 = (f32[8,1536]{1,0:T(8,128)S(1)}, f32[8,1536]{1,0:T(8,128)S(1)}, u32[]{:S(2)}, u32[]{:S(2)}) collective-permute-start(f32[8,1536]{1,0:T(8,128)S(1)} %get-tuple-element.59.refs_0_), channel_id=1, source_target_pairs={{0,1},{1,2},{2,3},{3,0},{4,5},{5,6},{6,7},{7,4},{8,9},{9,10},{10,1... | collective-permute-start | bytes 147464 | tf_op jit(solution)/shard_map/ppermute | solution.py:486
  53.5 5.5 %collective-permute-start.14 = (f32[8,1536]{1,0:T(8,128)S(1)}, f32[8,1536]{1,0:T(8,128)S(1)}, u32[]{:S(2)}, u32[]{:S(2)}) collective-permute-start(f32[8,1536]{1,0:T(8,128)S(1)} %get-tuple-element.59.refs_0_), channel_id=1, source_target_pairs={{0,2},{1,3},{2,0},{3,1},{4,6},{5,7},{6,4},{7,5},{8,10},{9,11},{10,... | collective-permute-start | bytes 147464 | tf_op jit(solution)/shard_map/ppermute | solution.py:486
  56.8 3.2 %collective-permute-start.15 = (f32[8,1536]{1,0:T(8,128)S(1)}, f32[8,1536]{1,0:T(8,128)}, u32[]{:S(2)}, u32[]{:S(2)}) collective-permute-start(f32[8,1536]{1,0:T(8,128)S(1)} %get-tuple-element.59.refs_0_), channel_id=1, source_target_pairs={{0,3},{1,0},{2,1},{3,2},{4,7},{5,4},{6,5},{7,6},{8,11},{9,8},{10,9... | collective-permute-start | bytes 147464 | tf_op jit(solution)/shard_map/ppermute | solution.py:486
  64.2 14.0 %collective-permute-start.16 = (bf16[384,640]{1,0:T(8,128)(2,1)}, bf16[384,640]{1,0:T(8,128)(2,1)}, u32[]{:S(2)}, u32[]{:S(2)}) collective-permute-start(bf16[384,640]{1,0:T(8,128)(2,1)} %get-tuple-element.64), channel_id=1, source_target_pairs={{0,1},{1,2},{2,3},{3,0},{4,5},{5,6},{6,7},{7,4},{8,9},{9,10},{10,1... | collective-permute-start | bytes 1474568 | tf_op jit(solution)/shard_map/ppermute | solution.py:493
  64.2 16.1 %collective-permute-start.17 = (bf16[384,640]{1,0:T(8,128)(2,1)}, bf16[384,640]{1,0:T(8,128)(2,1)}, u32[]{:S(2)}, u32[]{:S(2)}) collective-permute-start(bf16[384,640]{1,0:T(8,128)(2,1)} %get-tuple-element.67), channel_id=1, source_target_pairs={{0,3},{1,0},{2,1},{3,2},{4,7},{5,4},{6,5},{7,6},{8,11},{9,8},{10,9... | collective-permute-start | bytes 1474568 | tf_op jit(solution)/shard_map/ppermute | solution.py:494
  75.5 6.8 %copy-start.6 = (s32[5]{0:T(128)S(1)}, s32[5]{0:T(128)}, u32[]{:S(2)}) copy-start(s32[5]{0:T(128)} %stack.131.order_ref) | copy-start | bytes 64
  75.5 25.0 %collective-permute-start.18 = (bf16[384,640]{1,0:T(8,128)(2,1)}, bf16[384,640]{1,0:T(8,128)(2,1)S(1)}, u32[]{:S(2)}, u32[]{:S(2)}) collective-permute-start(bf16[384,640]{1,0:T(8,128)(2,1)} %get-tuple-element.72), channel_id=1, source_target_pairs={{0,1},{1,2},{2,3},{3,0},{4,5},{5,6},{6,7},{7,4},{8,9},{9,10},{10,1... | collective-permute-start | bytes 1474568 | tf_op jit(solution)/shard_map/ppermute | solution.py:496
  75.5 25.8 %collective-permute-start.19 = (bf16[384,640]{1,0:T(8,128)(2,1)}, bf16[384,640]{1,0:T(8,128)(2,1)S(1)}, u32[]{:S(2)}, u32[]{:S(2)}) collective-permute-start(bf16[384,640]{1,0:T(8,128)(2,1)} %get-tuple-element.73), channel_id=1, source_target_pairs={{0,3},{1,0},{2,1},{3,2},{4,7},{5,4},{6,5},{7,6},{8,11},{9,8},{10,9... | collective-permute-start | bytes 1474568 | tf_op jit(solution)/shard_map/ppermute | solution.py:497
  100.5 0.8 copy-start
  101.3 0.8 copy-start.2
  102.1 6.4 %collective-permute-start.20 = (bf16[16,40,1280]{2,1,0:T(8,128)(2,1)}, bf16[16,40,1280]{2,1,0:T(8,128)(2,1)S(1)}, u32[]{:S(2)}, u32[]{:S(2)}) collective-permute-start(bf16[16,40,1280]{2,1,0:T(8,128)(2,1)} %get-tuple-element.75), channel_id=1, source_target_pairs={{0,4},{4,0},{8,12},{12,8},{16,20},{20,16},{24,28},{28,24},{32,36},... | collective-permute-start | bytes 4915208 | tf_op jit(solution)/shard_map/ppermute | solution.py:94
  105.1 25.4 %collective-permute-start.24 = (bf16[384,640]{1,0:T(8,128)(2,1)}, bf16[384,640]{1,0:T(8,128)(2,1)S(1)}, u32[]{:S(2)}, u32[]{:S(2)}) collective-permute-start(bf16[384,640]{1,0:T(8,128)(2,1)} %add_convert_fusion.2), channel_id=1, source_target_pairs={{0,1},{1,2},{2,3},{3,0},{4,5},{5,6},{6,7},{7,4},{8,9},{9,10},{10,1... | collective-permute-start | bytes 1474568 | tf_op jit(solution)/shard_map/ppermute | solution.py:505
  105.1 25.4 %collective-permute-start.25 = (bf16[384,640]{1,0:T(8,128)(2,1)}, bf16[384,640]{1,0:T(8,128)(2,1)S(1)}, u32[]{:S(2)}, u32[]{:S(2)}) collective-permute-start(bf16[384,640]{1,0:T(8,128)(2,1)} %add_convert_fusion.1), channel_id=1, source_target_pairs={{0,3},{1,0},{2,1},{3,2},{4,7},{5,4},{6,5},{7,6},{8,11},{9,8},{10,9... | collective-permute-start | bytes 1474568 | tf_op jit(solution)/shard_map/ppermute | solution.py:506
  111.3 0.9 copy-start.9
  111.3 19.2 %copy-start.12 = (s32[1,2176]{1,0:T(1,128)S(1)}, s32[1,2176]{1,0:T(1,128)}, u32[]{:S(2)}) copy-start(s32[1,2176]{1,0:T(1,128)} %pad_add_fusion) | copy-start | bytes 26116
  111.3 22.8 %copy-start.1 = (bf16[384,640]{1,0:T(8,128)(2,1)S(1)}, bf16[384,640]{1,0:T(8,128)(2,1)}, u32[]{:S(2)}) copy-start(bf16[384,640]{1,0:T(8,128)(2,1)} %copy-done) | copy-start | bytes 1474564
  111.3 22.8 %copy-start.3 = (bf16[384,640]{1,0:T(8,128)(2,1)S(1)}, bf16[384,640]{1,0:T(8,128)(2,1)}, u32[]{:S(2)}) copy-start(bf16[384,640]{1,0:T(8,128)(2,1)} %copy-done.2) | copy-start | bytes 1474564
  111.3 22.8 %copy-start.4 = (bf16[384,640]{1,0:T(8,128)(2,1)S(1)}, bf16[384,640]{1,0:T(8,128)(2,1)}, u32[]{:S(2)}) copy-start(bf16[384,640]{1,0:T(8,128)(2,1)} %get-tuple-element.80.l1) | copy-start | bytes 1474564
  111.3 22.8 %copy-start.5 = (bf16[384,640]{1,0:T(8,128)(2,1)S(1)}, bf16[384,640]{1,0:T(8,128)(2,1)}, u32[]{:S(2)}) copy-start(bf16[384,640]{1,0:T(8,128)(2,1)} %get-tuple-element.83.r1) | copy-start | bytes 1474564
  113.1 11.6 %collective-permute-start.23 = (bf16[4,40,640]{2,1,0:T(8,128)(2,1)}, bf16[4,40,640]{2,1,0:T(8,128)(2,1)S(1)}, u32[]{:S(2)}, u32[]{:S(2)}) collective-permute-start(bf16[4,40,640]{2,1,0:T(8,128)(2,1)} %get-tuple-element.113), channel_id=1, source_target_pairs={{0,96},{4,100},{8,104},{12,108},{16,112},{20,116},{24,120},{28,124... | collective-permute-start | bytes 614408 | tf_op jit(solution)/shard_map/ppermute | solution.py:71
  116.0 8.7 %collective-permute-start.22 = (bf16[4,40,640]{2,1,0:T(8,128)(2,1)}, bf16[4,40,640]{2,1,0:T(8,128)(2,1)S(1)}, u32[]{:S(2)}, u32[]{:S(2)}) collective-permute-start(bf16[4,40,640]{2,1,0:T(8,128)(2,1)} %get-tuple-element.114), channel_id=1, source_target_pairs={{0,64},{4,68},{8,72},{12,76},{16,80},{20,84},{24,88},{28,92},{32,9... | collective-permute-start | bytes 614408 | tf_op jit(solution)/shard_map/ppermute | solution.py:71
  116.5 12.7 %collective-permute-start.21 = (bf16[4,40,640]{2,1,0:T(8,128)(2,1)}, bf16[4,40,640]{2,1,0:T(8,128)(2,1)}, u32[]{:S(2)}, u32[]{:S(2)}) collective-permute-start(bf16[4,40,640]{2,1,0:T(8,128)(2,1)} %get-tuple-element.112), channel_id=1, source_target_pairs={{0,32},{4,36},{8,40},{12,44},{16,48},{20,52},{24,56},{28,60},{32,6... | collective-permute-start | bytes 614408 | tf_op jit(solution)/shard_map/ppermute | solution.py:71
  124.6 0.7 copy-start.10
  125.3 0.7 copy-start.11
  131.8 12.6 %collective-permute-start.28 = (bf16[4,40,640]{2,1,0:T(8,128)(2,1)S(1)}, bf16[4,40,640]{2,1,0:T(8,128)(2,1)S(1)}, u32[]{:S(2)}, u32[]{:S(2)}) collective-permute-start(bf16[4,40,640]{2,1,0:T(8,128)(2,1)S(1)} %get-tuple-element.110), channel_id=1, source_target_pairs={{0,24},{4,28},{8,0},{12,4},{16,8},{20,12},{24,16},{28,20},{32,56},... | collective-permute-start | bytes 614408 | tf_op jit(solution)/shard_map/ppermute | solution.py:71
  133.4 11.0 %collective-permute-start.27 = (bf16[4,40,640]{2,1,0:T(8,128)(2,1)S(1)}, bf16[4,40,640]{2,1,0:T(8,128)(2,1)S(1)}, u32[]{:S(2)}, u32[]{:S(2)}) collective-permute-start(bf16[4,40,640]{2,1,0:T(8,128)(2,1)S(1)} %get-tuple-element.111), channel_id=1, source_target_pairs={{0,16},{4,20},{8,24},{12,28},{16,0},{20,4},{24,8},{28,12},{32,48},... | collective-permute-start | bytes 614408 | tf_op jit(solution)/shard_map/ppermute | solution.py:71
  133.5 12.4 %collective-permute-start.26 = (bf16[4,40,640]{2,1,0:T(8,128)(2,1)S(1)}, bf16[4,40,640]{2,1,0:T(8,128)(2,1)S(1)}, u32[]{:S(2)}, u32[]{:S(2)}) collective-permute-start(bf16[4,40,640]{2,1,0:T(8,128)(2,1)S(1)} %get-tuple-element.109), channel_id=1, source_target_pairs={{0,8},{4,12},{8,16},{12,20},{16,24},{20,28},{24,0},{28,4},{32,40},... | collective-permute-start | bytes 614408 | tf_op jit(solution)/shard_map/ppermute | solution.py:71
  147.6 47.1 %all-to-all-start = ((bf16[128,48,256]{2,1,0:T(8,128)(2,1)}), bf16[128,48,256]{2,1,0:T(8,128)(2,1)S(1)}, u32[]{:S(2)}, u32[]{:S(2)}) async-start(bf16[128,48,256]{2,1,0:T(8,128)(2,1)} %bitcast.75), calls=%async_computation | async-start | bytes 6291456 | tf_op jit(solution)/shard_map/all_to_all | solution.py:526
  152.8 33.2 %collective-permute-start.29 = (bf16[40,640]{1,0:T(8,128)(2,1)S(1)}, bf16[40,640]{1,0:T(8,128)(2,1)S(1)}, u32[]{:S(2)}, u32[]{:S(2)}) collective-permute-start(bf16[40,640]{1,0:T(8,128)(2,1)S(1)} %get-tuple-element.121), channel_id=1, source_target_pairs={{0,8},{4,12},{8,16},{12,20},{16,24},{20,28},{24,0},{28,4},{32,40},... | collective-permute-start | bytes 153608 | tf_op jit(solution)/shard_map/ppermute | solution.py:71
  154.2 52.1 %collective-permute-start.30 = (bf16[40,640]{1,0:T(8,128)(2,1)}, bf16[40,640]{1,0:T(8,128)(2,1)}, u32[]{:S(2)}, u32[]{:S(2)}) collective-permute-start(bf16[40,640]{1,0:T(8,128)(2,1)} %get-tuple-element.120), channel_id=1, source_target_pairs={{0,16},{4,20},{8,24},{12,28},{16,0},{20,4},{24,8},{28,12},{32,48},... | collective-permute-start | bytes 153608 | tf_op jit(solution)/shard_map/ppermute | solution.py:71
  156.7 49.7 %collective-permute-start.31 = (bf16[40,640]{1,0:T(8,128)(2,1)}, bf16[40,640]{1,0:T(8,128)(2,1)}, u32[]{:S(2)}, u32[]{:S(2)}) collective-permute-start(bf16[40,640]{1,0:T(8,128)(2,1)} %get-tuple-element.119), channel_id=1, source_target_pairs={{0,24},{4,28},{8,0},{12,4},{16,8},{20,12},{24,16},{28,20},{32,56},... | collective-permute-start | bytes 153608 | tf_op jit(solution)/shard_map/ppermute | solution.py:71
  159.3 47.0 %collective-permute-start.32 = (bf16[40,640]{1,0:T(8,128)(2,1)}, bf16[40,640]{1,0:T(8,128)(2,1)}, u32[]{:S(2)}, u32[]{:S(2)}) collective-permute-start(bf16[40,640]{1,0:T(8,128)(2,1)} %get-tuple-element.117), channel_id=1, source_target_pairs={{0,32},{4,36},{8,40},{12,44},{16,48},{20,52},{24,56},{28,60},{32,6... | collective-permute-start | bytes 153608 | tf_op jit(solution)/shard_map/ppermute | solution.py:71
  160.5 45.8 %collective-permute-start.33 = (bf16[40,640]{1,0:T(8,128)(2,1)}, bf16[40,640]{1,0:T(8,128)(2,1)}, u32[]{:S(2)}, u32[]{:S(2)}) collective-permute-start(bf16[40,640]{1,0:T(8,128)(2,1)} %get-tuple-element.116), channel_id=1, source_target_pairs={{0,64},{4,68},{8,72},{12,76},{16,80},{20,84},{24,88},{28,92},{32,9... | collective-permute-start | bytes 153608 | tf_op jit(solution)/shard_map/ppermute | solution.py:71
  186.0 20.4 %collective-permute-start.34 = (bf16[40,640]{1,0:T(8,128)(2,1)}, bf16[40,640]{1,0:T(8,128)(2,1)}, u32[]{:S(2)}, u32[]{:S(2)}) collective-permute-start(bf16[40,640]{1,0:T(8,128)(2,1)} %get-tuple-element.115), channel_id=1, source_target_pairs={{0,96},{4,100},{8,104},{12,108},{16,112},{20,116},{24,120},{28,124... | collective-permute-start | bytes 153608 | tf_op jit(solution)/shard_map/ppermute | solution.py:71
  (1 other events, 0.6 us)

commit v6 on v4

--- a/solution.py
+++ b/solution.py
@@ -97,8 +97,7 @@
     return (sent, kept)
 
 
-def sum_on_chip(sent, kept):
-    got = lax.ppermute(sent, "dp", other_core())
+def sum_on_chip(got, kept):
     both = (kept.astype(jnp.float32) + got.astype(jnp.float32)).astype(jnp.bfloat16)
     return both.reshape(4, 4, *both.shape[1:])
 
@@ -302,7 +301,7 @@
     one = pl.Buffered(1)
     return pl.pallas_call(
         pack_kernel,
-        out_shape=jax.ShapeDtypeStruct((total_slots, width), jnp.bfloat16),
+        out_shape=pltpu.HBM((total_slots, width), jnp.bfloat16),
         grid=(total_slots // per_step,),
         in_specs=[pl.BlockSpec(slot.shape, fixed)] * 2
         + [pl.BlockSpec(numbers.shape, fixed)]
@@ -454,14 +453,12 @@
         memory, both, (((0,), (0,)), ((), ())), preferred_element_type=jnp.float32
     ).astype(jnp.bfloat16)
     sent, kept = core_halves(weight_grads, c)
-    sent, kept, from_last_right, from_next_left = lax.optimization_barrier(
-        (sent, kept, from_last_right, from_next_left)
-    )
-    chip_grads = sum_on_chip(sent, kept)
-    chip_grads, slot, from_last_left, from_next_right = lax.optimization_barrier(
-        (chip_grads, slot, from_last_left, from_next_right)
-    )
-    key_part, value_part = sum_one_axis(chip_grads, x, y)
+    sent, kept, from_last_right, from_next_left, from_last_left, from_next_right = (
+        lax.optimization_barrier(
+            (sent, kept, from_last_right, from_next_left, from_last_left, from_next_right)
+        )
+    )
+    other = lax.ppermute(sent, "dp", other_core())
     send_rows = pack_rows(
         slot,
         numbers,
@@ -469,7 +466,8 @@
         owners * SLOTS,
         row_width,
     )
-    send_rows, key_part, value_part = lax.optimization_barrier((send_rows, key_part, value_part))
+    send_rows, other = lax.optimization_barrier((send_rows, other))
+    key_part, value_part = sum_one_axis(sum_on_chip(other, kept), x, y)
     key_pieces = ring_pieces(key_part, y, along_y)
     value_pieces = ring_pieces(value_part, x, along_x)
     got_rows = lax.all_to_all(

time: 201 us -> 193 us (0.960)
  waiting for transfers between devices: 52.3 us -> 44 us
    ppermute x12, waiting for transfers between devices: 31.6 us -> 27.8 us  [ring_pieces(): lax.ppermute(lax.dynamic_index_in_dim(tiles, (here + d) % 4, 0, keepdims=...]
    ppermute x1, waiting for transfers between devices: 8.75 us -> 5.75 us  [body(): from_last_left = lax.ppermute(next_left, 'tensor', along_z(1))]
    all_to_all x1, waiting for transfers between devices: 2.33 us -> 0.01 us  [body(): lax.all_to_all(send_rows.reshape(owners, SLOTS, row_width), ('dp', 'tenso...]
  transfers between devices with their start and end apart: 36 -> 36, of which waited for: 11 -> 9; matrix products, arithmetic and copies ran while one was open for 12% -> 15% of each run, Pallas kernels for 15% -> 16%
where the time goes in v6:
time: 193 us; the launch traced here: 192 us
  starting transfers between devices  65.4 us (34%)
  Pallas kernels  48.2 us (25%)
  waiting for transfers between devices  44 us (23%)
  other arithmetic  14.8 us (8%)
  matrix products  10.8 us (6%)
  local copies, waits for them, and re-layouts  7.78 us (4%)
    ppermute x12, waiting for transfers between devices, ring_pieces(): lax.ppermute(lax.dynamic_index_in_dim(tiles, (here + d) % 4, 0, keepdims=...  27.8 us
    ppermute x12, starting transfers between devices, ring_pieces(): lax.ppermute(lax.dynamic_index_in_dim(tiles, (here + d) % 4, 0, keepdims=...  19.7 us
    ppermute x12, starting transfers between devices, ring_gather(): return [shard] + [lax.ppermute(shard, 'dp', perm_of(d)) for d in STEPS]  17.6 us
    pallas_call x2, Pallas kernels, grads(): pl.pallas_call(grads_kernel, out_shape=(pltpu.HBM(both_shape, jnp.bfloat1...  14.5 us
    pallas_call x1, Pallas kernels, project(): pl.pallas_call(project_kernel, out_shape=(jax.ShapeDtypeStruct((mem, 2 *...  12.4 us
    pallas_call x1, Pallas kernels, adam_rows(): pl.pallas_call(adam_kernel, out_shape=(jax.ShapeDtypeStruct((rows_dev, wi...  11 us
    pallas_call x1, Pallas kernels, pack_rows(): pl.pallas_call(pack_kernel, out_shape=pltpu.HBM((total_slots, width), jnp...  10.3 us
    dot_general x1, matrix products, body(): lax.dot_general(memory, both, (((0,), (0,)), ((), ())), preferred_element...  7.79 us
  transfers between devices with their start and end apart: 36, of which 9 were waited for; matrix products, arithmetic and copies ran while one was open for 15% of the time, Pallas kernels for 16%

profile of v6, /device:TPU:1, one launch (start us, length us, event | category | flops | bytes accessed | tf_op | source)
XLA Modules:
  0.0 192.0 jit_solution(12835856358748973551)
XLA Ops:
  0.6 3.4 %collective-permute-start.2 = (bf16[40,640]{1,0:T(8,128)(2,1)}, bf16[40,640]{1,0:T(8,128)(2,1)S(1)}, u32[]{:S(2)}, u32[]{:S(2)}) collective-permute-start(bf16[40,640]{1,0:T(8,128)(2,1)} %param.12), channel_id=1, source_target_pairs={{0,96},{4,100},{8,104},{12,108},{16,112},{20,116},{24,120},{28,124... | collective-permute-start | bytes 153608 | tf_op jit(solution)/shard_map/ppermute | solution.py:65
  4.0 1.7 collective-permute-start.1
  5.7 1.3 collective-permute-start.3
  7.0 2.6 %collective-permute-start.4 = (bf16[40,640]{1,0:T(8,128)(2,1)}, bf16[40,640]{1,0:T(8,128)(2,1)S(1)}, u32[]{:S(2)}, u32[]{:S(2)}) collective-permute-start(bf16[40,640]{1,0:T(8,128)(2,1)} %param.13), channel_id=1, source_target_pairs={{0,16},{4,20},{8,24},{12,28},{16,0},{20,4},{24,8},{28,12},{32,48},... | collective-permute-start | bytes 153608 | tf_op jit(solution)/shard_map/ppermute | solution.py:65
  12.0 1.8 collective-permute-done.5
  14.7 3.3 %collective-permute-start.7 = (bf16[4,40,640]{2,1,0:T(8,128)(2,1)S(1)}, bf16[4,40,640]{2,1,0:T(8,128)(2,1)S(1)}, u32[]{:S(2)}, u32[]{:S(2)}) collective-permute-start(bf16[4,40,640]{2,1,0:T(8,128)(2,1)S(1)} %pad_maximum_fusion.1), channel_id=1, source_target_pairs={{0,16},{4,20},{8,24},{12,28},{16,0},{20,4},{24,8},{28,12},{32,48},... | collective-permute-start | bytes 614408 | tf_op jit(solution)/shard_map/ppermute | solution.py:65
  18.0 1.5 collective-permute-start.9
  21.0 1.8 fusion.2
  22.9 1.5 select_convert_fusion.2
  25.0 1.2 fusion.3
  26.3 1.7 collective-permute-start.11
  28.3 2.6 %collective-permute-done.11 = bf16[4,40,640]{2,1,0:T(8,128)(2,1)S(1)} collective-permute-done((bf16[4,40,640]{2,1,0:T(8,128)(2,1)S(1)}, bf16[4,40,640]{2,1,0:T(8,128)(2,1)S(1)}, u32[]{:S(2)}, u32[]{:S(2)}) %collective-permute-start.11) | collective-permute-done | bytes 204832 | tf_op jit(solution)/shard_map/ppermute | solution.py:65
  31.3 4.7 %collective-permute-start.12 = (bf16[2,16,40,640]{3,2,1,0:T(8,128)(2,1)S(1)}, bf16[2,16,40,640]{3,2,1,0:T(8,128)(2,1)}, u32[]{:S(2)}, u32[]{:S(2)}) collective-permute-start(bf16[2,16,40,640]{3,2,1,0:T(8,128)(2,1)S(1)} %bitcast.84), channel_id=1, source_target_pairs={{0,4},{4,0},{8,12},{12,8},{16,20},{20,16},{24,28},{28,24},{32,36},... | collective-permute-start | bytes 4915208 | tf_op jit(solution)/shard_map/ppermute | solution.py:433
  36.0 3.2 %collective-permute-done.12.got_ref = bf16[2,16,40,640]{3,2,1,0:T(8,128)(2,1)} collective-permute-done((bf16[2,16,40,640]{3,2,1,0:T(8,128)(2,1)S(1)}, bf16[2,16,40,640]{3,2,1,0:T(8,128)(2,1)}, u32[]{:S(2)}, u32[]{:S(2)}) %collective-permute-start.12) | collective-permute-done | bytes 1638432 | tf_op jit(solution)/shard_map/ppermute | solution.py:433
  39.2 12.4 %project.1 = (bf16[1280,1280]{1,0:T(8,128)(2,1)S(1)}, f32[1536,640]{1,0:T(8,128)}, f32[8,1536]{1,0:T(8,128)S(1)}) custom-call(s32[3]{0:T(128)S(1)} %pad_add_fusion.3.spot_ref, bf16[2,16,40,640]{3,2,1,0:T(8,128)(2,1)} %bitcast.85, bf16[2,16,40,640]{3,2,1,0:T(8,128)(2,1)} %collective-permute-done.12.got_ref, bf16[1536,1280]{1,0:T(8,128)(2,1)} %memory_ref.1, ...), custom_call_target="tpu_custom_call" | custom-call | tf_op jit(solution)/shard_map/project/pallas_call | solution.py:155
  51.6 1.6 collective-permute-start.13
  53.2 3.3 %collective-permute-start.14 = (f32[8,1536]{1,0:T(8,128)S(1)}, f32[8,1536]{1,0:T(8,128)S(1)}, u32[]{:S(2)}, u32[]{:S(2)}) collective-permute-start(f32[8,1536]{1,0:T(8,128)S(1)} %get-tuple-element.50.refs_0_), channel_id=1, source_target_pairs={{0,2},{1,3},{2,0},{3,1},{4,6},{5,7},{6,4},{7,5},{8,10},{9,11},{10,... | collective-permute-start | bytes 147464 | tf_op jit(solution)/shard_map/ppermute | solution.py:436
  57.3 1.5 collective-permute-done.14.refs_2_
  59.8 4.2 %grads_far.1 = (bf16[384,1280]{1,0:T(8,128)(2,1)}, bf16[384,640]{1,0:T(8,128)(2,1)}, bf16[384,640]{1,0:T(8,128)(2,1)}) custom-call(s32[1]{0:T(128)} %bitcast.3.order_ref, f32[8,1536]{1,0:T(8,128)S(1)} %get-tuple-element.50.refs_0_, f32[8,1536]{1,0:T(8,128)S(1)} %collective-permute-done.13.refs_1_, f32[8,1536]{1,0:T(8,128)S(1)} %collective-permute-done.14.refs_2_, ...), custom_call_target="tpu_custom_call" | custom-call | tf_op jit(solution)/shard_map/grads_far/pallas_call | solution.py:239
  64.0 1.8 collective-permute-start.17
  65.8 10.3 %grads_near.1 = (bf16[1536,1280]{1,0:T(8,128)(2,1)}, bf16[384,640]{1,0:T(8,128)(2,1)S(1)}, bf16[384,640]{1,0:T(8,128)(2,1)S(1)}, bf16[384,640]{1,0:T(8,128)(2,1)...) custom-call(s32[4]{0:T(128)S(1)} %pad_add_fusion.2.order_ref, ...), custom_call_target="tpu_custom_call" | custom-call | tf_op jit(solution)/shard_map/grads_near/pallas_call | solution.py:239
  76.1 2.7 %collective-permute-start.19 = (bf16[384,640]{1,0:T(8,128)(2,1)S(1)}, bf16[384,640]{1,0:T(8,128)(2,1)S(1)}, u32[]{:S(2)}, u32[]{:S(2)}) collective-permute-start(bf16[384,640]{1,0:T(8,128)(2,1)S(1)} %get-tuple-element.60), channel_id=1, source_target_pairs={{0,3},{1,0},{2,1},{3,2},{4,7},{5,4},{6,5},{7,6},{8,11},{9,8},{10,9... | collective-permute-start | bytes 1474568 | tf_op jit(solution)/shard_map/ppermute | solution.py:446
  78.8 1.2 add_convert_fusion.1
  80.0 1.2 add_convert_fusion.2
  81.2 2.7 %collective-permute-start.21 = (bf16[384,640]{1,0:T(8,128)(2,1)S(1)}, bf16[384,640]{1,0:T(8,128)(2,1)S(1)}, u32[]{:S(2)}, u32[]{:S(2)}) collective-permute-start(bf16[384,640]{1,0:T(8,128)(2,1)S(1)} %add_convert_fusion.1), channel_id=1, source_target_pairs={{0,3},{1,0},{2,1},{3,2},{4,7},{5,4},{6,5},{7,6},{8,11},{9,8},{10,9... | collective-permute-start | bytes 1474568 | tf_op jit(solution)/shard_map/ppermute | solution.py:451
  83.9 7.8 %convolution_convert_fusion = bf16[1280,1280]{0,1:T(8,128)(2,1)S(1)} fusion(bf16[1536,1280]{1,0:T(8,128)(2,1)} %get-tuple-element.58, bf16[1536,1280]{1,0:T(8,128)(2,1)S(1)} %copy-done.1), kind=kOutput, calls=%fused_computation.2 | convolution fusion | flops 5034803200 | bytes 11141120 | tf_op jit(solution)/shard_map/dot_general | solution.py:452
  91.7 1.4 dynamic-slice_bitcast_fusion
  93.1 5.7 %collective-permute-done.20.l2 = bf16[384,640]{1,0:T(8,128)(2,1)S(1)} collective-permute-done((bf16[384,640]{1,0:T(8,128)(2,1)S(1)}, bf16[384,640]{1,0:T(8,128)(2,1)S(1)}, u32[]{:S(2)}, u32[]{:S(2)}) %collective-permute-start.20) | collective-permute-done | bytes 491552 | tf_op jit(solution)/shard_map/ppermute | solution.py:450
  98.9 3.0 %collective-permute-start.22 = (bf16[16,40,1280]{2,1,0:T(8,128)(2,1)S(1)}, bf16[16,40,1280]{2,1,0:T(8,128)(2,1)}, u32[]{:S(2)}, u32[]{:S(2)}) collective-permute-start(bf16[16,40,1280]{2,1,0:T(8,128)(2,1)S(1)} %get-tuple-element.72), channel_id=1, source_target_pairs={{0,4},{4,0},{8,12},{12,8},{16,20},{20,16},{24,28},{28,24},{32,36},... | collective-permute-start | bytes 4915208 | tf_op jit(solution)/shard_map/ppermute | solution.py:461
  101.9 10.3 %pack_rows.1 = bf16[6144,256]{1,0:T(8,128)(2,1)} custom-call(s32[1,2176]{1,0:T(1,128)S(1)} %and_select_fusion.1.tile_ref, s32[1,2176]{1,0:T(1,128)S(1)} %get-tuple-element.89.spot_ref, bf16[256,256]{1,0:T(8,128)(2,1)S(1)} %pad.4.numbers_ref, bf16[384,640]{1,0:T(8,128)(2,1)S(1)} %get-tuple-element.66.l1, bf16[384,640]{1,0:T(8,128)(2,1)S(1)} %collective-permute-done.20.l2, ...), custom_call_target="tpu_custom_call" | custom-call | tf_op jit(solution)/shard_map/pack_rows/pallas_call | solution.py:302
  112.2 7.7 %all-to-all-start = ((bf16[128,48,256]{2,1,0:T(8,128)(2,1)}), bf16[128,48,256]{2,1,0:T(8,128)(2,1)S(1)}, u32[]{:S(2)}, u32[]{:S(2)}) async-start(bf16[128,48,256]{2,1,0:T(8,128)(2,1)} %bitcast.82), calls=%async_computation | async-start | bytes 6291456 | tf_op jit(solution)/shard_map/all_to_all | solution.py:473
  120.0 2.3 %add_convert_fusion = bf16[16,40,1280]{2,1,0:T(8,128)(2,1)S(1)} fusion(bf16[16,40,1280]{2,1,0:T(8,128)(2,1)} %collective-permute-done.22, bf16[16,40,1280]{2,1,0:T(8,128)(2,1)} %get-tuple-element.63), kind=kLoop, calls=%fused_computation.3 | loop fusion | flops 3276800 | bytes 4915200 | tf_op jit(solution)/shard_map/convert_element_type | solution.py:101
  125.1 1.4 collective-permute-start.29
  126.5 2.4 %collective-permute-start.30 = (bf16[4,40,640]{2,1,0:T(8,128)(2,1)}, bf16[4,40,640]{2,1,0:T(8,128)(2,1)S(1)}, u32[]{:S(2)}, u32[]{:S(2)}) collective-permute-start(bf16[4,40,640]{2,1,0:T(8,128)(2,1)} %get-tuple-element.97), channel_id=1, source_target_pairs={{0,16},{4,20},{8,24},{12,28},{16,0},{20,4},{24,8},{28,12},{32,48},... | collective-permute-start | bytes 614408 | tf_op jit(solution)/shard_map/ppermute | solution.py:71
  130.0 1.2 dynamic-slice_bitcast_fusion.7
  131.2 1.3 collective-permute-start.23
  132.5 2.4 %collective-permute-start.24 = (bf16[4,40,640]{2,1,0:T(8,128)(2,1)S(1)}, bf16[4,40,640]{2,1,0:T(8,128)(2,1)S(1)}, u32[]{:S(2)}, u32[]{:S(2)}) collective-permute-start(bf16[4,40,640]{2,1,0:T(8,128)(2,1)S(1)} %get-tuple-element.100), channel_id=1, source_target_pairs={{0,64},{4,68},{8,72},{12,76},{16,80},{20,84},{24,88},{28,92},{32,9... | collective-permute-start | bytes 614408 | tf_op jit(solution)/shard_map/ppermute | solution.py:71
  134.9 25.9 %collective-permute-done.29 = bf16[4,40,640]{2,1,0:T(8,128)(2,1)S(1)} collective-permute-done((bf16[4,40,640]{2,1,0:T(8,128)(2,1)}, bf16[4,40,640]{2,1,0:T(8,128)(2,1)S(1)}, u32[]{:S(2)}, u32[]{:S(2)}) %collective-permute-start.29) | collective-permute-done | bytes 204832 | tf_op jit(solution)/shard_map/ppermute | solution.py:71
  160.8 2.8 %collective-permute-start.25 = (bf16[4,40,640]{2,1,0:T(8,128)(2,1)S(1)}, bf16[4,40,640]{2,1,0:T(8,128)(2,1)S(1)}, u32[]{:S(2)}, u32[]{:S(2)}) collective-permute-start(bf16[4,40,640]{2,1,0:T(8,128)(2,1)S(1)} %get-tuple-element.99), channel_id=1, source_target_pairs={{0,96},{4,100},{8,104},{12,108},{16,112},{20,116},{24,120},{28,124... | collective-permute-start | bytes 614408 | tf_op jit(solution)/shard_map/ppermute | solution.py:71
  163.6 1.9 collective-permute-done.30
  167.3 1.3 collective-permute-start.32
  168.6 2.4 %collective-permute-start.33 = (bf16[40,640]{1,0:T(8,128)(2,1)}, bf16[40,640]{1,0:T(8,128)(2,1)S(1)}, u32[]{:S(2)}, u32[]{:S(2)}) collective-permute-start(bf16[40,640]{1,0:T(8,128)(2,1)} %get-tuple-element.102), channel_id=1, source_target_pairs={{0,64},{4,68},{8,72},{12,76},{16,80},{20,84},{24,88},{28,92},{32,9... | collective-permute-start | bytes 153608 | tf_op jit(solution)/shard_map/ppermute | solution.py:71
  171.0 1.1 collective-permute-start.34
  173.9 1.3 collective-permute-start.27
  175.2 2.1 %collective-permute-start.28 = (bf16[40,640]{1,0:T(8,128)(2,1)}, bf16[40,640]{1,0:T(8,128)(2,1)}, u32[]{:S(2)}, u32[]{:S(2)}) collective-permute-start(bf16[40,640]{1,0:T(8,128)(2,1)} %get-tuple-element.105), channel_id=1, source_target_pairs={{0,24},{4,28},{8,0},{12,4},{16,8},{20,12},{24,16},{28,20},{32,56},... | collective-permute-start | bytes 153608 | tf_op jit(solution)/shard_map/ppermute | solution.py:71
  178.0 11.0 %adam_rows.1 = (f32[2048,256]{1,0:T(8,128)}, f32[2048,256]{1,0:T(8,128)}, f32[2048,256]{1,0:T(8,128)}) custom-call(s32[1,6144]{1,0:T(1,128)S(1)} %reshape.247.tile_ref, s32[1,6144]{1,0:T(1,128)S(1)} %reshape.248.spot_ref, bf16[6144,256]{1,0:T(8,128)(2,1)S(1)} %bitcast.81, f32[2048,256]{1,0:T(8,128)} %table_ref.1, f32[2048,256]{1,0:T(8,128)} %first_ref.1, ...), custom_call_target="tpu_custom_call" | custom-call | tf_op jit(solution)/shard_map/adam_rows/pallas_call | solution.py:353
  189.0 1.5 convert_add_fusion.2
  190.5 1.5 convert_add_fusion.3
  (80 shorter events, 16.1 us)
Async XLA Ops:
  0.6 9.0 %collective-permute-start.2 = (bf16[40,640]{1,0:T(8,128)(2,1)}, bf16[40,640]{1,0:T(8,128)(2,1)S(1)}, u32[]{:S(2)}, u32[]{:S(2)}) collective-permute-start(bf16[40,640]{1,0:T(8,128)(2,1)} %param.12), channel_id=1, source_target_pairs={{0,96},{4,100},{8,104},{12,108},{16,112},{20,116},{24,120},{28,124... | collective-permute-start | bytes 153608 | tf_op jit(solution)/shard_map/ppermute | solution.py:65
  4.0 6.8 %collective-permute-start = (bf16[40,640]{1,0:T(8,128)(2,1)}, bf16[40,640]{1,0:T(8,128)(2,1)S(1)}, u32[]{:S(2)}, u32[]{:S(2)}) collective-permute-start(bf16[40,640]{1,0:T(8,128)(2,1)} %param.12), channel_id=1, source_target_pairs={{0,32},{4,36},{8,40},{12,44},{16,48},{20,52},{24,56},{28,60},{32,6... | collective-permute-start | bytes 153608 | tf_op jit(solution)/shard_map/ppermute | solution.py:65
  4.0 6.8 %collective-permute-start.1 = (bf16[40,640]{1,0:T(8,128)(2,1)}, bf16[40,640]{1,0:T(8,128)(2,1)S(1)}, u32[]{:S(2)}, u32[]{:S(2)}) collective-permute-start(bf16[40,640]{1,0:T(8,128)(2,1)} %param.12), channel_id=1, source_target_pairs={{0,64},{4,68},{8,72},{12,76},{16,80},{20,84},{24,88},{28,92},{32,9... | collective-permute-start | bytes 153608 | tf_op jit(solution)/shard_map/ppermute | solution.py:65
  5.7 5.9 %collective-permute-start.3 = (bf16[40,640]{1,0:T(8,128)(2,1)}, bf16[40,640]{1,0:T(8,128)(2,1)S(1)}, u32[]{:S(2)}, u32[]{:S(2)}) collective-permute-start(bf16[40,640]{1,0:T(8,128)(2,1)} %param.13), channel_id=1, source_target_pairs={{0,8},{4,12},{8,16},{12,20},{16,24},{20,28},{24,0},{28,4},{32,40},... | collective-permute-start | bytes 153608 | tf_op jit(solution)/shard_map/ppermute | solution.py:65
  7.0 4.9 %collective-permute-start.4 = (bf16[40,640]{1,0:T(8,128)(2,1)}, bf16[40,640]{1,0:T(8,128)(2,1)S(1)}, u32[]{:S(2)}, u32[]{:S(2)}) collective-permute-start(bf16[40,640]{1,0:T(8,128)(2,1)} %param.13), channel_id=1, source_target_pairs={{0,16},{4,20},{8,24},{12,28},{16,0},{20,4},{24,8},{28,12},{32,48},... | collective-permute-start | bytes 153608 | tf_op jit(solution)/shard_map/ppermute | solution.py:65
  9.7 4.1 %collective-permute-start.5 = (bf16[40,640]{1,0:T(8,128)(2,1)}, bf16[40,640]{1,0:T(8,128)(2,1)S(1)}, u32[]{:S(2)}, u32[]{:S(2)}) collective-permute-start(bf16[40,640]{1,0:T(8,128)(2,1)} %param.13), channel_id=1, source_target_pairs={{0,24},{4,28},{8,0},{12,4},{16,8},{20,12},{24,16},{28,20},{32,56},... | collective-permute-start | bytes 153608 | tf_op jit(solution)/shard_map/ppermute | solution.py:65
  14.6 11.7 %collective-permute-start.6 = (bf16[4,40,640]{2,1,0:T(8,128)(2,1)S(1)}, bf16[4,40,640]{2,1,0:T(8,128)(2,1)S(1)}, u32[]{:S(2)}, u32[]{:S(2)}) collective-permute-start(bf16[4,40,640]{2,1,0:T(8,128)(2,1)S(1)} %pad_maximum_fusion.1), channel_id=1, source_target_pairs={{0,8},{4,12},{8,16},{12,20},{16,24},{20,28},{24,0},{28,4},{32,40},... | collective-permute-start | bytes 614408 | tf_op jit(solution)/shard_map/ppermute | solution.py:65
  14.7 13.5 %collective-permute-start.7 = (bf16[4,40,640]{2,1,0:T(8,128)(2,1)S(1)}, bf16[4,40,640]{2,1,0:T(8,128)(2,1)S(1)}, u32[]{:S(2)}, u32[]{:S(2)}) collective-permute-start(bf16[4,40,640]{2,1,0:T(8,128)(2,1)S(1)} %pad_maximum_fusion.1), channel_id=1, source_target_pairs={{0,16},{4,20},{8,24},{12,28},{16,0},{20,4},{24,8},{28,12},{32,48},... | collective-permute-start | bytes 614408 | tf_op jit(solution)/shard_map/ppermute | solution.py:65
  18.0 10.2 %collective-permute-start.8 = (bf16[4,40,640]{2,1,0:T(8,128)(2,1)S(1)}, bf16[4,40,640]{2,1,0:T(8,128)(2,1)S(1)}, u32[]{:S(2)}, u32[]{:S(2)}) collective-permute-start(bf16[4,40,640]{2,1,0:T(8,128)(2,1)S(1)} %pad_maximum_fusion.1), channel_id=1, source_target_pairs={{0,24},{4,28},{8,0},{12,4},{16,8},{20,12},{24,16},{28,20},{32,56},... | collective-permute-start | bytes 614408 | tf_op jit(solution)/shard_map/ppermute | solution.py:65
  18.0 10.3 %collective-permute-start.9 = (bf16[4,40,640]{2,1,0:T(8,128)(2,1)S(1)}, bf16[4,40,640]{2,1,0:T(8,128)(2,1)S(1)}, u32[]{:S(2)}, u32[]{:S(2)}) collective-permute-start(bf16[4,40,640]{2,1,0:T(8,128)(2,1)S(1)} %pad_maximum_fusion.2), channel_id=1, source_target_pairs={{0,32},{4,36},{8,40},{12,44},{16,48},{20,52},{24,56},{28,60},{32,6... | collective-permute-start | bytes 614408 | tf_op jit(solution)/shard_map/ppermute | solution.py:65
  19.5 8.8 %collective-permute-start.10 = (bf16[4,40,640]{2,1,0:T(8,128)(2,1)S(1)}, bf16[4,40,640]{2,1,0:T(8,128)(2,1)S(1)}, u32[]{:S(2)}, u32[]{:S(2)}) collective-permute-start(bf16[4,40,640]{2,1,0:T(8,128)(2,1)S(1)} %pad_maximum_fusion.2), channel_id=1, source_target_pairs={{0,64},{4,68},{8,72},{12,76},{16,80},{20,84},{24,88},{28,92},{32,9... | collective-permute-start | bytes 614408 | tf_op jit(solution)/shard_map/ppermute | solution.py:65
  26.3 4.7 %collective-permute-start.11 = (bf16[4,40,640]{2,1,0:T(8,128)(2,1)S(1)}, bf16[4,40,640]{2,1,0:T(8,128)(2,1)S(1)}, u32[]{:S(2)}, u32[]{:S(2)}) collective-permute-start(bf16[4,40,640]{2,1,0:T(8,128)(2,1)S(1)} %pad_maximum_fusion.2), channel_id=1, source_target_pairs={{0,96},{4,100},{8,104},{12,108},{16,112},{20,116},{24,120},{28,124... | collective-permute-start | bytes 614408 | tf_op jit(solution)/shard_map/ppermute | solution.py:65
  31.3 4.8 %copy-start = (bf16[2,4,4,40,640]{4,3,2,1,0:T(8,128)(2,1)}, bf16[2,4,4,40,640]{4,3,2,1,0:T(8,128)(2,1)S(1)}, u32[]{:S(2)}) copy-start(bf16[2,4,4,40,640]{4,3,2,1,0:T(8,128)(2,1)S(1)} %pad_maximum_fusion) | copy-start | bytes 4915204
  31.3 7.9 %collective-permute-start.12 = (bf16[2,16,40,640]{3,2,1,0:T(8,128)(2,1)S(1)}, bf16[2,16,40,640]{3,2,1,0:T(8,128)(2,1)}, u32[]{:S(2)}, u32[]{:S(2)}) collective-permute-start(bf16[2,16,40,640]{3,2,1,0:T(8,128)(2,1)S(1)} %bitcast.84), channel_id=1, source_target_pairs={{0,4},{4,0},{8,12},{12,8},{16,20},{20,16},{24,28},{28,24},{32,36},... | collective-permute-start | bytes 4915208 | tf_op jit(solution)/shard_map/ppermute | solution.py:433
  51.6 5.7 %collective-permute-start.13 = (f32[8,1536]{1,0:T(8,128)S(1)}, f32[8,1536]{1,0:T(8,128)S(1)}, u32[]{:S(2)}, u32[]{:S(2)}) collective-permute-start(f32[8,1536]{1,0:T(8,128)S(1)} %get-tuple-element.50.refs_0_), channel_id=1, source_target_pairs={{0,1},{1,2},{2,3},{3,0},{4,5},{5,6},{6,7},{7,4},{8,9},{9,10},{10,1... | collective-permute-start | bytes 147464 | tf_op jit(solution)/shard_map/ppermute | solution.py:436
  53.2 5.6 %collective-permute-start.14 = (f32[8,1536]{1,0:T(8,128)S(1)}, f32[8,1536]{1,0:T(8,128)S(1)}, u32[]{:S(2)}, u32[]{:S(2)}) collective-permute-start(f32[8,1536]{1,0:T(8,128)S(1)} %get-tuple-element.50.refs_0_), channel_id=1, source_target_pairs={{0,2},{1,3},{2,0},{3,1},{4,6},{5,7},{6,4},{7,5},{8,10},{9,11},{10,... | collective-permute-start | bytes 147464 | tf_op jit(solution)/shard_map/ppermute | solution.py:436
  56.5 3.2 %collective-permute-start.15 = (f32[8,1536]{1,0:T(8,128)S(1)}, f32[8,1536]{1,0:T(8,128)}, u32[]{:S(2)}, u32[]{:S(2)}) collective-permute-start(f32[8,1536]{1,0:T(8,128)S(1)} %get-tuple-element.50.refs_0_), channel_id=1, source_target_pairs={{0,3},{1,0},{2,1},{3,2},{4,7},{5,4},{6,5},{7,6},{8,11},{9,8},{10,9... | collective-permute-start | bytes 147464 | tf_op jit(solution)/shard_map/ppermute | solution.py:436
  64.0 14.9 %collective-permute-start.17 = (bf16[384,640]{1,0:T(8,128)(2,1)}, bf16[384,640]{1,0:T(8,128)(2,1)}, u32[]{:S(2)}, u32[]{:S(2)}) collective-permute-start(bf16[384,640]{1,0:T(8,128)(2,1)} %get-tuple-element.56), channel_id=1, source_target_pairs={{0,3},{1,0},{2,1},{3,2},{4,7},{5,4},{6,5},{7,6},{8,11},{9,8},{10,9... | collective-permute-start | bytes 1474568 | tf_op jit(solution)/shard_map/ppermute | solution.py:441
  65.7 14.3 %collective-permute-start.16 = (bf16[384,640]{1,0:T(8,128)(2,1)}, bf16[384,640]{1,0:T(8,128)(2,1)}, u32[]{:S(2)}, u32[]{:S(2)}) collective-permute-start(bf16[384,640]{1,0:T(8,128)(2,1)} %get-tuple-element.54), channel_id=1, source_target_pairs={{0,1},{1,2},{2,3},{3,0},{4,5},{5,6},{6,7},{7,4},{8,9},{9,10},{10,1... | collective-permute-start | bytes 1474568 | tf_op jit(solution)/shard_map/ppermute | solution.py:440
  65.8 18.1 %copy-start.1 = (bf16[1536,1280]{1,0:T(8,128)(2,1)S(1)}, bf16[1536,1280]{1,0:T(8,128)(2,1)}, u32[]{:S(2)}) copy-start(bf16[1536,1280]{1,0:T(8,128)(2,1)} %memory_ref.1) | copy-start | bytes 11796484
  76.1 17.0 %collective-permute-start.18 = (bf16[384,640]{1,0:T(8,128)(2,1)S(1)}, bf16[384,640]{1,0:T(8,128)(2,1)S(1)}, u32[]{:S(2)}, u32[]{:S(2)}) collective-permute-start(bf16[384,640]{1,0:T(8,128)(2,1)S(1)} %get-tuple-element.59), channel_id=1, source_target_pairs={{0,1},{1,2},{2,3},{3,0},{4,5},{5,6},{6,7},{7,4},{8,9},{9,10},{10,1... | collective-permute-start | bytes 1474568 | tf_op jit(solution)/shard_map/ppermute | solution.py:445
  76.1 17.0 %collective-permute-start.19 = (bf16[384,640]{1,0:T(8,128)(2,1)S(1)}, bf16[384,640]{1,0:T(8,128)(2,1)S(1)}, u32[]{:S(2)}, u32[]{:S(2)}) collective-permute-start(bf16[384,640]{1,0:T(8,128)(2,1)S(1)} %get-tuple-element.60), channel_id=1, source_target_pairs={{0,3},{1,0},{2,1},{3,2},{4,7},{5,4},{6,5},{7,6},{8,11},{9,8},{10,9... | collective-permute-start | bytes 1474568 | tf_op jit(solution)/shard_map/ppermute | solution.py:446
  81.2 17.7 %collective-permute-start.20 = (bf16[384,640]{1,0:T(8,128)(2,1)S(1)}, bf16[384,640]{1,0:T(8,128)(2,1)S(1)}, u32[]{:S(2)}, u32[]{:S(2)}) collective-permute-start(bf16[384,640]{1,0:T(8,128)(2,1)S(1)} %add_convert_fusion.2), channel_id=1, source_target_pairs={{0,1},{1,2},{2,3},{3,0},{4,5},{5,6},{6,7},{7,4},{8,9},{9,10},{10,1... | collective-permute-start | bytes 1474568 | tf_op jit(solution)/shard_map/ppermute | solution.py:450
  81.2 17.6 %collective-permute-start.21 = (bf16[384,640]{1,0:T(8,128)(2,1)S(1)}, bf16[384,640]{1,0:T(8,128)(2,1)S(1)}, u32[]{:S(2)}, u32[]{:S(2)}) collective-permute-start(bf16[384,640]{1,0:T(8,128)(2,1)S(1)} %add_convert_fusion.1), channel_id=1, source_target_pairs={{0,3},{1,0},{2,1},{3,2},{4,7},{5,4},{6,5},{7,6},{8,11},{9,8},{10,9... | collective-permute-start | bytes 1474568 | tf_op jit(solution)/shard_map/ppermute | solution.py:451
  91.7 10.1 %copy-start.3 = (s32[1,2176]{1,0:T(1,128)S(1)}, s32[1,2176]{1,0:T(1,128)}, u32[]{:S(2)}) copy-start(s32[1,2176]{1,0:T(1,128)} %pad_add_fusion) | copy-start | bytes 26116
  98.9 13.4 %collective-permute-start.22 = (bf16[16,40,1280]{2,1,0:T(8,128)(2,1)S(1)}, bf16[16,40,1280]{2,1,0:T(8,128)(2,1)}, u32[]{:S(2)}, u32[]{:S(2)}) collective-permute-start(bf16[16,40,1280]{2,1,0:T(8,128)(2,1)S(1)} %get-tuple-element.72), channel_id=1, source_target_pairs={{0,4},{4,0},{8,12},{12,8},{16,20},{20,16},{24,28},{28,24},{32,36},... | collective-permute-start | bytes 4915208 | tf_op jit(solution)/shard_map/ppermute | solution.py:461
  112.2 65.0 %all-to-all-start = ((bf16[128,48,256]{2,1,0:T(8,128)(2,1)}), bf16[128,48,256]{2,1,0:T(8,128)(2,1)S(1)}, u32[]{:S(2)}, u32[]{:S(2)}) async-start(bf16[128,48,256]{2,1,0:T(8,128)(2,1)} %bitcast.82), calls=%async_computation | async-start | bytes 6291456 | tf_op jit(solution)/shard_map/all_to_all | solution.py:473
  123.3 0.9 copy-start.2
  125.1 35.7 %collective-permute-start.29 = (bf16[4,40,640]{2,1,0:T(8,128)(2,1)}, bf16[4,40,640]{2,1,0:T(8,128)(2,1)S(1)}, u32[]{:S(2)}, u32[]{:S(2)}) collective-permute-start(bf16[4,40,640]{2,1,0:T(8,128)(2,1)} %get-tuple-element.95), channel_id=1, source_target_pairs={{0,8},{4,12},{8,16},{12,20},{16,24},{20,28},{24,0},{28,4},{32,40},... | collective-permute-start | bytes 614408 | tf_op jit(solution)/shard_map/ppermute | solution.py:71
  126.5 39.0 %collective-permute-start.30 = (bf16[4,40,640]{2,1,0:T(8,128)(2,1)}, bf16[4,40,640]{2,1,0:T(8,128)(2,1)S(1)}, u32[]{:S(2)}, u32[]{:S(2)}) collective-permute-start(bf16[4,40,640]{2,1,0:T(8,128)(2,1)} %get-tuple-element.97), channel_id=1, source_target_pairs={{0,16},{4,20},{8,24},{12,28},{16,0},{20,4},{24,8},{28,12},{32,48},... | collective-permute-start | bytes 614408 | tf_op jit(solution)/shard_map/ppermute | solution.py:71
  128.9 36.6 %collective-permute-start.31 = (bf16[4,40,640]{2,1,0:T(8,128)(2,1)}, bf16[4,40,640]{2,1,0:T(8,128)(2,1)}, u32[]{:S(2)}, u32[]{:S(2)}) collective-permute-start(bf16[4,40,640]{2,1,0:T(8,128)(2,1)} %get-tuple-element.96), channel_id=1, source_target_pairs={{0,24},{4,28},{8,0},{12,4},{16,8},{20,12},{24,16},{28,20},{32,56},... | collective-permute-start | bytes 614408 | tf_op jit(solution)/shard_map/ppermute | solution.py:71
  131.2 39.8 %collective-permute-start.23 = (bf16[4,40,640]{2,1,0:T(8,128)(2,1)S(1)}, bf16[4,40,640]{2,1,0:T(8,128)(2,1)S(1)}, u32[]{:S(2)}, u32[]{:S(2)}) collective-permute-start(bf16[4,40,640]{2,1,0:T(8,128)(2,1)S(1)} %get-tuple-element.98), channel_id=1, source_target_pairs={{0,32},{4,36},{8,40},{12,44},{16,48},{20,52},{24,56},{28,60},{32,6... | collective-permute-start | bytes 614408 | tf_op jit(solution)/shard_map/ppermute | solution.py:71
  132.5 39.7 %collective-permute-start.24 = (bf16[4,40,640]{2,1,0:T(8,128)(2,1)S(1)}, bf16[4,40,640]{2,1,0:T(8,128)(2,1)S(1)}, u32[]{:S(2)}, u32[]{:S(2)}) collective-permute-start(bf16[4,40,640]{2,1,0:T(8,128)(2,1)S(1)} %get-tuple-element.100), channel_id=1, source_target_pairs={{0,64},{4,68},{8,72},{12,76},{16,80},{20,84},{24,88},{28,92},{32,9... | collective-permute-start | bytes 614408 | tf_op jit(solution)/shard_map/ppermute | solution.py:71
  160.8 11.4 %collective-permute-start.25 = (bf16[4,40,640]{2,1,0:T(8,128)(2,1)S(1)}, bf16[4,40,640]{2,1,0:T(8,128)(2,1)S(1)}, u32[]{:S(2)}, u32[]{:S(2)}) collective-permute-start(bf16[4,40,640]{2,1,0:T(8,128)(2,1)S(1)} %get-tuple-element.99), channel_id=1, source_target_pairs={{0,96},{4,100},{8,104},{12,108},{16,112},{20,116},{24,120},{28,124... | collective-permute-start | bytes 614408 | tf_op jit(solution)/shard_map/ppermute | solution.py:71
  167.3 7.9 %collective-permute-start.32 = (bf16[40,640]{1,0:T(8,128)(2,1)S(1)}, bf16[40,640]{1,0:T(8,128)(2,1)S(1)}, u32[]{:S(2)}, u32[]{:S(2)}) collective-permute-start(bf16[40,640]{1,0:T(8,128)(2,1)S(1)} %get-tuple-element.103), channel_id=1, source_target_pairs={{0,32},{4,36},{8,40},{12,44},{16,48},{20,52},{24,56},{28,60},{32,6... | collective-permute-start | bytes 153608 | tf_op jit(solution)/shard_map/ppermute | solution.py:71
  168.6 20.4 %collective-permute-start.33 = (bf16[40,640]{1,0:T(8,128)(2,1)}, bf16[40,640]{1,0:T(8,128)(2,1)S(1)}, u32[]{:S(2)}, u32[]{:S(2)}) collective-permute-start(bf16[40,640]{1,0:T(8,128)(2,1)} %get-tuple-element.102), channel_id=1, source_target_pairs={{0,64},{4,68},{8,72},{12,76},{16,80},{20,84},{24,88},{28,92},{32,9... | collective-permute-start | bytes 153608 | tf_op jit(solution)/shard_map/ppermute | solution.py:71
  171.0 18.0 %collective-permute-start.34 = (bf16[40,640]{1,0:T(8,128)(2,1)}, bf16[40,640]{1,0:T(8,128)(2,1)}, u32[]{:S(2)}, u32[]{:S(2)}) collective-permute-start(bf16[40,640]{1,0:T(8,128)(2,1)} %get-tuple-element.101), channel_id=1, source_target_pairs={{0,96},{4,100},{8,104},{12,108},{16,112},{20,116},{24,120},{28,124... | collective-permute-start | bytes 153608 | tf_op jit(solution)/shard_map/ppermute | solution.py:71
  173.9 15.1 %collective-permute-start.26 = (bf16[40,640]{1,0:T(8,128)(2,1)}, bf16[40,640]{1,0:T(8,128)(2,1)}, u32[]{:S(2)}, u32[]{:S(2)}) collective-permute-start(bf16[40,640]{1,0:T(8,128)(2,1)} %get-tuple-element.107), channel_id=1, source_target_pairs={{0,8},{4,12},{8,16},{12,20},{16,24},{20,28},{24,0},{28,4},{32,40},... | collective-permute-start | bytes 153608 | tf_op jit(solution)/shard_map/ppermute | solution.py:71
  173.9 15.1 %collective-permute-start.27 = (bf16[40,640]{1,0:T(8,128)(2,1)}, bf16[40,640]{1,0:T(8,128)(2,1)}, u32[]{:S(2)}, u32[]{:S(2)}) collective-permute-start(bf16[40,640]{1,0:T(8,128)(2,1)} %get-tuple-element.106), channel_id=1, source_target_pairs={{0,16},{4,20},{8,24},{12,28},{16,0},{20,4},{24,8},{28,12},{32,48},... | collective-permute-start | bytes 153608 | tf_op jit(solution)/shard_map/ppermute | solution.py:71
  175.2 13.8 %collective-permute-start.28 = (bf16[40,640]{1,0:T(8,128)(2,1)}, bf16[40,640]{1,0:T(8,128)(2,1)}, u32[]{:S(2)}, u32[]{:S(2)}) collective-permute-start(bf16[40,640]{1,0:T(8,128)(2,1)} %get-tuple-element.105), channel_id=1, source_target_pairs={{0,24},{4,28},{8,0},{12,4},{16,8},{20,12},{24,16},{28,20},{32,56},... | collective-permute-start | bytes 153608 | tf_op jit(solution)/shard_map/ppermute | solution.py:71

commit v7 on v6

--- a/solution.py
+++ b/solution.py
@@ -23,18 +23,18 @@
     return (x % 4) * 8 + (y % 4) * 2 + c
 
 
-def along_x(d):
+def along_first(d):
     return [
-        (dp_index(x, y, c), dp_index(x + d, y, c))
+        (dp_index(x, y, c), dp_index(x, y + d, c) if c else dp_index(x + d, y, c))
         for x in range(4)
         for y in range(4)
         for c in range(2)
     ]
 
 
-def along_y(d):
+def along_second(d):
     return [
-        (dp_index(x, y, c), dp_index(x, y + d, c))
+        (dp_index(x, y, c), dp_index(x + d, y, c) if c else dp_index(x, y + d, c))
         for x in range(4)
         for y in range(4)
         for c in range(2)
@@ -79,15 +79,17 @@
     return sum(p.astype(jnp.float32) for p in ring_pieces(tiles, here, perm_of))
 
 
-def gather_weights(key_weight, value_weight, row_ids):
-    key_x = ring_gather(key_weight, along_x)
-    value_y = ring_gather(value_weight, along_y)
-    key_x = jnp.stack(key_x)
-    value_y = jnp.stack(value_y)
-    key_x, value_y, row_ids = lax.optimization_barrier((key_x, value_y, row_ids))
-    key_all = ring_gather(key_x, along_y)
-    value_all = ring_gather(value_y, along_x)
-    return (jnp.stack([jnp.stack(key_all), jnp.stack(value_all)]), row_ids)
+def gather_weights(key_weight, value_weight, routed):
+    both = jnp.concatenate([key_weight, value_weight], axis=1)
+    line = jnp.stack(ring_gather(both, along_first))
+    line, routed = lax.optimization_barrier((line, routed))
+    return (jnp.stack(ring_gather(line, along_second)), *routed)
+
+
+def sum_on_chip(got, kept, c):
+    both = (kept.astype(jnp.float32) + got.astype(jnp.float32)).astype(jnp.bfloat16)
+    both = both.reshape(4, 4, *both.shape[1:])
+    return jnp.where(c == 0, both, jnp.swapaxes(both, 0, 1))
 
 
 def core_halves(weight_grads, c):
@@ -97,18 +99,6 @@
     return (sent, kept)
 
 
-def sum_on_chip(got, kept):
-    both = (kept.astype(jnp.float32) + got.astype(jnp.float32)).astype(jnp.bfloat16)
-    return both.reshape(4, 4, *both.shape[1:])
-
-
-def sum_one_axis(both, x, y):
-    half = both.shape[3] // 2
-    key_part = ring_sum(both[:, :, :, :half], x, along_x).astype(jnp.bfloat16)
-    value_part = ring_sum(jnp.swapaxes(both[:, :, :, half:], 0, 1), y, along_y).astype(jnp.bfloat16)
-    return (key_part, value_part)
-
-
 def project_kernel(
     spot_ref, mine_ref, got_ref, memory_ref, hidden_ref, grad_ref, weight_ref, key_proj_ref, sums_ref
 ):
@@ -117,21 +107,16 @@
     @pl.when(pl.program_id(0) == 0)
     def _():
         x, y, c = spot_ref[0], spot_ref[1], spot_ref[2]
-        rows = mine_ref.shape[2]
-        for one in range(4):
-            for two in range(4):
-                for half_index in range(2):
-                    a = mine_ref[half_index, one * 4 + two].astype(jnp.float32)
-                    b = got_ref[half_index, one * 4 + two].astype(jnp.float32)
-                    low = jnp.where(c == 0, a, b)
-                    high = jnp.where(c == 0, b, a)
-                    dx, dy = (two, one) if half_index == 0 else (one, two)
-                    at = ((x + 4 - dx) % 4) * 4 + (y + 4 - dy) % 4
-                    both = jnp.concatenate([low, high], axis=0).astype(jnp.bfloat16)
-                    weight_ref[
-                        pl.ds(pl.multiple_of(at * (2 * rows), 16), 2 * rows),
-                        half_index * half : (half_index + 1) * half,
-                    ] = both
+        rows = mine_ref.shape[1]
+        for dx in range(4):
+            for dy in range(4):
+                mine_low, mine_high = mine_ref[dy * 4 + dx], mine_ref[dx * 4 + dy]
+                got_low, got_high = got_ref[dy * 4 + dx], got_ref[dx * 4 + dy]
+                low = jnp.where(c == 0, mine_low.astype(jnp.float32), got_low.astype(jnp.float32))
+                high = jnp.where(c == 0, got_high.astype(jnp.float32), mine_high.astype(jnp.float32))
+                at = ((x + 4 - dx) % 4) * 4 + (y + 4 - dy) % 4
+                both = jnp.concatenate([low, high], axis=0).astype(jnp.bfloat16)
+                weight_ref[pl.ds(pl.multiple_of(at * (2 * rows), 16), 2 * rows), :] = both
 
     memory = memory_ref[...]
     key_proj = jnp.dot(memory, weight_ref[:, :half], preferred_element_type=jnp.float32)
@@ -163,8 +148,8 @@
             num_scalar_prefetch=1,
             grid=(4,),
             in_specs=[
-                pl.BlockSpec(mine.shape, lambda i, s: (0, 0, 0, 0), pipeline_mode=pl.Buffered(1)),
-                pl.BlockSpec(got.shape, lambda i, s: (0, 0, 0, 0), pipeline_mode=pl.Buffered(1)),
+                pl.BlockSpec(mine.shape, lambda i, s: (0, 0, 0), pipeline_mode=pl.Buffered(1)),
+                pl.BlockSpec(got.shape, lambda i, s: (0, 0, 0), pipeline_mode=pl.Buffered(1)),
                 pl.BlockSpec((tile, mem), lambda i, s: (i, 0)),
                 pl.BlockSpec((tile, half), lambda i, s: (i, 0)),
                 pl.BlockSpec((tile, half), lambda i, s: (i, 0)),
@@ -420,7 +405,6 @@
     owners = dp_count * tensor_count
     rows_dev, row_width = embed_table.shape
     block_rows = memory.shape[0] // tensor_count
-    mine, row_ids = gather_weights(key_weight, value_weight, row_ids)
     my_ids = lax.dynamic_slice_in_dim(
         row_ids, lax.axis_index("tensor") * block_rows, block_rows, 0
     )
@@ -428,8 +412,8 @@
     z = lax.axis_index("tensor")
     x, y, c = at // 8, (at // 2) % 4, at % 2
     slot, numbers = route(my_ids, owners, rows_dev, row_width)
-    mine, numbers, slot = lax.optimization_barrier((mine, numbers, slot))
-    mine = mine.reshape(2, 16, *key_weight.shape)
+    mine, slot, numbers = gather_weights(key_weight, value_weight, (slot, numbers))
+    mine = mine.reshape(16, *mine.shape[2:])
     got = lax.ppermute(mine, "dp", other_core())
     spot = jnp.stack([x, y, c]).astype(jnp.int32)
     weights, key_proj, sums = project(spot, mine, got, memory, hidden, grad_out)
@@ -467,9 +451,9 @@
         row_width,
     )
     send_rows, other = lax.optimization_barrier((send_rows, other))
-    key_part, value_part = sum_one_axis(sum_on_chip(other, kept), x, y)
-    key_pieces = ring_pieces(key_part, y, along_y)
-    value_pieces = ring_pieces(value_part, x, along_x)
+    chip_grads = sum_on_chip(other, kept, c)
+    line_grads = ring_sum(chip_grads, jnp.where(c == 0, x, y), along_first).astype(jnp.bfloat16)
+    pieces = ring_pieces(line_grads, jnp.where(c == 0, y, x), along_second)
     got_rows = lax.all_to_all(
         send_rows.reshape(owners, SLOTS, row_width),
         ("dp", "tensor"),
@@ -480,11 +464,11 @@
     new_table, new_first, new_second = adam_rows(
         got_rows, embed_table, first_moment, second_moment
     )
-    key_pieces, value_pieces, new_second = lax.optimization_barrier(
-        (key_pieces, value_pieces, new_second)
-    )
-    key_weight_grad = sum(p.astype(jnp.float32) for p in key_pieces)
-    value_weight_grad = sum(p.astype(jnp.float32) for p in value_pieces)
+    pieces, new_second = lax.optimization_barrier((pieces, new_second))
+    weight_sums = sum(p.astype(jnp.float32) for p in pieces)
+    half = weight_sums.shape[1] // 2
+    key_weight_grad = weight_sums[:, :half]
+    value_weight_grad = weight_sums[:, half:]
     return (key_weight_grad, value_weight_grad, new_table, new_first, new_second)
 
 

time: 193 us -> 181 us (0.938)
  starting transfers between devices: 65.4 us -> 45.1 us
  waiting for transfers between devices: 44 us -> 56.7 us
  other arithmetic: 14.8 us -> 10.6 us
    ppermute x12 -> x6, starting transfers between devices: 19.7 us -> 9.46 us  [ring_pieces(): lax.ppermute(lax.dynamic_index_in_dim(tiles, (here + d) % 4, 0, keepdims=...]
    ppermute x12 -> x6, waiting for transfers between devices: 27.8 us -> 36.4 us  [ring_pieces(): lax.ppermute(lax.dynamic_index_in_dim(tiles, (here + d) % 4, 0, keepdims=...]
    ppermute x12 -> x6, starting transfers between devices: 17.6 us -> 10.1 us  [ring_gather(): return [shard] + [lax.ppermute(shard, 'dp', perm_of(d)) for d in STEPS]]
    ppermute x12 -> x6, waiting for transfers between devices: 4.71 us -> 8.88 us  [ring_gather(): return [shard] + [lax.ppermute(shard, 'dp', perm_of(d)) for d in STEPS]]
    ppermute x1, starting transfers between devices: 4.67 us -> 2.53 us  [body(): got = lax.ppermute(mine, 'dp', other_core())]
    add x2 -> x1, other arithmetic: 3 us -> 1.05 us  [body(): weight_sums = sum((p.astype(jnp.float32) for p in pieces))]
  transfers between devices with their start and end apart: 36 -> 24, of which waited for: 9 -> 8; matrix products, arithmetic and copies ran while one was open for 15% -> 13% of each run, Pallas kernels for 16% -> 18%
where the time goes in v7:
time: 181 us; the launch traced here: 180 us
  waiting for transfers between devices  56.7 us (31%)
  Pallas kernels  48.1 us (27%)
  starting transfers between devices  45.1 us (25%)
  matrix products  10.8 us (6%)
  other arithmetic  10.6 us (6%)
  local copies, waits for them, and re-layouts  7.67 us (4%)
    ppermute x6, waiting for transfers between devices, ring_pieces(): lax.ppermute(lax.dynamic_index_in_dim(tiles, (here + d) % 4, 0, keepdims=...  36.4 us
    pallas_call x2, Pallas kernels, grads(): pl.pallas_call(grads_kernel, out_shape=(pltpu.HBM(both_shape, jnp.bfloat1...  14.5 us
    pallas_call x1, Pallas kernels, project(): pl.pallas_call(project_kernel, out_shape=(jax.ShapeDtypeStruct((mem, 2 *...  12.2 us
    pallas_call x1, Pallas kernels, adam_rows(): pl.pallas_call(adam_kernel, out_shape=(jax.ShapeDtypeStruct((rows_dev, wi...  11 us
    pallas_call x1, Pallas kernels, pack_rows(): pl.pallas_call(pack_kernel, out_shape=pltpu.HBM((total_slots, width), jnp...  10.3 us
    ppermute x6, starting transfers between devices, ring_gather(): return [shard] + [lax.ppermute(shard, 'dp', perm_of(d)) for d in STEPS]  10.1 us
    ppermute x6, starting transfers between devices, ring_pieces(): lax.ppermute(lax.dynamic_index_in_dim(tiles, (here + d) % 4, 0, keepdims=...  9.46 us
    ppermute x6, waiting for transfers between devices, ring_gather(): return [shard] + [lax.ppermute(shard, 'dp', perm_of(d)) for d in STEPS]  8.88 us
  transfers between devices with their start and end apart: 24, of which 8 were waited for; matrix products, arithmetic and copies ran while one was open for 13% of the time, Pallas kernels for 18%

profile of v7, /device:TPU:1, one launch (start us, length us, event | category | flops | bytes accessed | tf_op | source)
XLA Modules:
  0.0 179.9 jit_solution(13156979635942982867)
XLA Ops:
  0.6 0.8 constant_dynamic-update-slice_fusion.1
  1.4 0.8 constant_dynamic-update-slice_fusion
  2.3 3.6 %collective-permute-start.2 = (bf16[40,1280]{1,0:T(8,128)(2,1)S(1)}, bf16[40,1280]{1,0:T(8,128)(2,1)S(1)}, u32[]{:S(2)}, u32[]{:S(2)}) collective-permute-start(bf16[40,1280]{1,0:T(8,128)(2,1)S(1)} %constant_dynamic-update-slice_fusion), channel_id=1, source_target_pairs={{0,96},{4,28},{8,104},{12,4},{16,112},{20,12},{24,120},{28,20},{32... | collective-permute-start | bytes 307208 | tf_op jit(solution)/shard_map/ppermute | solution.py:65
  5.8 1.6 collective-permute-start.1
  8.2 1.8 fusion.2
  10.0 1.5 select_convert_fusion.2
  11.5 1.2 fusion.3
  13.8 1.3 collective-permute-start.3
  15.0 2.5 %collective-permute-start.4 = (bf16[4,40,1280]{2,1,0:T(8,128)(2,1)S(1)}, bf16[4,40,1280]{2,1,0:T(8,128)(2,1)S(1)}, u32[]{:S(2)}, u32[]{:S(2)}) collective-permute-start(bf16[4,40,1280]{2,1,0:T(8,128)(2,1)S(1)} %pad_maximum_fusion.1), channel_id=1, source_target_pairs={{0,16},{4,68},{8,24},{12,76},{16,0},{20,84},{24,8},{28,92},{32,48}... | collective-permute-start | bytes 1228808 | tf_op jit(solution)/shard_map/ppermute | solution.py:65
  17.5 1.1 collective-permute-start.5
  18.6 3.5 %collective-permute-done.3 = bf16[4,40,1280]{2,1,0:T(8,128)(2,1)S(1)} collective-permute-done((bf16[4,40,1280]{2,1,0:T(8,128)(2,1)S(1)}, bf16[4,40,1280]{2,1,0:T(8,128)(2,1)S(1)}, u32[]{:S(2)}, u32[]{:S(2)}) %collective-permute-start.3) | collective-permute-done | bytes 409632 | tf_op jit(solution)/shard_map/ppermute | solution.py:65
  22.1 5.4 %collective-permute-done.4 = bf16[4,40,1280]{2,1,0:T(8,128)(2,1)S(1)} collective-permute-done((bf16[4,40,1280]{2,1,0:T(8,128)(2,1)S(1)}, bf16[4,40,1280]{2,1,0:T(8,128)(2,1)S(1)}, u32[]{:S(2)}, u32[]{:S(2)}) %collective-permute-start.4) | collective-permute-done | bytes 409632 | tf_op jit(solution)/shard_map/ppermute | solution.py:65
  27.7 2.5 %collective-permute-start.6 = (bf16[16,40,1280]{2,1,0:T(8,128)(2,1)S(1)}, bf16[16,40,1280]{2,1,0:T(8,128)(2,1)}, u32[]{:S(2)}, u32[]{:S(2)}) collective-permute-start(bf16[16,40,1280]{2,1,0:T(8,128)(2,1)S(1)} %bitcast.57), channel_id=1, source_target_pairs={{0,4},{4,0},{8,12},{12,8},{16,20},{20,16},{24,28},{28,24},{32,36},... | collective-permute-start | bytes 4915208 | tf_op jit(solution)/shard_map/ppermute | solution.py:417
  30.3 3.2 %collective-permute-done.6.got_ref = bf16[16,40,1280]{2,1,0:T(8,128)(2,1)} collective-permute-done((bf16[16,40,1280]{2,1,0:T(8,128)(2,1)S(1)}, bf16[16,40,1280]{2,1,0:T(8,128)(2,1)}, u32[]{:S(2)}, u32[]{:S(2)}) %collective-permute-start.6) | collective-permute-done | bytes 1638432 | tf_op jit(solution)/shard_map/ppermute | solution.py:417
  33.5 12.2 %project.1 = (bf16[1280,1280]{1,0:T(8,128)(2,1)S(1)}, f32[1536,640]{1,0:T(8,128)}, f32[8,1536]{1,0:T(8,128)S(1)}) custom-call(s32[3]{0:T(128)S(1)} %pad_add_fusion.3.spot_ref, bf16[16,40,1280]{2,1,0:T(8,128)(2,1)} %bitcast.58, bf16[16,40,1280]{2,1,0:T(8,128)(2,1)} %collective-permute-done.6.got_ref, bf16[1536,1280]{1,0:T(8,128)(2,1)} %memory_ref.1, ...), custom_call_target="tpu_custom_call" | custom-call | tf_op jit(solution)/shard_map/project/pallas_call | solution.py:140
  45.7 1.6 collective-permute-start.7
  47.4 3.3 %collective-permute-start.8 = (f32[8,1536]{1,0:T(8,128)S(1)}, f32[8,1536]{1,0:T(8,128)S(1)}, u32[]{:S(2)}, u32[]{:S(2)}) collective-permute-start(f32[8,1536]{1,0:T(8,128)S(1)} %get-tuple-element.40.refs_0_), channel_id=1, source_target_pairs={{0,2},{1,3},{2,0},{3,1},{4,6},{5,7},{6,4},{7,5},{8,10},{9,11},{10,... | collective-permute-start | bytes 147464 | tf_op jit(solution)/shard_map/ppermute | solution.py:420
  50.7 0.7 collective-permute-start.9
  51.4 1.5 collective-permute-done.8.refs_2_
  52.9 1.0 collective-permute-done.9.refs_3_
  53.9 4.2 %grads_far.1 = (bf16[384,1280]{1,0:T(8,128)(2,1)}, bf16[384,640]{1,0:T(8,128)(2,1)}, bf16[384,640]{1,0:T(8,128)(2,1)}) custom-call(s32[1]{0:T(128)} %bitcast.3.order_ref, f32[8,1536]{1,0:T(8,128)S(1)} %get-tuple-element.40.refs_0_, f32[8,1536]{1,0:T(8,128)S(1)} %collective-permute-done.7.refs_1_, f32[8,1536]{1,0:T(8,128)S(1)} %collective-permute-done.8.refs_2_, ...), custom_call_target="tpu_custom_call" | custom-call | tf_op jit(solution)/shard_map/grads_far/pallas_call | solution.py:224
  58.1 1.8 collective-permute-start.11
  59.9 10.4 %grads_near.1 = (bf16[1536,1280]{1,0:T(8,128)(2,1)}, bf16[384,640]{1,0:T(8,128)(2,1)S(1)}, bf16[384,640]{1,0:T(8,128)(2,1)S(1)}, bf16[384,640]{1,0:T(8,128)(2,1)...) custom-call(s32[4]{0:T(128)S(1)} %pad_add_fusion.2.order_ref, ...), custom_call_target="tpu_custom_call" | custom-call | tf_op jit(solution)/shard_map/grads_near/pallas_call | solution.py:224
  70.3 2.7 %collective-permute-start.13 = (bf16[384,640]{1,0:T(8,128)(2,1)S(1)}, bf16[384,640]{1,0:T(8,128)(2,1)S(1)}, u32[]{:S(2)}, u32[]{:S(2)}) collective-permute-start(bf16[384,640]{1,0:T(8,128)(2,1)S(1)} %get-tuple-element.50), channel_id=1, source_target_pairs={{0,3},{1,0},{2,1},{3,2},{4,7},{5,4},{6,5},{7,6},{8,11},{9,8},{10,9... | collective-permute-start | bytes 1474568 | tf_op jit(solution)/shard_map/ppermute | solution.py:430
  73.0 1.2 add_convert_fusion.1
  74.2 1.2 add_convert_fusion.2
  75.4 2.7 %collective-permute-start.15 = (bf16[384,640]{1,0:T(8,128)(2,1)S(1)}, bf16[384,640]{1,0:T(8,128)(2,1)S(1)}, u32[]{:S(2)}, u32[]{:S(2)}) collective-permute-start(bf16[384,640]{1,0:T(8,128)(2,1)S(1)} %add_convert_fusion.1), channel_id=1, source_target_pairs={{0,3},{1,0},{2,1},{3,2},{4,7},{5,4},{6,5},{7,6},{8,11},{9,8},{10,9... | collective-permute-start | bytes 1474568 | tf_op jit(solution)/shard_map/ppermute | solution.py:435
  78.1 7.8 %convolution_convert_fusion = bf16[1280,1280]{0,1:T(8,128)(2,1)S(1)} fusion(bf16[1536,1280]{1,0:T(8,128)(2,1)} %get-tuple-element.48, bf16[1536,1280]{1,0:T(8,128)(2,1)S(1)} %copy-done.2), kind=kOutput, calls=%fused_computation.2 | convolution fusion | flops 5034803200 | bytes 11141120 | tf_op jit(solution)/shard_map/dot_general | solution.py:436
  85.9 1.4 dynamic-slice_bitcast_fusion
  87.3 5.7 %collective-permute-done.14.l2 = bf16[384,640]{1,0:T(8,128)(2,1)S(1)} collective-permute-done((bf16[384,640]{1,0:T(8,128)(2,1)S(1)}, bf16[384,640]{1,0:T(8,128)(2,1)S(1)}, u32[]{:S(2)}, u32[]{:S(2)}) %collective-permute-start.14) | collective-permute-done | bytes 491552 | tf_op jit(solution)/shard_map/ppermute | solution.py:434
  93.0 3.0 %collective-permute-start.16 = (bf16[16,40,1280]{2,1,0:T(8,128)(2,1)S(1)}, bf16[16,40,1280]{2,1,0:T(8,128)(2,1)}, u32[]{:S(2)}, u32[]{:S(2)}) collective-permute-start(bf16[16,40,1280]{2,1,0:T(8,128)(2,1)S(1)} %get-tuple-element.62), channel_id=1, source_target_pairs={{0,4},{4,0},{8,12},{12,8},{16,20},{20,16},{24,28},{28,24},{32,36},... | collective-permute-start | bytes 4915208 | tf_op jit(solution)/shard_map/ppermute | solution.py:445
  96.1 10.3 %pack_rows.1 = bf16[6144,256]{1,0:T(8,128)(2,1)} custom-call(s32[1,2176]{1,0:T(1,128)S(1)} %and_select_fusion.1.tile_ref, s32[1,2176]{1,0:T(1,128)S(1)} %get-tuple-element.75.spot_ref, bf16[256,256]{1,0:T(8,128)(2,1)S(1)} %pad.4.numbers_ref, bf16[384,640]{1,0:T(8,128)(2,1)S(1)} %get-tuple-element.56.l1, bf16[384,640]{1,0:T(8,128)(2,1)S(1)} %collective-permute-done.14.l2, ...), custom_call_target="tpu_custom_call" | custom-call | tf_op jit(solution)/shard_map/pack_rows/pallas_call | solution.py:287
  106.4 7.2 %all-to-all-start = ((bf16[128,48,256]{2,1,0:T(8,128)(2,1)}), bf16[128,48,256]{2,1,0:T(8,128)(2,1)S(1)}, u32[]{:S(2)}, u32[]{:S(2)}) async-start(bf16[128,48,256]{2,1,0:T(8,128)(2,1)} %bitcast.55), calls=%async_computation | async-start | bytes 6291456 | tf_op jit(solution)/shard_map/all_to_all | solution.py:457
  113.6 2.3 %add_convert_fusion = bf16[16,40,1280]{2,1,0:T(8,128)(2,1)S(1)} fusion(bf16[16,40,1280]{2,1,0:T(8,128)(2,1)} %collective-permute-done.16, bf16[16,40,1280]{2,1,0:T(8,128)(2,1)} %get-tuple-element.53), kind=kLoop, calls=%fused_computation.3 | loop fusion | flops 3276800 | bytes 4915200 | tf_op jit(solution)/shard_map/convert_element_type | solution.py:90
  116.1 1.2 copy-done
  117.3 1.0 dynamic-slice_bitcast_fusion.4
  118.2 1.4 collective-permute-start.17
  119.6 2.4 %collective-permute-start.18 = (bf16[4,40,1280]{2,1,0:T(8,128)(2,1)}, bf16[4,40,1280]{2,1,0:T(8,128)(2,1)}, u32[]{:S(2)}, u32[]{:S(2)}) collective-permute-start(bf16[4,40,1280]{2,1,0:T(8,128)(2,1)} %get-tuple-element.81), channel_id=1, source_target_pairs={{0,64},{4,20},{8,72},{12,28},{16,80},{20,4},{24,88},{28,12},{32,96... | collective-permute-start | bytes 1228808 | tf_op jit(solution)/shard_map/ppermute | solution.py:71
  122.1 1.1 collective-permute-start.19
  123.2 31.7 %collective-permute-done.17 = bf16[4,40,1280]{2,1,0:T(8,128)(2,1)} collective-permute-done((bf16[4,40,1280]{2,1,0:T(8,128)(2,1)}, bf16[4,40,1280]{2,1,0:T(8,128)(2,1)}, u32[]{:S(2)}, u32[]{:S(2)}) %collective-permute-start.17) | collective-permute-done | bytes 409632 | tf_op jit(solution)/shard_map/ppermute | solution.py:71
  154.9 4.7 %collective-permute-done.18 = bf16[4,40,1280]{2,1,0:T(8,128)(2,1)} collective-permute-done((bf16[4,40,1280]{2,1,0:T(8,128)(2,1)}, bf16[4,40,1280]{2,1,0:T(8,128)(2,1)}, u32[]{:S(2)}, u32[]{:S(2)}) %collective-permute-start.18) | collective-permute-done | bytes 409632 | tf_op jit(solution)/shard_map/ppermute | solution.py:71
  159.6 1.6 fusion.12
  161.2 0.7 dynamic-slice_bitcast_fusion.5
  161.9 0.9 collective-permute-start.20
  162.8 2.4 %collective-permute-start.21 = (bf16[40,1280]{1,0:T(8,128)(2,1)}, bf16[40,1280]{1,0:T(8,128)(2,1)}, u32[]{:S(2)}, u32[]{:S(2)}) collective-permute-start(bf16[40,1280]{1,0:T(8,128)(2,1)} %get-tuple-element.83), channel_id=1, source_target_pairs={{0,16},{4,68},{8,24},{12,76},{16,0},{20,84},{24,8},{28,92},{32,48}... | collective-permute-start | bytes 307208 | tf_op jit(solution)/shard_map/ppermute | solution.py:71
  165.2 1.2 collective-permute-start.22
  167.1 11.0 %adam_rows.1 = (f32[2048,256]{1,0:T(8,128)}, f32[2048,256]{1,0:T(8,128)}, f32[2048,256]{1,0:T(8,128)}) custom-call(s32[1,6144]{1,0:T(1,128)S(1)} %reshape.236.tile_ref, s32[1,6144]{1,0:T(1,128)S(1)} %reshape.237.spot_ref, bf16[6144,256]{1,0:T(8,128)(2,1)S(1)} %bitcast.54, f32[2048,256]{1,0:T(8,128)} %table_ref.1, f32[2048,256]{1,0:T(8,128)} %first_ref.1, ...), custom_call_target="tpu_custom_call" | custom-call | tf_op jit(solution)/shard_map/adam_rows/pallas_call | solution.py:338
  178.2 1.0 convert_add_fusion.1
  (52 shorter events, 3.7 us)
Async XLA Ops:
  2.3 11.4 %collective-permute-start.2 = (bf16[40,1280]{1,0:T(8,128)(2,1)S(1)}, bf16[40,1280]{1,0:T(8,128)(2,1)S(1)}, u32[]{:S(2)}, u32[]{:S(2)}) collective-permute-start(bf16[40,1280]{1,0:T(8,128)(2,1)S(1)} %constant_dynamic-update-slice_fusion), channel_id=1, source_target_pairs={{0,96},{4,28},{8,104},{12,4},{16,112},{20,12},{24,120},{28,20},{32... | collective-permute-start | bytes 307208 | tf_op jit(solution)/shard_map/ppermute | solution.py:65
  5.8 7.9 %collective-permute-start = (bf16[40,1280]{1,0:T(8,128)(2,1)S(1)}, bf16[40,1280]{1,0:T(8,128)(2,1)S(1)}, u32[]{:S(2)}, u32[]{:S(2)}) collective-permute-start(bf16[40,1280]{1,0:T(8,128)(2,1)S(1)} %constant_dynamic-update-slice_fusion), channel_id=1, source_target_pairs={{0,32},{4,12},{8,40},{12,20},{16,48},{20,28},{24,56},{28,4},{32,64... | collective-permute-start | bytes 307208 | tf_op jit(solution)/shard_map/ppermute | solution.py:65
  5.8 7.9 %collective-permute-start.1 = (bf16[40,1280]{1,0:T(8,128)(2,1)S(1)}, bf16[40,1280]{1,0:T(8,128)(2,1)S(1)}, u32[]{:S(2)}, u32[]{:S(2)}) collective-permute-start(bf16[40,1280]{1,0:T(8,128)(2,1)S(1)} %constant_dynamic-update-slice_fusion), channel_id=1, source_target_pairs={{0,64},{4,20},{8,72},{12,28},{16,80},{20,4},{24,88},{28,12},{32,96... | collective-permute-start | bytes 307208 | tf_op jit(solution)/shard_map/ppermute | solution.py:65
  13.8 8.4 %collective-permute-start.3 = (bf16[4,40,1280]{2,1,0:T(8,128)(2,1)S(1)}, bf16[4,40,1280]{2,1,0:T(8,128)(2,1)S(1)}, u32[]{:S(2)}, u32[]{:S(2)}) collective-permute-start(bf16[4,40,1280]{2,1,0:T(8,128)(2,1)S(1)} %pad_maximum_fusion.1), channel_id=1, source_target_pairs={{0,8},{4,36},{8,16},{12,44},{16,24},{20,52},{24,0},{28,60},{32,40}... | collective-permute-start | bytes 1228808 | tf_op jit(solution)/shard_map/ppermute | solution.py:65
  15.0 12.5 %collective-permute-start.4 = (bf16[4,40,1280]{2,1,0:T(8,128)(2,1)S(1)}, bf16[4,40,1280]{2,1,0:T(8,128)(2,1)S(1)}, u32[]{:S(2)}, u32[]{:S(2)}) collective-permute-start(bf16[4,40,1280]{2,1,0:T(8,128)(2,1)S(1)} %pad_maximum_fusion.1), channel_id=1, source_target_pairs={{0,16},{4,68},{8,24},{12,76},{16,0},{20,84},{24,8},{28,92},{32,48}... | collective-permute-start | bytes 1228808 | tf_op jit(solution)/shard_map/ppermute | solution.py:65
  17.5 10.0 %collective-permute-start.5 = (bf16[4,40,1280]{2,1,0:T(8,128)(2,1)S(1)}, bf16[4,40,1280]{2,1,0:T(8,128)(2,1)S(1)}, u32[]{:S(2)}, u32[]{:S(2)}) collective-permute-start(bf16[4,40,1280]{2,1,0:T(8,128)(2,1)S(1)} %pad_maximum_fusion.1), channel_id=1, source_target_pairs={{0,24},{4,100},{8,0},{12,108},{16,8},{20,116},{24,16},{28,124},{32... | collective-permute-start | bytes 1228808 | tf_op jit(solution)/shard_map/ppermute | solution.py:65
  27.7 2.6 %copy-start.1 = (bf16[4,4,40,1280]{3,2,1,0:T(8,128)(2,1)}, bf16[4,4,40,1280]{3,2,1,0:T(8,128)(2,1)S(1)}, u32[]{:S(2)}) copy-start(bf16[4,4,40,1280]{3,2,1,0:T(8,128)(2,1)S(1)} %pad_maximum_fusion) | copy-start | bytes 4915204
  27.7 5.8 %collective-permute-start.6 = (bf16[16,40,1280]{2,1,0:T(8,128)(2,1)S(1)}, bf16[16,40,1280]{2,1,0:T(8,128)(2,1)}, u32[]{:S(2)}, u32[]{:S(2)}) collective-permute-start(bf16[16,40,1280]{2,1,0:T(8,128)(2,1)S(1)} %bitcast.57), channel_id=1, source_target_pairs={{0,4},{4,0},{8,12},{12,8},{16,20},{20,16},{24,28},{28,24},{32,36},... | collective-permute-start | bytes 4915208 | tf_op jit(solution)/shard_map/ppermute | solution.py:417
  45.7 5.7 %collective-permute-start.7 = (f32[8,1536]{1,0:T(8,128)S(1)}, f32[8,1536]{1,0:T(8,128)S(1)}, u32[]{:S(2)}, u32[]{:S(2)}) collective-permute-start(f32[8,1536]{1,0:T(8,128)S(1)} %get-tuple-element.40.refs_0_), channel_id=1, source_target_pairs={{0,1},{1,2},{2,3},{3,0},{4,5},{5,6},{6,7},{7,4},{8,9},{9,10},{10,1... | collective-permute-start | bytes 147464 | tf_op jit(solution)/shard_map/ppermute | solution.py:420
  47.4 5.5 %collective-permute-start.8 = (f32[8,1536]{1,0:T(8,128)S(1)}, f32[8,1536]{1,0:T(8,128)S(1)}, u32[]{:S(2)}, u32[]{:S(2)}) collective-permute-start(f32[8,1536]{1,0:T(8,128)S(1)} %get-tuple-element.40.refs_0_), channel_id=1, source_target_pairs={{0,2},{1,3},{2,0},{3,1},{4,6},{5,7},{6,4},{7,5},{8,10},{9,11},{10,... | collective-permute-start | bytes 147464 | tf_op jit(solution)/shard_map/ppermute | solution.py:420
  50.7 3.2 %collective-permute-start.9 = (f32[8,1536]{1,0:T(8,128)S(1)}, f32[8,1536]{1,0:T(8,128)}, u32[]{:S(2)}, u32[]{:S(2)}) collective-permute-start(f32[8,1536]{1,0:T(8,128)S(1)} %get-tuple-element.40.refs_0_), channel_id=1, source_target_pairs={{0,3},{1,0},{2,1},{3,2},{4,7},{5,4},{6,5},{7,6},{8,11},{9,8},{10,9... | collective-permute-start | bytes 147464 | tf_op jit(solution)/shard_map/ppermute | solution.py:420
  58.1 14.9 %collective-permute-start.11 = (bf16[384,640]{1,0:T(8,128)(2,1)}, bf16[384,640]{1,0:T(8,128)(2,1)}, u32[]{:S(2)}, u32[]{:S(2)}) collective-permute-start(bf16[384,640]{1,0:T(8,128)(2,1)} %get-tuple-element.46), channel_id=1, source_target_pairs={{0,3},{1,0},{2,1},{3,2},{4,7},{5,4},{6,5},{7,6},{8,11},{9,8},{10,9... | collective-permute-start | bytes 1474568 | tf_op jit(solution)/shard_map/ppermute | solution.py:425
  59.8 14.3 %collective-permute-start.10 = (bf16[384,640]{1,0:T(8,128)(2,1)}, bf16[384,640]{1,0:T(8,128)(2,1)}, u32[]{:S(2)}, u32[]{:S(2)}) collective-permute-start(bf16[384,640]{1,0:T(8,128)(2,1)} %get-tuple-element.44), channel_id=1, source_target_pairs={{0,1},{1,2},{2,3},{3,0},{4,5},{5,6},{6,7},{7,4},{8,9},{9,10},{10,1... | collective-permute-start | bytes 1474568 | tf_op jit(solution)/shard_map/ppermute | solution.py:424
  59.9 18.1 %copy-start.2 = (bf16[1536,1280]{1,0:T(8,128)(2,1)S(1)}, bf16[1536,1280]{1,0:T(8,128)(2,1)}, u32[]{:S(2)}) copy-start(bf16[1536,1280]{1,0:T(8,128)(2,1)} %memory_ref.1) | copy-start | bytes 11796484
  70.3 17.0 %collective-permute-start.12 = (bf16[384,640]{1,0:T(8,128)(2,1)S(1)}, bf16[384,640]{1,0:T(8,128)(2,1)S(1)}, u32[]{:S(2)}, u32[]{:S(2)}) collective-permute-start(bf16[384,640]{1,0:T(8,128)(2,1)S(1)} %get-tuple-element.49), channel_id=1, source_target_pairs={{0,1},{1,2},{2,3},{3,0},{4,5},{5,6},{6,7},{7,4},{8,9},{9,10},{10,1... | collective-permute-start | bytes 1474568 | tf_op jit(solution)/shard_map/ppermute | solution.py:429
  70.3 17.0 %collective-permute-start.13 = (bf16[384,640]{1,0:T(8,128)(2,1)S(1)}, bf16[384,640]{1,0:T(8,128)(2,1)S(1)}, u32[]{:S(2)}, u32[]{:S(2)}) collective-permute-start(bf16[384,640]{1,0:T(8,128)(2,1)S(1)} %get-tuple-element.50), channel_id=1, source_target_pairs={{0,3},{1,0},{2,1},{3,2},{4,7},{5,4},{6,5},{7,6},{8,11},{9,8},{10,9... | collective-permute-start | bytes 1474568 | tf_op jit(solution)/shard_map/ppermute | solution.py:430
  75.3 17.6 %collective-permute-start.14 = (bf16[384,640]{1,0:T(8,128)(2,1)S(1)}, bf16[384,640]{1,0:T(8,128)(2,1)S(1)}, u32[]{:S(2)}, u32[]{:S(2)}) collective-permute-start(bf16[384,640]{1,0:T(8,128)(2,1)S(1)} %add_convert_fusion.2), channel_id=1, source_target_pairs={{0,1},{1,2},{2,3},{3,0},{4,5},{5,6},{6,7},{7,4},{8,9},{9,10},{10,1... | collective-permute-start | bytes 1474568 | tf_op jit(solution)/shard_map/ppermute | solution.py:434
  75.4 17.6 %collective-permute-start.15 = (bf16[384,640]{1,0:T(8,128)(2,1)S(1)}, bf16[384,640]{1,0:T(8,128)(2,1)S(1)}, u32[]{:S(2)}, u32[]{:S(2)}) collective-permute-start(bf16[384,640]{1,0:T(8,128)(2,1)S(1)} %add_convert_fusion.1), channel_id=1, source_target_pairs={{0,3},{1,0},{2,1},{3,2},{4,7},{5,4},{6,5},{7,6},{8,11},{9,8},{10,9... | collective-permute-start | bytes 1474568 | tf_op jit(solution)/shard_map/ppermute | solution.py:435
  85.9 10.1 %copy-start.3 = (s32[1,2176]{1,0:T(1,128)S(1)}, s32[1,2176]{1,0:T(1,128)}, u32[]{:S(2)}) copy-start(s32[1,2176]{1,0:T(1,128)} %pad_add_fusion) | copy-start | bytes 26116
  93.0 13.4 %collective-permute-start.16 = (bf16[16,40,1280]{2,1,0:T(8,128)(2,1)S(1)}, bf16[16,40,1280]{2,1,0:T(8,128)(2,1)}, u32[]{:S(2)}, u32[]{:S(2)}) collective-permute-start(bf16[16,40,1280]{2,1,0:T(8,128)(2,1)S(1)} %get-tuple-element.62), channel_id=1, source_target_pairs={{0,4},{4,0},{8,12},{12,8},{16,20},{20,16},{24,28},{28,24},{32,36},... | collective-permute-start | bytes 4915208 | tf_op jit(solution)/shard_map/ppermute | solution.py:445
  106.4 60.0 %all-to-all-start = ((bf16[128,48,256]{2,1,0:T(8,128)(2,1)}), bf16[128,48,256]{2,1,0:T(8,128)(2,1)S(1)}, u32[]{:S(2)}, u32[]{:S(2)}) async-start(bf16[128,48,256]{2,1,0:T(8,128)(2,1)} %bitcast.55), calls=%async_computation | async-start | bytes 6291456 | tf_op jit(solution)/shard_map/all_to_all | solution.py:457
  116.1 1.2 copy-start
  118.2 36.7 %collective-permute-start.17 = (bf16[4,40,1280]{2,1,0:T(8,128)(2,1)}, bf16[4,40,1280]{2,1,0:T(8,128)(2,1)}, u32[]{:S(2)}, u32[]{:S(2)}) collective-permute-start(bf16[4,40,1280]{2,1,0:T(8,128)(2,1)} %get-tuple-element.79), channel_id=1, source_target_pairs={{0,32},{4,12},{8,40},{12,20},{16,48},{20,28},{24,56},{28,4},{32,64... | collective-permute-start | bytes 1228808 | tf_op jit(solution)/shard_map/ppermute | solution.py:71
  119.6 40.0 %collective-permute-start.18 = (bf16[4,40,1280]{2,1,0:T(8,128)(2,1)}, bf16[4,40,1280]{2,1,0:T(8,128)(2,1)}, u32[]{:S(2)}, u32[]{:S(2)}) collective-permute-start(bf16[4,40,1280]{2,1,0:T(8,128)(2,1)} %get-tuple-element.81), channel_id=1, source_target_pairs={{0,64},{4,20},{8,72},{12,28},{16,80},{20,4},{24,88},{28,12},{32,96... | collective-permute-start | bytes 1228808 | tf_op jit(solution)/shard_map/ppermute | solution.py:71
  122.1 37.6 %collective-permute-start.19 = (bf16[4,40,1280]{2,1,0:T(8,128)(2,1)S(1)}, bf16[4,40,1280]{2,1,0:T(8,128)(2,1)}, u32[]{:S(2)}, u32[]{:S(2)}) collective-permute-start(bf16[4,40,1280]{2,1,0:T(8,128)(2,1)S(1)} %get-tuple-element.80), channel_id=1, source_target_pairs={{0,96},{4,28},{8,104},{12,4},{16,112},{20,12},{24,120},{28,20},{32... | collective-permute-start | bytes 1228808 | tf_op jit(solution)/shard_map/ppermute | solution.py:71
  161.9 16.2 %collective-permute-start.20 = (bf16[40,1280]{1,0:T(8,128)(2,1)}, bf16[40,1280]{1,0:T(8,128)(2,1)}, u32[]{:S(2)}, u32[]{:S(2)}) collective-permute-start(bf16[40,1280]{1,0:T(8,128)(2,1)} %get-tuple-element.84), channel_id=1, source_target_pairs={{0,8},{4,36},{8,16},{12,44},{16,24},{20,52},{24,0},{28,60},{32,40}... | collective-permute-start | bytes 307208 | tf_op jit(solution)/shard_map/ppermute | solution.py:71
  162.8 15.3 %collective-permute-start.21 = (bf16[40,1280]{1,0:T(8,128)(2,1)}, bf16[40,1280]{1,0:T(8,128)(2,1)}, u32[]{:S(2)}, u32[]{:S(2)}) collective-permute-start(bf16[40,1280]{1,0:T(8,128)(2,1)} %get-tuple-element.83), channel_id=1, source_target_pairs={{0,16},{4,68},{8,24},{12,76},{16,0},{20,84},{24,8},{28,92},{32,48}... | collective-permute-start | bytes 307208 | tf_op jit(solution)/shard_map/ppermute | solution.py:71
  165.2 12.9 %collective-permute-start.22 = (bf16[40,1280]{1,0:T(8,128)(2,1)S(1)}, bf16[40,1280]{1,0:T(8,128)(2,1)}, u32[]{:S(2)}, u32[]{:S(2)}) collective-permute-start(bf16[40,1280]{1,0:T(8,128)(2,1)S(1)} %get-tuple-element.82), channel_id=1, source_target_pairs={{0,24},{4,100},{8,0},{12,108},{16,8},{20,116},{24,16},{28,124},{32... | collective-permute-start | bytes 307208 | tf_op jit(solution)/shard_map/ppermute | solution.py:71

commit v8 on v7

--- a/solution.py
+++ b/solution.py
@@ -54,7 +54,8 @@
     return [(z, (z + d) % 4) for z in range(4)]
 
 
-STEPS = (1, 2, 3)
+STEPS = (2, 1, 3)
+POSITION = (0, 2, 1, 3)
 
 
 def in_hbm(*arrays):
@@ -104,19 +105,23 @@
 ):
     half = hidden_ref.shape[1]
 
-    @pl.when(pl.program_id(0) == 0)
-    def _():
-        x, y, c = spot_ref[0], spot_ref[1], spot_ref[2]
+    def place(core):
+        x, y = spot_ref[0], spot_ref[1]
         rows = mine_ref.shape[1]
+        low_ref, high_ref = (got_ref, mine_ref) if core else (mine_ref, got_ref)
         for dx in range(4):
             for dy in range(4):
-                mine_low, mine_high = mine_ref[dy * 4 + dx], mine_ref[dx * 4 + dy]
-                got_low, got_high = got_ref[dy * 4 + dx], got_ref[dx * 4 + dy]
-                low = jnp.where(c == 0, mine_low.astype(jnp.float32), got_low.astype(jnp.float32))
-                high = jnp.where(c == 0, got_high.astype(jnp.float32), mine_high.astype(jnp.float32))
+                low = low_ref[POSITION[dy] * 4 + POSITION[dx]].astype(jnp.float32)
+                high = high_ref[POSITION[dx] * 4 + POSITION[dy]].astype(jnp.float32)
                 at = ((x + 4 - dx) % 4) * 4 + (y + 4 - dy) % 4
                 both = jnp.concatenate([low, high], axis=0).astype(jnp.bfloat16)
                 weight_ref[pl.ds(pl.multiple_of(at * (2 * rows), 16), 2 * rows), :] = both
+
+    for core in range(2):
+
+        @pl.when((pl.program_id(0) == 0) & (spot_ref[2] == core))
+        def _():
+            place(core)
 
     memory = memory_ref[...]
     key_proj = jnp.dot(memory, weight_ref[:, :half], preferred_element_type=jnp.float32)
@@ -280,7 +285,7 @@
 
 
 def pack_rows(slot, numbers, parts, total_slots, width):
-    per_step = 3 * TILE
+    per_step = 6 * TILE
     tokens, half = parts[0].shape
     fixed = lambda i: (0, 0)
     one = pl.Buffered(1)

time: 181 us -> 180 us (level)
  starting transfers between devices: 45.1 us -> 48.4 us
  waiting for transfers between devices: 56.7 us -> 53.6 us
  transfers between devices with their start and end apart: 24 -> 24, of which waited for: 8 -> 8; matrix products, arithmetic and copies ran while one was open for 13% -> 14% of each run, Pallas kernels for 18% -> 17%
where the time goes in v8:
time: 180 us; the launch traced here: 179 us
  waiting for transfers between devices  53.6 us (30%)
  starting transfers between devices  48.4 us (27%)
  Pallas kernels  47 us (26%)
  matrix products  10.8 us (6%)
  other arithmetic  10.6 us (6%)
  local copies, waits for them, and re-layouts  7.67 us (4%)
    ppermute x6, waiting for transfers between devices, ring_pieces(): lax.ppermute(lax.dynamic_index_in_dim(tiles, (here + d) % 4, 0, keepdims=...  35.5 us
    pallas_call x2, Pallas kernels, grads(): pl.pallas_call(grads_kernel, out_shape=(pltpu.HBM(both_shape, jnp.bfloat1...  14.5 us
    pallas_call x1, Pallas kernels, project(): pl.pallas_call(project_kernel, out_shape=(jax.ShapeDtypeStruct((mem, 2 *...  11.7 us
    pallas_call x1, Pallas kernels, adam_rows(): pl.pallas_call(adam_kernel, out_shape=(jax.ShapeDtypeStruct((rows_dev, wi...  11 us
    ppermute x6, starting transfers between devices, ring_pieces(): lax.ppermute(lax.dynamic_index_in_dim(tiles, (here + d) % 4, 0, keepdims=...  10.7 us
    ppermute x6, starting transfers between devices, ring_gather(): return [shard] + [lax.ppermute(shard, 'dp', perm_of(d)) for d in STEPS]  10.1 us
    pallas_call x1, Pallas kernels, pack_rows(): pl.pallas_call(pack_kernel, out_shape=pltpu.HBM((total_slots, width), jnp...  9.73 us
    dot_general x1, matrix products, body(): lax.dot_general(memory, both, (((0,), (0,)), ((), ())), preferred_element...  7.79 us
  transfers between devices with their start and end apart: 24, of which 8 were waited for; matrix products, arithmetic and copies ran while one was open for 14% of the time, Pallas kernels for 17%

profile of v8, /device:TPU:1, one launch (start us, length us, event | category | flops | bytes accessed | tf_op | source)
XLA Modules:
  0.0 179.0 jit_solution(5779823170167360345)
XLA Ops:
  0.6 0.8 constant_dynamic-update-slice_fusion.1
  1.4 0.8 constant_dynamic-update-slice_fusion
  2.3 3.6 %collective-permute-start.2 = (bf16[40,1280]{1,0:T(8,128)(2,1)S(1)}, bf16[40,1280]{1,0:T(8,128)(2,1)S(1)}, u32[]{:S(2)}, u32[]{:S(2)}) collective-permute-start(bf16[40,1280]{1,0:T(8,128)(2,1)S(1)} %constant_dynamic-update-slice_fusion), channel_id=1, source_target_pairs={{0,96},{4,28},{8,104},{12,4},{16,112},{20,12},{24,120},{28,20},{32... | collective-permute-start | bytes 307208 | tf_op jit(solution)/shard_map/ppermute | solution.py:66
  6.2 0.7 collective-permute-start.1
  6.9 0.7 dynamic-slice_bitcast_fusion.9
  7.6 1.8 fusion.2
  9.4 1.5 select_convert_fusion.2
  10.9 1.2 fusion.3
  12.3 0.6 pad_add_fusion
  13.1 2.8 %collective-permute-start.3 = (bf16[4,40,1280]{2,1,0:T(8,128)(2,1)S(1)}, bf16[4,40,1280]{2,1,0:T(8,128)(2,1)S(1)}, u32[]{:S(2)}, u32[]{:S(2)}) collective-permute-start(bf16[4,40,1280]{2,1,0:T(8,128)(2,1)S(1)} %pad_maximum_fusion.1), channel_id=1, source_target_pairs={{0,16},{4,68},{8,24},{12,76},{16,0},{20,84},{24,8},{28,92},{32,48}... | collective-permute-start | bytes 1228808 | tf_op jit(solution)/shard_map/ppermute | solution.py:66
  16.3 2.4 %collective-permute-start.5 = (bf16[4,40,1280]{2,1,0:T(8,128)(2,1)S(1)}, bf16[4,40,1280]{2,1,0:T(8,128)(2,1)S(1)}, u32[]{:S(2)}, u32[]{:S(2)}) collective-permute-start(bf16[4,40,1280]{2,1,0:T(8,128)(2,1)S(1)} %pad_maximum_fusion.1), channel_id=1, source_target_pairs={{0,24},{4,100},{8,0},{12,108},{16,8},{20,116},{24,16},{28,124},{32... | collective-permute-start | bytes 1228808 | tf_op jit(solution)/shard_map/ppermute | solution.py:66
  18.6 3.2 %collective-permute-done.3 = bf16[4,40,1280]{2,1,0:T(8,128)(2,1)S(1)} collective-permute-done((bf16[4,40,1280]{2,1,0:T(8,128)(2,1)S(1)}, bf16[4,40,1280]{2,1,0:T(8,128)(2,1)S(1)}, u32[]{:S(2)}, u32[]{:S(2)}) %collective-permute-start.3) | collective-permute-done | bytes 409632 | tf_op jit(solution)/shard_map/ppermute | solution.py:66
  21.9 4.3 %collective-permute-done.4 = bf16[4,40,1280]{2,1,0:T(8,128)(2,1)S(1)} collective-permute-done((bf16[4,40,1280]{2,1,0:T(8,128)(2,1)S(1)}, bf16[4,40,1280]{2,1,0:T(8,128)(2,1)S(1)}, u32[]{:S(2)}, u32[]{:S(2)}) %collective-permute-start.4) | collective-permute-done | bytes 409632 | tf_op jit(solution)/shard_map/ppermute | solution.py:66
  26.6 2.5 %collective-permute-start.6 = (bf16[16,40,1280]{2,1,0:T(8,128)(2,1)S(1)}, bf16[16,40,1280]{2,1,0:T(8,128)(2,1)}, u32[]{:S(2)}, u32[]{:S(2)}) collective-permute-start(bf16[16,40,1280]{2,1,0:T(8,128)(2,1)S(1)} %bitcast.57), channel_id=1, source_target_pairs={{0,4},{4,0},{8,12},{12,8},{16,20},{20,16},{24,28},{28,24},{32,36},... | collective-permute-start | bytes 4915208 | tf_op jit(solution)/shard_map/ppermute | solution.py:422
  29.1 3.2 %collective-permute-done.6.got_ref = bf16[16,40,1280]{2,1,0:T(8,128)(2,1)} collective-permute-done((bf16[16,40,1280]{2,1,0:T(8,128)(2,1)S(1)}, bf16[16,40,1280]{2,1,0:T(8,128)(2,1)}, u32[]{:S(2)}, u32[]{:S(2)}) %collective-permute-start.6) | collective-permute-done | bytes 1638432 | tf_op jit(solution)/shard_map/ppermute | solution.py:422
  32.3 11.7 %project.1 = (bf16[1280,1280]{1,0:T(8,128)(2,1)S(1)}, f32[1536,640]{1,0:T(8,128)}, f32[8,1536]{1,0:T(8,128)S(1)}) custom-call(s32[3]{0:T(128)S(1)} %pad_add_fusion.3.spot_ref, bf16[16,40,1280]{2,1,0:T(8,128)(2,1)} %bitcast.58, bf16[16,40,1280]{2,1,0:T(8,128)(2,1)} %collective-permute-done.6.got_ref, bf16[1536,1280]{1,0:T(8,128)(2,1)} %memory_ref.1, ...), custom_call_target="tpu_custom_call" | custom-call | tf_op jit(solution)/shard_map/project/pallas_call | solution.py:145
  44.0 3.6 %collective-permute-start.7 = (f32[8,1536]{1,0:T(8,128)S(1)}, f32[8,1536]{1,0:T(8,128)S(1)}, u32[]{:S(2)}, u32[]{:S(2)}) collective-permute-start(f32[8,1536]{1,0:T(8,128)S(1)} %get-tuple-element.40.refs_0_), channel_id=1, source_target_pairs={{0,2},{1,3},{2,0},{3,1},{4,6},{5,7},{6,4},{7,5},{8,10},{9,11},{10,... | collective-permute-start | bytes 147464 | tf_op jit(solution)/shard_map/ppermute | solution.py:425
  47.6 0.7 collective-permute-start.8
  48.4 1.9 %collective-permute-start.9 = (f32[8,1536]{1,0:T(8,128)S(1)}, f32[8,1536]{1,0:T(8,128)}, u32[]{:S(2)}, u32[]{:S(2)}) collective-permute-start(f32[8,1536]{1,0:T(8,128)S(1)} %get-tuple-element.40.refs_0_), channel_id=1, source_target_pairs={{0,3},{1,0},{2,1},{3,2},{4,7},{5,4},{6,5},{7,6},{8,11},{9,8},{10,9... | collective-permute-start | bytes 147464 | tf_op jit(solution)/shard_map/ppermute | solution.py:425
  50.3 1.5 collective-permute-done.8.refs_2_
  51.8 4.2 %grads_far.1 = (bf16[384,1280]{1,0:T(8,128)(2,1)}, bf16[384,640]{1,0:T(8,128)(2,1)}, bf16[384,640]{1,0:T(8,128)(2,1)}) custom-call(s32[1]{0:T(128)} %bitcast.3.order_ref, f32[8,1536]{1,0:T(8,128)S(1)} %get-tuple-element.40.refs_0_, f32[8,1536]{1,0:T(8,128)S(1)} %collective-permute-done.7.refs_1_, f32[8,1536]{1,0:T(8,128)S(1)} %collective-permute-done.8.refs_2_, ...), custom_call_target="tpu_custom_call" | custom-call | tf_op jit(solution)/shard_map/grads_far/pallas_call | solution.py:229
  56.0 2.8 %collective-permute-start.11 = (bf16[384,640]{1,0:T(8,128)(2,1)}, bf16[384,640]{1,0:T(8,128)(2,1)}, u32[]{:S(2)}, u32[]{:S(2)}) collective-permute-start(bf16[384,640]{1,0:T(8,128)(2,1)} %get-tuple-element.46), channel_id=1, source_target_pairs={{0,3},{1,0},{2,1},{3,2},{4,7},{5,4},{6,5},{7,6},{8,11},{9,8},{10,9... | collective-permute-start | bytes 1474568 | tf_op jit(solution)/shard_map/ppermute | solution.py:430
  58.8 10.4 %grads_near.1 = (bf16[1536,1280]{1,0:T(8,128)(2,1)}, bf16[384,640]{1,0:T(8,128)(2,1)S(1)}, bf16[384,640]{1,0:T(8,128)(2,1)S(1)}, bf16[384,640]{1,0:T(8,128)(2,1)...) custom-call(s32[4]{0:T(128)S(1)} %pad_add_fusion.2.order_ref, ...), custom_call_target="tpu_custom_call" | custom-call | tf_op jit(solution)/shard_map/grads_near/pallas_call | solution.py:229
  69.2 2.7 %collective-permute-start.13 = (bf16[384,640]{1,0:T(8,128)(2,1)S(1)}, bf16[384,640]{1,0:T(8,128)(2,1)S(1)}, u32[]{:S(2)}, u32[]{:S(2)}) collective-permute-start(bf16[384,640]{1,0:T(8,128)(2,1)S(1)} %get-tuple-element.50), channel_id=1, source_target_pairs={{0,3},{1,0},{2,1},{3,2},{4,7},{5,4},{6,5},{7,6},{8,11},{9,8},{10,9... | collective-permute-start | bytes 1474568 | tf_op jit(solution)/shard_map/ppermute | solution.py:435
  71.9 1.2 add_convert_fusion.1
  73.1 1.2 add_convert_fusion.2
  74.3 2.7 %collective-permute-start.15 = (bf16[384,640]{1,0:T(8,128)(2,1)S(1)}, bf16[384,640]{1,0:T(8,128)(2,1)S(1)}, u32[]{:S(2)}, u32[]{:S(2)}) collective-permute-start(bf16[384,640]{1,0:T(8,128)(2,1)S(1)} %add_convert_fusion.1), channel_id=1, source_target_pairs={{0,3},{1,0},{2,1},{3,2},{4,7},{5,4},{6,5},{7,6},{8,11},{9,8},{10,9... | collective-permute-start | bytes 1474568 | tf_op jit(solution)/shard_map/ppermute | solution.py:440
  77.0 7.8 %convolution_convert_fusion = bf16[1280,1280]{0,1:T(8,128)(2,1)S(1)} fusion(bf16[1536,1280]{1,0:T(8,128)(2,1)} %get-tuple-element.48, bf16[1536,1280]{1,0:T(8,128)(2,1)S(1)} %copy-done.2), kind=kOutput, calls=%fused_computation.2 | convolution fusion | flops 5034803200 | bytes 11141120 | tf_op jit(solution)/shard_map/dot_general | solution.py:441
  84.8 1.4 dynamic-slice_bitcast_fusion
  86.2 5.7 %collective-permute-done.14.l2 = bf16[384,640]{1,0:T(8,128)(2,1)S(1)} collective-permute-done((bf16[384,640]{1,0:T(8,128)(2,1)S(1)}, bf16[384,640]{1,0:T(8,128)(2,1)S(1)}, u32[]{:S(2)}, u32[]{:S(2)}) %collective-permute-start.14) | collective-permute-done | bytes 491552 | tf_op jit(solution)/shard_map/ppermute | solution.py:439
  91.9 3.0 %collective-permute-start.16 = (bf16[16,40,1280]{2,1,0:T(8,128)(2,1)S(1)}, bf16[16,40,1280]{2,1,0:T(8,128)(2,1)}, u32[]{:S(2)}, u32[]{:S(2)}) collective-permute-start(bf16[16,40,1280]{2,1,0:T(8,128)(2,1)S(1)} %get-tuple-element.62), channel_id=1, source_target_pairs={{0,4},{4,0},{8,12},{12,8},{16,20},{20,16},{24,28},{28,24},{32,36},... | collective-permute-start | bytes 4915208 | tf_op jit(solution)/shard_map/ppermute | solution.py:450
  95.0 9.7 %pack_rows.1 = bf16[6144,256]{1,0:T(8,128)(2,1)} custom-call(s32[1,2176]{1,0:T(1,128)S(1)} %and_select_fusion.1.tile_ref, s32[1,2176]{1,0:T(1,128)S(1)} %get-tuple-element.75.spot_ref, bf16[256,256]{1,0:T(8,128)(2,1)S(1)} %pad.4.numbers_ref, bf16[384,640]{1,0:T(8,128)(2,1)S(1)} %get-tuple-element.56.l1, bf16[384,640]{1,0:T(8,128)(2,1)S(1)} %collective-permute-done.14.l2, ...), custom_call_target="tpu_custom_call" | custom-call | tf_op jit(solution)/shard_map/pack_rows/pallas_call | solution.py:292
  104.7 7.5 %all-to-all-start = ((bf16[128,48,256]{2,1,0:T(8,128)(2,1)}), bf16[128,48,256]{2,1,0:T(8,128)(2,1)S(1)}, u32[]{:S(2)}, u32[]{:S(2)}) async-start(bf16[128,48,256]{2,1,0:T(8,128)(2,1)} %bitcast.55), calls=%async_computation | async-start | bytes 6291456 | tf_op jit(solution)/shard_map/all_to_all | solution.py:462
  112.3 2.3 %add_convert_fusion = bf16[16,40,1280]{2,1,0:T(8,128)(2,1)S(1)} fusion(bf16[16,40,1280]{2,1,0:T(8,128)(2,1)} %collective-permute-done.16, bf16[16,40,1280]{2,1,0:T(8,128)(2,1)} %get-tuple-element.53), kind=kLoop, calls=%fused_computation.3 | loop fusion | flops 3276800 | bytes 4915200 | tf_op jit(solution)/shard_map/convert_element_type | solution.py:91
  114.8 1.2 copy-done
  116.0 1.0 dynamic-slice_bitcast_fusion.4
  116.9 2.9 %collective-permute-start.17 = (bf16[4,40,1280]{2,1,0:T(8,128)(2,1)}, bf16[4,40,1280]{2,1,0:T(8,128)(2,1)}, u32[]{:S(2)}, u32[]{:S(2)}) collective-permute-start(bf16[4,40,1280]{2,1,0:T(8,128)(2,1)} %get-tuple-element.79), channel_id=1, source_target_pairs={{0,64},{4,20},{8,72},{12,28},{16,80},{20,4},{24,88},{28,12},{32,96... | collective-permute-start | bytes 1228808 | tf_op jit(solution)/shard_map/ppermute | solution.py:72
  120.1 2.3 %collective-permute-start.19 = (bf16[4,40,1280]{2,1,0:T(8,128)(2,1)S(1)}, bf16[4,40,1280]{2,1,0:T(8,128)(2,1)}, u32[]{:S(2)}, u32[]{:S(2)}) collective-permute-start(bf16[4,40,1280]{2,1,0:T(8,128)(2,1)S(1)} %get-tuple-element.80), channel_id=1, source_target_pairs={{0,96},{4,28},{8,104},{12,4},{16,112},{20,12},{24,120},{28,20},{32... | collective-permute-start | bytes 1228808 | tf_op jit(solution)/shard_map/ppermute | solution.py:72
  122.5 31.4 %collective-permute-done.17 = bf16[4,40,1280]{2,1,0:T(8,128)(2,1)} collective-permute-done((bf16[4,40,1280]{2,1,0:T(8,128)(2,1)}, bf16[4,40,1280]{2,1,0:T(8,128)(2,1)}, u32[]{:S(2)}, u32[]{:S(2)}) %collective-permute-start.17) | collective-permute-done | bytes 409632 | tf_op jit(solution)/shard_map/ppermute | solution.py:72
  153.9 4.1 %collective-permute-done.18 = bf16[4,40,1280]{2,1,0:T(8,128)(2,1)} collective-permute-done((bf16[4,40,1280]{2,1,0:T(8,128)(2,1)}, bf16[4,40,1280]{2,1,0:T(8,128)(2,1)}, u32[]{:S(2)}, u32[]{:S(2)}) %collective-permute-start.18) | collective-permute-done | bytes 409632 | tf_op jit(solution)/shard_map/ppermute | solution.py:72
  158.0 1.6 fusion.12
  159.6 0.7 dynamic-slice_bitcast_fusion.5
  160.3 2.5 %collective-permute-start.20 = (bf16[40,1280]{1,0:T(8,128)(2,1)}, bf16[40,1280]{1,0:T(8,128)(2,1)}, u32[]{:S(2)}, u32[]{:S(2)}) collective-permute-start(bf16[40,1280]{1,0:T(8,128)(2,1)} %get-tuple-element.84), channel_id=1, source_target_pairs={{0,16},{4,68},{8,24},{12,76},{16,0},{20,84},{24,8},{28,92},{32,48}... | collective-permute-start | bytes 307208 | tf_op jit(solution)/shard_map/ppermute | solution.py:72
  162.8 0.5 collective-permute-start.21
  163.3 2.2 %collective-permute-start.22 = (bf16[40,1280]{1,0:T(8,128)(2,1)S(1)}, bf16[40,1280]{1,0:T(8,128)(2,1)}, u32[]{:S(2)}, u32[]{:S(2)}) collective-permute-start(bf16[40,1280]{1,0:T(8,128)(2,1)S(1)} %get-tuple-element.82), channel_id=1, source_target_pairs={{0,24},{4,100},{8,0},{12,108},{16,8},{20,116},{24,16},{28,124},{32... | collective-permute-start | bytes 307208 | tf_op jit(solution)/shard_map/ppermute | solution.py:72
  166.2 11.0 %adam_rows.1 = (f32[2048,256]{1,0:T(8,128)}, f32[2048,256]{1,0:T(8,128)}, f32[2048,256]{1,0:T(8,128)}) custom-call(s32[1,6144]{1,0:T(1,128)S(1)} %reshape.236.tile_ref, s32[1,6144]{1,0:T(1,128)S(1)} %reshape.237.spot_ref, bf16[6144,256]{1,0:T(8,128)(2,1)S(1)} %bitcast.54, f32[2048,256]{1,0:T(8,128)} %table_ref.1, f32[2048,256]{1,0:T(8,128)} %first_ref.1, ...), custom_call_target="tpu_custom_call" | custom-call | tf_op jit(solution)/shard_map/adam_rows/pallas_call | solution.py:343
  177.2 1.0 convert_add_fusion.1
  178.3 0.7 fusion.25
  (52 shorter events, 2.9 us)
Async XLA Ops:
  2.3 10.8 %collective-permute-start.2 = (bf16[40,1280]{1,0:T(8,128)(2,1)S(1)}, bf16[40,1280]{1,0:T(8,128)(2,1)S(1)}, u32[]{:S(2)}, u32[]{:S(2)}) collective-permute-start(bf16[40,1280]{1,0:T(8,128)(2,1)S(1)} %constant_dynamic-update-slice_fusion), channel_id=1, source_target_pairs={{0,96},{4,28},{8,104},{12,4},{16,112},{20,12},{24,120},{28,20},{32... | collective-permute-start | bytes 307208 | tf_op jit(solution)/shard_map/ppermute | solution.py:66
  5.8 7.2 %collective-permute-start = (bf16[40,1280]{1,0:T(8,128)(2,1)S(1)}, bf16[40,1280]{1,0:T(8,128)(2,1)S(1)}, u32[]{:S(2)}, u32[]{:S(2)}) collective-permute-start(bf16[40,1280]{1,0:T(8,128)(2,1)S(1)} %constant_dynamic-update-slice_fusion), channel_id=1, source_target_pairs={{0,64},{4,20},{8,72},{12,28},{16,80},{20,4},{24,88},{28,12},{32,96... | collective-permute-start | bytes 307208 | tf_op jit(solution)/shard_map/ppermute | solution.py:66
  6.2 6.9 %collective-permute-start.1 = (bf16[40,1280]{1,0:T(8,128)(2,1)S(1)}, bf16[40,1280]{1,0:T(8,128)(2,1)S(1)}, u32[]{:S(2)}, u32[]{:S(2)}) collective-permute-start(bf16[40,1280]{1,0:T(8,128)(2,1)S(1)} %constant_dynamic-update-slice_fusion), channel_id=1, source_target_pairs={{0,32},{4,12},{8,40},{12,20},{16,48},{20,28},{24,56},{28,4},{32,64... | collective-permute-start | bytes 307208 | tf_op jit(solution)/shard_map/ppermute | solution.py:66
  13.1 8.7 %collective-permute-start.3 = (bf16[4,40,1280]{2,1,0:T(8,128)(2,1)S(1)}, bf16[4,40,1280]{2,1,0:T(8,128)(2,1)S(1)}, u32[]{:S(2)}, u32[]{:S(2)}) collective-permute-start(bf16[4,40,1280]{2,1,0:T(8,128)(2,1)S(1)} %pad_maximum_fusion.1), channel_id=1, source_target_pairs={{0,16},{4,68},{8,24},{12,76},{16,0},{20,84},{24,8},{28,92},{32,48}... | collective-permute-start | bytes 1228808 | tf_op jit(solution)/shard_map/ppermute | solution.py:66
  16.0 10.3 %collective-permute-start.4 = (bf16[4,40,1280]{2,1,0:T(8,128)(2,1)S(1)}, bf16[4,40,1280]{2,1,0:T(8,128)(2,1)S(1)}, u32[]{:S(2)}, u32[]{:S(2)}) collective-permute-start(bf16[4,40,1280]{2,1,0:T(8,128)(2,1)S(1)} %pad_maximum_fusion.1), channel_id=1, source_target_pairs={{0,8},{4,36},{8,16},{12,44},{16,24},{20,52},{24,0},{28,60},{32,40}... | collective-permute-start | bytes 1228808 | tf_op jit(solution)/shard_map/ppermute | solution.py:66
  16.3 10.0 %collective-permute-start.5 = (bf16[4,40,1280]{2,1,0:T(8,128)(2,1)S(1)}, bf16[4,40,1280]{2,1,0:T(8,128)(2,1)S(1)}, u32[]{:S(2)}, u32[]{:S(2)}) collective-permute-start(bf16[4,40,1280]{2,1,0:T(8,128)(2,1)S(1)} %pad_maximum_fusion.1), channel_id=1, source_target_pairs={{0,24},{4,100},{8,0},{12,108},{16,8},{20,116},{24,16},{28,124},{32... | collective-permute-start | bytes 1228808 | tf_op jit(solution)/shard_map/ppermute | solution.py:66
  26.5 2.6 %copy-start.1 = (bf16[4,4,40,1280]{3,2,1,0:T(8,128)(2,1)}, bf16[4,4,40,1280]{3,2,1,0:T(8,128)(2,1)S(1)}, u32[]{:S(2)}) copy-start(bf16[4,4,40,1280]{3,2,1,0:T(8,128)(2,1)S(1)} %pad_maximum_fusion) | copy-start | bytes 4915204
  26.6 5.8 %collective-permute-start.6 = (bf16[16,40,1280]{2,1,0:T(8,128)(2,1)S(1)}, bf16[16,40,1280]{2,1,0:T(8,128)(2,1)}, u32[]{:S(2)}, u32[]{:S(2)}) collective-permute-start(bf16[16,40,1280]{2,1,0:T(8,128)(2,1)S(1)} %bitcast.57), channel_id=1, source_target_pairs={{0,4},{4,0},{8,12},{12,8},{16,20},{20,16},{24,28},{28,24},{32,36},... | collective-permute-start | bytes 4915208 | tf_op jit(solution)/shard_map/ppermute | solution.py:422
  44.0 6.3 %collective-permute-start.7 = (f32[8,1536]{1,0:T(8,128)S(1)}, f32[8,1536]{1,0:T(8,128)S(1)}, u32[]{:S(2)}, u32[]{:S(2)}) collective-permute-start(f32[8,1536]{1,0:T(8,128)S(1)} %get-tuple-element.40.refs_0_), channel_id=1, source_target_pairs={{0,2},{1,3},{2,0},{3,1},{4,6},{5,7},{6,4},{7,5},{8,10},{9,11},{10,... | collective-permute-start | bytes 147464 | tf_op jit(solution)/shard_map/ppermute | solution.py:425
  47.6 4.2 %collective-permute-start.8 = (f32[8,1536]{1,0:T(8,128)S(1)}, f32[8,1536]{1,0:T(8,128)S(1)}, u32[]{:S(2)}, u32[]{:S(2)}) collective-permute-start(f32[8,1536]{1,0:T(8,128)S(1)} %get-tuple-element.40.refs_0_), channel_id=1, source_target_pairs={{0,1},{1,2},{2,3},{3,0},{4,5},{5,6},{6,7},{7,4},{8,9},{9,10},{10,1... | collective-permute-start | bytes 147464 | tf_op jit(solution)/shard_map/ppermute | solution.py:425
  48.4 3.4 %collective-permute-start.9 = (f32[8,1536]{1,0:T(8,128)S(1)}, f32[8,1536]{1,0:T(8,128)}, u32[]{:S(2)}, u32[]{:S(2)}) collective-permute-start(f32[8,1536]{1,0:T(8,128)S(1)} %get-tuple-element.40.refs_0_), channel_id=1, source_target_pairs={{0,3},{1,0},{2,1},{3,2},{4,7},{5,4},{6,5},{7,6},{8,11},{9,8},{10,9... | collective-permute-start | bytes 147464 | tf_op jit(solution)/shard_map/ppermute | solution.py:425
  56.0 15.9 %collective-permute-start.11 = (bf16[384,640]{1,0:T(8,128)(2,1)}, bf16[384,640]{1,0:T(8,128)(2,1)}, u32[]{:S(2)}, u32[]{:S(2)}) collective-permute-start(bf16[384,640]{1,0:T(8,128)(2,1)} %get-tuple-element.46), channel_id=1, source_target_pairs={{0,3},{1,0},{2,1},{3,2},{4,7},{5,4},{6,5},{7,6},{8,11},{9,8},{10,9... | collective-permute-start | bytes 1474568 | tf_op jit(solution)/shard_map/ppermute | solution.py:430
  58.8 14.3 %collective-permute-start.10 = (bf16[384,640]{1,0:T(8,128)(2,1)}, bf16[384,640]{1,0:T(8,128)(2,1)}, u32[]{:S(2)}, u32[]{:S(2)}) collective-permute-start(bf16[384,640]{1,0:T(8,128)(2,1)} %get-tuple-element.44), channel_id=1, source_target_pairs={{0,1},{1,2},{2,3},{3,0},{4,5},{5,6},{6,7},{7,4},{8,9},{9,10},{10,1... | collective-permute-start | bytes 1474568 | tf_op jit(solution)/shard_map/ppermute | solution.py:429
  58.8 18.1 %copy-start.2 = (bf16[1536,1280]{1,0:T(8,128)(2,1)S(1)}, bf16[1536,1280]{1,0:T(8,128)(2,1)}, u32[]{:S(2)}) copy-start(bf16[1536,1280]{1,0:T(8,128)(2,1)} %memory_ref.1) | copy-start | bytes 11796484
  69.2 17.0 %collective-permute-start.12 = (bf16[384,640]{1,0:T(8,128)(2,1)S(1)}, bf16[384,640]{1,0:T(8,128)(2,1)S(1)}, u32[]{:S(2)}, u32[]{:S(2)}) collective-permute-start(bf16[384,640]{1,0:T(8,128)(2,1)S(1)} %get-tuple-element.49), channel_id=1, source_target_pairs={{0,1},{1,2},{2,3},{3,0},{4,5},{5,6},{6,7},{7,4},{8,9},{9,10},{10,1... | collective-permute-start | bytes 1474568 | tf_op jit(solution)/shard_map/ppermute | solution.py:434
  69.2 17.0 %collective-permute-start.13 = (bf16[384,640]{1,0:T(8,128)(2,1)S(1)}, bf16[384,640]{1,0:T(8,128)(2,1)S(1)}, u32[]{:S(2)}, u32[]{:S(2)}) collective-permute-start(bf16[384,640]{1,0:T(8,128)(2,1)S(1)} %get-tuple-element.50), channel_id=1, source_target_pairs={{0,3},{1,0},{2,1},{3,2},{4,7},{5,4},{6,5},{7,6},{8,11},{9,8},{10,9... | collective-permute-start | bytes 1474568 | tf_op jit(solution)/shard_map/ppermute | solution.py:435
  74.2 17.6 %collective-permute-start.14 = (bf16[384,640]{1,0:T(8,128)(2,1)S(1)}, bf16[384,640]{1,0:T(8,128)(2,1)S(1)}, u32[]{:S(2)}, u32[]{:S(2)}) collective-permute-start(bf16[384,640]{1,0:T(8,128)(2,1)S(1)} %add_convert_fusion.2), channel_id=1, source_target_pairs={{0,1},{1,2},{2,3},{3,0},{4,5},{5,6},{6,7},{7,4},{8,9},{9,10},{10,1... | collective-permute-start | bytes 1474568 | tf_op jit(solution)/shard_map/ppermute | solution.py:439
  74.3 17.6 %collective-permute-start.15 = (bf16[384,640]{1,0:T(8,128)(2,1)S(1)}, bf16[384,640]{1,0:T(8,128)(2,1)S(1)}, u32[]{:S(2)}, u32[]{:S(2)}) collective-permute-start(bf16[384,640]{1,0:T(8,128)(2,1)S(1)} %add_convert_fusion.1), channel_id=1, source_target_pairs={{0,3},{1,0},{2,1},{3,2},{4,7},{5,4},{6,5},{7,6},{8,11},{9,8},{10,9... | collective-permute-start | bytes 1474568 | tf_op jit(solution)/shard_map/ppermute | solution.py:440
  84.8 10.1 %copy-start.3 = (s32[1,2176]{1,0:T(1,128)S(1)}, s32[1,2176]{1,0:T(1,128)}, u32[]{:S(2)}) copy-start(s32[1,2176]{1,0:T(1,128)} %pad_add_fusion) | copy-start | bytes 26116
  91.9 12.8 %collective-permute-start.16 = (bf16[16,40,1280]{2,1,0:T(8,128)(2,1)S(1)}, bf16[16,40,1280]{2,1,0:T(8,128)(2,1)}, u32[]{:S(2)}, u32[]{:S(2)}) collective-permute-start(bf16[16,40,1280]{2,1,0:T(8,128)(2,1)S(1)} %get-tuple-element.62), channel_id=1, source_target_pairs={{0,4},{4,0},{8,12},{12,8},{16,20},{20,16},{24,28},{28,24},{32,36},... | collective-permute-start | bytes 4915208 | tf_op jit(solution)/shard_map/ppermute | solution.py:450
  104.7 60.8 %all-to-all-start = ((bf16[128,48,256]{2,1,0:T(8,128)(2,1)}), bf16[128,48,256]{2,1,0:T(8,128)(2,1)S(1)}, u32[]{:S(2)}, u32[]{:S(2)}) async-start(bf16[128,48,256]{2,1,0:T(8,128)(2,1)} %bitcast.55), calls=%async_computation | async-start | bytes 6291456 | tf_op jit(solution)/shard_map/all_to_all | solution.py:462
  114.8 1.2 copy-start
  116.9 37.0 %collective-permute-start.17 = (bf16[4,40,1280]{2,1,0:T(8,128)(2,1)}, bf16[4,40,1280]{2,1,0:T(8,128)(2,1)}, u32[]{:S(2)}, u32[]{:S(2)}) collective-permute-start(bf16[4,40,1280]{2,1,0:T(8,128)(2,1)} %get-tuple-element.79), channel_id=1, source_target_pairs={{0,64},{4,20},{8,72},{12,28},{16,80},{20,4},{24,88},{28,12},{32,96... | collective-permute-start | bytes 1228808 | tf_op jit(solution)/shard_map/ppermute | solution.py:72
  119.8 38.2 %collective-permute-start.18 = (bf16[4,40,1280]{2,1,0:T(8,128)(2,1)}, bf16[4,40,1280]{2,1,0:T(8,128)(2,1)}, u32[]{:S(2)}, u32[]{:S(2)}) collective-permute-start(bf16[4,40,1280]{2,1,0:T(8,128)(2,1)} %get-tuple-element.81), channel_id=1, source_target_pairs={{0,32},{4,12},{8,40},{12,20},{16,48},{20,28},{24,56},{28,4},{32,64... | collective-permute-start | bytes 1228808 | tf_op jit(solution)/shard_map/ppermute | solution.py:72
  120.1 37.9 %collective-permute-start.19 = (bf16[4,40,1280]{2,1,0:T(8,128)(2,1)S(1)}, bf16[4,40,1280]{2,1,0:T(8,128)(2,1)}, u32[]{:S(2)}, u32[]{:S(2)}) collective-permute-start(bf16[4,40,1280]{2,1,0:T(8,128)(2,1)S(1)} %get-tuple-element.80), channel_id=1, source_target_pairs={{0,96},{4,28},{8,104},{12,4},{16,112},{20,12},{24,120},{28,20},{32... | collective-permute-start | bytes 1228808 | tf_op jit(solution)/shard_map/ppermute | solution.py:72
  160.3 16.9 %collective-permute-start.20 = (bf16[40,1280]{1,0:T(8,128)(2,1)}, bf16[40,1280]{1,0:T(8,128)(2,1)}, u32[]{:S(2)}, u32[]{:S(2)}) collective-permute-start(bf16[40,1280]{1,0:T(8,128)(2,1)} %get-tuple-element.84), channel_id=1, source_target_pairs={{0,16},{4,68},{8,24},{12,76},{16,0},{20,84},{24,8},{28,92},{32,48}... | collective-permute-start | bytes 307208 | tf_op jit(solution)/shard_map/ppermute | solution.py:72
  162.8 14.4 %collective-permute-start.21 = (bf16[40,1280]{1,0:T(8,128)(2,1)}, bf16[40,1280]{1,0:T(8,128)(2,1)}, u32[]{:S(2)}, u32[]{:S(2)}) collective-permute-start(bf16[40,1280]{1,0:T(8,128)(2,1)} %get-tuple-element.83), channel_id=1, source_target_pairs={{0,8},{4,36},{8,16},{12,44},{16,24},{20,52},{24,0},{28,60},{32,40}... | collective-permute-start | bytes 307208 | tf_op jit(solution)/shard_map/ppermute | solution.py:72
  163.3 13.9 %collective-permute-start.22 = (bf16[40,1280]{1,0:T(8,128)(2,1)S(1)}, bf16[40,1280]{1,0:T(8,128)(2,1)}, u32[]{:S(2)}, u32[]{:S(2)}) collective-permute-start(bf16[40,1280]{1,0:T(8,128)(2,1)S(1)} %get-tuple-element.82), channel_id=1, source_target_pairs={{0,24},{4,100},{8,0},{12,108},{16,8},{20,116},{24,16},{28,124},{32... | collective-permute-start | bytes 307208 | tf_op jit(solution)/shard_map/ppermute | solution.py:72

commit v9 on v8

--- a/solution.py
+++ b/solution.py
@@ -1,3 +1,4 @@
+import functools
 import math
 
 import jax
@@ -306,9 +307,8 @@
     )(slot // TILE, slot % TILE, numbers, *parts)
 
 
-def adam_kernel(
-    tile_ref, spot_ref, rows_ref, table_ref, first_ref, second_ref, new_table_ref, new_first_ref, new_second_ref
-):
+def adam_kernel(part, tile_ref, spot_ref, rows_ref, table_ref, first_ref, second_ref, *outs):
+    new_table_ref, new_first_ref, new_second_ref = outs[-3:]
     steps = table_ref.shape[0] // TILE
     width = table_ref.shape[1]
     entries = rows_ref.shape[0]
@@ -316,7 +316,7 @@
     place = lax.broadcasted_iota(jnp.int32, (TILE, chunk), 0).astype(jnp.bfloat16)
     one, zero = jnp.ones((), jnp.bfloat16), jnp.zeros((), jnp.bfloat16)
     for s in range(steps):
-        here = pl.program_id(0) * steps + s
+        here = (pl.program_id(0) + part * pl.num_programs(0)) * steps + s
         grad = jnp.zeros((TILE, width), jnp.float32)
         for k in range(0, entries, chunk):
             spot = jnp.where(tile_ref[:, k : k + chunk] == here, spot_ref[:, k : k + chunk], -1)
@@ -332,18 +332,16 @@
         new_second_ref[at, :] = new_second
 
 
-def adam_rows(got, embed_table, first_moment, second_moment):
-    rows_dev, width = embed_table.shape
+def adam_rows(part, tile, spot, got_rows, tables, done):
+    rows_dev, width = tables[0].shape
     per_step = 2 * TILE
-    block = pl.BlockSpec((per_step, width), lambda i: (i, 0))
-    tile = got[:, SLOT_CAP, :SLOTS].astype(jnp.int32).reshape(1, -1)
-    spot = got[:, SLOT_CAP + 1, :SLOTS].astype(jnp.int32).reshape(1, -1)
-    got_rows = got.reshape(-1, width)
+    steps = rows_dev // per_step // 2
+    block = pl.BlockSpec((per_step, width), lambda i: (i + part * steps, 0))
     whole = pl.BlockSpec(tile.shape, lambda i: (0, 0))
     return pl.pallas_call(
-        adam_kernel,
-        out_shape=(jax.ShapeDtypeStruct((rows_dev, width), jnp.float32),) * 3,
-        grid=(rows_dev // per_step,),
+        functools.partial(adam_kernel, part),
+        out_shape=(pltpu.HBM((rows_dev, width), jnp.float32),) * 3,
+        grid=(steps,),
         in_specs=[
             whole,
             whole,
@@ -351,11 +349,13 @@
             block,
             block,
             block,
-        ],
+        ]
+        + [pl.BlockSpec(memory_space=pl.ANY)] * len(done),
         out_specs=(block,) * 3,
+        input_output_aliases={6: 0, 7: 1, 8: 2} if done else {},
         compiler_params=pltpu.CompilerParams(vmem_limit_bytes=26 * 1024 * 1024),
-        name="adam_rows",
-    )(tile, spot, got_rows, *in_hbm(embed_table, first_moment, second_moment))
+        name="adam_first" if part == 0 else "adam_second",
+    )(tile, spot, got_rows, *in_hbm(*tables), *done)
 
 
 def route(my_ids, owners, rows_dev, row_width):
@@ -457,18 +457,24 @@
     )
     send_rows, other = lax.optimization_barrier((send_rows, other))
     chip_grads = sum_on_chip(other, kept, c)
-    line_grads = ring_sum(chip_grads, jnp.where(c == 0, x, y), along_first).astype(jnp.bfloat16)
-    pieces = ring_pieces(line_grads, jnp.where(c == 0, y, x), along_second)
-    got_rows = lax.all_to_all(
+    line_pieces = ring_pieces(chip_grads, jnp.where(c == 0, x, y), along_first)
+    got = lax.all_to_all(
         send_rows.reshape(owners, SLOTS, row_width),
         ("dp", "tensor"),
         split_axis=0,
         concat_axis=0,
         tiled=True,
     )
-    new_table, new_first, new_second = adam_rows(
-        got_rows, embed_table, first_moment, second_moment
-    )
+    tile = got[:, SLOT_CAP, :SLOTS].astype(jnp.int32).reshape(1, -1)
+    spot_row = got[:, SLOT_CAP + 1, :SLOTS].astype(jnp.int32).reshape(1, -1)
+    got_rows = got.reshape(-1, row_width)
+    tables = (embed_table, first_moment, second_moment)
+    done = adam_rows(0, tile, spot_row, got_rows, tables, ())
+    line_pieces, done = lax.optimization_barrier((line_pieces, tuple(done)))
+    line_grads = sum(p.astype(jnp.float32) for p in line_pieces).astype(jnp.bfloat16)
+    line_grads, tile = lax.optimization_barrier((line_grads, tile))
+    pieces = ring_pieces(line_grads, jnp.where(c == 0, y, x), along_second)
+    new_table, new_first, new_second = adam_rows(1, tile, spot_row, got_rows, tables, done)
     pieces, new_second = lax.optimization_barrier((pieces, new_second))
     weight_sums = sum(p.astype(jnp.float32) for p in pieces)
     half = weight_sums.shape[1] // 2

time: 180 us -> 176 us (0.978)
  Pallas kernels: 47 us -> 49.5 us
  starting transfers between devices: 48.4 us -> 46 us
    ppermute x6, waiting for transfers between devices: 35.5 us -> 0.02 us  [ring_pieces(): lax.ppermute(lax.dynamic_index_in_dim(tiles, (here + d) % 4, 0, keepdims=...]
    all_to_all x1, waiting for transfers between devices: 0.01 us -> 35 us  [body(): lax.all_to_all(send_rows.reshape(owners, SLOTS, row_width), ('dp', 'tenso...]
    pallas_call x1 -> x2, Pallas kernels: 11 us -> 13.5 us  [adam_rows(): pl.pallas_call(functools.partial(adam_kernel, part), out_shape=(pltpu.HBM...]
    ppermute x6, starting transfers between devices: 10.7 us -> 8.4 us  [ring_pieces(): lax.ppermute(lax.dynamic_index_in_dim(tiles, (here + d) % 4, 0, keepdims=...]
  transfers between devices with their start and end apart: 24 -> 24, of which waited for: 8 -> 7; matrix products, arithmetic and copies ran while one was open for 14% -> 13% of each run, Pallas kernels for 17% -> 19%
where the time goes in v9:
time: 176 us
  waiting for transfers between devices  53 us (30%)
  Pallas kernels  49.5 us (28%)
  starting transfers between devices  46 us (26%)
  matrix products  10.8 us (6%)
  other arithmetic  9.46 us (5%)
  local copies, waits for them, and re-layouts  6.07 us (3%)
    all_to_all x1, waiting for transfers between devices, body(): lax.all_to_all(send_rows.reshape(owners, SLOTS, row_width), ('dp', 'tenso...  35 us
    pallas_call x2, Pallas kernels, grads(): pl.pallas_call(grads_kernel, out_shape=(pltpu.HBM(both_shape, jnp.bfloat1...  14.5 us
    pallas_call x2, Pallas kernels, adam_rows(): pl.pallas_call(functools.partial(adam_kernel, part), out_shape=(pltpu.HBM...  13.5 us
    pallas_call x1, Pallas kernels, project(): pl.pallas_call(project_kernel, out_shape=(jax.ShapeDtypeStruct((mem, 2 *...  11.7 us
    ppermute x6, starting transfers between devices, ring_gather(): return [shard] + [lax.ppermute(shard, 'dp', perm_of(d)) for d in STEPS]  10.1 us
    pallas_call x1, Pallas kernels, pack_rows(): pl.pallas_call(pack_kernel, out_shape=pltpu.HBM((total_slots, width), jnp...  9.74 us
    ppermute x6, starting transfers between devices, ring_pieces(): lax.ppermute(lax.dynamic_index_in_dim(tiles, (here + d) % 4, 0, keepdims=...  8.4 us
    dot_general x1, matrix products, body(): lax.dot_general(memory, both, (((0,), (0,)), ((), ())), preferred_element...  7.79 us
  transfers between devices with their start and end apart: 24, of which 7 were waited for; matrix products, arithmetic and copies ran while one was open for 13% of the time, Pallas kernels for 19%

profile of v9, /device:TPU:1, one launch (start us, length us, event | category | flops | bytes accessed | tf_op | source)
XLA Modules:
  0.0 175.9 jit_solution(8571715544987187507)
XLA Ops:
  0.6 0.8 constant_dynamic-update-slice_fusion.1
  1.4 0.8 constant_dynamic-update-slice_fusion
  2.3 3.6 %collective-permute-start.2 = (bf16[40,1280]{1,0:T(8,128)(2,1)S(1)}, bf16[40,1280]{1,0:T(8,128)(2,1)S(1)}, u32[]{:S(2)}, u32[]{:S(2)}) collective-permute-start(bf16[40,1280]{1,0:T(8,128)(2,1)S(1)} %constant_dynamic-update-slice_fusion), channel_id=1, source_target_pairs={{0,96},{4,28},{8,104},{12,4},{16,112},{20,12},{24,120},{28,20},{32... | collective-permute-start | bytes 307208 | tf_op jit(solution)/shard_map/ppermute | solution.py:67
  5.8 0.3 collective-permute-start
  6.2 0.7 collective-permute-start.1
  6.9 0.7 dynamic-slice_bitcast_fusion.10
  7.6 1.8 %fusion.2 = f32[1920]{0:T(1024)S(1)} fusion(s32[1920]{0:T(1024)S(1)} %get-tuple-element.120), kind=kOutput, calls=%fused_computation.9 | convolution fusion | flops 948877440 | bytes 15360 | tf_op jit(solution)/shard_map/dot_general | solution.py:372
  9.4 1.5 select_convert_fusion.2
  10.9 1.2 fusion.3
  12.3 0.6 pad_add_fusion
  13.1 2.8 %collective-permute-start.3 = (bf16[4,40,1280]{2,1,0:T(8,128)(2,1)S(1)}, bf16[4,40,1280]{2,1,0:T(8,128)(2,1)S(1)}, u32[]{:S(2)}, u32[]{:S(2)}) collective-permute-start(bf16[4,40,1280]{2,1,0:T(8,128)(2,1)S(1)} %pad_maximum_fusion.1), channel_id=1, source_target_pairs={{0,16},{4,68},{8,24},{12,76},{16,0},{20,84},{24,8},{28,92},{32,48}... | collective-permute-start | bytes 1228808 | tf_op jit(solution)/shard_map/ppermute | solution.py:67
  16.0 0.3 collective-permute-start.4
  16.3 2.4 %collective-permute-start.5 = (bf16[4,40,1280]{2,1,0:T(8,128)(2,1)S(1)}, bf16[4,40,1280]{2,1,0:T(8,128)(2,1)S(1)}, u32[]{:S(2)}, u32[]{:S(2)}) collective-permute-start(bf16[4,40,1280]{2,1,0:T(8,128)(2,1)S(1)} %pad_maximum_fusion.1), channel_id=1, source_target_pairs={{0,24},{4,100},{8,0},{12,108},{16,8},{20,116},{24,16},{28,124},{32... | collective-permute-start | bytes 1228808 | tf_op jit(solution)/shard_map/ppermute | solution.py:67
  18.6 3.2 %collective-permute-done.3 = bf16[4,40,1280]{2,1,0:T(8,128)(2,1)S(1)} collective-permute-done((bf16[4,40,1280]{2,1,0:T(8,128)(2,1)S(1)}, bf16[4,40,1280]{2,1,0:T(8,128)(2,1)S(1)}, u32[]{:S(2)}, u32[]{:S(2)}) %collective-permute-start.3) | collective-permute-done | bytes 409632 | tf_op jit(solution)/shard_map/ppermute | solution.py:67
  21.9 4.3 %collective-permute-done.4 = bf16[4,40,1280]{2,1,0:T(8,128)(2,1)S(1)} collective-permute-done((bf16[4,40,1280]{2,1,0:T(8,128)(2,1)S(1)}, bf16[4,40,1280]{2,1,0:T(8,128)(2,1)S(1)}, u32[]{:S(2)}, u32[]{:S(2)}) %collective-permute-start.4) | collective-permute-done | bytes 409632 | tf_op jit(solution)/shard_map/ppermute | solution.py:67
  26.3 0.2 pad_maximum_fusion
  26.6 2.5 %collective-permute-start.6 = (bf16[16,40,1280]{2,1,0:T(8,128)(2,1)S(1)}, bf16[16,40,1280]{2,1,0:T(8,128)(2,1)}, u32[]{:S(2)}, u32[]{:S(2)}) collective-permute-start(bf16[16,40,1280]{2,1,0:T(8,128)(2,1)S(1)} %bitcast.57), channel_id=1, source_target_pairs={{0,4},{4,0},{8,12},{12,8},{16,20},{20,16},{24,28},{28,24},{32,36},... | collective-permute-start | bytes 4915208 | tf_op jit(solution)/shard_map/ppermute | solution.py:422
  29.1 3.2 %collective-permute-done.6.got_ref = bf16[16,40,1280]{2,1,0:T(8,128)(2,1)} collective-permute-done((bf16[16,40,1280]{2,1,0:T(8,128)(2,1)S(1)}, bf16[16,40,1280]{2,1,0:T(8,128)(2,1)}, u32[]{:S(2)}, u32[]{:S(2)}) %collective-permute-start.6) | collective-permute-done | bytes 1638432 | tf_op jit(solution)/shard_map/ppermute | solution.py:422
  32.3 11.7 %project.1 = (bf16[1280,1280]{1,0:T(8,128)(2,1)S(1)}, f32[1536,640]{1,0:T(8,128)}, f32[8,1536]{1,0:T(8,128)S(1)}) custom-call(s32[3]{0:T(128)S(1)} %pad_add_fusion.3.spot_ref, bf16[16,40,1280]{2,1,0:T(8,128)(2,1)} %bitcast.58, bf16[16,40,1280]{2,1,0:T(8,128)(2,1)} %collective-permute-done.6.got_ref, bf16[1536,1280]{1,0:T(8,128)(2,1)} %memory_ref.1, ...), custom_call_target="tpu_custom_call" | custom-call | tf_op jit(solution)/shard_map/project/pallas_call | solution.py:146
  44.0 3.6 %collective-permute-start.7 = (f32[8,1536]{1,0:T(8,128)S(1)}, f32[8,1536]{1,0:T(8,128)S(1)}, u32[]{:S(2)}, u32[]{:S(2)}) collective-permute-start(f32[8,1536]{1,0:T(8,128)S(1)} %get-tuple-element.52.refs_0_), channel_id=1, source_target_pairs={{0,2},{1,3},{2,0},{3,1},{4,6},{5,7},{6,4},{7,5},{8,10},{9,11},{10,... | collective-permute-start | bytes 147464 | tf_op jit(solution)/shard_map/ppermute | solution.py:425
  47.6 0.7 collective-permute-start.8
  48.4 1.9 %collective-permute-start.9 = (f32[8,1536]{1,0:T(8,128)S(1)}, f32[8,1536]{1,0:T(8,128)}, u32[]{:S(2)}, u32[]{:S(2)}) collective-permute-start(f32[8,1536]{1,0:T(8,128)S(1)} %get-tuple-element.52.refs_0_), channel_id=1, source_target_pairs={{0,3},{1,0},{2,1},{3,2},{4,7},{5,4},{6,5},{7,6},{8,11},{9,8},{10,9... | collective-permute-start | bytes 147464 | tf_op jit(solution)/shard_map/ppermute | solution.py:425
  50.3 1.5 collective-permute-done.8.refs_2_
  51.8 4.2 %grads_far.1 = (bf16[384,1280]{1,0:T(8,128)(2,1)}, bf16[384,640]{1,0:T(8,128)(2,1)}, bf16[384,640]{1,0:T(8,128)(2,1)}) custom-call(s32[1]{0:T(128)} %bitcast.3.order_ref, f32[8,1536]{1,0:T(8,128)S(1)} %get-tuple-element.52.refs_0_, f32[8,1536]{1,0:T(8,128)S(1)} %collective-permute-done.7.refs_1_, f32[8,1536]{1,0:T(8,128)S(1)} %collective-permute-done.8.refs_2_, ...), custom_call_target="tpu_custom_call" | custom-call | tf_op jit(solution)/shard_map/grads_far/pallas_call | solution.py:230
  56.0 2.8 %collective-permute-start.11 = (bf16[384,640]{1,0:T(8,128)(2,1)}, bf16[384,640]{1,0:T(8,128)(2,1)}, u32[]{:S(2)}, u32[]{:S(2)}) collective-permute-start(bf16[384,640]{1,0:T(8,128)(2,1)} %get-tuple-element.58), channel_id=1, source_target_pairs={{0,3},{1,0},{2,1},{3,2},{4,7},{5,4},{6,5},{7,6},{8,11},{9,8},{10,9... | collective-permute-start | bytes 1474568 | tf_op jit(solution)/shard_map/ppermute | solution.py:430
  58.8 10.4 %grads_near.1 = (bf16[1536,1280]{1,0:T(8,128)(2,1)}, bf16[384,640]{1,0:T(8,128)(2,1)S(1)}, bf16[384,640]{1,0:T(8,128)(2,1)S(1)}, bf16[384,640]{1,0:T(8,128)(2,1)...) custom-call(s32[4]{0:T(128)S(1)} %pad_add_fusion.2.order_ref, ...), custom_call_target="tpu_custom_call" | custom-call | tf_op jit(solution)/shard_map/grads_near/pallas_call | solution.py:230
  69.2 2.7 %collective-permute-start.13 = (bf16[384,640]{1,0:T(8,128)(2,1)S(1)}, bf16[384,640]{1,0:T(8,128)(2,1)S(1)}, u32[]{:S(2)}, u32[]{:S(2)}) collective-permute-start(bf16[384,640]{1,0:T(8,128)(2,1)S(1)} %get-tuple-element.62), channel_id=1, source_target_pairs={{0,3},{1,0},{2,1},{3,2},{4,7},{5,4},{6,5},{7,6},{8,11},{9,8},{10,9... | collective-permute-start | bytes 1474568 | tf_op jit(solution)/shard_map/ppermute | solution.py:435
  71.9 1.2 add_convert_fusion.1
  73.0 1.2 add_convert_fusion.2
  74.3 2.7 %collective-permute-start.15 = (bf16[384,640]{1,0:T(8,128)(2,1)S(1)}, bf16[384,640]{1,0:T(8,128)(2,1)S(1)}, u32[]{:S(2)}, u32[]{:S(2)}) collective-permute-start(bf16[384,640]{1,0:T(8,128)(2,1)S(1)} %add_convert_fusion.1), channel_id=1, source_target_pairs={{0,3},{1,0},{2,1},{3,2},{4,7},{5,4},{6,5},{7,6},{8,11},{9,8},{10,9... | collective-permute-start | bytes 1474568 | tf_op jit(solution)/shard_map/ppermute | solution.py:440
  77.0 7.8 %convolution_convert_fusion = bf16[1280,1280]{0,1:T(8,128)(2,1)S(1)} fusion(bf16[1536,1280]{1,0:T(8,128)(2,1)} %get-tuple-element.60, bf16[1536,1280]{1,0:T(8,128)(2,1)S(1)} %copy-done.1), kind=kOutput, calls=%fused_computation.2 | convolution fusion | flops 5034803200 | bytes 11141120 | tf_op jit(solution)/shard_map/dot_general | solution.py:441
  84.8 1.4 dynamic-slice_bitcast_fusion
  86.2 5.7 %collective-permute-done.14.l2 = bf16[384,640]{1,0:T(8,128)(2,1)S(1)} collective-permute-done((bf16[384,640]{1,0:T(8,128)(2,1)S(1)}, bf16[384,640]{1,0:T(8,128)(2,1)S(1)}, u32[]{:S(2)}, u32[]{:S(2)}) %collective-permute-start.14) | collective-permute-done | bytes 491552 | tf_op jit(solution)/shard_map/ppermute | solution.py:439
  91.8 3.0 %collective-permute-start.16 = (bf16[16,40,1280]{2,1,0:T(8,128)(2,1)S(1)}, bf16[16,40,1280]{2,1,0:T(8,128)(2,1)}, u32[]{:S(2)}, u32[]{:S(2)}) collective-permute-start(bf16[16,40,1280]{2,1,0:T(8,128)(2,1)S(1)} %get-tuple-element.74), channel_id=1, source_target_pairs={{0,4},{4,0},{8,12},{12,8},{16,20},{20,16},{24,28},{28,24},{32,36},... | collective-permute-start | bytes 4915208 | tf_op jit(solution)/shard_map/ppermute | solution.py:450
  94.9 9.7 %pack_rows.1 = bf16[6144,256]{1,0:T(8,128)(2,1)} custom-call(s32[1,2176]{1,0:T(1,128)S(1)} %and_select_fusion.1.tile_ref, s32[1,2176]{1,0:T(1,128)S(1)} %get-tuple-element.99.spot_ref, bf16[256,256]{1,0:T(8,128)(2,1)S(1)} %pad.4.numbers_ref, bf16[384,640]{1,0:T(8,128)(2,1)S(1)} %get-tuple-element.68.l1, bf16[384,640]{1,0:T(8,128)(2,1)S(1)} %collective-permute-done.14.l2, ...), custom_call_target="tpu_custom_call" | custom-call | tf_op jit(solution)/shard_map/pack_rows/pallas_call | solution.py:293
  104.7 7.5 %all-to-all-start = ((bf16[128,48,256]{2,1,0:T(8,128)(2,1)}), bf16[128,48,256]{2,1,0:T(8,128)(2,1)S(1)}, u32[]{:S(2)}, u32[]{:S(2)}) async-start(bf16[128,48,256]{2,1,0:T(8,128)(2,1)} %bitcast.55), calls=%async_computation | async-start | bytes 6291456 | tf_op jit(solution)/shard_map/all_to_all | solution.py:461
  112.3 2.3 %add_convert_fusion = bf16[16,40,1280]{2,1,0:T(8,128)(2,1)S(1)} fusion(bf16[16,40,1280]{2,1,0:T(8,128)(2,1)} %collective-permute-done.16, bf16[16,40,1280]{2,1,0:T(8,128)(2,1)} %get-tuple-element.65), kind=kLoop, calls=%fused_computation.3 | loop fusion | flops 3276800 | bytes 4915200 | tf_op jit(solution)/shard_map/convert_element_type | solution.py:92
  114.8 1.2 dynamic-slice_bitcast_fusion.2
  116.0 2.9 %collective-permute-start.17 = (bf16[4,40,1280]{2,1,0:T(8,128)(2,1)}, bf16[4,40,1280]{2,1,0:T(8,128)(2,1)}, u32[]{:S(2)}, u32[]{:S(2)}) collective-permute-start(bf16[4,40,1280]{2,1,0:T(8,128)(2,1)} %get-tuple-element.105), channel_id=1, source_target_pairs={{0,64},{4,20},{8,72},{12,28},{16,80},{20,4},{24,88},{28,12},{32,96... | collective-permute-start | bytes 1228808 | tf_op jit(solution)/shard_map/ppermute | solution.py:73
  118.9 0.3 collective-permute-start.18
  119.2 2.3 %collective-permute-start.19 = (bf16[4,40,1280]{2,1,0:T(8,128)(2,1)}, bf16[4,40,1280]{2,1,0:T(8,128)(2,1)}, u32[]{:S(2)}, u32[]{:S(2)}) collective-permute-start(bf16[4,40,1280]{2,1,0:T(8,128)(2,1)} %get-tuple-element.103), channel_id=1, source_target_pairs={{0,96},{4,28},{8,104},{12,4},{16,112},{20,12},{24,120},{28,20},{32... | collective-permute-start | bytes 1228808 | tf_op jit(solution)/shard_map/ppermute | solution.py:73
  121.6 35.0 %all-to-all-done = bf16[128,48,256]{2,1,0:T(8,128)(2,1)S(1)} async-done(((bf16[128,48,256]{2,1,0:T(8,128)(2,1)}), bf16[128,48,256]{2,1,0:T(8,128)(2,1)S(1)}, u32[]{:S(2)}, u32[]{:S(2)}) %all-to-all-start) | async-done | bytes 3145760 | tf_op jit(solution)/shard_map/all_to_all | solution.py:461
  156.5 0.5 fusion.12
  157.2 6.8 %adam_first.1 = (f32[2048,256]{1,0:T(8,128)}, f32[2048,256]{1,0:T(8,128)}, f32[2048,256]{1,0:T(8,128)}) custom-call(s32[1,6144]{1,0:T(1,128)S(1)} %reshape.233.tile_ref, s32[1,6144]{1,0:T(1,128)S(1)} %reshape.234.spot_ref, bf16[6144,256]{1,0:T(8,128)(2,1)S(1)} %bitcast.53, f32[2048,256]{1,0:T(8,128)} %table_ref.3, f32[2048,256]{1,0:T(8,128)} %first_ref.3, ...), custom_call_target="tpu_custom_call" | custom-call | tf_op jit(solution)/shard_map/adam_first/pallas_call | solution.py:341
  164.0 1.5 add_convert_fusion.3
  165.7 2.7 %collective-permute-start.22 = (bf16[40,1280]{1,0:T(8,128)(2,1)S(1)}, bf16[40,1280]{1,0:T(8,128)(2,1)S(1)}, u32[]{:S(2)}, u32[]{:S(2)}) collective-permute-start(bf16[40,1280]{1,0:T(8,128)(2,1)S(1)} %get-tuple-element.107), channel_id=1, source_target_pairs={{0,24},{4,100},{8,0},{12,108},{16,8},{20,116},{24,16},{28,124},{32... | collective-permute-start | bytes 307208 | tf_op jit(solution)/shard_map/ppermute | solution.py:73
  168.4 6.7 %adam_second.1 = (f32[2048,256]{1,0:T(8,128)}, f32[2048,256]{1,0:T(8,128)}, f32[2048,256]{1,0:T(8,128)}) custom-call(s32[1,6144]{1,0:T(1,128)S(1)} %reshape.233.tile_ref, s32[1,6144]{1,0:T(1,128)S(1)} %reshape.234.spot_ref, bf16[6144,256]{1,0:T(8,128)(2,1)S(1)} %bitcast.54, ...), custom_call_target="tpu_custom_call", output_to_operand_aliasing={{0}: (6, {}), {1}: (7, {}), {2}: (8, {})} | custom-call | tf_op jit(solution)/shard_map/adam_second/pallas_call | solution.py:341
  175.2 0.7 fusion.22
  (53 shorter events, 1.4 us)
Async XLA Ops:
  2.3 10.8 %collective-permute-start.2 = (bf16[40,1280]{1,0:T(8,128)(2,1)S(1)}, bf16[40,1280]{1,0:T(8,128)(2,1)S(1)}, u32[]{:S(2)}, u32[]{:S(2)}) collective-permute-start(bf16[40,1280]{1,0:T(8,128)(2,1)S(1)} %constant_dynamic-update-slice_fusion), channel_id=1, source_target_pairs={{0,96},{4,28},{8,104},{12,4},{16,112},{20,12},{24,120},{28,20},{32... | collective-permute-start | bytes 307208 | tf_op jit(solution)/shard_map/ppermute | solution.py:67
  5.8 7.2 %collective-permute-start = (bf16[40,1280]{1,0:T(8,128)(2,1)S(1)}, bf16[40,1280]{1,0:T(8,128)(2,1)S(1)}, u32[]{:S(2)}, u32[]{:S(2)}) collective-permute-start(bf16[40,1280]{1,0:T(8,128)(2,1)S(1)} %constant_dynamic-update-slice_fusion), channel_id=1, source_target_pairs={{0,64},{4,20},{8,72},{12,28},{16,80},{20,4},{24,88},{28,12},{32,96... | collective-permute-start | bytes 307208 | tf_op jit(solution)/shard_map/ppermute | solution.py:67
  6.2 6.9 %collective-permute-start.1 = (bf16[40,1280]{1,0:T(8,128)(2,1)S(1)}, bf16[40,1280]{1,0:T(8,128)(2,1)S(1)}, u32[]{:S(2)}, u32[]{:S(2)}) collective-permute-start(bf16[40,1280]{1,0:T(8,128)(2,1)S(1)} %constant_dynamic-update-slice_fusion), channel_id=1, source_target_pairs={{0,32},{4,12},{8,40},{12,20},{16,48},{20,28},{24,56},{28,4},{32,64... | collective-permute-start | bytes 307208 | tf_op jit(solution)/shard_map/ppermute | solution.py:67
  13.1 8.7 %collective-permute-start.3 = (bf16[4,40,1280]{2,1,0:T(8,128)(2,1)S(1)}, bf16[4,40,1280]{2,1,0:T(8,128)(2,1)S(1)}, u32[]{:S(2)}, u32[]{:S(2)}) collective-permute-start(bf16[4,40,1280]{2,1,0:T(8,128)(2,1)S(1)} %pad_maximum_fusion.1), channel_id=1, source_target_pairs={{0,16},{4,68},{8,24},{12,76},{16,0},{20,84},{24,8},{28,92},{32,48}... | collective-permute-start | bytes 1228808 | tf_op jit(solution)/shard_map/ppermute | solution.py:67
  16.0 10.3 %collective-permute-start.4 = (bf16[4,40,1280]{2,1,0:T(8,128)(2,1)S(1)}, bf16[4,40,1280]{2,1,0:T(8,128)(2,1)S(1)}, u32[]{:S(2)}, u32[]{:S(2)}) collective-permute-start(bf16[4,40,1280]{2,1,0:T(8,128)(2,1)S(1)} %pad_maximum_fusion.1), channel_id=1, source_target_pairs={{0,8},{4,36},{8,16},{12,44},{16,24},{20,52},{24,0},{28,60},{32,40}... | collective-permute-start | bytes 1228808 | tf_op jit(solution)/shard_map/ppermute | solution.py:67
  16.3 10.0 %collective-permute-start.5 = (bf16[4,40,1280]{2,1,0:T(8,128)(2,1)S(1)}, bf16[4,40,1280]{2,1,0:T(8,128)(2,1)S(1)}, u32[]{:S(2)}, u32[]{:S(2)}) collective-permute-start(bf16[4,40,1280]{2,1,0:T(8,128)(2,1)S(1)} %pad_maximum_fusion.1), channel_id=1, source_target_pairs={{0,24},{4,100},{8,0},{12,108},{16,8},{20,116},{24,16},{28,124},{32... | collective-permute-start | bytes 1228808 | tf_op jit(solution)/shard_map/ppermute | solution.py:67
  26.5 2.6 %copy-start = (bf16[4,4,40,1280]{3,2,1,0:T(8,128)(2,1)}, bf16[4,4,40,1280]{3,2,1,0:T(8,128)(2,1)S(1)}, u32[]{:S(2)}) copy-start(bf16[4,4,40,1280]{3,2,1,0:T(8,128)(2,1)S(1)} %pad_maximum_fusion) | copy-start | bytes 4915204
  26.6 5.8 %collective-permute-start.6 = (bf16[16,40,1280]{2,1,0:T(8,128)(2,1)S(1)}, bf16[16,40,1280]{2,1,0:T(8,128)(2,1)}, u32[]{:S(2)}, u32[]{:S(2)}) collective-permute-start(bf16[16,40,1280]{2,1,0:T(8,128)(2,1)S(1)} %bitcast.57), channel_id=1, source_target_pairs={{0,4},{4,0},{8,12},{12,8},{16,20},{20,16},{24,28},{28,24},{32,36},... | collective-permute-start | bytes 4915208 | tf_op jit(solution)/shard_map/ppermute | solution.py:422
  44.0 6.3 %collective-permute-start.7 = (f32[8,1536]{1,0:T(8,128)S(1)}, f32[8,1536]{1,0:T(8,128)S(1)}, u32[]{:S(2)}, u32[]{:S(2)}) collective-permute-start(f32[8,1536]{1,0:T(8,128)S(1)} %get-tuple-element.52.refs_0_), channel_id=1, source_target_pairs={{0,2},{1,3},{2,0},{3,1},{4,6},{5,7},{6,4},{7,5},{8,10},{9,11},{10,... | collective-permute-start | bytes 147464 | tf_op jit(solution)/shard_map/ppermute | solution.py:425
  47.6 4.2 %collective-permute-start.8 = (f32[8,1536]{1,0:T(8,128)S(1)}, f32[8,1536]{1,0:T(8,128)S(1)}, u32[]{:S(2)}, u32[]{:S(2)}) collective-permute-start(f32[8,1536]{1,0:T(8,128)S(1)} %get-tuple-element.52.refs_0_), channel_id=1, source_target_pairs={{0,1},{1,2},{2,3},{3,0},{4,5},{5,6},{6,7},{7,4},{8,9},{9,10},{10,1... | collective-permute-start | bytes 147464 | tf_op jit(solution)/shard_map/ppermute | solution.py:425
  48.4 3.4 %collective-permute-start.9 = (f32[8,1536]{1,0:T(8,128)S(1)}, f32[8,1536]{1,0:T(8,128)}, u32[]{:S(2)}, u32[]{:S(2)}) collective-permute-start(f32[8,1536]{1,0:T(8,128)S(1)} %get-tuple-element.52.refs_0_), channel_id=1, source_target_pairs={{0,3},{1,0},{2,1},{3,2},{4,7},{5,4},{6,5},{7,6},{8,11},{9,8},{10,9... | collective-permute-start | bytes 147464 | tf_op jit(solution)/shard_map/ppermute | solution.py:425
  56.0 15.9 %collective-permute-start.11 = (bf16[384,640]{1,0:T(8,128)(2,1)}, bf16[384,640]{1,0:T(8,128)(2,1)}, u32[]{:S(2)}, u32[]{:S(2)}) collective-permute-start(bf16[384,640]{1,0:T(8,128)(2,1)} %get-tuple-element.58), channel_id=1, source_target_pairs={{0,3},{1,0},{2,1},{3,2},{4,7},{5,4},{6,5},{7,6},{8,11},{9,8},{10,9... | collective-permute-start | bytes 1474568 | tf_op jit(solution)/shard_map/ppermute | solution.py:430
  58.7 14.3 %collective-permute-start.10 = (bf16[384,640]{1,0:T(8,128)(2,1)}, bf16[384,640]{1,0:T(8,128)(2,1)}, u32[]{:S(2)}, u32[]{:S(2)}) collective-permute-start(bf16[384,640]{1,0:T(8,128)(2,1)} %get-tuple-element.56), channel_id=1, source_target_pairs={{0,1},{1,2},{2,3},{3,0},{4,5},{5,6},{6,7},{7,4},{8,9},{9,10},{10,1... | collective-permute-start | bytes 1474568 | tf_op jit(solution)/shard_map/ppermute | solution.py:429
  58.8 18.1 %copy-start.1 = (bf16[1536,1280]{1,0:T(8,128)(2,1)S(1)}, bf16[1536,1280]{1,0:T(8,128)(2,1)}, u32[]{:S(2)}) copy-start(bf16[1536,1280]{1,0:T(8,128)(2,1)} %memory_ref.1) | copy-start | bytes 11796484
  69.2 17.0 %collective-permute-start.12 = (bf16[384,640]{1,0:T(8,128)(2,1)S(1)}, bf16[384,640]{1,0:T(8,128)(2,1)S(1)}, u32[]{:S(2)}, u32[]{:S(2)}) collective-permute-start(bf16[384,640]{1,0:T(8,128)(2,1)S(1)} %get-tuple-element.61), channel_id=1, source_target_pairs={{0,1},{1,2},{2,3},{3,0},{4,5},{5,6},{6,7},{7,4},{8,9},{9,10},{10,1... | collective-permute-start | bytes 1474568 | tf_op jit(solution)/shard_map/ppermute | solution.py:434
  69.2 17.0 %collective-permute-start.13 = (bf16[384,640]{1,0:T(8,128)(2,1)S(1)}, bf16[384,640]{1,0:T(8,128)(2,1)S(1)}, u32[]{:S(2)}, u32[]{:S(2)}) collective-permute-start(bf16[384,640]{1,0:T(8,128)(2,1)S(1)} %get-tuple-element.62), channel_id=1, source_target_pairs={{0,3},{1,0},{2,1},{3,2},{4,7},{5,4},{6,5},{7,6},{8,11},{9,8},{10,9... | collective-permute-start | bytes 1474568 | tf_op jit(solution)/shard_map/ppermute | solution.py:435
  74.2 17.6 %collective-permute-start.14 = (bf16[384,640]{1,0:T(8,128)(2,1)S(1)}, bf16[384,640]{1,0:T(8,128)(2,1)S(1)}, u32[]{:S(2)}, u32[]{:S(2)}) collective-permute-start(bf16[384,640]{1,0:T(8,128)(2,1)S(1)} %add_convert_fusion.2), channel_id=1, source_target_pairs={{0,1},{1,2},{2,3},{3,0},{4,5},{5,6},{6,7},{7,4},{8,9},{9,10},{10,1... | collective-permute-start | bytes 1474568 | tf_op jit(solution)/shard_map/ppermute | solution.py:439
  74.3 17.6 %collective-permute-start.15 = (bf16[384,640]{1,0:T(8,128)(2,1)S(1)}, bf16[384,640]{1,0:T(8,128)(2,1)S(1)}, u32[]{:S(2)}, u32[]{:S(2)}) collective-permute-start(bf16[384,640]{1,0:T(8,128)(2,1)S(1)} %add_convert_fusion.1), channel_id=1, source_target_pairs={{0,3},{1,0},{2,1},{3,2},{4,7},{5,4},{6,5},{7,6},{8,11},{9,8},{10,9... | collective-permute-start | bytes 1474568 | tf_op jit(solution)/shard_map/ppermute | solution.py:440
  84.7 10.1 %copy-start.3 = (s32[1,2176]{1,0:T(1,128)S(1)}, s32[1,2176]{1,0:T(1,128)}, u32[]{:S(2)}) copy-start(s32[1,2176]{1,0:T(1,128)} %pad_add_fusion) | copy-start | bytes 26116
  91.8 12.8 %collective-permute-start.16 = (bf16[16,40,1280]{2,1,0:T(8,128)(2,1)S(1)}, bf16[16,40,1280]{2,1,0:T(8,128)(2,1)}, u32[]{:S(2)}, u32[]{:S(2)}) collective-permute-start(bf16[16,40,1280]{2,1,0:T(8,128)(2,1)S(1)} %get-tuple-element.74), channel_id=1, source_target_pairs={{0,4},{4,0},{8,12},{12,8},{16,20},{20,16},{24,28},{28,24},{32,36},... | collective-permute-start | bytes 4915208 | tf_op jit(solution)/shard_map/ppermute | solution.py:450
  104.7 51.8 %all-to-all-start = ((bf16[128,48,256]{2,1,0:T(8,128)(2,1)}), bf16[128,48,256]{2,1,0:T(8,128)(2,1)S(1)}, u32[]{:S(2)}, u32[]{:S(2)}) async-start(bf16[128,48,256]{2,1,0:T(8,128)(2,1)} %bitcast.55), calls=%async_computation | async-start | bytes 6291456 | tf_op jit(solution)/shard_map/all_to_all | solution.py:461
  116.0 48.0 %collective-permute-start.17 = (bf16[4,40,1280]{2,1,0:T(8,128)(2,1)}, bf16[4,40,1280]{2,1,0:T(8,128)(2,1)}, u32[]{:S(2)}, u32[]{:S(2)}) collective-permute-start(bf16[4,40,1280]{2,1,0:T(8,128)(2,1)} %get-tuple-element.105), channel_id=1, source_target_pairs={{0,64},{4,20},{8,72},{12,28},{16,80},{20,4},{24,88},{28,12},{32,96... | collective-permute-start | bytes 1228808 | tf_op jit(solution)/shard_map/ppermute | solution.py:73
  118.9 45.1 %collective-permute-start.18 = (bf16[4,40,1280]{2,1,0:T(8,128)(2,1)}, bf16[4,40,1280]{2,1,0:T(8,128)(2,1)}, u32[]{:S(2)}, u32[]{:S(2)}) collective-permute-start(bf16[4,40,1280]{2,1,0:T(8,128)(2,1)} %get-tuple-element.104), channel_id=1, source_target_pairs={{0,32},{4,12},{8,40},{12,20},{16,48},{20,28},{24,56},{28,4},{32,64... | collective-permute-start | bytes 1228808 | tf_op jit(solution)/shard_map/ppermute | solution.py:73
  119.2 44.8 %collective-permute-start.19 = (bf16[4,40,1280]{2,1,0:T(8,128)(2,1)}, bf16[4,40,1280]{2,1,0:T(8,128)(2,1)}, u32[]{:S(2)}, u32[]{:S(2)}) collective-permute-start(bf16[4,40,1280]{2,1,0:T(8,128)(2,1)} %get-tuple-element.103), channel_id=1, source_target_pairs={{0,96},{4,28},{8,104},{12,4},{16,112},{20,12},{24,120},{28,20},{32... | collective-permute-start | bytes 1228808 | tf_op jit(solution)/shard_map/ppermute | solution.py:73
  157.2 6.8 %copy-start.2 = (bf16[4,40,1280]{2,1,0:T(8,128)(2,1)S(1)}, bf16[4,40,1280]{2,1,0:T(8,128)(2,1)}, u32[]{:S(2)}) copy-start(bf16[4,40,1280]{2,1,0:T(8,128)(2,1)} %get-tuple-element.80) | copy-start | bytes 1228804
  165.5 9.6 %collective-permute-start.20 = (bf16[40,1280]{1,0:T(8,128)(2,1)S(1)}, bf16[40,1280]{1,0:T(8,128)(2,1)S(1)}, u32[]{:S(2)}, u32[]{:S(2)}) collective-permute-start(bf16[40,1280]{1,0:T(8,128)(2,1)S(1)} %get-tuple-element.109), channel_id=1, source_target_pairs={{0,16},{4,68},{8,24},{12,76},{16,0},{20,84},{24,8},{28,92},{32,48}... | collective-permute-start | bytes 307208 | tf_op jit(solution)/shard_map/ppermute | solution.py:73
  165.6 9.5 %collective-permute-start.21 = (bf16[40,1280]{1,0:T(8,128)(2,1)S(1)}, bf16[40,1280]{1,0:T(8,128)(2,1)S(1)}, u32[]{:S(2)}, u32[]{:S(2)}) collective-permute-start(bf16[40,1280]{1,0:T(8,128)(2,1)S(1)} %get-tuple-element.108), channel_id=1, source_target_pairs={{0,8},{4,36},{8,16},{12,44},{16,24},{20,52},{24,0},{28,60},{32,40}... | collective-permute-start | bytes 307208 | tf_op jit(solution)/shard_map/ppermute | solution.py:73
  165.7 9.4 %collective-permute-start.22 = (bf16[40,1280]{1,0:T(8,128)(2,1)S(1)}, bf16[40,1280]{1,0:T(8,128)(2,1)S(1)}, u32[]{:S(2)}, u32[]{:S(2)}) collective-permute-start(bf16[40,1280]{1,0:T(8,128)(2,1)S(1)} %get-tuple-element.107), channel_id=1, source_target_pairs={{0,24},{4,100},{8,0},{12,108},{16,8},{20,116},{24,16},{28,124},{32... | collective-permute-start | bytes 307208 | tf_op jit(solution)/shard_map/ppermute | solution.py:73

commit v10 on v9

--- a/solution.py
+++ b/solution.py
@@ -476,10 +476,9 @@
     pieces = ring_pieces(line_grads, jnp.where(c == 0, y, x), along_second)
     new_table, new_first, new_second = adam_rows(1, tile, spot_row, got_rows, tables, done)
     pieces, new_second = lax.optimization_barrier((pieces, new_second))
-    weight_sums = sum(p.astype(jnp.float32) for p in pieces)
-    half = weight_sums.shape[1] // 2
-    key_weight_grad = weight_sums[:, :half]
-    value_weight_grad = weight_sums[:, half:]
+    half = pieces[0].shape[1] // 2
+    key_weight_grad = sum(p[:, :half].astype(jnp.float32) for p in pieces)
+    value_weight_grad = sum(p[:, half:].astype(jnp.float32) for p in pieces)
     return (key_weight_grad, value_weight_grad, new_table, new_first, new_second)
 
 

time: 176 us -> 176 us (level)
  no operation moved by 1% of the time
where the time goes in v10:
time: 176 us
  waiting for transfers between devices  53 us (30%)
  Pallas kernels  49.5 us (28%)
  starting transfers between devices  46 us (26%)
  matrix products  10.8 us (6%)
  other arithmetic  10.1 us (6%)
  local copies, waits for them, and re-layouts  5.37 us (3%)
    all_to_all x1, waiting for transfers between devices, body(): lax.all_to_all(send_rows.reshape(owners, SLOTS, row_width), ('dp', 'tenso...  35 us
    pallas_call x2, Pallas kernels, grads(): pl.pallas_call(grads_kernel, out_shape=(pltpu.HBM(both_shape, jnp.bfloat1...  14.5 us
    pallas_call x2, Pallas kernels, adam_rows(): pl.pallas_call(functools.partial(adam_kernel, part), out_shape=(pltpu.HBM...  13.5 us
    pallas_call x1, Pallas kernels, project(): pl.pallas_call(project_kernel, out_shape=(jax.ShapeDtypeStruct((mem, 2 *...  11.7 us
    ppermute x6, starting transfers between devices, ring_gather(): return [shard] + [lax.ppermute(shard, 'dp', perm_of(d)) for d in STEPS]  10.1 us
    pallas_call x1, Pallas kernels, pack_rows(): pl.pallas_call(pack_kernel, out_shape=pltpu.HBM((total_slots, width), jnp...  9.74 us
    ppermute x6, starting transfers between devices, ring_pieces(): lax.ppermute(lax.dynamic_index_in_dim(tiles, (here + d) % 4, 0, keepdims=...  8.4 us
    dot_general x1, matrix products, body(): lax.dot_general(memory, both, (((0,), (0,)), ((), ())), preferred_element...  7.79 us
  transfers between devices with their start and end apart: 24, of which 7 were waited for; matrix products, arithmetic and copies ran while one was open for 13% of the time, Pallas kernels for 19%

profile of v10, /device:TPU:1, one launch (start us, length us, event | category | flops | bytes accessed | tf_op | source)
XLA Modules:
  0.0 175.9 jit_solution(11886284638389389860)
XLA Ops:
  0.6 0.8 constant_dynamic-update-slice_fusion.1
  1.4 0.8 constant_dynamic-update-slice_fusion
  2.3 3.6 %collective-permute-start.2 = (bf16[40,1280]{1,0:T(8,128)(2,1)S(1)}, bf16[40,1280]{1,0:T(8,128)(2,1)S(1)}, u32[]{:S(2)}, u32[]{:S(2)}) collective-permute-start(bf16[40,1280]{1,0:T(8,128)(2,1)S(1)} %constant_dynamic-update-slice_fusion), channel_id=1, source_target_pairs={{0,96},{4,28},{8,104},{12,4},{16,112},{20,12},{24,120},{28,20},{32... | collective-permute-start | bytes 307208 | tf_op jit(solution)/shard_map/ppermute | solution.py:67
  5.8 0.3 collective-permute-start
  6.2 0.7 collective-permute-start.1
  6.9 0.7 dynamic-slice_bitcast_fusion.10
  7.6 1.8 %fusion.2 = f32[1920]{0:T(1024)S(1)} fusion(s32[1920]{0:T(1024)S(1)} %get-tuple-element.120), kind=kOutput, calls=%fused_computation.9 | convolution fusion | flops 948877440 | bytes 15360 | tf_op jit(solution)/shard_map/dot_general | solution.py:372
  9.4 1.5 select_convert_fusion.2
  10.9 1.2 fusion.3
  12.3 0.6 pad_add_fusion
  13.1 2.8 %collective-permute-start.3 = (bf16[4,40,1280]{2,1,0:T(8,128)(2,1)S(1)}, bf16[4,40,1280]{2,1,0:T(8,128)(2,1)S(1)}, u32[]{:S(2)}, u32[]{:S(2)}) collective-permute-start(bf16[4,40,1280]{2,1,0:T(8,128)(2,1)S(1)} %pad_maximum_fusion.1), channel_id=1, source_target_pairs={{0,16},{4,68},{8,24},{12,76},{16,0},{20,84},{24,8},{28,92},{32,48}... | collective-permute-start | bytes 1228808 | tf_op jit(solution)/shard_map/ppermute | solution.py:67
  16.0 0.3 collective-permute-start.4
  16.3 2.4 %collective-permute-start.5 = (bf16[4,40,1280]{2,1,0:T(8,128)(2,1)S(1)}, bf16[4,40,1280]{2,1,0:T(8,128)(2,1)S(1)}, u32[]{:S(2)}, u32[]{:S(2)}) collective-permute-start(bf16[4,40,1280]{2,1,0:T(8,128)(2,1)S(1)} %pad_maximum_fusion.1), channel_id=1, source_target_pairs={{0,24},{4,100},{8,0},{12,108},{16,8},{20,116},{24,16},{28,124},{32... | collective-permute-start | bytes 1228808 | tf_op jit(solution)/shard_map/ppermute | solution.py:67
  18.6 3.2 %collective-permute-done.3 = bf16[4,40,1280]{2,1,0:T(8,128)(2,1)S(1)} collective-permute-done((bf16[4,40,1280]{2,1,0:T(8,128)(2,1)S(1)}, bf16[4,40,1280]{2,1,0:T(8,128)(2,1)S(1)}, u32[]{:S(2)}, u32[]{:S(2)}) %collective-permute-start.3) | collective-permute-done | bytes 409632 | tf_op jit(solution)/shard_map/ppermute | solution.py:67
  21.9 4.3 %collective-permute-done.4 = bf16[4,40,1280]{2,1,0:T(8,128)(2,1)S(1)} collective-permute-done((bf16[4,40,1280]{2,1,0:T(8,128)(2,1)S(1)}, bf16[4,40,1280]{2,1,0:T(8,128)(2,1)S(1)}, u32[]{:S(2)}, u32[]{:S(2)}) %collective-permute-start.4) | collective-permute-done | bytes 409632 | tf_op jit(solution)/shard_map/ppermute | solution.py:67
  26.3 0.2 pad_maximum_fusion
  26.6 2.5 %collective-permute-start.6 = (bf16[16,40,1280]{2,1,0:T(8,128)(2,1)S(1)}, bf16[16,40,1280]{2,1,0:T(8,128)(2,1)}, u32[]{:S(2)}, u32[]{:S(2)}) collective-permute-start(bf16[16,40,1280]{2,1,0:T(8,128)(2,1)S(1)} %bitcast.57), channel_id=1, source_target_pairs={{0,4},{4,0},{8,12},{12,8},{16,20},{20,16},{24,28},{28,24},{32,36},... | collective-permute-start | bytes 4915208 | tf_op jit(solution)/shard_map/ppermute | solution.py:422
  29.1 3.2 %collective-permute-done.6.got_ref = bf16[16,40,1280]{2,1,0:T(8,128)(2,1)} collective-permute-done((bf16[16,40,1280]{2,1,0:T(8,128)(2,1)S(1)}, bf16[16,40,1280]{2,1,0:T(8,128)(2,1)}, u32[]{:S(2)}, u32[]{:S(2)}) %collective-permute-start.6) | collective-permute-done | bytes 1638432 | tf_op jit(solution)/shard_map/ppermute | solution.py:422
  32.3 11.7 %project.1 = (bf16[1280,1280]{1,0:T(8,128)(2,1)S(1)}, f32[1536,640]{1,0:T(8,128)}, f32[8,1536]{1,0:T(8,128)S(1)}) custom-call(s32[3]{0:T(128)S(1)} %pad_add_fusion.3.spot_ref, bf16[16,40,1280]{2,1,0:T(8,128)(2,1)} %bitcast.58, bf16[16,40,1280]{2,1,0:T(8,128)(2,1)} %collective-permute-done.6.got_ref, bf16[1536,1280]{1,0:T(8,128)(2,1)} %memory_ref.1, ...), custom_call_target="tpu_custom_call" | custom-call | tf_op jit(solution)/shard_map/project/pallas_call | solution.py:146
  44.0 3.6 %collective-permute-start.7 = (f32[8,1536]{1,0:T(8,128)S(1)}, f32[8,1536]{1,0:T(8,128)S(1)}, u32[]{:S(2)}, u32[]{:S(2)}) collective-permute-start(f32[8,1536]{1,0:T(8,128)S(1)} %get-tuple-element.52.refs_0_), channel_id=1, source_target_pairs={{0,2},{1,3},{2,0},{3,1},{4,6},{5,7},{6,4},{7,5},{8,10},{9,11},{10,... | collective-permute-start | bytes 147464 | tf_op jit(solution)/shard_map/ppermute | solution.py:425
  47.6 0.7 collective-permute-start.8
  48.4 1.9 %collective-permute-start.9 = (f32[8,1536]{1,0:T(8,128)S(1)}, f32[8,1536]{1,0:T(8,128)}, u32[]{:S(2)}, u32[]{:S(2)}) collective-permute-start(f32[8,1536]{1,0:T(8,128)S(1)} %get-tuple-element.52.refs_0_), channel_id=1, source_target_pairs={{0,3},{1,0},{2,1},{3,2},{4,7},{5,4},{6,5},{7,6},{8,11},{9,8},{10,9... | collective-permute-start | bytes 147464 | tf_op jit(solution)/shard_map/ppermute | solution.py:425
  50.3 1.5 collective-permute-done.8.refs_2_
  51.8 4.2 %grads_far.1 = (bf16[384,1280]{1,0:T(8,128)(2,1)}, bf16[384,640]{1,0:T(8,128)(2,1)}, bf16[384,640]{1,0:T(8,128)(2,1)}) custom-call(s32[1]{0:T(128)} %bitcast.3.order_ref, f32[8,1536]{1,0:T(8,128)S(1)} %get-tuple-element.52.refs_0_, f32[8,1536]{1,0:T(8,128)S(1)} %collective-permute-done.7.refs_1_, f32[8,1536]{1,0:T(8,128)S(1)} %collective-permute-done.8.refs_2_, ...), custom_call_target="tpu_custom_call" | custom-call | tf_op jit(solution)/shard_map/grads_far/pallas_call | solution.py:230
  56.0 2.8 %collective-permute-start.11 = (bf16[384,640]{1,0:T(8,128)(2,1)}, bf16[384,640]{1,0:T(8,128)(2,1)}, u32[]{:S(2)}, u32[]{:S(2)}) collective-permute-start(bf16[384,640]{1,0:T(8,128)(2,1)} %get-tuple-element.58), channel_id=1, source_target_pairs={{0,3},{1,0},{2,1},{3,2},{4,7},{5,4},{6,5},{7,6},{8,11},{9,8},{10,9... | collective-permute-start | bytes 1474568 | tf_op jit(solution)/shard_map/ppermute | solution.py:430
  58.8 10.4 %grads_near.1 = (bf16[1536,1280]{1,0:T(8,128)(2,1)}, bf16[384,640]{1,0:T(8,128)(2,1)S(1)}, bf16[384,640]{1,0:T(8,128)(2,1)S(1)}, bf16[384,640]{1,0:T(8,128)(2,1)...) custom-call(s32[4]{0:T(128)S(1)} %pad_add_fusion.2.order_ref, ...), custom_call_target="tpu_custom_call" | custom-call | tf_op jit(solution)/shard_map/grads_near/pallas_call | solution.py:230
  69.2 2.7 %collective-permute-start.13 = (bf16[384,640]{1,0:T(8,128)(2,1)S(1)}, bf16[384,640]{1,0:T(8,128)(2,1)S(1)}, u32[]{:S(2)}, u32[]{:S(2)}) collective-permute-start(bf16[384,640]{1,0:T(8,128)(2,1)S(1)} %get-tuple-element.62), channel_id=1, source_target_pairs={{0,3},{1,0},{2,1},{3,2},{4,7},{5,4},{6,5},{7,6},{8,11},{9,8},{10,9... | collective-permute-start | bytes 1474568 | tf_op jit(solution)/shard_map/ppermute | solution.py:435
  71.9 1.2 add_convert_fusion.1
  73.0 1.2 add_convert_fusion.2
  74.3 2.7 %collective-permute-start.15 = (bf16[384,640]{1,0:T(8,128)(2,1)S(1)}, bf16[384,640]{1,0:T(8,128)(2,1)S(1)}, u32[]{:S(2)}, u32[]{:S(2)}) collective-permute-start(bf16[384,640]{1,0:T(8,128)(2,1)S(1)} %add_convert_fusion.1), channel_id=1, source_target_pairs={{0,3},{1,0},{2,1},{3,2},{4,7},{5,4},{6,5},{7,6},{8,11},{9,8},{10,9... | collective-permute-start | bytes 1474568 | tf_op jit(solution)/shard_map/ppermute | solution.py:440
  77.0 7.8 %convolution_convert_fusion = bf16[1280,1280]{0,1:T(8,128)(2,1)S(1)} fusion(bf16[1536,1280]{1,0:T(8,128)(2,1)} %get-tuple-element.60, bf16[1536,1280]{1,0:T(8,128)(2,1)S(1)} %copy-done.1), kind=kOutput, calls=%fused_computation.2 | convolution fusion | flops 5034803200 | bytes 11141120 | tf_op jit(solution)/shard_map/dot_general | solution.py:441
  84.8 1.4 dynamic-slice_bitcast_fusion
  86.2 5.7 %collective-permute-done.14.l2 = bf16[384,640]{1,0:T(8,128)(2,1)S(1)} collective-permute-done((bf16[384,640]{1,0:T(8,128)(2,1)S(1)}, bf16[384,640]{1,0:T(8,128)(2,1)S(1)}, u32[]{:S(2)}, u32[]{:S(2)}) %collective-permute-start.14) | collective-permute-done | bytes 491552 | tf_op jit(solution)/shard_map/ppermute | solution.py:439
  91.8 3.0 %collective-permute-start.16 = (bf16[16,40,1280]{2,1,0:T(8,128)(2,1)S(1)}, bf16[16,40,1280]{2,1,0:T(8,128)(2,1)}, u32[]{:S(2)}, u32[]{:S(2)}) collective-permute-start(bf16[16,40,1280]{2,1,0:T(8,128)(2,1)S(1)} %get-tuple-element.74), channel_id=1, source_target_pairs={{0,4},{4,0},{8,12},{12,8},{16,20},{20,16},{24,28},{28,24},{32,36},... | collective-permute-start | bytes 4915208 | tf_op jit(solution)/shard_map/ppermute | solution.py:450
  94.9 9.7 %pack_rows.1 = bf16[6144,256]{1,0:T(8,128)(2,1)} custom-call(s32[1,2176]{1,0:T(1,128)S(1)} %and_select_fusion.1.tile_ref, s32[1,2176]{1,0:T(1,128)S(1)} %get-tuple-element.99.spot_ref, bf16[256,256]{1,0:T(8,128)(2,1)S(1)} %pad.4.numbers_ref, bf16[384,640]{1,0:T(8,128)(2,1)S(1)} %get-tuple-element.68.l1, bf16[384,640]{1,0:T(8,128)(2,1)S(1)} %collective-permute-done.14.l2, ...), custom_call_target="tpu_custom_call" | custom-call | tf_op jit(solution)/shard_map/pack_rows/pallas_call | solution.py:293
  104.7 7.5 %all-to-all-start = ((bf16[128,48,256]{2,1,0:T(8,128)(2,1)}), bf16[128,48,256]{2,1,0:T(8,128)(2,1)S(1)}, u32[]{:S(2)}, u32[]{:S(2)}) async-start(bf16[128,48,256]{2,1,0:T(8,128)(2,1)} %bitcast.55), calls=%async_computation | async-start | bytes 6291456 | tf_op jit(solution)/shard_map/all_to_all | solution.py:461
  112.3 2.3 %add_convert_fusion = bf16[16,40,1280]{2,1,0:T(8,128)(2,1)S(1)} fusion(bf16[16,40,1280]{2,1,0:T(8,128)(2,1)} %collective-permute-done.16, bf16[16,40,1280]{2,1,0:T(8,128)(2,1)} %get-tuple-element.65), kind=kLoop, calls=%fused_computation.3 | loop fusion | flops 3276800 | bytes 4915200 | tf_op jit(solution)/shard_map/convert_element_type | solution.py:92
  114.8 1.2 dynamic-slice_bitcast_fusion.2
  116.0 2.9 %collective-permute-start.17 = (bf16[4,40,1280]{2,1,0:T(8,128)(2,1)}, bf16[4,40,1280]{2,1,0:T(8,128)(2,1)}, u32[]{:S(2)}, u32[]{:S(2)}) collective-permute-start(bf16[4,40,1280]{2,1,0:T(8,128)(2,1)} %get-tuple-element.105), channel_id=1, source_target_pairs={{0,64},{4,20},{8,72},{12,28},{16,80},{20,4},{24,88},{28,12},{32,96... | collective-permute-start | bytes 1228808 | tf_op jit(solution)/shard_map/ppermute | solution.py:73
  118.9 0.3 collective-permute-start.18
  119.2 2.3 %collective-permute-start.19 = (bf16[4,40,1280]{2,1,0:T(8,128)(2,1)}, bf16[4,40,1280]{2,1,0:T(8,128)(2,1)}, u32[]{:S(2)}, u32[]{:S(2)}) collective-permute-start(bf16[4,40,1280]{2,1,0:T(8,128)(2,1)} %get-tuple-element.103), channel_id=1, source_target_pairs={{0,96},{4,28},{8,104},{12,4},{16,112},{20,12},{24,120},{28,20},{32... | collective-permute-start | bytes 1228808 | tf_op jit(solution)/shard_map/ppermute | solution.py:73
  121.6 35.0 %all-to-all-done = bf16[128,48,256]{2,1,0:T(8,128)(2,1)S(1)} async-done(((bf16[128,48,256]{2,1,0:T(8,128)(2,1)}), bf16[128,48,256]{2,1,0:T(8,128)(2,1)S(1)}, u32[]{:S(2)}, u32[]{:S(2)}) %all-to-all-start) | async-done | bytes 3145760 | tf_op jit(solution)/shard_map/all_to_all | solution.py:461
  156.5 0.5 fusion.12
  157.2 6.8 %adam_first.1 = (f32[2048,256]{1,0:T(8,128)}, f32[2048,256]{1,0:T(8,128)}, f32[2048,256]{1,0:T(8,128)}) custom-call(s32[1,6144]{1,0:T(1,128)S(1)} %reshape.233.tile_ref, s32[1,6144]{1,0:T(1,128)S(1)} %reshape.234.spot_ref, bf16[6144,256]{1,0:T(8,128)(2,1)S(1)} %bitcast.53, f32[2048,256]{1,0:T(8,128)} %table_ref.3, f32[2048,256]{1,0:T(8,128)} %first_ref.3, ...), custom_call_target="tpu_custom_call" | custom-call | tf_op jit(solution)/shard_map/adam_first/pallas_call | solution.py:341
  164.0 1.5 add_convert_fusion.3
  165.7 2.7 %collective-permute-start.22 = (bf16[40,1280]{1,0:T(8,128)(2,1)S(1)}, bf16[40,1280]{1,0:T(8,128)(2,1)S(1)}, u32[]{:S(2)}, u32[]{:S(2)}) collective-permute-start(bf16[40,1280]{1,0:T(8,128)(2,1)S(1)} %get-tuple-element.109), channel_id=1, source_target_pairs={{0,24},{4,100},{8,0},{12,108},{16,8},{20,116},{24,16},{28,124},{32... | collective-permute-start | bytes 307208 | tf_op jit(solution)/shard_map/ppermute | solution.py:73
  168.4 6.7 %adam_second.1 = (f32[2048,256]{1,0:T(8,128)}, f32[2048,256]{1,0:T(8,128)}, f32[2048,256]{1,0:T(8,128)}) custom-call(s32[1,6144]{1,0:T(1,128)S(1)} %reshape.233.tile_ref, s32[1,6144]{1,0:T(1,128)S(1)} %reshape.234.spot_ref, bf16[6144,256]{1,0:T(8,128)(2,1)S(1)} %bitcast.54, ...), custom_call_target="tpu_custom_call", output_to_operand_aliasing={{0}: (6, {}), {1}: (7, {}), {2}: (8, {})} | custom-call | tf_op jit(solution)/shard_map/adam_second/pallas_call | solution.py:341
  175.1 0.7 convert_add_fusion
  (52 shorter events, 1.4 us)
Async XLA Ops:
  2.3 10.8 %collective-permute-start.2 = (bf16[40,1280]{1,0:T(8,128)(2,1)S(1)}, bf16[40,1280]{1,0:T(8,128)(2,1)S(1)}, u32[]{:S(2)}, u32[]{:S(2)}) collective-permute-start(bf16[40,1280]{1,0:T(8,128)(2,1)S(1)} %constant_dynamic-update-slice_fusion), channel_id=1, source_target_pairs={{0,96},{4,28},{8,104},{12,4},{16,112},{20,12},{24,120},{28,20},{32... | collective-permute-start | bytes 307208 | tf_op jit(solution)/shard_map/ppermute | solution.py:67
  5.8 7.2 %collective-permute-start = (bf16[40,1280]{1,0:T(8,128)(2,1)S(1)}, bf16[40,1280]{1,0:T(8,128)(2,1)S(1)}, u32[]{:S(2)}, u32[]{:S(2)}) collective-permute-start(bf16[40,1280]{1,0:T(8,128)(2,1)S(1)} %constant_dynamic-update-slice_fusion), channel_id=1, source_target_pairs={{0,64},{4,20},{8,72},{12,28},{16,80},{20,4},{24,88},{28,12},{32,96... | collective-permute-start | bytes 307208 | tf_op jit(solution)/shard_map/ppermute | solution.py:67
  6.2 6.9 %collective-permute-start.1 = (bf16[40,1280]{1,0:T(8,128)(2,1)S(1)}, bf16[40,1280]{1,0:T(8,128)(2,1)S(1)}, u32[]{:S(2)}, u32[]{:S(2)}) collective-permute-start(bf16[40,1280]{1,0:T(8,128)(2,1)S(1)} %constant_dynamic-update-slice_fusion), channel_id=1, source_target_pairs={{0,32},{4,12},{8,40},{12,20},{16,48},{20,28},{24,56},{28,4},{32,64... | collective-permute-start | bytes 307208 | tf_op jit(solution)/shard_map/ppermute | solution.py:67
  13.1 8.7 %collective-permute-start.3 = (bf16[4,40,1280]{2,1,0:T(8,128)(2,1)S(1)}, bf16[4,40,1280]{2,1,0:T(8,128)(2,1)S(1)}, u32[]{:S(2)}, u32[]{:S(2)}) collective-permute-start(bf16[4,40,1280]{2,1,0:T(8,128)(2,1)S(1)} %pad_maximum_fusion.1), channel_id=1, source_target_pairs={{0,16},{4,68},{8,24},{12,76},{16,0},{20,84},{24,8},{28,92},{32,48}... | collective-permute-start | bytes 1228808 | tf_op jit(solution)/shard_map/ppermute | solution.py:67
  16.0 10.3 %collective-permute-start.4 = (bf16[4,40,1280]{2,1,0:T(8,128)(2,1)S(1)}, bf16[4,40,1280]{2,1,0:T(8,128)(2,1)S(1)}, u32[]{:S(2)}, u32[]{:S(2)}) collective-permute-start(bf16[4,40,1280]{2,1,0:T(8,128)(2,1)S(1)} %pad_maximum_fusion.1), channel_id=1, source_target_pairs={{0,8},{4,36},{8,16},{12,44},{16,24},{20,52},{24,0},{28,60},{32,40}... | collective-permute-start | bytes 1228808 | tf_op jit(solution)/shard_map/ppermute | solution.py:67
  16.3 10.0 %collective-permute-start.5 = (bf16[4,40,1280]{2,1,0:T(8,128)(2,1)S(1)}, bf16[4,40,1280]{2,1,0:T(8,128)(2,1)S(1)}, u32[]{:S(2)}, u32[]{:S(2)}) collective-permute-start(bf16[4,40,1280]{2,1,0:T(8,128)(2,1)S(1)} %pad_maximum_fusion.1), channel_id=1, source_target_pairs={{0,24},{4,100},{8,0},{12,108},{16,8},{20,116},{24,16},{28,124},{32... | collective-permute-start | bytes 1228808 | tf_op jit(solution)/shard_map/ppermute | solution.py:67
  26.5 2.6 %copy-start = (bf16[4,4,40,1280]{3,2,1,0:T(8,128)(2,1)}, bf16[4,4,40,1280]{3,2,1,0:T(8,128)(2,1)S(1)}, u32[]{:S(2)}) copy-start(bf16[4,4,40,1280]{3,2,1,0:T(8,128)(2,1)S(1)} %pad_maximum_fusion) | copy-start | bytes 4915204
  26.6 5.8 %collective-permute-start.6 = (bf16[16,40,1280]{2,1,0:T(8,128)(2,1)S(1)}, bf16[16,40,1280]{2,1,0:T(8,128)(2,1)}, u32[]{:S(2)}, u32[]{:S(2)}) collective-permute-start(bf16[16,40,1280]{2,1,0:T(8,128)(2,1)S(1)} %bitcast.57), channel_id=1, source_target_pairs={{0,4},{4,0},{8,12},{12,8},{16,20},{20,16},{24,28},{28,24},{32,36},... | collective-permute-start | bytes 4915208 | tf_op jit(solution)/shard_map/ppermute | solution.py:422
  44.0 6.3 %collective-permute-start.7 = (f32[8,1536]{1,0:T(8,128)S(1)}, f32[8,1536]{1,0:T(8,128)S(1)}, u32[]{:S(2)}, u32[]{:S(2)}) collective-permute-start(f32[8,1536]{1,0:T(8,128)S(1)} %get-tuple-element.52.refs_0_), channel_id=1, source_target_pairs={{0,2},{1,3},{2,0},{3,1},{4,6},{5,7},{6,4},{7,5},{8,10},{9,11},{10,... | collective-permute-start | bytes 147464 | tf_op jit(solution)/shard_map/ppermute | solution.py:425
  47.6 4.2 %collective-permute-start.8 = (f32[8,1536]{1,0:T(8,128)S(1)}, f32[8,1536]{1,0:T(8,128)S(1)}, u32[]{:S(2)}, u32[]{:S(2)}) collective-permute-start(f32[8,1536]{1,0:T(8,128)S(1)} %get-tuple-element.52.refs_0_), channel_id=1, source_target_pairs={{0,1},{1,2},{2,3},{3,0},{4,5},{5,6},{6,7},{7,4},{8,9},{9,10},{10,1... | collective-permute-start | bytes 147464 | tf_op jit(solution)/shard_map/ppermute | solution.py:425
  48.4 3.4 %collective-permute-start.9 = (f32[8,1536]{1,0:T(8,128)S(1)}, f32[8,1536]{1,0:T(8,128)}, u32[]{:S(2)}, u32[]{:S(2)}) collective-permute-start(f32[8,1536]{1,0:T(8,128)S(1)} %get-tuple-element.52.refs_0_), channel_id=1, source_target_pairs={{0,3},{1,0},{2,1},{3,2},{4,7},{5,4},{6,5},{7,6},{8,11},{9,8},{10,9... | collective-permute-start | bytes 147464 | tf_op jit(solution)/shard_map/ppermute | solution.py:425
  56.0 15.9 %collective-permute-start.11 = (bf16[384,640]{1,0:T(8,128)(2,1)}, bf16[384,640]{1,0:T(8,128)(2,1)}, u32[]{:S(2)}, u32[]{:S(2)}) collective-permute-start(bf16[384,640]{1,0:T(8,128)(2,1)} %get-tuple-element.58), channel_id=1, source_target_pairs={{0,3},{1,0},{2,1},{3,2},{4,7},{5,4},{6,5},{7,6},{8,11},{9,8},{10,9... | collective-permute-start | bytes 1474568 | tf_op jit(solution)/shard_map/ppermute | solution.py:430
  58.7 14.3 %collective-permute-start.10 = (bf16[384,640]{1,0:T(8,128)(2,1)}, bf16[384,640]{1,0:T(8,128)(2,1)}, u32[]{:S(2)}, u32[]{:S(2)}) collective-permute-start(bf16[384,640]{1,0:T(8,128)(2,1)} %get-tuple-element.56), channel_id=1, source_target_pairs={{0,1},{1,2},{2,3},{3,0},{4,5},{5,6},{6,7},{7,4},{8,9},{9,10},{10,1... | collective-permute-start | bytes 1474568 | tf_op jit(solution)/shard_map/ppermute | solution.py:429
  58.8 18.1 %copy-start.1 = (bf16[1536,1280]{1,0:T(8,128)(2,1)S(1)}, bf16[1536,1280]{1,0:T(8,128)(2,1)}, u32[]{:S(2)}) copy-start(bf16[1536,1280]{1,0:T(8,128)(2,1)} %memory_ref.1) | copy-start | bytes 11796484
  69.2 17.0 %collective-permute-start.12 = (bf16[384,640]{1,0:T(8,128)(2,1)S(1)}, bf16[384,640]{1,0:T(8,128)(2,1)S(1)}, u32[]{:S(2)}, u32[]{:S(2)}) collective-permute-start(bf16[384,640]{1,0:T(8,128)(2,1)S(1)} %get-tuple-element.61), channel_id=1, source_target_pairs={{0,1},{1,2},{2,3},{3,0},{4,5},{5,6},{6,7},{7,4},{8,9},{9,10},{10,1... | collective-permute-start | bytes 1474568 | tf_op jit(solution)/shard_map/ppermute | solution.py:434
  69.2 17.0 %collective-permute-start.13 = (bf16[384,640]{1,0:T(8,128)(2,1)S(1)}, bf16[384,640]{1,0:T(8,128)(2,1)S(1)}, u32[]{:S(2)}, u32[]{:S(2)}) collective-permute-start(bf16[384,640]{1,0:T(8,128)(2,1)S(1)} %get-tuple-element.62), channel_id=1, source_target_pairs={{0,3},{1,0},{2,1},{3,2},{4,7},{5,4},{6,5},{7,6},{8,11},{9,8},{10,9... | collective-permute-start | bytes 1474568 | tf_op jit(solution)/shard_map/ppermute | solution.py:435
  74.2 17.6 %collective-permute-start.14 = (bf16[384,640]{1,0:T(8,128)(2,1)S(1)}, bf16[384,640]{1,0:T(8,128)(2,1)S(1)}, u32[]{:S(2)}, u32[]{:S(2)}) collective-permute-start(bf16[384,640]{1,0:T(8,128)(2,1)S(1)} %add_convert_fusion.2), channel_id=1, source_target_pairs={{0,1},{1,2},{2,3},{3,0},{4,5},{5,6},{6,7},{7,4},{8,9},{9,10},{10,1... | collective-permute-start | bytes 1474568 | tf_op jit(solution)/shard_map/ppermute | solution.py:439
  74.3 17.6 %collective-permute-start.15 = (bf16[384,640]{1,0:T(8,128)(2,1)S(1)}, bf16[384,640]{1,0:T(8,128)(2,1)S(1)}, u32[]{:S(2)}, u32[]{:S(2)}) collective-permute-start(bf16[384,640]{1,0:T(8,128)(2,1)S(1)} %add_convert_fusion.1), channel_id=1, source_target_pairs={{0,3},{1,0},{2,1},{3,2},{4,7},{5,4},{6,5},{7,6},{8,11},{9,8},{10,9... | collective-permute-start | bytes 1474568 | tf_op jit(solution)/shard_map/ppermute | solution.py:440
  84.7 10.1 %copy-start.3 = (s32[1,2176]{1,0:T(1,128)S(1)}, s32[1,2176]{1,0:T(1,128)}, u32[]{:S(2)}) copy-start(s32[1,2176]{1,0:T(1,128)} %pad_add_fusion) | copy-start | bytes 26116
  91.8 12.8 %collective-permute-start.16 = (bf16[16,40,1280]{2,1,0:T(8,128)(2,1)S(1)}, bf16[16,40,1280]{2,1,0:T(8,128)(2,1)}, u32[]{:S(2)}, u32[]{:S(2)}) collective-permute-start(bf16[16,40,1280]{2,1,0:T(8,128)(2,1)S(1)} %get-tuple-element.74), channel_id=1, source_target_pairs={{0,4},{4,0},{8,12},{12,8},{16,20},{20,16},{24,28},{28,24},{32,36},... | collective-permute-start | bytes 4915208 | tf_op jit(solution)/shard_map/ppermute | solution.py:450
  104.7 51.8 %all-to-all-start = ((bf16[128,48,256]{2,1,0:T(8,128)(2,1)}), bf16[128,48,256]{2,1,0:T(8,128)(2,1)S(1)}, u32[]{:S(2)}, u32[]{:S(2)}) async-start(bf16[128,48,256]{2,1,0:T(8,128)(2,1)} %bitcast.55), calls=%async_computation | async-start | bytes 6291456 | tf_op jit(solution)/shard_map/all_to_all | solution.py:461
  116.0 48.0 %collective-permute-start.17 = (bf16[4,40,1280]{2,1,0:T(8,128)(2,1)}, bf16[4,40,1280]{2,1,0:T(8,128)(2,1)}, u32[]{:S(2)}, u32[]{:S(2)}) collective-permute-start(bf16[4,40,1280]{2,1,0:T(8,128)(2,1)} %get-tuple-element.105), channel_id=1, source_target_pairs={{0,64},{4,20},{8,72},{12,28},{16,80},{20,4},{24,88},{28,12},{32,96... | collective-permute-start | bytes 1228808 | tf_op jit(solution)/shard_map/ppermute | solution.py:73
  118.9 45.1 %collective-permute-start.18 = (bf16[4,40,1280]{2,1,0:T(8,128)(2,1)}, bf16[4,40,1280]{2,1,0:T(8,128)(2,1)}, u32[]{:S(2)}, u32[]{:S(2)}) collective-permute-start(bf16[4,40,1280]{2,1,0:T(8,128)(2,1)} %get-tuple-element.104), channel_id=1, source_target_pairs={{0,32},{4,12},{8,40},{12,20},{16,48},{20,28},{24,56},{28,4},{32,64... | collective-permute-start | bytes 1228808 | tf_op jit(solution)/shard_map/ppermute | solution.py:73
  119.2 44.8 %collective-permute-start.19 = (bf16[4,40,1280]{2,1,0:T(8,128)(2,1)}, bf16[4,40,1280]{2,1,0:T(8,128)(2,1)}, u32[]{:S(2)}, u32[]{:S(2)}) collective-permute-start(bf16[4,40,1280]{2,1,0:T(8,128)(2,1)} %get-tuple-element.103), channel_id=1, source_target_pairs={{0,96},{4,28},{8,104},{12,4},{16,112},{20,12},{24,120},{28,20},{32... | collective-permute-start | bytes 1228808 | tf_op jit(solution)/shard_map/ppermute | solution.py:73
  157.2 6.8 %copy-start.2 = (bf16[4,40,1280]{2,1,0:T(8,128)(2,1)S(1)}, bf16[4,40,1280]{2,1,0:T(8,128)(2,1)}, u32[]{:S(2)}) copy-start(bf16[4,40,1280]{2,1,0:T(8,128)(2,1)} %get-tuple-element.80) | copy-start | bytes 1228804
  165.5 9.6 %collective-permute-start.20 = (bf16[40,1280]{1,0:T(8,128)(2,1)S(1)}, bf16[40,1280]{1,0:T(8,128)(2,1)S(1)}, u32[]{:S(2)}, u32[]{:S(2)}) collective-permute-start(bf16[40,1280]{1,0:T(8,128)(2,1)S(1)} %get-tuple-element.111), channel_id=1, source_target_pairs={{0,16},{4,68},{8,24},{12,76},{16,0},{20,84},{24,8},{28,92},{32,48}... | collective-permute-start | bytes 307208 | tf_op jit(solution)/shard_map/ppermute | solution.py:73
  165.6 9.5 %collective-permute-start.21 = (bf16[40,1280]{1,0:T(8,128)(2,1)S(1)}, bf16[40,1280]{1,0:T(8,128)(2,1)S(1)}, u32[]{:S(2)}, u32[]{:S(2)}) collective-permute-start(bf16[40,1280]{1,0:T(8,128)(2,1)S(1)} %get-tuple-element.110), channel_id=1, source_target_pairs={{0,8},{4,36},{8,16},{12,44},{16,24},{20,52},{24,0},{28,60},{32,40}... | collective-permute-start | bytes 307208 | tf_op jit(solution)/shard_map/ppermute | solution.py:73
  165.7 9.4 %collective-permute-start.22 = (bf16[40,1280]{1,0:T(8,128)(2,1)S(1)}, bf16[40,1280]{1,0:T(8,128)(2,1)S(1)}, u32[]{:S(2)}, u32[]{:S(2)}) collective-permute-start(bf16[40,1280]{1,0:T(8,128)(2,1)S(1)} %get-tuple-element.109), channel_id=1, source_target_pairs={{0,24},{4,100},{8,0},{12,108},{16,8},{20,116},{24,16},{28,124},{32... | collective-permute-start | bytes 307208 | tf_op jit(solution)/shard_map/ppermute | solution.py:73
